TPU v7x, 128 devices: a whole 4x4x4 slice. The times are simulated.
128 devices in a mesh: tm: 4 (over z_lo, core), rows: 32 (over y, z_hi, x).
Axes of the slice: x: 4, y: 4, z: 4 (z_hi: 2, z_lo: 2; z = z_hi * 2 + z_lo), core: 2. Of those that a mesh axis runs over, the one named last changes fastest.
Arguments:
- latent_feat: bfloat16 [16, 64, 128, 384], P('tm', 'rows'), may hold values from -6 to 6
- norm_gain: float32 [384], replicated, may hold values from 0.25 to 1.75
- conv_weight: bfloat16 [27, 384, 384], replicated, may hold values from -0.0625 to 0.0625
- rgb_weight: bfloat16 [384, 3], replicated, may hold values from -0.3125 to 0.3125
- real_frames: bfloat16 [3, 16, 64, 128], P(None, 'tm', 'rows'), may hold values from -6 to 6
- disc_first: bfloat16 [27, 64, 3], replicated, may hold values from -0.625 to 0.625
- disc_second: bfloat16 [27, 128, 64], replicated, may hold values from -0.15625 to 0.15625
Outputs:
- decoded: bfloat16 [16, 64, 128, 384], P('tm', 'rows')
- match_map: float32 [16, 64, 128], P('tm', 'rows')
All inputs are finite; a program needn't handle non-finite values.
Results may differ from a plain program's by a relative error of at most 0.0033.
Values may be sent and summed in bfloat16 or wider, within the bound.
No kernel may reach another device: no remote copies, remote signals or barrier semaphores. Data moves between devices by JAX's collectives and lax.ppermute only.
A program may use at most 128 MiB of HBM per device.

v0:
```python
import jax
import jax.numpy as jnp
from jax import lax
from jax.sharding import PartitionSpec as P


def from_behind(block, axis, distance):
    devices = range(lax.axis_size(axis))
    route = [(i - distance, i) for i in devices if i - distance in devices]
    return lax.ppermute(block, axis, route)


def extended_2(cells, sides, width):
    for axis, dim in sides:
        count = lax.axis_size(axis)
        ends = count - 1
        head = lax.slice_in_dim(cells, 0, width, axis=dim)
        tail = lax.slice_in_dim(cells, cells.shape[dim] - width, cells.shape[dim], axis=dim)
        cells = jnp.concatenate(
            [
                lax.ppermute(tail, axis, [(i, (i + 1) % count) for i in range(ends)]),
                cells,
                lax.ppermute(head, axis, [((i + 1) % count, i) for i in range(ends)]),
            ],
            axis=dim,
        )
    return cells


def leaky(value):
    return jnp.maximum(value, 0.2 * value)


def conv_valid(extended, weights):
    frames = extended.shape[1] - 2
    height = extended.shape[2] - 2
    width = extended.shape[3] - 2
    total = jnp.zeros((weights.shape[1], frames, height, width), jnp.float32)
    for tap in range(27):
        dt, dh, dw = (tap // 9, tap // 3 % 3, tap % 3)
        piece = extended[:, dt : dt + frames, dh : dh + height, dw : dw + width]
        total = total + jnp.einsum(
            "oc,cthw->othw", weights[tap], piece, preferred_element_type=jnp.float32
        )
    return leaky(total)


def per_device(
    latent_feat, norm_gain, conv_weight, rgb_weight, real_frames, disc_first, disc_second
):
    feats = latent_feat.astype(jnp.float32)
    normed = feats * lax.rsqrt(jnp.mean(feats * feats, axis=-1, keepdims=True) + 1e-06) * norm_gain
    act = jax.nn.silu(normed).astype(jnp.bfloat16)
    frames, height, width, chans = act.shape
    cached = from_behind(act[frames - 2 :], "tm", 1)
    extended = jnp.concatenate([cached, act], axis=0)
    extended = extended_2(extended, (("rows", 1),), 1)
    extended = jnp.pad(extended, ((0, 0), (0, 0), (1, 1), (0, 0)))
    total = jnp.zeros((frames * height * width, chans), jnp.float32)
    for tap in range(27):
        dt, dh, dw = (tap // 9, tap // 3 % 3, tap % 3)
        piece = extended[dt : dt + frames, dh : dh + height, dw : dw + width].reshape(-1, chans)
        total = total + jnp.dot(piece, conv_weight[tap], preferred_element_type=jnp.float32)
    decoded = (feats + total.reshape(frames, height, width, chans)).astype(jnp.bfloat16)
    colour = jnp.dot(
        decoded.reshape(-1, chans), rgb_weight, preferred_element_type=jnp.float32
    ).astype(jnp.bfloat16)
    fake = jnp.transpose(colour.reshape(frames, height, width, 3), (3, 0, 1, 2))
    stacked = jnp.concatenate([fake, real_frames], axis=0)
    ext_in = extended_2(stacked, (("tm", 1), ("rows", 2)), 1)
    ext_in = jnp.pad(ext_in, ((0, 0), (0, 0), (0, 0), (1, 1)))
    first_fake = conv_valid(ext_in[:3], disc_first).astype(jnp.bfloat16)
    first_real = conv_valid(ext_in[3:], disc_first).astype(jnp.bfloat16)
    both_first = jnp.concatenate([first_fake, first_real], axis=0)
    ext_mid = extended_2(both_first, (("tm", 1), ("rows", 2)), 1)
    ext_mid = jnp.pad(ext_mid, ((0, 0), (0, 0), (0, 0), (1, 1)))
    depth = first_fake.shape[0]
    second_fake = conv_valid(ext_mid[:depth], disc_second).astype(jnp.bfloat16)
    second_real = conv_valid(ext_mid[depth:], disc_second).astype(jnp.bfloat16)
    match_map = jnp.mean(
        jnp.abs(first_fake.astype(jnp.float32) - first_real.astype(jnp.float32)), axis=0
    )
    match_map = match_map + jnp.mean(
        jnp.abs(second_fake.astype(jnp.float32) - second_real.astype(jnp.float32)), axis=0
    )
    return (decoded, match_map)


def solution(mesh):
    placed = (P("tm", "rows", None, None), P(), P(), P(), P(None, "tm", "rows", None), P(), P())
    return jax.shard_map(
        per_device,
        mesh=mesh,
        in_specs=placed,
        out_specs=(P("tm", "rows", None, None), P("tm", "rows", None)),
        check_vma=False,
    )
```

profile of v0, /device:TPU:17, one launch (start us, length us, event | category | flops | bytes accessed | tf_op | source)
XLA Modules:
  0.0 172.2 jit_solution(17012841360301679242)
XLA Ops:
  3.8 4.4 %collective-permute-start = (bf16[2,2,128,384]{3,2,1,0:T(8,128)(2,1)S(1)}, bf16[2,2,128,384]{3,2,1,0:T(8,128)(2,1)S(1)}, u32[]{:S(2)}, u32[]{:S(2)}) collective-permute-start(bf16[2,2,128,384]{3,2,1,0:T(8,128)(2,1)S(1)} %slice.1161), channel_id=1, source_target_pairs={{0,32},{32,64},{64,96},{1,33},{33,65},{65,97},{2,34},{34,66},{66,9... | collective-permute-start | bytes 1179656 | tf_op jit(solution)/shard_map/ppermute | solution.py:10
  9.8 3.0 %collective-permute-done = bf16[2,2,128,384]{3,2,1,0:T(8,128)(2,1)S(1)} collective-permute-done((bf16[2,2,128,384]{3,2,1,0:T(8,128)(2,1)S(1)}, bf16[2,2,128,384]{3,2,1,0:T(8,128)(2,1)S(1)}, u32[]{:S(2)}, u32[]{:S(2)}) %collective-permute-start) | collective-permute-done | bytes 393248 | tf_op jit(solution)/shard_map/ppermute | solution.py:10
  13.0 3.1 %collective-permute-start.1 = (bf16[6,1,128,384]{3,2,1,0:T(8,128)(2,1)S(1)}, bf16[6,1,128,384]{3,2,1,0:T(8,128)(2,1)S(1)}, u32[]{:S(2)}, u32[]{:S(2)}) collective-permute-start(bf16[6,1,128,384]{3,2,1,0:T(8,128)(2,1)S(1)} %get-tuple-element.30), channel_id=1, source_target_pairs={{0,1},{1,2},{2,3},{3,4},{4,5},{5,6},{6,7},{7,8},{8,9},{9,10},{10,1... | collective-permute-start | bytes 1769480 | tf_op jit(solution)/shard_map/ppermute | solution.py:21
  16.1 6.7 %collective-permute-start.2 = (bf16[6,1,128,384]{3,2,1,0:T(8,128)(2,1)S(1)}, bf16[6,1,128,384]{3,2,1,0:T(8,128)(2,1)S(1)}, u32[]{:S(2)}, u32[]{:S(2)}) collective-permute-start(bf16[6,1,128,384]{3,2,1,0:T(8,128)(2,1)S(1)} %get-tuple-element.31), channel_id=1, source_target_pairs={{1,0},{2,1},{3,2},{4,3},{5,4},{6,5},{7,6},{8,7},{9,8},{10,9},{11,1... | collective-permute-start | bytes 1769480 | tf_op jit(solution)/shard_map/ppermute | solution.py:23
  23.0 1.8 %fusion.139 = f32[1024,384]{1,0:T(8,128)} fusion(bf16[1024,384]{1,0:T(8,128)(2,1)S(1)} %bitcast.836, bf16[27,384,384]{2,1,0:T(8,128)(2,1)S(1)} %copy-done.1), kind=kOutput, calls=%fused_computation.240 | convolution fusion | flops 301989888 | bytes 2654208 | tf_op jit(solution)/shard_map/dot_general | solution.py:63
  26.6 3.8 %collective-permute-done.1 = bf16[6,1,128,384]{3,2,1,0:T(8,128)(2,1)S(1)} collective-permute-done((bf16[6,1,128,384]{3,2,1,0:T(8,128)(2,1)S(1)}, bf16[6,1,128,384]{3,2,1,0:T(8,128)(2,1)S(1)}, u32[]{:S(2)}, u32[]{:S(2)}) %collective-permute-start.1) | collective-permute-done | bytes 589856 | tf_op jit(solution)/shard_map/ppermute | solution.py:21
  33.4 1.8 %fusion.115 = f32[1024,384]{1,0:T(8,128)} fusion(bf16[1024,384]{1,0:T(8,128)(2,1)S(1)} %bitcast.834, bf16[27,384,384]{2,1,0:T(8,128)(2,1)S(1)} %copy-done.1), kind=kOutput, calls=%fused_computation.216 | convolution fusion | flops 301989888 | bytes 2654208 | tf_op jit(solution)/shard_map/dot_general | solution.py:63
  35.2 1.9 %fusion.127 = f32[1024,384]{1,0:T(8,128)} fusion(bf16[1024,384]{1,0:T(8,128)(2,1)S(1)} %bitcast.833, bf16[27,384,384]{2,1,0:T(8,128)(2,1)S(1)} %copy-done.1), kind=kOutput, calls=%fused_computation.228 | convolution fusion | flops 301989888 | bytes 2654208 | tf_op jit(solution)/shard_map/dot_general | solution.py:63
  37.0 1.8 %fusion.133 = f32[1024,384]{1,0:T(8,128)} fusion(bf16[1024,384]{1,0:T(8,128)(2,1)S(1)} %bitcast.832, bf16[27,384,384]{2,1,0:T(8,128)(2,1)S(1)} %copy-done.1), kind=kOutput, calls=%fused_computation.234 | convolution fusion | flops 301989888 | bytes 2654208 | tf_op jit(solution)/shard_map/dot_general | solution.py:63
  45.6 3.4 %fusion.477 = (bf16[4,2,128,384]{3,2,1,0:T(8,128)(2,1)S(1)}, bf16[4,2,128,384]{3,2,1,0:T(8,128)(2,1)S(1)}, bf16[4,2,128,384]{3,2,1,0:T(8,128)(2,1)S(1)}, bf16[4,...) fusion(bf16[6,4,130,384]{3,2,1,0:T(8,128)(2,1)S(1)} %select_max, ...), kind=kLoop, calls=%fused_computation.625 | loop fusion | bytes 28311552 | tf_op jit(solution)/shard_map/slice | solution.py:62
  50.8 1.8 %fusion.119 = f32[1024,384]{1,0:T(8,128)} fusion(bf16[1024,384]{1,0:T(8,128)(2,1)S(1)} %bitcast.825, bf16[27,384,384]{2,1,0:T(8,128)(2,1)S(1)} %copy-done.1), kind=kOutput, calls=%fused_computation.220 | convolution fusion | flops 301989888 | bytes 2654208 | tf_op jit(solution)/shard_map/dot_general | solution.py:63
  52.6 1.8 %fusion.123 = f32[1024,384]{1,0:T(8,128)} fusion(bf16[1024,384]{1,0:T(8,128)(2,1)S(1)} %bitcast.824, bf16[27,384,384]{2,1,0:T(8,128)(2,1)S(1)} %copy-done.1), kind=kOutput, calls=%fused_computation.224 | convolution fusion | flops 301989888 | bytes 2654208 | tf_op jit(solution)/shard_map/dot_general | solution.py:63
  57.9 1.8 %fusion.131 = f32[1024,384]{1,0:T(8,128)} fusion(bf16[1024,384]{1,0:T(8,128)(2,1)S(1)} %bitcast.821, bf16[27,384,384]{2,1,0:T(8,128)(2,1)S(1)} %copy-done.1), kind=kOutput, calls=%fused_computation.232 | convolution fusion | flops 301989888 | bytes 2654208 | tf_op jit(solution)/shard_map/dot_general | solution.py:63
  59.7 1.8 %fusion.135 = f32[1024,384]{1,0:T(8,128)} fusion(bf16[1024,384]{1,0:T(8,128)(2,1)S(1)} %bitcast.820, bf16[27,384,384]{2,1,0:T(8,128)(2,1)S(1)} %copy-done.1), kind=kOutput, calls=%fused_computation.236 | convolution fusion | flops 301989888 | bytes 2654208 | tf_op jit(solution)/shard_map/dot_general | solution.py:63
  65.1 1.8 %fusion.143 = f32[1024,384]{1,0:T(8,128)} fusion(bf16[1024,384]{1,0:T(8,128)(2,1)S(1)} %bitcast.817, bf16[27,384,384]{2,1,0:T(8,128)(2,1)S(1)} %copy-done.1), kind=kOutput, calls=%fused_computation.244 | convolution fusion | flops 301989888 | bytes 2654208 | tf_op jit(solution)/shard_map/dot_general | solution.py:63
  66.9 1.8 %fusion.147 = f32[1024,384]{1,0:T(8,128)} fusion(bf16[1024,384]{1,0:T(8,128)(2,1)S(1)} %bitcast.816, bf16[27,384,384]{2,1,0:T(8,128)(2,1)S(1)} %copy-done.1), kind=kOutput, calls=%fused_computation.248 | convolution fusion | flops 301989888 | bytes 2654208 | tf_op jit(solution)/shard_map/dot_general | solution.py:63
  68.7 1.8 %fusion.149 = f32[1024,384]{1,0:T(8,128)} fusion(bf16[1024,384]{1,0:T(8,128)(2,1)S(1)} %bitcast.815, bf16[27,384,384]{2,1,0:T(8,128)(2,1)S(1)} %copy-done.1), kind=kOutput, calls=%fused_computation.250 | convolution fusion | flops 301989888 | bytes 2654208 | tf_op jit(solution)/shard_map/dot_general | solution.py:63
  70.5 1.9 %fusion.153 = f32[1024,384]{1,0:T(8,128)} fusion(bf16[1024,384]{1,0:T(8,128)(2,1)S(1)} %bitcast.814, bf16[27,384,384]{2,1,0:T(8,128)(2,1)S(1)} %copy-done.1), kind=kOutput, calls=%fused_computation.254 | convolution fusion | flops 301989888 | bytes 2654208 | tf_op jit(solution)/shard_map/dot_general | solution.py:63
  74.2 1.8 %fusion.159 = f32[1024,384]{1,0:T(8,128)} fusion(bf16[1024,384]{1,0:T(8,128)(2,1)S(1)} %bitcast.812, bf16[27,384,384]{2,1,0:T(8,128)(2,1)S(1)} %copy-done.1), kind=kOutput, calls=%fused_computation.260 | convolution fusion | flops 301989888 | bytes 2654208 | tf_op jit(solution)/shard_map/dot_general | solution.py:63
  77.8 1.8 %fusion.165 = f32[1024,384]{1,0:T(8,128)} fusion(bf16[1024,384]{1,0:T(8,128)(2,1)S(1)} %bitcast.810, bf16[27,384,384]{2,1,0:T(8,128)(2,1)S(1)} %copy-done.1), kind=kOutput, calls=%fused_computation.266 | convolution fusion | flops 301989888 | bytes 2654208 | tf_op jit(solution)/shard_map/dot_general | solution.py:63
  79.6 13.8 %add_add_fusion = f32[1024,384]{1,0:T(8,128)S(1)} fusion(f32[1024,384]{1,0:T(8,128)} %fusion.115, f32[1024,384]{1,0:T(8,128)} %fusion.117, f32[1024,384]{1,0:T(8,128)} %fusion.119, f32[1024,384]{1,0:T(8,128)S(1)} %fusion.121, f32[1024,384]{1,0:T(8,128)} %fusion.123, f32[1024,384]{1,0:T(8,128)} %fusion.125, f32[1024,384]{1,0:T(8,128)} %fusion.127, ...), kind=kOutput, calls=%fused_computation.37 | convolution fusion | flops 312213504 | bytes 43548672 | tf_op jit(solution)/shard_map/dot_general | solution.py:63
  94.0 3.0 %collective-permute-start.3 = (bf16[6,1,2,128]{3,0,2,1:T(8,128)(2,1)S(1)}, bf16[6,1,2,128]{3,0,2,1:T(8,128)(2,1)S(1)}, u32[]{:S(2)}, u32[]{:S(2)}) collective-permute-start(bf16[6,1,2,128]{3,0,2,1:T(8,128)(2,1)S(1)} %get-tuple-element.69), channel_id=1, source_target_pairs={{0,32},{32,64},{64,96},{1,33},{33,65},{65,97},{2,34},{34,66},{66,9... | collective-permute-start | bytes 9224 | tf_op jit(solution)/shard_map/ppermute | solution.py:21
  97.0 1.9 %collective-permute-start.4 = (bf16[6,1,2,128]{3,0,2,1:T(8,128)(2,1)S(1)}, bf16[6,1,2,128]{3,0,2,1:T(8,128)(2,1)S(1)}, u32[]{:S(2)}, u32[]{:S(2)}) collective-permute-start(bf16[6,1,2,128]{3,0,2,1:T(8,128)(2,1)S(1)} %get-tuple-element.70), channel_id=1, source_target_pairs={{32,0},{64,32},{96,64},{33,1},{65,33},{97,65},{34,2},{66,34},{98,6... | collective-permute-start | bytes 9224 | tf_op jit(solution)/shard_map/ppermute | solution.py:23
  98.9 3.0 %collective-permute-done.4 = bf16[6,1,2,128]{3,0,2,1:T(8,128)(2,1)S(1)} collective-permute-done((bf16[6,1,2,128]{3,0,2,1:T(8,128)(2,1)S(1)}, bf16[6,1,2,128]{3,0,2,1:T(8,128)(2,1)S(1)}, u32[]{:S(2)}, u32[]{:S(2)}) %collective-permute-start.4) | collective-permute-done | bytes 3104 | tf_op jit(solution)/shard_map/ppermute | solution.py:23
  101.9 1.9 %collective-permute-start.5 = (bf16[6,6,1,128]{3,0,2,1:T(8,128)(2,1)S(1)}, bf16[6,6,1,128]{3,0,2,1:T(8,128)(2,1)S(1)}, u32[]{:S(2)}, u32[]{:S(2)}) collective-permute-start(bf16[6,6,1,128]{3,0,2,1:T(8,128)(2,1)S(1)} %get-tuple-element.67), channel_id=1, source_target_pairs={{0,1},{1,2},{2,3},{3,4},{4,5},{5,6},{6,7},{7,8},{8,9},{9,10},{10,1... | collective-permute-start | bytes 27656 | tf_op jit(solution)/shard_map/ppermute | solution.py:21
  103.9 9.4 %collective-permute-start.6 = (bf16[6,6,1,128]{3,0,2,1:T(8,128)(2,1)S(1)}, bf16[6,6,1,128]{3,0,2,1:T(8,128)(2,1)S(1)}, u32[]{:S(2)}, u32[]{:S(2)}) collective-permute-start(bf16[6,6,1,128]{3,0,2,1:T(8,128)(2,1)S(1)} %get-tuple-element.68), channel_id=1, source_target_pairs={{1,0},{2,1},{3,2},{4,3},{5,4},{6,5},{7,6},{8,7},{9,8},{10,9},{11,1... | collective-permute-start | bytes 27656 | tf_op jit(solution)/shard_map/ppermute | solution.py:23
  126.7 2.2 %collective-permute-start.7 = (bf16[128,1,2,128]{3,0,2,1:T(8,128)(2,1)S(1)}, bf16[128,1,2,128]{3,0,2,1:T(8,128)(2,1)S(1)}, u32[]{:S(2)}, u32[]{:S(2)}) collective-permute-start(bf16[128,1,2,128]{3,0,2,1:T(8,128)(2,1)S(1)} %get-tuple-element.36), channel_id=1, source_target_pairs={{0,32},{32,64},{64,96},{1,33},{33,65},{65,97},{2,34},{34,66},{66,9... | collective-permute-start | bytes 196616 | tf_op jit(solution)/shard_map/ppermute | solution.py:21
  128.9 2.1 %collective-permute-start.8 = (bf16[128,1,2,128]{3,0,2,1:T(8,128)(2,1)S(1)}, bf16[128,1,2,128]{3,0,2,1:T(8,128)(2,1)S(1)}, u32[]{:S(2)}, u32[]{:S(2)}) collective-permute-start(bf16[128,1,2,128]{3,0,2,1:T(8,128)(2,1)S(1)} %get-tuple-element.37), channel_id=1, source_target_pairs={{32,0},{64,32},{96,64},{33,1},{65,33},{97,65},{34,2},{66,34},{98,6... | collective-permute-start | bytes 196616 | tf_op jit(solution)/shard_map/ppermute | solution.py:23
  131.6 2.9 %collective-permute-done.8 = bf16[128,1,2,128]{3,0,2,1:T(8,128)(2,1)S(1)} collective-permute-done((bf16[128,1,2,128]{3,0,2,1:T(8,128)(2,1)S(1)}, bf16[128,1,2,128]{3,0,2,1:T(8,128)(2,1)S(1)}, u32[]{:S(2)}, u32[]{:S(2)}) %collective-permute-start.8) | collective-permute-done | bytes 65568 | tf_op jit(solution)/shard_map/ppermute | solution.py:23
  134.6 9.0 %collective-permute-start.10 = (bf16[128,6,1,128]{3,0,2,1:T(8,128)(2,1)S(1)}, bf16[128,6,1,128]{3,0,2,1:T(8,128)(2,1)S(1)}, u32[]{:S(2)}, u32[]{:S(2)}) collective-permute-start(bf16[128,6,1,128]{3,0,2,1:T(8,128)(2,1)S(1)} %get-tuple-element.35), channel_id=1, source_target_pairs={{1,0},{2,1},{3,2},{4,3},{5,4},{6,5},{7,6},{8,7},{9,8},{10,9},{11,1... | collective-permute-start | bytes 589832 | tf_op jit(solution)/shard_map/ppermute | solution.py:23
  143.6 1.9 %collective-permute-start.9 = (bf16[128,6,1,128]{3,0,2,1:T(8,128)(2,1)S(1)}, bf16[128,6,1,128]{3,0,2,1:T(8,128)(2,1)S(1)}, u32[]{:S(2)}, u32[]{:S(2)}) collective-permute-start(bf16[128,6,1,128]{3,0,2,1:T(8,128)(2,1)S(1)} %get-tuple-element.34), channel_id=1, source_target_pairs={{0,1},{1,2},{2,3},{3,4},{4,5},{5,6},{6,7},{7,8},{8,9},{9,10},{10,1... | collective-permute-start | bytes 589832 | tf_op jit(solution)/shard_map/ppermute | solution.py:21
  146.7 8.3 %collective-permute-done.9 = bf16[128,6,1,128]{3,0,2,1:T(8,128)(2,1)S(1)} collective-permute-done((bf16[128,6,1,128]{3,0,2,1:T(8,128)(2,1)S(1)}, bf16[128,6,1,128]{3,0,2,1:T(8,128)(2,1)S(1)}, u32[]{:S(2)}, u32[]{:S(2)}) %collective-permute-start.9) | collective-permute-done | bytes 196640 | tf_op jit(solution)/shard_map/ppermute | solution.py:21
  (165 shorter events, 61.0 us)
Async XLA Ops:
  0.6 93.0 %copy-start = (bf16[384,3]{0,1:T(4,128)(2,1)S(1)}, bf16[384,3]{0,1:T(4,128)(2,1)}, u32[]{:S(2)}) copy-start(bf16[384,3]{0,1:T(4,128)(2,1)} %param.10) | copy-start | bytes 6916
  0.6 7.5 %copy-start.5 = (bf16[27,64,3]{1,0,2:T(8,128)(2,1)S(1)}, bf16[27,64,3]{1,0,2:T(8,128)(2,1)}, u32[]{:S(2)}) copy-start(bf16[27,64,3]{1,0,2:T(8,128)(2,1)} %param.12) | copy-start | bytes 31108
  0.7 7.6 %copy-start.6 = (bf16[3,4,2,128]{3,2,1,0:T(2,128)(2,1)S(1)}, bf16[3,4,2,128]{3,2,1,0:T(2,128)(2,1)}, u32[]{:S(2)}) copy-start(bf16[3,4,2,128]{3,2,1,0:T(2,128)(2,1)} %param.11) | copy-start | bytes 18436
  3.7 19.3 %copy-start.1 = (bf16[27,384,384]{2,1,0:T(8,128)(2,1)S(1)}, bf16[27,384,384]{2,1,0:T(8,128)(2,1)}, u32[]{:S(2)}) copy-start(bf16[27,384,384]{2,1,0:T(8,128)(2,1)} %param.9) | copy-start | bytes 23887876
  3.8 9.1 %collective-permute-start = (bf16[2,2,128,384]{3,2,1,0:T(8,128)(2,1)S(1)}, bf16[2,2,128,384]{3,2,1,0:T(8,128)(2,1)S(1)}, u32[]{:S(2)}, u32[]{:S(2)}) collective-permute-start(bf16[2,2,128,384]{3,2,1,0:T(8,128)(2,1)S(1)} %slice.1161), channel_id=1, source_target_pairs={{0,32},{32,64},{64,96},{1,33},{33,65},{65,97},{2,34},{34,66},{66,9... | collective-permute-start | bytes 1179656 | tf_op jit(solution)/shard_map/ppermute | solution.py:10
  13.0 17.4 %collective-permute-start.1 = (bf16[6,1,128,384]{3,2,1,0:T(8,128)(2,1)S(1)}, bf16[6,1,128,384]{3,2,1,0:T(8,128)(2,1)S(1)}, u32[]{:S(2)}, u32[]{:S(2)}) collective-permute-start(bf16[6,1,128,384]{3,2,1,0:T(8,128)(2,1)S(1)} %get-tuple-element.30), channel_id=1, source_target_pairs={{0,1},{1,2},{2,3},{3,4},{4,5},{5,6},{6,7},{7,8},{8,9},{9,10},{10,1... | collective-permute-start | bytes 1769480 | tf_op jit(solution)/shard_map/ppermute | solution.py:21
  16.1 16.0 %collective-permute-start.2 = (bf16[6,1,128,384]{3,2,1,0:T(8,128)(2,1)S(1)}, bf16[6,1,128,384]{3,2,1,0:T(8,128)(2,1)S(1)}, u32[]{:S(2)}, u32[]{:S(2)}) collective-permute-start(bf16[6,1,128,384]{3,2,1,0:T(8,128)(2,1)S(1)} %get-tuple-element.31), channel_id=1, source_target_pairs={{1,0},{2,1},{3,2},{4,3},{5,4},{6,5},{7,6},{8,7},{9,8},{10,9},{11,1... | collective-permute-start | bytes 1769480 | tf_op jit(solution)/shard_map/ppermute | solution.py:23
  79.6 13.8 %copy-start.2 = (bf16[4,2,128,384]{3,2,1,0:T(8,128)(2,1)S(1)}, bf16[4,2,128,384]{3,2,1,0:T(8,128)(2,1)}, u32[]{:S(2)}) copy-start(bf16[4,2,128,384]{3,2,1,0:T(8,128)(2,1)} %param.7) | copy-start | bytes 2359300
  93.6 21.9 %copy-start.3 = (bf16[4,2,128,384]{3,2,1,0:T(8,128)(2,1)}, bf16[4,2,128,384]{3,2,1,0:T(8,128)(2,1)S(1)}, u32[]{:S(2)}) copy-start(bf16[4,2,128,384]{3,2,1,0:T(8,128)(2,1)S(1)} %fusion.13) | copy-start | bytes 2359300
  94.0 5.0 %collective-permute-start.3 = (bf16[6,1,2,128]{3,0,2,1:T(8,128)(2,1)S(1)}, bf16[6,1,2,128]{3,0,2,1:T(8,128)(2,1)S(1)}, u32[]{:S(2)}, u32[]{:S(2)}) collective-permute-start(bf16[6,1,2,128]{3,0,2,1:T(8,128)(2,1)S(1)} %get-tuple-element.69), channel_id=1, source_target_pairs={{0,32},{32,64},{64,96},{1,33},{33,65},{65,97},{2,34},{34,66},{66,9... | collective-permute-start | bytes 9224 | tf_op jit(solution)/shard_map/ppermute | solution.py:21
  97.0 4.9 %collective-permute-start.4 = (bf16[6,1,2,128]{3,0,2,1:T(8,128)(2,1)S(1)}, bf16[6,1,2,128]{3,0,2,1:T(8,128)(2,1)S(1)}, u32[]{:S(2)}, u32[]{:S(2)}) collective-permute-start(bf16[6,1,2,128]{3,0,2,1:T(8,128)(2,1)S(1)} %get-tuple-element.70), channel_id=1, source_target_pairs={{32,0},{64,32},{96,64},{33,1},{65,33},{97,65},{34,2},{66,34},{98,6... | collective-permute-start | bytes 9224 | tf_op jit(solution)/shard_map/ppermute | solution.py:23
  101.9 11.6 %collective-permute-start.5 = (bf16[6,6,1,128]{3,0,2,1:T(8,128)(2,1)S(1)}, bf16[6,6,1,128]{3,0,2,1:T(8,128)(2,1)S(1)}, u32[]{:S(2)}, u32[]{:S(2)}) collective-permute-start(bf16[6,6,1,128]{3,0,2,1:T(8,128)(2,1)S(1)} %get-tuple-element.67), channel_id=1, source_target_pairs={{0,1},{1,2},{2,3},{3,4},{4,5},{5,6},{6,7},{7,8},{8,9},{9,10},{10,1... | collective-permute-start | bytes 27656 | tf_op jit(solution)/shard_map/ppermute | solution.py:21
  103.9 10.0 %collective-permute-start.6 = (bf16[6,6,1,128]{3,0,2,1:T(8,128)(2,1)S(1)}, bf16[6,6,1,128]{3,0,2,1:T(8,128)(2,1)S(1)}, u32[]{:S(2)}, u32[]{:S(2)}) collective-permute-start(bf16[6,6,1,128]{3,0,2,1:T(8,128)(2,1)S(1)} %get-tuple-element.68), channel_id=1, source_target_pairs={{1,0},{2,1},{3,2},{4,3},{5,4},{6,5},{7,6},{8,7},{9,8},{10,9},{11,1... | collective-permute-start | bytes 27656 | tf_op jit(solution)/shard_map/ppermute | solution.py:23
  126.0 5.1 %copy-start.4 = (bf16[27,128,64]{1,2,0:T(8,128)(2,1)S(1)}, bf16[27,128,64]{1,2,0:T(8,128)(2,1)}, u32[]{:S(2)}) copy-start(bf16[27,128,64]{1,2,0:T(8,128)(2,1)} %param.13) | copy-start | bytes 1327108
  126.7 4.9 %collective-permute-start.7 = (bf16[128,1,2,128]{3,0,2,1:T(8,128)(2,1)S(1)}, bf16[128,1,2,128]{3,0,2,1:T(8,128)(2,1)S(1)}, u32[]{:S(2)}, u32[]{:S(2)}) collective-permute-start(bf16[128,1,2,128]{3,0,2,1:T(8,128)(2,1)S(1)} %get-tuple-element.36), channel_id=1, source_target_pairs={{0,32},{32,64},{64,96},{1,33},{33,65},{65,97},{2,34},{34,66},{66,9... | collective-permute-start | bytes 196616 | tf_op jit(solution)/shard_map/ppermute | solution.py:21
  128.9 5.6 %collective-permute-start.8 = (bf16[128,1,2,128]{3,0,2,1:T(8,128)(2,1)S(1)}, bf16[128,1,2,128]{3,0,2,1:T(8,128)(2,1)S(1)}, u32[]{:S(2)}, u32[]{:S(2)}) collective-permute-start(bf16[128,1,2,128]{3,0,2,1:T(8,128)(2,1)S(1)} %get-tuple-element.37), channel_id=1, source_target_pairs={{32,0},{64,32},{96,64},{33,1},{65,33},{97,65},{34,2},{66,34},{98,6... | collective-permute-start | bytes 196616 | tf_op jit(solution)/shard_map/ppermute | solution.py:23
  134.6 12.1 %collective-permute-start.10 = (bf16[128,6,1,128]{3,0,2,1:T(8,128)(2,1)S(1)}, bf16[128,6,1,128]{3,0,2,1:T(8,128)(2,1)S(1)}, u32[]{:S(2)}, u32[]{:S(2)}) collective-permute-start(bf16[128,6,1,128]{3,0,2,1:T(8,128)(2,1)S(1)} %get-tuple-element.35), channel_id=1, source_target_pairs={{1,0},{2,1},{3,2},{4,3},{5,4},{6,5},{7,6},{8,7},{9,8},{10,9},{11,1... | collective-permute-start | bytes 589832 | tf_op jit(solution)/shard_map/ppermute | solution.py:23
  143.6 11.3 %collective-permute-start.9 = (bf16[128,6,1,128]{3,0,2,1:T(8,128)(2,1)S(1)}, bf16[128,6,1,128]{3,0,2,1:T(8,128)(2,1)S(1)}, u32[]{:S(2)}, u32[]{:S(2)}) collective-permute-start(bf16[128,6,1,128]{3,0,2,1:T(8,128)(2,1)S(1)} %get-tuple-element.34), channel_id=1, source_target_pairs={{0,1},{1,2},{2,3},{3,4},{4,5},{5,6},{6,7},{7,8},{8,9},{9,10},{10,1... | collective-permute-start | bytes 589832 | tf_op jit(solution)/shard_map/ppermute | solution.py:21
where the time goes:
time: 173 us; the launch traced here: 172 us
  matrix products  89 us (51%)
  starting transfers between devices  45.7 us (26%)
  waiting for transfers between devices  23.1 us (13%)
  other arithmetic  8.19 us (5%)
  local copies, waits for them, and re-layouts  4.29 us (2%)
  between operations  1.84 us (1%)
    dot_general x27, matrix products, per_device(): jnp.dot(piece, conv_weight[tap], preferred_element_type=jnp.float32)  60.3 us
    ppermute x5, starting transfers between devices, extended_2(): lax.ppermute(head, axis, [((i + 1) % count, i) for i in range(ends)])  29.2 us
    dot_general x108, matrix products, conv_valid(): jnp.einsum('oc,cthw->othw', weights[tap], piece, preferred_element_type=j...  28.4 us
    ppermute x5, starting transfers between devices, extended_2(): lax.ppermute(tail, axis, [(i, (i + 1) % count) for i in range(ends)])  12.2 us
    ppermute x5, waiting for transfers between devices, extended_2(): lax.ppermute(tail, axis, [(i, (i + 1) % count) for i in range(ends)])  12.1 us
    ppermute x5, waiting for transfers between devices, extended_2(): lax.ppermute(head, axis, [((i + 1) % count, i) for i in range(ends)])  7.96 us
    ppermute x1, starting transfers between devices, from_behind(): return lax.ppermute(block, axis, route)  4.37 us
    slice x2, local copies, waits for them, and re-layouts, per_device(): extended[dt:dt + frames, dh:dh + height, dw:dw + width].reshape(-1, chans)  4.12 us
  transfers between devices with their start and end apart: 11, of which 7 were waited for; matrix products, arithmetic and copies ran while one was open for 4% of the time, Pallas kernels for 0%

commit v1 on v0

v1 whole, which is shorter than its diff:
```python
import jax
import jax.numpy as jnp
from jax import lax
from jax.experimental import pallas as pl
from jax.experimental.pallas import tpu as pltpu
from jax.sharding import PartitionSpec as P

F32 = jnp.float32
BF16 = jnp.bfloat16
VMEM = pl.BlockSpec(memory_space=pltpu.VMEM)
SMEM = pl.BlockSpec(memory_space=pltpu.SMEM)


def pairs(count, first):
    route = []
    for i in range(first, count - 1, 2):
        route += [(i, i + 1), (i + 1, i)]
    return route


def swap(block, axis, first):
    return lax.ppermute(block, axis, pairs(lax.axis_size(axis), first))


def leaky(value):
    return jnp.maximum(value, 0.2 * value)


def act_kernel(pos_ref, feat_ref, gain_ref, to_a_ref, to_b_ref, tail_ref):
    odd = lax.rem(pos_ref[1], 2)
    gain = gain_ref[...]
    frames = feat_ref.shape[0]
    for row_sel, out_ref in ((1 - odd, to_a_ref), (odd, to_b_ref)):
        for t in range(frames):
            feats = feat_ref[t, row_sel].astype(F32)
            mean = jnp.mean(feats * feats, axis=-1, keepdims=True)
            normed = feats * lax.rsqrt(mean + 1e-06) * gain
            act = (normed * jax.nn.sigmoid(normed)).astype(BF16)
            out_ref[t] = act
            if t >= frames - 2:
                tail_ref[0 if out_ref is to_a_ref else 1, t - frames + 2] = act


def stack_frames(lines, frames, width):
    return [lines[dt : dt + frames].reshape(frames * width, lines.shape[-1]) for dt in range(3)]


def rhs_tile(w_ref, columns):
    halves = []
    for dhs, dw, off in columns:
        halves.append(
            jnp.concatenate(
                [w_ref[9 * dt + 3 * dh + dw, :, off : off + 128] for dh in dhs for dt in range(3)],
                axis=0,
            )
        )
    return halves[0] if len(halves) == 1 else jnp.concatenate(halves, axis=1)


def merge_columns(y0, y1, y2):
    width = y0.shape[0]
    col = lax.broadcasted_iota(jnp.int32, y0.shape, 0)
    left = jnp.where(col == 0, 0.0, pltpu.roll(y0, 1, 0))
    right = jnp.where(col == width - 1, 0.0, pltpu.roll(y2, width - 1, 0))
    return y1 + left + right


def own_kernel(pos_ref, a_ref, b_ref, past_ref, w_ref, part_ref, lines_ref, y_ref):
    odd = lax.rem(pos_ref[1], 2)
    frames, width, chans = a_ref.shape
    for row, own_ref, k in ((1 - odd, a_ref, 0), (odd, b_ref, 1)):
        lines_ref[row, pl.ds(0, 2)] = past_ref[k]
        lines_ref[row, pl.ds(2, frames)] = own_ref[...]
    lhs = jnp.concatenate(
        stack_frames(lines_ref[0], frames, width) + stack_frames(lines_ref[1], frames, width), axis=1
    )
    columns = [
        (dhs, dw, off)
        for dhs in ((1, 2), (0, 1))
        for dw in range(3)
        for off in range(0, chans, 128)
    ]
    for j in range(0, len(columns), 2):
        y_ref[:, j * 128 : (j + 2) * 128] = jnp.dot(
            lhs, rhs_tile(w_ref, columns[j : j + 2]), preferred_element_type=F32
        )
    for row in range(2):
        for t in range(frames):
            ys = [
                y_ref[t * width : (t + 1) * width, (row * 3 + dw) * chans : (row * 3 + dw + 1) * chans]
                for dw in range(3)
            ]
            part_ref[t, row] = merge_columns(*ys)


def halo_kernel(
    pos_ref, a_ref, b_ref, past_a_ref, past_b_ref, w_ref, part_ref, feat_ref, rgb_ref, real_ref,
    decoded_ref, colour_ref, lines_ref, y_ref,
):
    odd = lax.rem(pos_ref[1], 2)
    frames, width, chans = a_ref.shape
    for side, own_ref, past in ((1 - odd, a_ref, past_a_ref), (odd, b_ref, past_b_ref)):
        lines_ref[side, pl.ds(0, 2)] = past[...]
        lines_ref[side, pl.ds(2, frames)] = own_ref[...]
    for row in range(2):
        lhs = jnp.concatenate(stack_frames(lines_ref[row], frames, width), axis=1)
        columns = [((2 * row,), dw, off) for dw in range(3) for off in range(0, chans, 128)]
        for j in range(0, len(columns), 2):
            some = columns[j : j + 2]
            y_ref[row, :, j * 128 : (j + len(some)) * 128] = jnp.dot(
                lhs, rhs_tile(w_ref, some), preferred_element_type=F32
            )
        for t in range(frames):
            ys = [
                y_ref[row, t * width : (t + 1) * width, dw * chans : (dw + 1) * chans]
                for dw in range(3)
            ]
            total = merge_columns(*ys) + part_ref[t, row]
            decoded = (feat_ref[t, row].astype(F32) + total).astype(BF16)
            decoded_ref[t, row] = decoded
            colour = lax.dot_general(
                rgb_ref[...], decoded, (((1,), (1,)), ((), ())), preferred_element_type=F32
            )
            colour_ref[t, row] = (
                colour.astype(BF16).astype(F32) + real_ref[t, row].astype(F32)
            ).astype(BF16)


def disc_kernel(
    pos_ref, mid_ref, ta_ref, tb_ref, w1_ref, w2_ref, out_ref, x_ref, f_ref, *, tm_count, row_count
):
    tm, band = pos_ref[0], pos_ref[1]
    odd_t, odd_r = lax.rem(tm, 2), lax.rem(band, 2)
    width = out_ref.shape[-1]
    frames = out_ref.shape[0]
    col = lax.broadcasted_iota(jnp.int32, (8, width), 1)

    def put(t, h, line):
        x = line.astype(F32)
        x_ref[t, h, 0:8] = jnp.where(col == 0, 0.0, pltpu.roll(x, 1, 1))
        x_ref[t, h, 8:16] = x
        x_ref[t, h, 16:24] = jnp.where(col == width - 1, 0.0, pltpu.roll(x, width - 1, 1))

    row_at = [4 * (1 - odd_r), 4 * (1 - odd_r) + 1, 2, 3, 4 * odd_r, 4 * odd_r + 1]
    a_at = (frames + 2) * (1 - odd_t)
    b_at = (frames + 2) * odd_t
    for k in range(6):
        for t in range(frames):
            put(t + 2, row_at[k], mid_ref[t, k])
        for t in range(2):
            put(a_at + t, row_at[k], ta_ref[t, k])
            put(b_at + t, row_at[k], tb_ref[t, k])

    w1 = w1_ref[...]
    near = {}
    for t in range(frames + 2):
        for h in range(0, 4, 2):
            cols = []
            for hh in (h, h + 1):
                cols.append(
                    jnp.concatenate(
                        [x_ref[t + dt, hh + dh] for dt in range(3) for dh in range(3)], axis=0
                    ).astype(BF16)
                )
            first = leaky(jnp.dot(w1, jnp.concatenate(cols, axis=1), preferred_element_type=F32))
            for i, hh in enumerate((h, h + 1)):
                part = first[:, i * width : (i + 1) * width]
                keep = None
                if t == 0:
                    keep = tm > 0
                if t == frames + 1:
                    keep = tm < tm_count - 1
                edge = None
                if hh == 0:
                    edge = band > 0
                if hh == 3:
                    edge = band < row_count - 1
                if keep is not None and edge is not None:
                    keep = jnp.logical_and(keep, edge)
                elif keep is None:
                    keep = edge
                if keep is not None:
                    part = jnp.where(keep, part, 0.0)
                part = part.astype(BF16)
                f_ref[t, hh] = part
                if 1 <= t <= frames and 1 <= hh <= 2:
                    wide = part.astype(F32)
                    half = wide.shape[0] // 2
                    near[t - 1, hh - 1] = jnp.mean(
                        jnp.abs(wide[:half] - wide[half:]), axis=0, keepdims=True
                    )

    w2 = w2_ref[...]
    depth2 = w2.shape[0] // 3
    half = f_ref.shape[2] // 2
    colw = lax.broadcasted_iota(jnp.int32, (depth2, width), 1)
    for t in range(frames):
        for h in range(2):
            sides = []
            for s in range(2):
                sides.append(
                    jnp.concatenate(
                        [
                            f_ref[t + dt, h + dh, s * half : (s + 1) * half]
                            for dt in range(3)
                            for dh in range(3)
                        ],
                        axis=0,
                    )
                )
            y = jnp.dot(w2, jnp.concatenate(sides, axis=1), preferred_element_type=F32)
            outs = []
            for s in range(2):
                y0, y1, y2 = (
                    y[d * depth2 : (d + 1) * depth2, s * width : (s + 1) * width] for d in range(3)
                )
                total = (
                    y1
                    + jnp.where(colw == 0, 0.0, pltpu.roll(y0, 1, 1))
                    + jnp.where(colw == width - 1, 0.0, pltpu.roll(y2, width - 1, 1))
                )
                outs.append(leaky(total).astype(BF16).astype(F32))
            far = jnp.mean(jnp.abs(outs[0] - outs[1]), axis=0, keepdims=True)
            out_ref[t, h : h + 1] = near[t, h] + far


def shape(dims, dtype):
    return jax.ShapeDtypeStruct(dims, dtype)


def per_device(
    latent_feat, norm_gain, conv_weight, rgb_weight, real_frames, disc_first, disc_second
):
    frames, height, width, chans = latent_feat.shape
    pos = jnp.stack([lax.axis_index("tm"), lax.axis_index("rows")]).astype(jnp.int32)
    depth1, depth2 = disc_first.shape[1], disc_second.shape[1]

    rgb = jnp.pad(rgb_weight.T, ((0, 5), (0, 0)))
    real = jnp.pad(jnp.transpose(real_frames, (1, 2, 0, 3)), ((0, 0), (0, 0), (3, 2), (0, 0)))
    w1 = jnp.transpose(disc_first, (1, 0, 2))
    w1 = jnp.concatenate(
        [jnp.pad(w1, ((0, 0), (0, 0), (0, 5))), jnp.pad(w1, ((0, 0), (0, 0), (3, 2)))], axis=0
    ).reshape(2 * depth1, 27 * 8)
    w2 = disc_second.reshape(9, 3, depth2, depth1)
    w2 = jnp.transpose(w2, (1, 2, 0, 3)).reshape(3 * depth2, 9 * depth1)

    to_a, to_b, tail = pl.pallas_call(
        act_kernel,
        out_shape=(
            shape((frames, width, chans), BF16),
            shape((frames, width, chans), BF16),
            shape((2, 2, width, chans), BF16),
        ),
        in_specs=[SMEM, VMEM, VMEM],
        out_specs=(VMEM,) * 3,
        name="act",
    )(pos, latent_feat, norm_gain.reshape(1, chans))

    from_b = swap(to_b, "rows", 1)
    from_a = swap(to_a, "rows", 0)
    count = lax.axis_size("tm")
    past = lax.ppermute(tail, "tm", [(i, i + 1) for i in range(count - 1)])
    past_b = swap(past[1], "rows", 1)
    past_a = swap(past[0], "rows", 0)

    flops = 2 * frames * width * 9 * chans * chans
    part = pl.pallas_call(
        own_kernel,
        out_shape=shape((frames, height, width, chans), F32),
        in_specs=[SMEM] + [VMEM] * 4,
        out_specs=VMEM,
        scratch_shapes=[
            pltpu.VMEM((2, frames + 2, width, chans), BF16),
            pltpu.VMEM((frames * width, 6 * chans), F32),
        ],
        cost_estimate=pl.CostEstimate(flops=4 * flops, bytes_accessed=10**7, transcendentals=0),
        name="own",
    )(pos, to_a, to_b, past, conv_weight)

    decoded, colour = pl.pallas_call(
        halo_kernel,
        out_shape=(
            shape((frames, height, width, chans), BF16),
            shape((frames, height, 8, width), BF16),
        ),
        in_specs=[SMEM] + [VMEM] * 9,
        out_specs=(VMEM,) * 2,
        scratch_shapes=[
            pltpu.VMEM((2, frames + 2, width, chans), BF16),
            pltpu.VMEM((2, frames * width, 3 * chans), F32),
        ],
        cost_estimate=pl.CostEstimate(flops=2 * flops, bytes_accessed=10**7, transcendentals=0),
        name="halo",
    )(pos, from_a, from_b, past_a, past_b, conv_weight, part, latent_feat, rgb, real)

    side_b = swap(colour, "rows", 1)
    side_a = swap(colour, "rows", 0)
    mid = jnp.concatenate([side_a, colour, side_b], axis=1)
    odd_t = lax.rem(pos[0], 2)
    for_a = lax.dynamic_slice_in_dim(mid, (frames - 2) * (1 - odd_t), 2, axis=0)
    for_b = lax.dynamic_slice_in_dim(mid, (frames - 2) * odd_t, 2, axis=0)
    time_b = swap(for_b, "tm", 1)
    time_a = swap(for_a, "tm", 0)

    match_map = pl.pallas_call(
        lambda *refs: disc_kernel(
            *refs, tm_count=lax.axis_size("tm"), row_count=lax.axis_size("rows")
        ),
        out_shape=shape((frames, height, width), F32),
        in_specs=[SMEM] + [VMEM] * 5,
        out_specs=VMEM,
        scratch_shapes=[
            pltpu.VMEM((frames + 4, height + 4, 24, width), F32),
            pltpu.VMEM((frames + 2, height + 2, 2 * depth1, width), BF16),
        ],
        name="disc",
    )(pos, mid, time_a, time_b, w1, w2)
    return (decoded, match_map)


def solution(mesh):
    placed = (P("tm", "rows", None, None), P(), P(), P(), P(None, "tm", "rows", None), P(), P())
    return jax.shard_map(
        per_device,
        mesh=mesh,
        in_specs=placed,
        out_specs=(P("tm", "rows", None, None), P("tm", "rows", None)),
        check_vma=False,
    )
```

time: 173 us -> 78.2 us (0.45)
  matrix products: 89 us -> 0 us
  Pallas kernels: 0 us -> 26.1 us
  waiting for transfers between devices: 23.1 us -> 5.1 us
  starting transfers between devices: 45.7 us -> 35.1 us
  other arithmetic: 8.19 us -> 0.77 us
  local copies, waits for them, and re-layouts: 4.29 us -> 9.65 us
    dot_general x136 -> x0, matrix products: 89 us -> none  [the longest x27 60.3 us: per_device(): jnp.dot(piece, conv_weight[tap], preferred_element_type=jnp.float32)]
    pallas_call x0 -> x4, Pallas kernels: none -> 26.1 us  [the longest x1 10.5 us: per_device(): pl.pallas_call(own_kernel, out_shape=shape((frames, height, width, chans)...]
    ppermute x11 -> x9, waiting for transfers between devices: 23.1 us -> 5.1 us  [the longest x8 5.09 us: swap(): return lax.ppermute(block, axis, pairs(lax.axis_size(axis), first))]
    ppermute x11 -> x9, starting transfers between devices: 45.7 us -> 35.1 us  [the longest x8 31 us: swap(): return lax.ppermute(block, axis, pairs(lax.axis_size(axis), first))]
    concatenate x10 -> x0, other arithmetic: 4.3 us -> none  [the longest x8 4 us: extended_2(): jnp.concatenate([lax.ppermute(tail, axis, [(i, (i + 1) % count) for i in...]
    unnamed x15 -> x25, local copies, waits for them, and re-layouts: 0.05 us -> 4.35 us
    slice x7 -> x0, local copies, waits for them, and re-layouts: 4.24 us -> none  [the longest x2 4.12 us: per_device(): extended[dt:dt + frames, dh:dh + height, dw:dw + width].reshape(-1, chans)]
    reshape x0 -> x4, local copies, waits for them, and re-layouts: none -> 3.37 us  [the longest x1 1.25 us: per_device(): norm_gain.reshape(1, chans)]
  transfers between devices with their start and end apart: 11 -> 9, of which waited for: 7 -> 1; matrix products, arithmetic and copies ran while one was open for 4% -> 7% of each run, Pallas kernels for 0% -> 14%
where the time goes in v1:
time: 78.2 us; the launch traced here: 77.5 us
  starting transfers between devices  35.1 us (45%)
  Pallas kernels  26.1 us (33%)
  local copies, waits for them, and re-layouts  9.65 us (12%)
  waiting for transfers between devices  5.1 us (7%)
  between operations  0.84 us (1%)
    ppermute x8, starting transfers between devices, swap(): return lax.ppermute(block, axis, pairs(lax.axis_size(axis), first))  31 us
    pallas_call x1, Pallas kernels, per_device(): pl.pallas_call(own_kernel, out_shape=shape((frames, height, width, chans)...  10.5 us
    pallas_call x1, Pallas kernels, per_device(): pl.pallas_call(halo_kernel, out_shape=(shape((frames, height, width, chan...  9.45 us
    ppermute x8, waiting for transfers between devices, swap(): return lax.ppermute(block, axis, pairs(lax.axis_size(axis), first))  5.09 us
    unnamed x25, local copies, waits for them, and re-layouts  4.35 us
    ppermute x1, starting transfers between devices, per_device(): past = lax.ppermute(tail, 'tm', [(i, i + 1) for i in range(count - 1)])  4.09 us
    pallas_call x1, Pallas kernels, per_device(): pl.pallas_call(lambda *refs: disc_kernel(*refs, tm_count=lax.axis_size('t...  3.57 us
    pallas_call x1, Pallas kernels, per_device(): pl.pallas_call(act_kernel, out_shape=(shape((frames, width, chans), BF16)...  2.52 us
  transfers between devices with their start and end apart: 9, of which 1 were waited for; matrix products, arithmetic and copies ran while one was open for 7% of the time, Pallas kernels for 14%

profile of v1, /device:TPU:17, one launch (start us, length us, event | category | flops | bytes accessed | tf_op | source)
XLA Modules:
  0.0 77.5 jit_solution(14696855147620785540)
XLA Ops:
  0.6 1.2 %reshape.16.gain_ref = f32[1,384]{1,0:T(1,128)} reshape(f32[384]{0:T(512)} %param.8) | data formatting | bytes 3072 | tf_op jit(solution)/shard_map/reshape | solution.py:257
  1.9 0.7 pad_add_fusion.pos_ref.refs_0_
  2.5 2.5 %act.1 = (bf16[4,128,384]{2,1,0:T(8,128)(2,1)}, bf16[4,128,384]{2,1,0:T(8,128)(2,1)}, bf16[2,2,128,384]{3,2,1,0:T(8,128)(2,1)}) custom-call(s32[2]{0:T(128)} %pad_add_fusion.pos_ref.refs_0_, bf16[4,2,128,384]{3,2,1,0:T(8,128)(2,1)} %feat_ref.3, f32[1,384]{1,0:T(1,128)} %reshape.16.gain_ref), custom_call_target="tpu_custom_call" | custom-call | tf_op jit(solution)/shard_map/act/pallas_call | solution.py:247
  5.1 4.1 %collective-permute-start.2 = (bf16[2,2,128,384]{3,2,1,0:T(8,128)(2,1)}, bf16[2,2,128,384]{3,2,1,0:T(8,128)(2,1)S(1)}, u32[]{:S(2)}, u32[]{:S(2)}) collective-permute-start(bf16[2,2,128,384]{3,2,1,0:T(8,128)(2,1)} %get-tuple-element.9), channel_id=1, source_target_pairs={{0,32},{32,64},{64,96},{1,33},{33,65},{65,97},{2,34},{34,66},{66,9... | collective-permute-start | bytes 1179656 | tf_op jit(solution)/shard_map/ppermute | solution.py:262
  9.2 1.3 %collective-permute-start = (bf16[4,128,384]{2,1,0:T(8,128)(2,1)}, bf16[4,128,384]{2,1,0:T(8,128)(2,1)S(1)}, u32[]{:S(2)}, u32[]{:S(2)}) collective-permute-start(bf16[4,128,384]{2,1,0:T(8,128)(2,1)} %get-tuple-element.7.a_ref), channel_id=1, source_target_pairs={{0,1},{1,0},{2,3},{3,2},{4,5},{5,4},{6,7},{7,6},{8,9},{9,8},{10,11... | collective-permute-start | bytes 1179656 | tf_op jit(solution)/shard_map/ppermute | solution.py:22
  10.5 6.6 %collective-permute-start.1 = (bf16[4,128,384]{2,1,0:T(8,128)(2,1)}, bf16[4,128,384]{2,1,0:T(8,128)(2,1)S(1)}, u32[]{:S(2)}, u32[]{:S(2)}) collective-permute-start(bf16[4,128,384]{2,1,0:T(8,128)(2,1)} %get-tuple-element.8.b_ref), channel_id=1, source_target_pairs={{1,2},{2,1},{3,4},{4,3},{5,6},{6,5},{7,8},{8,7},{9,10},{10,9},{11,... | collective-permute-start | bytes 1179656 | tf_op jit(solution)/shard_map/ppermute | solution.py:22
  17.1 0.7 copy.23
  17.8 0.6 pad.17.real_ref
  18.4 1.3 %pad.16.rgb_ref = bf16[8,384]{1,0:T(8,128)(2,1)} pad(bf16[3,384]{1,0:T(4,128)(2,1)} %bitcast.29, bf16[]{:T(256)} %constant.16.clone.1), padding=0_5x0_0 | pad | bytes 8450 | tf_op jit(solution)/shard_map/jit(_pad)/pad | solution.py:238
  19.7 0.0 collective-permute-done.2.past_ref
  19.7 0.1 collective-permute-start.3
  19.8 14.5 %collective-permute-start.4 = (bf16[2,128,384]{2,1,0:T(8,128)(2,1)S(1)}, bf16[2,128,384]{2,1,0:T(8,128)(2,1)S(1)}, u32[]{:S(2)}, u32[]{:S(2)}) collective-permute-start(bf16[2,128,384]{2,1,0:T(8,128)(2,1)S(1)} %get-tuple-element.12), channel_id=1, source_target_pairs={{1,2},{2,1},{3,4},{4,3},{5,6},{6,5},{7,8},{8,7},{9,10},{10,9},{11,... | collective-permute-start | bytes 589832 | tf_op jit(solution)/shard_map/ppermute | solution.py:22
  34.3 10.5 %own.1.part_ref = f32[4,2,128,384]{3,2,1,0:T(8,128)} custom-call(s32[2]{0:T(128)} %pad_add_fusion.pos_ref.refs_0_, bf16[4,128,384]{2,1,0:T(8,128)(2,1)} %get-tuple-element.7.a_ref, bf16[4,128,384]{2,1,0:T(8,128)(2,1)} %get-tuple-element.8.b_ref, bf16[2,2,128,384]{3,2,1,0:T(8,128)(2,1)} %copy-done.3, bf16[27,384,384]{2,1,0:T(8,128)(2,1)} %w_ref.3), custom_call_target="tpu_custom_call" | custom-call | flops 5435817984 | bytes 10000000 | tf_op jit(solution)/shard_map/own/pallas_call | solution.py:267
  44.8 0.0 collective-permute-done.a_ref
  44.9 0.7 copy-done.1
  45.6 0.1 copy-done.2
  45.7 0.1 copy-done.5
  45.8 0.7 copy-done.6
  46.5 9.4 %halo.1 = (bf16[4,2,128,384]{3,2,1,0:T(8,128)(2,1)}, bf16[4,2,8,128]{3,2,1,0:T(8,128)(2,1)}) custom-call(s32[2]{0:T(128)} %pad_add_fusion.pos_ref.refs_0_, bf16[4,128,384]{2,1,0:T(8,128)(2,1)} %copy-done.1, bf16[4,128,384]{2,1,0:T(8,128)(2,1)} %copy-done.2, bf16[2,128,384]{2,1,0:T(8,128)(2,1)} %copy-done.5, bf16[2,128,384]{2,1,0:T(8,128)(2,1)} %copy-done.6, ...), custom_call_target="tpu_custom_call" | custom-call | flops 2717908992 | bytes 10000000 | tf_op jit(solution)/shard_map/halo/pallas_call | solution.py:280
  56.0 3.3 %collective-permute-start.6 = (bf16[4,2,8,128]{3,2,1,0:T(8,128)(2,1)}, bf16[4,2,8,128]{3,2,1,0:T(8,128)(2,1)S(1)}, u32[]{:S(2)}, u32[]{:S(2)}) collective-permute-start(bf16[4,2,8,128]{3,2,1,0:T(8,128)(2,1)} %get-tuple-element.11), channel_id=1, source_target_pairs={{1,2},{2,1},{3,4},{4,3},{5,6},{6,5},{7,8},{8,7},{9,10},{10,9},{11,... | collective-permute-start | bytes 49160 | tf_op jit(solution)/shard_map/ppermute | solution.py:22
  59.4 0.8 constant_dynamic-update-slice_fusion.1
  60.1 5.1 %collective-permute-done.6 = bf16[4,2,8,128]{3,2,1,0:T(8,128)(2,1)S(1)} collective-permute-done((bf16[4,2,8,128]{3,2,1,0:T(8,128)(2,1)}, bf16[4,2,8,128]{3,2,1,0:T(8,128)(2,1)S(1)}, u32[]{:S(2)}, u32[]{:S(2)}) %collective-permute-start.6) | collective-permute-done | bytes 16416 | tf_op jit(solution)/shard_map/ppermute | solution.py:22
  65.2 0.1 collective-permute-start.7
  65.3 5.1 %collective-permute-start.8 = (bf16[2,6,8,128]{3,2,1,0:T(8,128)(2,1)S(1)}, bf16[2,6,8,128]{3,2,1,0:T(8,128)(2,1)S(1)}, u32[]{:S(2)}, u32[]{:S(2)}) collective-permute-start(bf16[2,6,8,128]{3,2,1,0:T(8,128)(2,1)S(1)} %get-tuple-element.14), channel_id=1, source_target_pairs={{32,64},{64,32},{33,65},{65,33},{34,66},{66,34},{35,67},{67,35},{3... | collective-permute-start | bytes 73736 | tf_op jit(solution)/shard_map/ppermute | solution.py:22
  70.4 0.1 fusion.3
  70.5 0.4 copy.14
  70.9 0.1 copy.21
  71.0 1.0 %copy.16.refs_5_ = bf16[384,576]{1,0:T(8,128)(2,1)} copy(bf16[384,576]{0,1:T(8,128)(2,1)S(1)} %bitcast.25) | data formatting | bytes 884736 | tf_op jit(solution)/shard_map/reshape | solution.py:245
  72.0 0.7 copy.15.refs_4_
  72.7 0.6 copy-done.7
  73.3 0.6 copy-done.8
  73.9 3.6 %disc.1 = f32[4,2,128]{2,1,0:T(2,128)} custom-call(s32[2]{0:T(128)} %pad_add_fusion.pos_ref.refs_0_, bf16[4,6,8,128]{3,2,1,0:T(8,128)(2,1)} %copy-done.4, bf16[2,6,8,128]{3,2,1,0:T(8,128)(2,1)} %copy-done.7, bf16[2,6,8,128]{3,2,1,0:T(8,128)(2,1)} %copy-done.8, bf16[128,216]{1,0:T(8,128)(2,1)} %copy.15.refs_4_, bf16[384,576]{1,0:T(8,128)(2,1)} %copy.16.refs_5_), custom_call_target="tpu_custom_call" | custom-call | tf_op jit(solution)/shard_map/disc/pallas_call | solution.py:305
  (26 shorter events, 0.1 us)
Async XLA Ops:
  5.1 14.6 %collective-permute-start.2 = (bf16[2,2,128,384]{3,2,1,0:T(8,128)(2,1)}, bf16[2,2,128,384]{3,2,1,0:T(8,128)(2,1)S(1)}, u32[]{:S(2)}, u32[]{:S(2)}) collective-permute-start(bf16[2,2,128,384]{3,2,1,0:T(8,128)(2,1)} %get-tuple-element.9), channel_id=1, source_target_pairs={{0,32},{32,64},{64,96},{1,33},{33,65},{65,97},{2,34},{34,66},{66,9... | collective-permute-start | bytes 1179656 | tf_op jit(solution)/shard_map/ppermute | solution.py:262
  9.2 35.7 %collective-permute-start = (bf16[4,128,384]{2,1,0:T(8,128)(2,1)}, bf16[4,128,384]{2,1,0:T(8,128)(2,1)S(1)}, u32[]{:S(2)}, u32[]{:S(2)}) collective-permute-start(bf16[4,128,384]{2,1,0:T(8,128)(2,1)} %get-tuple-element.7.a_ref), channel_id=1, source_target_pairs={{0,1},{1,0},{2,3},{3,2},{4,5},{5,4},{6,7},{7,6},{8,9},{9,8},{10,11... | collective-permute-start | bytes 1179656 | tf_op jit(solution)/shard_map/ppermute | solution.py:22
  10.5 34.4 %collective-permute-start.1 = (bf16[4,128,384]{2,1,0:T(8,128)(2,1)}, bf16[4,128,384]{2,1,0:T(8,128)(2,1)S(1)}, u32[]{:S(2)}, u32[]{:S(2)}) collective-permute-start(bf16[4,128,384]{2,1,0:T(8,128)(2,1)} %get-tuple-element.8.b_ref), channel_id=1, source_target_pairs={{1,2},{2,1},{3,4},{4,3},{5,6},{6,5},{7,8},{8,7},{9,10},{10,9},{11,... | collective-permute-start | bytes 1179656 | tf_op jit(solution)/shard_map/ppermute | solution.py:22
  19.7 14.6 %copy-start.3 = (bf16[2,2,128,384]{3,2,1,0:T(8,128)(2,1)}, bf16[2,2,128,384]{3,2,1,0:T(8,128)(2,1)S(1)}, u32[]{:S(2)}) copy-start(bf16[2,2,128,384]{3,2,1,0:T(8,128)(2,1)S(1)} %collective-permute-done.2.past_ref) | copy-start | bytes 1179652
  19.7 25.2 %collective-permute-start.3 = (bf16[2,128,384]{2,1,0:T(8,128)(2,1)S(1)}, bf16[2,128,384]{2,1,0:T(8,128)(2,1)S(1)}, u32[]{:S(2)}, u32[]{:S(2)}) collective-permute-start(bf16[2,128,384]{2,1,0:T(8,128)(2,1)S(1)} %get-tuple-element.13), channel_id=1, source_target_pairs={{0,1},{1,0},{2,3},{3,2},{4,5},{5,4},{6,7},{7,6},{8,9},{9,8},{10,11... | collective-permute-start | bytes 589832 | tf_op jit(solution)/shard_map/ppermute | solution.py:22
  19.8 25.1 %collective-permute-start.4 = (bf16[2,128,384]{2,1,0:T(8,128)(2,1)S(1)}, bf16[2,128,384]{2,1,0:T(8,128)(2,1)S(1)}, u32[]{:S(2)}, u32[]{:S(2)}) collective-permute-start(bf16[2,128,384]{2,1,0:T(8,128)(2,1)S(1)} %get-tuple-element.12), channel_id=1, source_target_pairs={{1,2},{2,1},{3,4},{4,3},{5,6},{6,5},{7,8},{8,7},{9,10},{10,9},{11,... | collective-permute-start | bytes 589832 | tf_op jit(solution)/shard_map/ppermute | solution.py:22
  44.8 11.1 %copy-start.9 = (bf16[27,64,3]{1,0,2:T(8,128)(2,1)S(1)}, bf16[27,64,3]{1,0,2:T(8,128)(2,1)}, u32[]{:S(2)}) copy-start(bf16[27,64,3]{1,0,2:T(8,128)(2,1)} %param.12) | copy-start | bytes 31108
  44.8 25.7 %copy-start = (bf16[27,128,64]{1,2,0:T(8,128)(2,1)S(1)}, bf16[27,128,64]{1,2,0:T(8,128)(2,1)}, u32[]{:S(2)}) copy-start(bf16[27,128,64]{1,2,0:T(8,128)(2,1)} %param.13) | copy-start | bytes 1327108
  44.8 0.8 copy-start.1
  44.9 0.9 %copy-start.2 = (bf16[4,128,384]{2,1,0:T(8,128)(2,1)}, bf16[4,128,384]{2,1,0:T(8,128)(2,1)S(1)}, u32[]{:S(2)}) copy-start(bf16[4,128,384]{2,1,0:T(8,128)(2,1)S(1)} %collective-permute-done.1.b_ref) | copy-start | bytes 1179652
  44.9 0.9 %copy-start.5 = (bf16[2,128,384]{2,1,0:T(8,128)(2,1)}, bf16[2,128,384]{2,1,0:T(8,128)(2,1)S(1)}, u32[]{:S(2)}) copy-start(bf16[2,128,384]{2,1,0:T(8,128)(2,1)S(1)} %collective-permute-done.3.past_a_ref) | copy-start | bytes 589828
  45.8 0.7 copy-start.6
  56.0 3.4 %collective-permute-start.5 = (bf16[4,2,8,128]{3,2,1,0:T(8,128)(2,1)}, bf16[4,2,8,128]{3,2,1,0:T(8,128)(2,1)S(1)}, u32[]{:S(2)}, u32[]{:S(2)}) collective-permute-start(bf16[4,2,8,128]{3,2,1,0:T(8,128)(2,1)} %get-tuple-element.11), channel_id=1, source_target_pairs={{0,1},{1,0},{2,3},{3,2},{4,5},{5,4},{6,7},{7,6},{8,9},{9,8},{10,11... | collective-permute-start | bytes 49160 | tf_op jit(solution)/shard_map/ppermute | solution.py:22
  56.0 9.2 %collective-permute-start.6 = (bf16[4,2,8,128]{3,2,1,0:T(8,128)(2,1)}, bf16[4,2,8,128]{3,2,1,0:T(8,128)(2,1)S(1)}, u32[]{:S(2)}, u32[]{:S(2)}) collective-permute-start(bf16[4,2,8,128]{3,2,1,0:T(8,128)(2,1)} %get-tuple-element.11), channel_id=1, source_target_pairs={{1,2},{2,1},{3,4},{4,3},{5,6},{6,5},{7,8},{8,7},{9,10},{10,9},{11,... | collective-permute-start | bytes 49160 | tf_op jit(solution)/shard_map/ppermute | solution.py:22
  65.2 7.5 %copy-start.4 = (bf16[4,6,8,128]{3,2,1,0:T(8,128)(2,1)}, bf16[4,6,8,128]{3,2,1,0:T(8,128)(2,1)S(1)}, u32[]{:S(2)}) copy-start(bf16[4,6,8,128]{3,2,1,0:T(8,128)(2,1)S(1)} %constant_dynamic-update-slice_fusion.refs_1_) | copy-start | bytes 147460
  65.2 7.5 %collective-permute-start.7 = (bf16[2,6,8,128]{3,2,1,0:T(8,128)(2,1)S(1)}, bf16[2,6,8,128]{3,2,1,0:T(8,128)(2,1)S(1)}, u32[]{:S(2)}, u32[]{:S(2)}) collective-permute-start(bf16[2,6,8,128]{3,2,1,0:T(8,128)(2,1)S(1)} %get-tuple-element.15), channel_id=1, source_target_pairs={{0,32},{32,0},{64,96},{96,64},{1,33},{33,1},{65,97},{97,65},{2,34}... | collective-permute-start | bytes 73736 | tf_op jit(solution)/shard_map/ppermute | solution.py:22
  65.3 7.4 %collective-permute-start.8 = (bf16[2,6,8,128]{3,2,1,0:T(8,128)(2,1)S(1)}, bf16[2,6,8,128]{3,2,1,0:T(8,128)(2,1)S(1)}, u32[]{:S(2)}, u32[]{:S(2)}) collective-permute-start(bf16[2,6,8,128]{3,2,1,0:T(8,128)(2,1)S(1)} %get-tuple-element.14), channel_id=1, source_target_pairs={{32,64},{64,32},{33,65},{65,33},{34,66},{66,34},{35,67},{67,35},{3... | collective-permute-start | bytes 73736 | tf_op jit(solution)/shard_map/ppermute | solution.py:22
  72.7 0.6 copy-start.7
  73.3 0.6 copy-start.8

commit v2 on v1

v2 whole, which is shorter than its diff:
```python
import jax
import jax.numpy as jnp
from jax import lax
from jax.experimental import pallas as pl
from jax.experimental.pallas import tpu as pltpu
from jax.sharding import PartitionSpec as P


F32 = jnp.float32
BF16 = jnp.bfloat16
VMEM = pl.BlockSpec(memory_space=pltpu.VMEM)
HBM = pl.BlockSpec(memory_space=pltpu.HBM)
NT = (((1,), (1,)), ((), ()))


def pairs(count, first):
    route = []
    for i in range(first, count - 1, 2):
        route += [(i, i + 1), (i + 1, i)]
    return route


def swap(block, axis, first):
    return lax.ppermute(block, axis, pairs(lax.axis_size(axis), first))


def onward(block, axis):
    return lax.ppermute(block, axis, [(i, i + 1) for i in range(lax.axis_size(axis) - 1)])


def local(kernel, outs, args, scratch=(), aliases=None, flops=0, hbm=(), limit=24):
    args = [
        pltpu.with_memory_space_constraint(a, pltpu.HBM if i in hbm else pltpu.VMEM)
        for i, a in enumerate(args)
    ]
    return pl.pallas_call(
        kernel,
        out_shape=outs,
        in_specs=[HBM if i in hbm else VMEM for i in range(len(args))],
        out_specs=jax.tree.map(lambda _: VMEM, outs),
        scratch_shapes=scratch,
        input_output_aliases=aliases or {},
        compiler_params=pltpu.CompilerParams(vmem_limit_bytes=limit << 20),
        cost_estimate=pl.CostEstimate(flops=flops, bytes_accessed=10**6, transcendentals=0),
    )(*args)


def kept(*dims, dtype=BF16):
    return pltpu.VMEM(dims, dtype)


def leaky(value):
    return jnp.maximum(value, 0.2 * value)


def act_kernel(feat_ref, gain_ref, to_a_ref, to_b_ref, tail_ref):
    odd = lax.rem(lax.axis_index("rows"), 2)
    gain = gain_ref[...]
    frames = feat_ref.shape[0]
    for k, (row, out_ref) in enumerate(((odd, to_b_ref), (1 - odd, to_a_ref))):
        for t in range(frames):
            feats = feat_ref[t, row].astype(F32)
            mean = jnp.mean(feats * feats, axis=-1, keepdims=True)
            normed = feats * lax.rsqrt(mean + 1e-06) * gain
            act = (normed * jax.nn.sigmoid(normed)).astype(BF16)
            out_ref[t] = act
            if t >= frames - 2:
                tail_ref[1 - k, t - frames + 2] = act


def column_blocks(rows, chans):
    return [(o, dw, off) for o in rows for dw in range(3) for off in range(0, chans, 128)]


def rhs_tile(w_ref, blocks, inputs):
    halves = [
        jnp.concatenate(
            [w_ref[9 * dt + 3 * (i - o + 1) + dw, :, off : off + 128] for dt, i in inputs], axis=0
        )
        for o, dw, off in blocks
    ]
    return halves[0] if len(halves) == 1 else jnp.concatenate(halves, axis=1)


def tiles(blocks):
    return [(j, blocks[j : j + 2]) for j in range(0, len(blocks), 2)]


def own_kernel(
    a_ref, b_ref, weight_ref, d2_ref, d1_ref, y_ref, w2_ref, w1_ref, w_ref, lines_ref, sems
):
    odd = lax.rem(lax.axis_index("rows"), 2)
    frames, width, chans = a_ref.shape
    order = [9 * dt + k for dt in (2, 1, 0) for k in range(9)]
    loads = {
        tap: pltpu.make_async_copy(weight_ref.at[tap], w_ref.at[tap], sems.at[tap]) for tap in order
    }
    for tap in order:
        loads[tap].start()
    lines_ref[1 - odd] = a_ref[...]
    lines_ref[odd] = b_ref[...]
    lhs = jnp.concatenate(
        [lines_ref[i].reshape(frames * width, chans) for i in range(2)], axis=1
    )
    for dt in (2, 1, 0):
        for tap in range(9 * dt, 9 * dt + 9):
            loads[tap].wait()
        used = frames - 2 + dt
        for j, some in tiles(column_blocks((0, 1), chans)):
            cols = slice(j * 128, (j + len(some)) * 128)
            got = jnp.dot(
                lhs[: used * width],
                rhs_tile(w_ref, some, [(dt, 0), (dt, 1)]),
                preferred_element_type=F32,
            )
            if dt == 2:
                y_ref[:, cols] = got
            else:
                y_ref[(frames - used) * width :, cols] += got
    depth2, depth1 = d2_ref.shape[2], d2_ref.shape[1]
    for tap in range(27):
        dw, rest = tap % 3, tap // 3
        if rest % 2 == 0:
            parts = [d2_ref[tap].astype(F32)]
            if rest < 8:
                parts.append(d2_ref[tap + 3].astype(F32))
            wide = jnp.concatenate(parts, axis=0)
            w2_ref[dw * depth2 : (dw + 1) * depth2, rest * depth1 : rest * depth1 + wide.shape[0]] = (
                wide.T.astype(BF16)
            )
    w1_ref[...] = d1_ref[...].astype(F32).T.astype(BF16)


def past_lhs(lines, zeros):
    first = [line[0] for line in lines] + [line[1] for line in lines]
    second = [line[1] for line in lines] + [zeros for _ in lines]
    return jnp.concatenate(
        [jnp.concatenate(first, axis=1), jnp.concatenate(second, axis=1)], axis=0
    )


def past_kernel(past_ref, w_ref, sum_ref, y_ref, lines_ref):
    odd = lax.rem(lax.axis_index("rows"), 2)
    width, chans = past_ref.shape[2:]
    lines_ref[1 - odd] = past_ref[0]
    lines_ref[odd] = past_ref[1]
    zeros = jnp.zeros((width, chans), BF16)
    lhs = past_lhs([lines_ref[i] for i in range(2)], zeros)
    inputs = [(dt, i) for dt in range(2) for i in range(2)]
    for j, some in tiles(column_blocks((0, 1), chans)):
        y_ref[: 2 * width, j * 128 : (j + len(some)) * 128] += jnp.dot(
            lhs, rhs_tile(w_ref, some, inputs), preferred_element_type=F32
        )


def rows_kernel(a_ref, b_ref, w_ref, sum_ref, y_ref, lines_ref):
    odd = lax.rem(lax.axis_index("rows"), 2)
    frames, width, chans = a_ref.shape
    lines_ref[1 - odd] = a_ref[...]
    lines_ref[odd] = b_ref[...]
    zeros = jnp.zeros((width, chans), BF16)
    for o in range(2):
        line = [zeros, zeros] + [lines_ref[o, t] for t in range(frames)]
        lhs = jnp.concatenate(
            [jnp.concatenate(line[dt : dt + frames], axis=0) for dt in range(3)], axis=1
        )
        inputs = [(dt, 3 * o - 1) for dt in range(3)]
        base = o * 3 * chans
        for j, some in tiles(column_blocks((o,), chans)):
            y_ref[:, base + j * 128 : base + (j + len(some)) * 128] += jnp.dot(
                lhs, rhs_tile(w_ref, some, inputs), preferred_element_type=F32
            )


def corner_kernel(
    past_ref, w_ref, sum_ref, feat_ref, rgb_ref, real_ref, decoded_ref, colour_ref, y_ref, lines_ref
):
    odd = lax.rem(lax.axis_index("rows"), 2)
    width, chans = past_ref.shape[2:]
    frames = feat_ref.shape[0]
    lines_ref[1 - odd] = past_ref[0]
    lines_ref[odd] = past_ref[1]
    zeros = jnp.zeros((width, chans), BF16)
    col = lax.broadcasted_iota(jnp.int32, (width, chans), 0)
    for o in range(2):
        lhs = past_lhs([lines_ref[o]], zeros)
        inputs = [(dt, 3 * o - 1) for dt in range(2)]
        for j, some in tiles(column_blocks((o,), chans)):
            y_ref[o, :, j * 128 : (j + len(some)) * 128] = jnp.dot(
                lhs, rhs_tile(w_ref, some, inputs), preferred_element_type=F32
            )
    for t in reversed(range(frames)):
        for o in range(2):
            ys = []
            for dw in range(3):
                at = (o * 3 + dw) * chans
                y = sum_ref[t * width : (t + 1) * width, at : at + chans]
                if t < 2:
                    y = y + y_ref[o, t * width : (t + 1) * width, dw * chans : (dw + 1) * chans]
                ys.append(y)
            total = (
                ys[1]
                + jnp.where(col == 0, 0.0, pltpu.roll(ys[0], 1, 0))
                + jnp.where(col == width - 1, 0.0, pltpu.roll(ys[2], width - 1, 0))
            )
            decoded = (feat_ref[t, o].astype(F32) + total).astype(BF16)
            decoded_ref[t, o] = decoded
            colour = lax.dot_general(rgb_ref[...], decoded, NT, preferred_element_type=F32)
            real = [real_ref[c, t, o : o + 1].astype(F32) for c in range(3)]
            colour_ref[t, o] = jnp.concatenate(
                [colour.astype(BF16).astype(F32)] + real + [jnp.zeros((2, width), F32)], axis=0
            ).astype(BF16)


def pack_kernel(a_ref, own_ref, b_ref, for_a_ref, for_b_ref):
    odd = lax.rem(lax.axis_index("tm"), 2)
    frames = own_ref.shape[0]
    for start, out_ref in (((frames - 2) * (1 - odd), for_a_ref), ((frames - 2) * odd, for_b_ref)):
        for k, ref in enumerate((a_ref, own_ref, b_ref)):
            out_ref[:, 2 * k : 2 * k + 2] = ref[pl.ds(start, 2)]


def disc_kernel(a_ref, own_ref, b_ref, ta_ref, tb_ref, w1_ref, w2_ref, out_ref, x_ref, f_ref):
    tm, band = lax.axis_index("tm"), lax.axis_index("rows")
    tm_count, row_count = lax.axis_size("tm"), lax.axis_size("rows")
    odd_t, odd_r = lax.rem(tm, 2), lax.rem(band, 2)
    width = out_ref.shape[-1]
    frames = out_ref.shape[0]
    col = lax.broadcasted_iota(jnp.int32, (8, width), 1)

    def put(t, h, line):
        x = line.astype(F32)
        x_ref[t, h, 0:8] = jnp.where(col == 0, 0.0, pltpu.roll(x, 1, 1))
        x_ref[t, h, 8:16] = x
        x_ref[t, h, 16:24] = jnp.where(col == width - 1, 0.0, pltpu.roll(x, width - 1, 1))

    row_at = [4 * (1 - odd_r), 4 * (1 - odd_r) + 1, 2, 3, 4 * odd_r, 4 * odd_r + 1]
    a_at = (frames + 2) * (1 - odd_t)
    b_at = (frames + 2) * odd_t
    for k in range(6):
        for t in range(frames):
            put(t + 2, row_at[k], (a_ref, own_ref, b_ref)[k // 2][t, k % 2])
        for t in range(2):
            put(a_at + t, row_at[k], ta_ref[t, k])
            put(b_at + t, row_at[k], tb_ref[t, k])

    w1 = w1_ref[...]
    near = {}
    for t in range(frames + 2):
        for h in range(0, 4, 2):
            cols = []
            for hh in (h, h + 1):
                cols.append(
                    jnp.concatenate(
                        [x_ref[t + dt, hh + dh] for dt in range(3) for dh in range(3)], axis=0
                    ).astype(BF16)
                )
            first = leaky(jnp.dot(w1, jnp.concatenate(cols, axis=1), preferred_element_type=F32))
            for i, hh in enumerate((h, h + 1)):
                part = first[:, i * width : (i + 1) * width]
                inside = []
                if t == 0:
                    inside.append(tm > 0)
                if t == frames + 1:
                    inside.append(tm < tm_count - 1)
                if hh == 0:
                    inside.append(band > 0)
                if hh == 3:
                    inside.append(band < row_count - 1)
                if inside:
                    keep = inside[0] if len(inside) == 1 else jnp.logical_and(*inside)
                    part = jnp.where(keep, part, 0.0)
                part = part.astype(BF16)
                f_ref[t, hh] = part
                if 1 <= t <= frames and 1 <= hh <= 2:
                    wide = part.astype(F32)
                    half = wide.shape[0] // 2
                    near[t - 1, hh - 1] = jnp.mean(
                        jnp.abs(wide[:half] - wide[half:]), axis=0, keepdims=True
                    )

    w2 = w2_ref[...]
    depth2 = w2.shape[0] // 3
    half = f_ref.shape[2] // 2
    colw = lax.broadcasted_iota(jnp.int32, (depth2, width), 1)
    for t in range(frames):
        for h in range(2):
            sides = []
            for s in range(2):
                sides.append(
                    jnp.concatenate(
                        [
                            f_ref[t + dt, h + dh, s * half : (s + 1) * half]
                            for dt in range(3)
                            for dh in range(3)
                        ],
                        axis=0,
                    )
                )
            y = jnp.dot(w2, jnp.concatenate(sides, axis=1), preferred_element_type=F32)
            outs = []
            for s in range(2):
                y0, y1, y2 = (
                    y[d * depth2 : (d + 1) * depth2, s * width : (s + 1) * width] for d in range(3)
                )
                total = (
                    y1
                    + jnp.where(colw == 0, 0.0, pltpu.roll(y0, 1, 1))
                    + jnp.where(colw == width - 1, 0.0, pltpu.roll(y2, width - 1, 1))
                )
                outs.append(leaky(total).astype(BF16).astype(F32))
            far = jnp.mean(jnp.abs(outs[0] - outs[1]), axis=0, keepdims=True)
            out_ref[t, h : h + 1] = near[t, h] + far


def per_device(
    latent_feat, norm_gain, conv_weight, rgb_weight, real_frames, disc_first, disc_second
):
    frames, height, width, chans = latent_feat.shape
    depth1, depth2 = disc_first.shape[1], disc_second.shape[1]
    cells = frames * width

    d1 = jnp.transpose(disc_first, (0, 2, 1))
    d1 = (
        jnp.pad(d1, ((0, 0), (0, 5), (0, depth1))) + jnp.pad(d1, ((0, 0), (3, 2), (depth1, 0)))
    ).reshape(27 * 8, 2 * depth1)
    d2 = jnp.transpose(disc_second, (0, 2, 1))

    to_a, to_b, tail = local(
        act_kernel,
        (kept(frames, width, chans), kept(frames, width, chans), kept(2, 2, width, chans)),
        (latent_feat, norm_gain),
    )
    from_b = swap(to_b, "rows", 1)
    from_a = swap(to_a, "rows", 0)
    past = onward(tail, "tm")

    line = 2 * width * chans * chans
    sums = kept(cells, 6 * chans, dtype=F32)
    y, w2, w1, weight = local(
        own_kernel,
        (sums, kept(3 * depth2, 9 * depth1), kept(2 * depth1, 27 * 8), kept(*conv_weight.shape)),
        (to_a, to_b, conv_weight, d2, d1),
        hbm=(2,),
        scratch=[pltpu.VMEM((2, frames, width, chans), BF16), pltpu.SemaphoreType.DMA((27,))],
        flops=36 * 3 * line,
    )
    y = local(
        past_kernel,
        sums,
        (past, weight, y),
        scratch=[pltpu.VMEM((2, 2, width, chans), BF16)],
        aliases={2: 0},
        flops=12 * 3 * line,
    )
    corner = onward(jnp.stack([from_a[frames - 2 :], from_b[frames - 2 :]]), "tm")
    y = local(
        rows_kernel,
        sums,
        (from_a, from_b, weight, y),
        scratch=[pltpu.VMEM((2, frames, width, chans), BF16)],
        aliases={3: 0},
        flops=18 * 3 * line,
    )
    decoded, colour = local(
        corner_kernel,
        (jax.ShapeDtypeStruct((frames, height, width, chans), BF16), kept(frames, height, 8, width)),
        (corner, weight, y, latent_feat, rgb_weight.T, real_frames),
        scratch=[
            pltpu.VMEM((2, 2 * width, 3 * chans), F32),
            pltpu.VMEM((2, 2, width, chans), BF16),
        ],
        flops=6 * 3 * line,
    )

    side_b = swap(colour, "rows", 1)
    side_a = swap(colour, "rows", 0)
    ends = kept(2, height + 4, 8, width)
    for_a, for_b = local(pack_kernel, (ends, ends), (side_a, colour, side_b))
    time_b = swap(for_b, "tm", 1)
    time_a = swap(for_a, "tm", 0)

    match_map = local(
        disc_kernel,
        jax.ShapeDtypeStruct((frames, height, width), F32),
        (side_a, colour, side_b, time_a, time_b, w1, w2),
        scratch=[
            pltpu.VMEM((frames + 4, height + 4, 24, width), F32),
            pltpu.VMEM((frames + 2, height + 2, 2 * depth1, width), BF16),
        ],
    )
    return (decoded, match_map)


def solution(mesh):
    placed = (P("tm", "rows", None, None), P(), P(), P(), P(None, "tm", "rows", None), P(), P())
    return jax.shard_map(
        per_device,
        mesh=mesh,
        in_specs=placed,
        out_specs=(P("tm", "rows", None, None), P("tm", "rows", None)),
        check_vma=False,
    )
```

time: 78.2 us -> 58.5 us (0.75)
  starting transfers between devices: 35.1 us -> 25.8 us
  Pallas kernels: 26.1 us -> 18 us
  local copies, waits for them, and re-layouts: 9.65 us -> 2.9 us
  waiting for transfers between devices: 5.1 us -> 9.26 us
    ppermute x8 -> x6, starting transfers between devices: 31 us -> 18 us  [swap(): return lax.ppermute(block, axis, pairs(lax.axis_size(axis), first))]
    pallas_call x4 -> x7, Pallas kernels: 26.1 us -> 18 us  [local(): pl.pallas_call(kernel, out_shape=outs, in_specs=[HBM if i in hbm else VME...]
    ppermute x8 -> x6, waiting for transfers between devices: 5.09 us -> 9.26 us  [swap(): return lax.ppermute(block, axis, pairs(lax.axis_size(axis), first))]
    ppermute x1 -> x2, starting transfers between devices: 4.09 us -> 7.83 us  [onward(): lax.ppermute(block, axis, [(i, i + 1) for i in range(lax.axis_size(axis)...]
    reshape x4 -> x0, local copies, waits for them, and re-layouts: 3.37 us -> none  [the longest x1 1.25 us: per_device(): norm_gain.reshape(1, chans)]
    pad x2 -> x0, local copies, waits for them, and re-layouts: 1.88 us -> none  [the longest x1 1.27 us: per_device(): rgb = jnp.pad(rgb_weight.T, ((0, 5), (0, 0)))]
    unnamed x25 -> x12, local copies, waits for them, and re-layouts: 4.35 us -> 2.84 us
    add x0 -> x1, other arithmetic: none -> 0.9 us  [per_device(): jnp.pad(d1, ((0, 0), (0, 5), (0, depth1)))]
  transfers between devices with their start and end apart: 9 -> 8, of which waited for: 1 -> 4; matrix products, arithmetic and copies ran while one was open for 7% -> 2% of each run, Pallas kernels for 14% -> 22%
where the time goes in v2:
time: 58.5 us; the launch traced here: 57.8 us
  starting transfers between devices  25.8 us (44%)
  Pallas kernels  18 us (31%)
  waiting for transfers between devices  9.26 us (16%)
  local copies, waits for them, and re-layouts  2.9 us (5%)
  other arithmetic  0.94 us (2%)
  between operations  0.82 us (1%)
    pallas_call x7, Pallas kernels, local(): pl.pallas_call(kernel, out_shape=outs, in_specs=[HBM if i in hbm else VME...  18 us
    ppermute x6, starting transfers between devices, swap(): return lax.ppermute(block, axis, pairs(lax.axis_size(axis), first))  18 us
    ppermute x6, waiting for transfers between devices, swap(): return lax.ppermute(block, axis, pairs(lax.axis_size(axis), first))  9.26 us
    ppermute x2, starting transfers between devices, onward(): lax.ppermute(block, axis, [(i, i + 1) for i in range(lax.axis_size(axis)...  7.83 us
    unnamed x12, local copies, waits for them, and re-layouts  2.84 us
  transfers between devices with their start and end apart: 8, of which 4 were waited for; matrix products, arithmetic and copies ran while one was open for 2% of the time, Pallas kernels for 22%

profile of v2, /device:TPU:17, one launch (start us, length us, event | category | flops | bytes accessed | tf_op | source)
XLA Modules:
  0.0 57.8 jit_solution(9729523088995377422)
XLA Ops:
  0.6 0.0 copy-start
  0.6 1.1 %copy-done = bf16[4,2,128,384]{3,2,1,0:T(8,128)(2,1)S(1)} copy-done((bf16[4,2,128,384]{3,2,1,0:T(8,128)(2,1)S(1)}, bf16[4,2,128,384]{3,2,1,0:T(8,128)(2,1)}, u32[]{:S(2)}) %copy-start) | copy-done | bytes 786456
  1.8 0.7 %copy-done.4 = f32[384]{0:T(512)S(1)} copy-done((f32[384]{0:T(512)S(1)}, f32[384]{0:T(512)}, u32[]{:S(2)}) %copy-start.4) | copy-done | bytes 1560
  2.4 0.5 shard_map.86
  2.9 7.6 %collective-permute-start.1 = (bf16[4,128,384]{2,1,0:T(8,128)(2,1)S(1)}, bf16[4,128,384]{2,1,0:T(8,128)(2,1)S(1)}, u32[]{:S(2)}, u32[]{:S(2)}) collective-permute-start(bf16[4,128,384]{2,1,0:T(8,128)(2,1)S(1)} %get-tuple-element.14.b_ref), channel_id=1, source_target_pairs={{1,2},{2,1},{3,4},{4,3},{5,6},{6,5},{7,8},{8,7},{9,10},{10,9},{11,... | collective-permute-start | bytes 1179656 | tf_op jit(solution)/shard_map/ppermute | solution.py:24
  10.5 0.1 collective-permute-start
  10.6 3.5 %collective-permute-start.3 = (bf16[2,2,128,384]{3,2,1,0:T(8,128)(2,1)S(1)}, bf16[2,2,128,384]{3,2,1,0:T(8,128)(2,1)S(1)}, u32[]{:S(2)}, u32[]{:S(2)}) collective-permute-start(bf16[2,2,128,384]{3,2,1,0:T(8,128)(2,1)S(1)} %get-tuple-element.16), channel_id=1, source_target_pairs={{0,32},{32,64},{64,96},{1,33},{33,65},{65,97},{2,34},{34,66},{66,9... | collective-permute-start | bytes 1179656 | tf_op jit(solution)/shard_map/ppermute | solution.py:28
  14.1 0.9 %pad_add_fusion = bf16[27,8,128]{2,0,1:T(8,128)(2,1)S(1)} fusion(bf16[27,3,64]{2,0,1:T(8,128)(2,1)} %bitcast.13), kind=kLoop, calls=%fused_computation.3 | loop fusion | flops 110592 | bytes 65664 | tf_op jit(solution)/shard_map/add | solution.py:325
  15.0 4.3 %collective-permute-done.1.b_ref = bf16[4,128,384]{2,1,0:T(8,128)(2,1)S(1)} collective-permute-done((bf16[4,128,384]{2,1,0:T(8,128)(2,1)S(1)}, bf16[4,128,384]{2,1,0:T(8,128)(2,1)S(1)}, u32[]{:S(2)}, u32[]{:S(2)}) %collective-permute-start.1) | collective-permute-done | bytes 393248 | tf_op jit(solution)/shard_map/ppermute | solution.py:24
  19.4 1.0 %collective-permute-done.a_ref = bf16[4,128,384]{2,1,0:T(8,128)(2,1)S(1)} collective-permute-done((bf16[4,128,384]{2,1,0:T(8,128)(2,1)S(1)}, bf16[4,128,384]{2,1,0:T(8,128)(2,1)S(1)}, u32[]{:S(2)}, u32[]{:S(2)}) %collective-permute-start) | collective-permute-done | bytes 393248 | tf_op jit(solution)/shard_map/ppermute | solution.py:24
  20.4 4.3 %collective-permute-start.2 = (bf16[2,2,128,384]{3,2,1,0:T(8,128)(2,1)S(1)}, bf16[2,2,128,384]{3,2,1,0:T(8,128)(2,1)S(1)}, u32[]{:S(2)}, u32[]{:S(2)}) collective-permute-start(bf16[2,2,128,384]{3,2,1,0:T(8,128)(2,1)S(1)} %pad_maximum_fusion), channel_id=1, source_target_pairs={{0,32},{32,64},{64,96},{1,33},{33,65},{65,97},{2,34},{34,66},{66,9... | collective-permute-start | bytes 1179656 | tf_op jit(solution)/shard_map/ppermute | solution.py:28
  24.8 0.0 copy-start.5
  24.8 1.0 %copy-done.5 = bf16[27,128,64]{1,2,0:T(8,128)(2,1)S(1)} copy-done((bf16[27,128,64]{1,2,0:T(8,128)(2,1)S(1)}, bf16[27,128,64]{1,2,0:T(8,128)(2,1)}, u32[]{:S(2)}) %copy-start.5) | copy-done | bytes 442392
  25.8 7.0 %shard_map.87 = (f32[512,2304]{1,0:T(8,128)S(1)}, bf16[384,576]{1,0:T(8,128)(2,1)S(1)}, bf16[128,216]{1,0:T(8,128)(2,1)S(1)}, bf16[27,384,384]{2,1,0:T(8,128)(2,1)S(1)}) custom-call(bf16[4,128,384]{2,1,0:T(8,128)(2,1)S(1)} %get-tuple-element.13.a_ref, bf16[4,128,384]{2,1,0:T(8,128)(2,1)S(1)} %get-tuple-element.14.b_ref, bf16[27,384,384]{2,1,0:T(8,128)(2,1)} %weight_ref.1, ...), custom_call_target="tpu_custom_call" | custom-call | flops 4076863488 | bytes 1000000 | tf_op jit(solution)/shard_map/pallas_call | solution.py:36
  32.7 0.0 collective-permute-done.3.past_ref
  32.8 2.1 %shard_map.88.sum_ref = f32[512,2304]{1,0:T(8,128)S(1)} custom-call(bf16[2,2,128,384]{3,2,1,0:T(8,128)(2,1)S(1)} %collective-permute-done.3.past_ref, bf16[27,384,384]{2,1,0:T(8,128)(2,1)S(1)} %get-tuple-element.15.w_ref, f32[512,2304]{1,0:T(8,128)S(1)} %get-tuple-element.17.sum_ref), custom_call_target="tpu_custom_call", output_to_operand_aliasing={{}: (2, {})} | custom-call | flops 1358954496 | bytes 1000000 | tf_op jit(solution)/shard_map/pallas_call | solution.py:36
  34.9 0.0 copy-start.1
  34.9 0.0 copy-start.2
  34.9 0.0 copy-start.3
  34.9 3.6 %shard_map.89.sum_ref = f32[512,2304]{1,0:T(8,128)S(1)} custom-call(bf16[4,128,384]{2,1,0:T(8,128)(2,1)S(1)} %collective-permute-done.a_ref, bf16[4,128,384]{2,1,0:T(8,128)(2,1)S(1)} %collective-permute-done.1.b_ref, bf16[27,384,384]{2,1,0:T(8,128)(2,1)S(1)} %get-tuple-element.15.w_ref, ...), custom_call_target="tpu_custom_call", output_to_operand_aliasing={{}: (3, {})} | custom-call | flops 2038431744 | bytes 1000000 | tf_op jit(solution)/shard_map/pallas_call | solution.py:36
  38.5 0.0 collective-permute-done.2.past_ref
  38.5 0.0 copy-done.1
  38.5 2.5 %shard_map.90 = (bf16[4,2,128,384]{3,2,1,0:T(8,128)(2,1)}, bf16[4,2,8,128]{3,2,1,0:T(8,128)(2,1)S(1)}) custom-call(bf16[2,2,128,384]{3,2,1,0:T(8,128)(2,1)S(1)} %collective-permute-done.2.past_ref, bf16[27,384,384]{2,1,0:T(8,128)(2,1)S(1)} %get-tuple-element.15.w_ref, f32[512,2304]{1,0:T(8,128)S(1)} %shard_map.89.sum_ref, ...), custom_call_target="tpu_custom_call" | custom-call | flops 679477248 | bytes 1000000 | tf_op jit(solution)/shard_map/pallas_call | solution.py:36
  41.0 0.0 collective-permute-start.4
  41.0 7.0 %collective-permute-start.5 = (bf16[4,2,8,128]{3,2,1,0:T(8,128)(2,1)S(1)}, bf16[4,2,8,128]{3,2,1,0:T(8,128)(2,1)S(1)}, u32[]{:S(2)}, u32[]{:S(2)}) collective-permute-start(bf16[4,2,8,128]{3,2,1,0:T(8,128)(2,1)S(1)} %get-tuple-element.19.own_ref), channel_id=1, source_target_pairs={{1,2},{2,1},{3,4},{4,3},{5,6},{6,5},{7,8},{8,7},{9,10},{10,9},{11,... | collective-permute-start | bytes 49160 | tf_op jit(solution)/shard_map/ppermute | solution.py:24
  48.0 0.0 collective-permute-done.4.a_ref
  48.0 2.0 %collective-permute-done.5.b_ref = bf16[4,2,8,128]{3,2,1,0:T(8,128)(2,1)S(1)} collective-permute-done((bf16[4,2,8,128]{3,2,1,0:T(8,128)(2,1)S(1)}, bf16[4,2,8,128]{3,2,1,0:T(8,128)(2,1)S(1)}, u32[]{:S(2)}, u32[]{:S(2)}) %collective-permute-start.5) | collective-permute-done | bytes 16416 | tf_op jit(solution)/shard_map/ppermute | solution.py:24
  50.0 0.2 collective-permute-start.6
  50.2 3.1 %collective-permute-start.7 = (bf16[2,6,8,128]{3,2,1,0:T(8,128)(2,1)S(1)}, bf16[2,6,8,128]{3,2,1,0:T(8,128)(2,1)S(1)}, u32[]{:S(2)}, u32[]{:S(2)}) collective-permute-start(bf16[2,6,8,128]{3,2,1,0:T(8,128)(2,1)S(1)} %get-tuple-element.21), channel_id=1, source_target_pairs={{32,64},{64,32},{33,65},{65,33},{34,66},{66,34},{35,67},{67,35},{3... | collective-permute-start | bytes 73736 | tf_op jit(solution)/shard_map/ppermute | solution.py:24
  53.4 0.0 collective-permute-done.6.ta_ref
  53.4 2.0 %collective-permute-done.7.tb_ref = bf16[2,6,8,128]{3,2,1,0:T(8,128)(2,1)S(1)} collective-permute-done((bf16[2,6,8,128]{3,2,1,0:T(8,128)(2,1)S(1)}, bf16[2,6,8,128]{3,2,1,0:T(8,128)(2,1)S(1)}, u32[]{:S(2)}, u32[]{:S(2)}) %collective-permute-start.7) | collective-permute-done | bytes 24608 | tf_op jit(solution)/shard_map/ppermute | solution.py:24
  55.3 2.4 %shard_map.92 = f32[4,2,128]{2,1,0:T(2,128)} custom-call(bf16[4,2,8,128]{3,2,1,0:T(8,128)(2,1)S(1)} %collective-permute-done.4.a_ref, bf16[4,2,8,128]{3,2,1,0:T(8,128)(2,1)S(1)} %get-tuple-element.19.own_ref, bf16[4,2,8,128]{3,2,1,0:T(8,128)(2,1)S(1)} %collective-permute-done.5.b_ref, bf16[2,6,8,128]{3,2,1,0:T(8,128)(2,1)S(1)} %collective-permute-done.6.ta_ref, ...), custom_call_target="tpu_custom_call" | custom-call | bytes 1000000 | tf_op jit(solution)/shard_map/pallas_call | solution.py:36
  (8 shorter events, 0.1 us)
Async XLA Ops:
  0.6 1.1 %copy-start = (bf16[4,2,128,384]{3,2,1,0:T(8,128)(2,1)S(1)}, bf16[4,2,128,384]{3,2,1,0:T(8,128)(2,1)}, u32[]{:S(2)}) copy-start(bf16[4,2,128,384]{3,2,1,0:T(8,128)(2,1)} %feat_ref.3) | copy-start | bytes 2359300
  1.8 0.7 %copy-start.4 = (f32[384]{0:T(512)S(1)}, f32[384]{0:T(512)}, u32[]{:S(2)}) copy-start(f32[384]{0:T(512)} %gain_ref.1) | copy-start | bytes 4612
  2.9 16.4 %collective-permute-start.1 = (bf16[4,128,384]{2,1,0:T(8,128)(2,1)S(1)}, bf16[4,128,384]{2,1,0:T(8,128)(2,1)S(1)}, u32[]{:S(2)}, u32[]{:S(2)}) collective-permute-start(bf16[4,128,384]{2,1,0:T(8,128)(2,1)S(1)} %get-tuple-element.14.b_ref), channel_id=1, source_target_pairs={{1,2},{2,1},{3,4},{4,3},{5,6},{6,5},{7,8},{8,7},{9,10},{10,9},{11,... | collective-permute-start | bytes 1179656 | tf_op jit(solution)/shard_map/ppermute | solution.py:24
  10.5 9.8 %collective-permute-start = (bf16[4,128,384]{2,1,0:T(8,128)(2,1)S(1)}, bf16[4,128,384]{2,1,0:T(8,128)(2,1)S(1)}, u32[]{:S(2)}, u32[]{:S(2)}) collective-permute-start(bf16[4,128,384]{2,1,0:T(8,128)(2,1)S(1)} %get-tuple-element.13.a_ref), channel_id=1, source_target_pairs={{0,1},{1,0},{2,3},{3,2},{4,5},{5,4},{6,7},{7,6},{8,9},{9,8},{10,11... | collective-permute-start | bytes 1179656 | tf_op jit(solution)/shard_map/ppermute | solution.py:24
  10.6 22.1 %collective-permute-start.3 = (bf16[2,2,128,384]{3,2,1,0:T(8,128)(2,1)S(1)}, bf16[2,2,128,384]{3,2,1,0:T(8,128)(2,1)S(1)}, u32[]{:S(2)}, u32[]{:S(2)}) collective-permute-start(bf16[2,2,128,384]{3,2,1,0:T(8,128)(2,1)S(1)} %get-tuple-element.16), channel_id=1, source_target_pairs={{0,32},{32,64},{64,96},{1,33},{33,65},{65,97},{2,34},{34,66},{66,9... | collective-permute-start | bytes 1179656 | tf_op jit(solution)/shard_map/ppermute | solution.py:28
  20.4 18.1 %collective-permute-start.2 = (bf16[2,2,128,384]{3,2,1,0:T(8,128)(2,1)S(1)}, bf16[2,2,128,384]{3,2,1,0:T(8,128)(2,1)S(1)}, u32[]{:S(2)}, u32[]{:S(2)}) collective-permute-start(bf16[2,2,128,384]{3,2,1,0:T(8,128)(2,1)S(1)} %pad_maximum_fusion), channel_id=1, source_target_pairs={{0,32},{32,64},{64,96},{1,33},{33,65},{65,97},{2,34},{34,66},{66,9... | collective-permute-start | bytes 1179656 | tf_op jit(solution)/shard_map/ppermute | solution.py:28
  24.8 1.0 %copy-start.5 = (bf16[27,128,64]{1,2,0:T(8,128)(2,1)S(1)}, bf16[27,128,64]{1,2,0:T(8,128)(2,1)}, u32[]{:S(2)}) copy-start(bf16[27,128,64]{1,2,0:T(8,128)(2,1)} %param.13) | copy-start | bytes 1327108
  34.9 3.6 %copy-start.1 = (bf16[4,2,128,384]{3,2,1,0:T(8,128)(2,1)S(1)}, bf16[4,2,128,384]{3,2,1,0:T(8,128)(2,1)}, u32[]{:S(2)}) copy-start(bf16[4,2,128,384]{3,2,1,0:T(8,128)(2,1)} %feat_ref.3) | copy-start | bytes 2359300
  34.9 3.6 %copy-start.2 = (bf16[3,4,2,128]{3,2,1,0:T(2,128)(2,1)S(1)}, bf16[3,4,2,128]{3,2,1,0:T(2,128)(2,1)}, u32[]{:S(2)}) copy-start(bf16[3,4,2,128]{3,2,1,0:T(2,128)(2,1)} %real_ref.1) | copy-start | bytes 18436
  34.9 3.6 %copy-start.3 = (bf16[384,3]{0,1:T(4,128)(2,1)S(1)}, bf16[384,3]{0,1:T(4,128)(2,1)}, u32[]{:S(2)}) copy-start(bf16[384,3]{0,1:T(4,128)(2,1)} %param.10) | copy-start | bytes 6916
  41.0 7.0 %collective-permute-start.4 = (bf16[4,2,8,128]{3,2,1,0:T(8,128)(2,1)S(1)}, bf16[4,2,8,128]{3,2,1,0:T(8,128)(2,1)S(1)}, u32[]{:S(2)}, u32[]{:S(2)}) collective-permute-start(bf16[4,2,8,128]{3,2,1,0:T(8,128)(2,1)S(1)} %get-tuple-element.19.own_ref), channel_id=1, source_target_pairs={{0,1},{1,0},{2,3},{3,2},{4,5},{5,4},{6,7},{7,6},{8,9},{9,8},{10,11... | collective-permute-start | bytes 49160 | tf_op jit(solution)/shard_map/ppermute | solution.py:24
  41.0 9.0 %collective-permute-start.5 = (bf16[4,2,8,128]{3,2,1,0:T(8,128)(2,1)S(1)}, bf16[4,2,8,128]{3,2,1,0:T(8,128)(2,1)S(1)}, u32[]{:S(2)}, u32[]{:S(2)}) collective-permute-start(bf16[4,2,8,128]{3,2,1,0:T(8,128)(2,1)S(1)} %get-tuple-element.19.own_ref), channel_id=1, source_target_pairs={{1,2},{2,1},{3,4},{4,3},{5,6},{6,5},{7,8},{8,7},{9,10},{10,9},{11,... | collective-permute-start | bytes 49160 | tf_op jit(solution)/shard_map/ppermute | solution.py:24
  50.0 3.4 %collective-permute-start.6 = (bf16[2,6,8,128]{3,2,1,0:T(8,128)(2,1)S(1)}, bf16[2,6,8,128]{3,2,1,0:T(8,128)(2,1)S(1)}, u32[]{:S(2)}, u32[]{:S(2)}) collective-permute-start(bf16[2,6,8,128]{3,2,1,0:T(8,128)(2,1)S(1)} %get-tuple-element.20), channel_id=1, source_target_pairs={{0,32},{32,0},{64,96},{96,64},{1,33},{33,1},{65,97},{97,65},{2,34}... | collective-permute-start | bytes 73736 | tf_op jit(solution)/shard_map/ppermute | solution.py:24
  50.2 5.1 %collective-permute-start.7 = (bf16[2,6,8,128]{3,2,1,0:T(8,128)(2,1)S(1)}, bf16[2,6,8,128]{3,2,1,0:T(8,128)(2,1)S(1)}, u32[]{:S(2)}, u32[]{:S(2)}) collective-permute-start(bf16[2,6,8,128]{3,2,1,0:T(8,128)(2,1)S(1)} %get-tuple-element.21), channel_id=1, source_target_pairs={{32,64},{64,32},{33,65},{65,33},{34,66},{66,34},{35,67},{67,35},{3... | collective-permute-start | bytes 73736 | tf_op jit(solution)/shard_map/ppermute | solution.py:24

commit v3 on v2

--- a/solution.py
+++ b/solution.py
@@ -53,19 +53,27 @@
     return jnp.maximum(value, 0.2 * value)
 
 
-def act_kernel(feat_ref, gain_ref, to_a_ref, to_b_ref, tail_ref):
+def act_kernel(feat_ref, gain_ref, to_a_ref, to_b_ref, tail_ref, feats_ref, scale_ref, sems):
     odd = lax.rem(lax.axis_index("rows"), 2)
-    gain = gain_ref[...]
     frames = feat_ref.shape[0]
-    for k, (row, out_ref) in enumerate(((odd, to_b_ref), (1 - odd, to_a_ref))):
-        for t in range(frames):
-            feats = feat_ref[t, row].astype(F32)
+    order = [frames - 2, frames - 1] + list(range(frames - 2))
+    fetch_gain = pltpu.make_async_copy(gain_ref, scale_ref, sems.at[frames])
+    fetch = [pltpu.make_async_copy(feat_ref.at[t], feats_ref.at[t], sems.at[t]) for t in range(frames)]
+    fetch_gain.start()
+    for t in order:
+        fetch[t].start()
+    fetch_gain.wait()
+    gain = scale_ref[...]
+    for t in order:
+        fetch[t].wait()
+        for k, (row, out_ref) in enumerate(((1 - odd, to_a_ref), (odd, to_b_ref))):
+            feats = feats_ref[t, row].astype(F32)
             mean = jnp.mean(feats * feats, axis=-1, keepdims=True)
             normed = feats * lax.rsqrt(mean + 1e-06) * gain
             act = (normed * jax.nn.sigmoid(normed)).astype(BF16)
             out_ref[t] = act
             if t >= frames - 2:
-                tail_ref[1 - k, t - frames + 2] = act
+                tail_ref[k, t - frames + 2] = act
 
 
 def column_blocks(rows, chans):
@@ -86,9 +94,7 @@
     return [(j, blocks[j : j + 2]) for j in range(0, len(blocks), 2)]
 
 
-def own_kernel(
-    a_ref, b_ref, weight_ref, d2_ref, d1_ref, y_ref, w2_ref, w1_ref, w_ref, lines_ref, sems
-):
+def own_kernel(a_ref, b_ref, past_ref, weight_ref, y_ref, w_ref, lines_ref, sems):
     odd = lax.rem(lax.axis_index("rows"), 2)
     frames, width, chans = a_ref.shape
     order = [9 * dt + k for dt in (2, 1, 0) for k in range(9)]
@@ -97,27 +103,28 @@
     }
     for tap in order:
         loads[tap].start()
-    lines_ref[1 - odd] = a_ref[...]
-    lines_ref[odd] = b_ref[...]
-    lhs = jnp.concatenate(
-        [lines_ref[i].reshape(frames * width, chans) for i in range(2)], axis=1
-    )
+    for k, (row, line_ref) in enumerate(((1 - odd, a_ref), (odd, b_ref))):
+        lines_ref[row, pl.ds(0, 2)] = past_ref[k]
+        lines_ref[row, pl.ds(2, frames)] = line_ref[...]
     for dt in (2, 1, 0):
         for tap in range(9 * dt, 9 * dt + 9):
             loads[tap].wait()
-        used = frames - 2 + dt
+        lhs = jnp.concatenate(
+            [lines_ref[i, dt : dt + frames].reshape(frames * width, chans) for i in range(2)], axis=1
+        )
         for j, some in tiles(column_blocks((0, 1), chans)):
             cols = slice(j * 128, (j + len(some)) * 128)
             got = jnp.dot(
-                lhs[: used * width],
-                rhs_tile(w_ref, some, [(dt, 0), (dt, 1)]),
-                preferred_element_type=F32,
+                lhs, rhs_tile(w_ref, some, [(dt, 0), (dt, 1)]), preferred_element_type=F32
             )
             if dt == 2:
                 y_ref[:, cols] = got
             else:
-                y_ref[(frames - used) * width :, cols] += got
-    depth2, depth1 = d2_ref.shape[2], d2_ref.shape[1]
+                y_ref[:, cols] += got
+
+
+def prep_kernel(d2_ref, d1_ref, w2_ref, w1_ref):
+    depth1, depth2 = d2_ref.shape[1:]
     for tap in range(27):
         dw, rest = tap % 3, tap // 3
         if rest % 2 == 0:
@@ -128,7 +135,16 @@
             w2_ref[dw * depth2 : (dw + 1) * depth2, rest * depth1 : rest * depth1 + wide.shape[0]] = (
                 wide.T.astype(BF16)
             )
-    w1_ref[...] = d1_ref[...].astype(F32).T.astype(BF16)
+    tap = lax.broadcasted_iota(jnp.int32, (27, 27 * 8), 0)
+    place = lax.broadcasted_iota(jnp.int32, (27, 27 * 8), 1)
+    for side in range(2):
+        total = jnp.zeros((depth1, 27 * 8), F32)
+        for c in range(3):
+            pick = jnp.where(place == 8 * tap + 3 * side + c, 1.0, 0.0).astype(BF16)
+            total = total + lax.dot_general(
+                d1_ref[c], pick, (((0,), (0,)), ((), ())), preferred_element_type=F32
+            )
+        w1_ref[side * depth1 : (side + 1) * depth1] = total.astype(BF16)
 
 
 def past_lhs(lines, zeros):
@@ -139,21 +155,29 @@
     )
 
 
-def past_kernel(past_ref, w_ref, sum_ref, y_ref, lines_ref):
-    odd = lax.rem(lax.axis_index("rows"), 2)
-    width, chans = past_ref.shape[2:]
-    lines_ref[1 - odd] = past_ref[0]
-    lines_ref[odd] = past_ref[1]
-    zeros = jnp.zeros((width, chans), BF16)
-    lhs = past_lhs([lines_ref[i] for i in range(2)], zeros)
-    inputs = [(dt, i) for dt in range(2) for i in range(2)]
-    for j, some in tiles(column_blocks((0, 1), chans)):
-        y_ref[: 2 * width, j * 128 : (j + len(some)) * 128] += jnp.dot(
-            lhs, rhs_tile(w_ref, some, inputs), preferred_element_type=F32
-        )
-
-
-def rows_kernel(a_ref, b_ref, w_ref, sum_ref, y_ref, lines_ref):
+def finish(ys, feats, rgb, reals):
+    width, chans = ys[1].shape
+    col = lax.broadcasted_iota(jnp.int32, (width, chans), 0)
+    total = (
+        ys[1]
+        + jnp.where(col == 0, 0.0, pltpu.roll(ys[0], 1, 0))
+        + jnp.where(col == width - 1, 0.0, pltpu.roll(ys[2], width - 1, 0))
+    )
+    decoded = (feats.astype(F32) + total).astype(BF16)
+    colour = lax.dot_general(rgb, decoded, NT, preferred_element_type=F32)
+    both = jnp.concatenate(
+        [colour.astype(BF16).astype(F32)]
+        + [real.astype(F32) for real in reals]
+        + [jnp.zeros((2, width), F32)],
+        axis=0,
+    )
+    return decoded, both.astype(BF16)
+
+
+def rows_kernel(
+    a_ref, b_ref, w_ref, sum_ref, feat_ref, rgb_ref, real_ref, y_ref, decoded_ref, colour_ref,
+    lines_ref, late_ref,
+):
     odd = lax.rem(lax.axis_index("rows"), 2)
     frames, width, chans = a_ref.shape
     lines_ref[1 - odd] = a_ref[...]
@@ -167,49 +191,55 @@
         inputs = [(dt, 3 * o - 1) for dt in range(3)]
         base = o * 3 * chans
         for j, some in tiles(column_blocks((o,), chans)):
-            y_ref[:, base + j * 128 : base + (j + len(some)) * 128] += jnp.dot(
-                lhs, rhs_tile(w_ref, some, inputs), preferred_element_type=F32
+            cols = slice(base + j * 128, base + (j + len(some)) * 128)
+            got = jnp.dot(lhs, rhs_tile(w_ref, some, inputs), preferred_element_type=F32)
+            got = got + sum_ref[:, cols]
+            y_ref[:, cols] = got[: 2 * width]
+            late_ref[:, cols] = got[2 * width :]
+        for t in range(frames - 2):
+            ys = [
+                late_ref[t * width : (t + 1) * width, base + dw * chans : base + (dw + 1) * chans]
+                for dw in range(3)
+            ]
+            decoded_ref[t, o], colour_ref[t, o] = finish(
+                ys,
+                feat_ref[t + 2, o],
+                rgb_ref[...],
+                [real_ref[c, t + 2, o : o + 1] for c in range(3)],
             )
 
 
 def corner_kernel(
-    past_ref, w_ref, sum_ref, feat_ref, rgb_ref, real_ref, decoded_ref, colour_ref, y_ref, lines_ref
+    past_ref, w_ref, sum_ref, feat_ref, rgb_ref, real_ref, done_ref, shown_ref,
+    decoded_ref, colour_ref, y_ref, lines_ref,
 ):
     odd = lax.rem(lax.axis_index("rows"), 2)
     width, chans = past_ref.shape[2:]
-    frames = feat_ref.shape[0]
+    decoded_ref[2:] = done_ref[...]
+    colour_ref[2:] = shown_ref[...]
     lines_ref[1 - odd] = past_ref[0]
     lines_ref[odd] = past_ref[1]
     zeros = jnp.zeros((width, chans), BF16)
-    col = lax.broadcasted_iota(jnp.int32, (width, chans), 0)
     for o in range(2):
         lhs = past_lhs([lines_ref[o]], zeros)
         inputs = [(dt, 3 * o - 1) for dt in range(2)]
+        base = o * 3 * chans
         for j, some in tiles(column_blocks((o,), chans)):
-            y_ref[o, :, j * 128 : (j + len(some)) * 128] = jnp.dot(
+            cols = slice(base + j * 128, base + (j + len(some)) * 128)
+            y_ref[:, cols] = sum_ref[:, cols] + jnp.dot(
                 lhs, rhs_tile(w_ref, some, inputs), preferred_element_type=F32
             )
-    for t in reversed(range(frames)):
-        for o in range(2):
-            ys = []
-            for dw in range(3):
-                at = (o * 3 + dw) * chans
-                y = sum_ref[t * width : (t + 1) * width, at : at + chans]
-                if t < 2:
-                    y = y + y_ref[o, t * width : (t + 1) * width, dw * chans : (dw + 1) * chans]
-                ys.append(y)
-            total = (
-                ys[1]
-                + jnp.where(col == 0, 0.0, pltpu.roll(ys[0], 1, 0))
-                + jnp.where(col == width - 1, 0.0, pltpu.roll(ys[2], width - 1, 0))
-            )
-            decoded = (feat_ref[t, o].astype(F32) + total).astype(BF16)
-            decoded_ref[t, o] = decoded
-            colour = lax.dot_general(rgb_ref[...], decoded, NT, preferred_element_type=F32)
-            real = [real_ref[c, t, o : o + 1].astype(F32) for c in range(3)]
-            colour_ref[t, o] = jnp.concatenate(
-                [colour.astype(BF16).astype(F32)] + real + [jnp.zeros((2, width), F32)], axis=0
-            ).astype(BF16)
+        for t in range(2):
+            ys = [
+                y_ref[t * width : (t + 1) * width, base + dw * chans : base + (dw + 1) * chans]
+                for dw in range(3)
+            ]
+            decoded_ref[t, o], colour_ref[t, o] = finish(
+                ys,
+                feat_ref[t, o],
+                rgb_ref[...],
+                [real_ref[c, t, o : o + 1] for c in range(3)],
+            )
 
 
 def pack_kernel(a_ref, own_ref, b_ref, for_a_ref, for_b_ref):
@@ -320,57 +350,63 @@
     depth1, depth2 = disc_first.shape[1], disc_second.shape[1]
     cells = frames * width
 
-    d1 = jnp.transpose(disc_first, (0, 2, 1))
-    d1 = (
-        jnp.pad(d1, ((0, 0), (0, 5), (0, depth1))) + jnp.pad(d1, ((0, 0), (3, 2), (depth1, 0)))
-    ).reshape(27 * 8, 2 * depth1)
-    d2 = jnp.transpose(disc_second, (0, 2, 1))
-
     to_a, to_b, tail = local(
         act_kernel,
         (kept(frames, width, chans), kept(frames, width, chans), kept(2, 2, width, chans)),
         (latent_feat, norm_gain),
-    )
+        hbm=(0, 1),
+        scratch=[
+            pltpu.VMEM(latent_feat.shape, BF16),
+            pltpu.VMEM(norm_gain.shape, F32),
+            pltpu.SemaphoreType.DMA((frames + 1,)),
+        ],
+    )
+    past = onward(tail, "tm")
     from_b = swap(to_b, "rows", 1)
     from_a = swap(to_a, "rows", 0)
-    past = onward(tail, "tm")
 
     line = 2 * width * chans * chans
-    sums = kept(cells, 6 * chans, dtype=F32)
-    y, w2, w1, weight = local(
+    y, weight = local(
         own_kernel,
-        (sums, kept(3 * depth2, 9 * depth1), kept(2 * depth1, 27 * 8), kept(*conv_weight.shape)),
-        (to_a, to_b, conv_weight, d2, d1),
-        hbm=(2,),
-        scratch=[pltpu.VMEM((2, frames, width, chans), BF16), pltpu.SemaphoreType.DMA((27,))],
-        flops=36 * 3 * line,
-    )
-    y = local(
-        past_kernel,
-        sums,
-        (past, weight, y),
-        scratch=[pltpu.VMEM((2, 2, width, chans), BF16)],
-        aliases={2: 0},
-        flops=12 * 3 * line,
+        (kept(cells, 6 * chans, dtype=F32), kept(*conv_weight.shape)),
+        (to_a, to_b, past, conv_weight),
+        hbm=(3,),
+        scratch=[
+            pltpu.VMEM((2, frames + 2, width, chans), BF16),
+            pltpu.SemaphoreType.DMA((27,)),
+        ],
+        flops=48 * 3 * line,
     )
     corner = onward(jnp.stack([from_a[frames - 2 :], from_b[frames - 2 :]]), "tm")
-    y = local(
+    rgb = rgb_weight.T
+    y, done, shown = local(
         rows_kernel,
-        sums,
-        (from_a, from_b, weight, y),
-        scratch=[pltpu.VMEM((2, frames, width, chans), BF16)],
-        aliases={3: 0},
+        (
+            kept(2 * width, 6 * chans, dtype=F32),
+            kept(frames - 2, height, width, chans),
+            kept(frames - 2, height, 8, width),
+        ),
+        (from_a, from_b, weight, y, latent_feat, rgb, real_frames),
+        scratch=[
+            pltpu.VMEM((2, frames, width, chans), BF16),
+            pltpu.VMEM((cells - 2 * width, 6 * chans), F32),
+        ],
         flops=18 * 3 * line,
     )
     decoded, colour = local(
         corner_kernel,
         (jax.ShapeDtypeStruct((frames, height, width, chans), BF16), kept(frames, height, 8, width)),
-        (corner, weight, y, latent_feat, rgb_weight.T, real_frames),
+        (corner, weight, y, latent_feat, rgb, real_frames, done, shown),
         scratch=[
-            pltpu.VMEM((2, 2 * width, 3 * chans), F32),
+            pltpu.VMEM((2 * width, 6 * chans), F32),
             pltpu.VMEM((2, 2, width, chans), BF16),
         ],
         flops=6 * 3 * line,
+    )
+    w2, w1 = local(
+        prep_kernel,
+        (kept(3 * depth2, 9 * depth1), kept(2 * depth1, 27 * 8)),
+        (jnp.transpose(disc_second, (0, 2, 1)), jnp.transpose(disc_first, (2, 0, 1))),
     )
 
     side_b = swap(colour, "rows", 1)

time: 58.5 us -> 57.3 us (0.979)
  local copies, waits for them, and re-layouts: 2.9 us -> 0.07 us
  Pallas kernels: 18 us -> 19.8 us
  starting transfers between devices: 25.8 us -> 26.9 us
  other arithmetic: 0.94 us -> 0.05 us
    unnamed x12 -> x10, local copies, waits for them, and re-layouts: 2.84 us -> 0.03 us
    pallas_call x7, Pallas kernels: 18 us -> 19.8 us  [local(): pl.pallas_call(kernel, out_shape=outs, in_specs=[HBM if i in hbm else VME...]
    ppermute x6, starting transfers between devices: 18 us -> 18.9 us  [swap(): return lax.ppermute(block, axis, pairs(lax.axis_size(axis), first))]
    add x1 -> x0, other arithmetic: 0.9 us -> none  [per_device(): jnp.pad(d1, ((0, 0), (0, 5), (0, depth1)))]
  transfers between devices with their start and end apart: 8 -> 8, of which waited for: 4 -> 4; matrix products, arithmetic and copies ran while one was open for 2% -> 0% of each run, Pallas kernels for 22% -> 23%
where the time goes in v3:
time: 57.3 us; the launch traced here: 57 us
  starting transfers between devices  26.9 us (47%)
  Pallas kernels  19.8 us (35%)
  waiting for transfers between devices  9.33 us (16%)
  between operations  0.83 us (1%)
    pallas_call x7, Pallas kernels, local(): pl.pallas_call(kernel, out_shape=outs, in_specs=[HBM if i in hbm else VME...  19.8 us
    ppermute x6, starting transfers between devices, swap(): return lax.ppermute(block, axis, pairs(lax.axis_size(axis), first))  18.9 us
    ppermute x6, waiting for transfers between devices, swap(): return lax.ppermute(block, axis, pairs(lax.axis_size(axis), first))  9.32 us
    ppermute x2, starting transfers between devices, onward(): lax.ppermute(block, axis, [(i, i + 1) for i in range(lax.axis_size(axis)...  7.96 us
  transfers between devices with their start and end apart: 8, of which 4 were waited for; matrix products, arithmetic and copies ran while one was open for 0% of the time, Pallas kernels for 23%

profile of v3, /device:TPU:17, one launch (start us, length us, event | category | flops | bytes accessed | tf_op | source)
XLA Modules:
  0.0 57.0 jit_solution(1085271981140987626)
XLA Ops:
  0.6 1.7 %shard_map.86 = (bf16[4,128,384]{2,1,0:T(8,128)(2,1)S(1)}, bf16[4,128,384]{2,1,0:T(8,128)(2,1)S(1)}, bf16[2,2,128,384]{3,2,1,0:T(8,128)(2,1)S(1)}) custom-call(bf16[4,2,128,384]{3,2,1,0:T(8,128)(2,1)} %feat_ref.5, f32[384]{0:T(512)} %gain_ref.1), custom_call_target="tpu_custom_call" | custom-call | bytes 1000000 | tf_op jit(solution)/shard_map/pallas_call | solution.py:36
  2.3 7.6 %collective-permute-start.1 = (bf16[4,128,384]{2,1,0:T(8,128)(2,1)S(1)}, bf16[4,128,384]{2,1,0:T(8,128)(2,1)S(1)}, u32[]{:S(2)}, u32[]{:S(2)}) collective-permute-start(bf16[4,128,384]{2,1,0:T(8,128)(2,1)S(1)} %get-tuple-element.17.b_ref), channel_id=1, source_target_pairs={{1,2},{2,1},{3,4},{4,3},{5,6},{6,5},{7,8},{8,7},{9,10},{10,9},{11,... | collective-permute-start | bytes 1179656 | tf_op jit(solution)/shard_map/ppermute | solution.py:24
  9.9 0.1 collective-permute-start
  10.0 3.5 %collective-permute-start.3 = (bf16[2,2,128,384]{3,2,1,0:T(8,128)(2,1)S(1)}, bf16[2,2,128,384]{3,2,1,0:T(8,128)(2,1)S(1)}, u32[]{:S(2)}, u32[]{:S(2)}) collective-permute-start(bf16[2,2,128,384]{3,2,1,0:T(8,128)(2,1)S(1)} %get-tuple-element.18), channel_id=1, source_target_pairs={{0,32},{32,64},{64,96},{1,33},{33,65},{65,97},{2,34},{34,66},{66,9... | collective-permute-start | bytes 1179656 | tf_op jit(solution)/shard_map/ppermute | solution.py:28
  13.5 5.2 %collective-permute-done.1.b_ref = bf16[4,128,384]{2,1,0:T(8,128)(2,1)S(1)} collective-permute-done((bf16[4,128,384]{2,1,0:T(8,128)(2,1)S(1)}, bf16[4,128,384]{2,1,0:T(8,128)(2,1)S(1)}, u32[]{:S(2)}, u32[]{:S(2)}) %collective-permute-start.1) | collective-permute-done | bytes 393248 | tf_op jit(solution)/shard_map/ppermute | solution.py:24
  18.8 1.0 %collective-permute-done.a_ref = bf16[4,128,384]{2,1,0:T(8,128)(2,1)S(1)} collective-permute-done((bf16[4,128,384]{2,1,0:T(8,128)(2,1)S(1)}, bf16[4,128,384]{2,1,0:T(8,128)(2,1)S(1)}, u32[]{:S(2)}, u32[]{:S(2)}) %collective-permute-start) | collective-permute-done | bytes 393248 | tf_op jit(solution)/shard_map/ppermute | solution.py:24
  19.8 0.0 copy-start
  19.8 0.0 copy-start.2
  19.8 0.0 copy-start.4
  19.8 4.5 %collective-permute-start.2 = (bf16[2,2,128,384]{3,2,1,0:T(8,128)(2,1)S(1)}, bf16[2,2,128,384]{3,2,1,0:T(8,128)(2,1)S(1)}, u32[]{:S(2)}, u32[]{:S(2)}) collective-permute-start(bf16[2,2,128,384]{3,2,1,0:T(8,128)(2,1)S(1)} %pad_maximum_fusion), channel_id=1, source_target_pairs={{0,32},{32,64},{64,96},{1,33},{33,65},{65,97},{2,34},{34,66},{66,9... | collective-permute-start | bytes 1179656 | tf_op jit(solution)/shard_map/ppermute | solution.py:28
  24.3 0.0 collective-permute-done.3.past_ref
  24.3 8.6 %shard_map.87 = (f32[512,2304]{1,0:T(8,128)S(1)}, bf16[27,384,384]{2,1,0:T(8,128)(2,1)S(1)}) custom-call(bf16[4,128,384]{2,1,0:T(8,128)(2,1)S(1)} %get-tuple-element.16.a_ref, bf16[4,128,384]{2,1,0:T(8,128)(2,1)S(1)} %get-tuple-element.17.b_ref, bf16[2,2,128,384]{3,2,1,0:T(8,128)(2,1)S(1)} %collective-permute-done.3.past_ref, bf16[27,384,384]{2,1,0:T(8,128)(2,1)} %weight_ref.1), custom_call_target="tpu_custom_call" | custom-call | flops 5435817984 | bytes 1000000 | tf_op jit(solution)/shard_map/pallas_call | solution.py:36
  33.0 0.0 copy-done
  33.0 0.0 copy-done.2
  33.0 0.0 copy-done.4
  33.0 4.4 %shard_map.88 = (f32[256,2304]{1,0:T(8,128)S(1)}, bf16[2,2,128,384]{3,2,1,0:T(8,128)(2,1)S(1)}, bf16[2,2,8,128]{3,2,1,0:T(8,128)(2,1)S(1)}) custom-call(bf16[4,128,384]{2,1,0:T(8,128)(2,1)S(1)} %collective-permute-done.a_ref, bf16[4,128,384]{2,1,0:T(8,128)(2,1)S(1)} %collective-permute-done.1.b_ref, bf16[27,384,384]{2,1,0:T(8,128)(2,1)S(1)} %get-tuple-element.19.w_ref, ...), custom_call_target="tpu_custom_call" | custom-call | flops 2038431744 | bytes 1000000 | tf_op jit(solution)/shard_map/pallas_call | solution.py:36
  37.3 0.0 copy-start.1
  37.3 0.0 copy-start.3
  37.4 0.0 collective-permute-done.2.past_ref
  37.4 2.4 %shard_map.89 = (bf16[4,2,128,384]{3,2,1,0:T(8,128)(2,1)}, bf16[4,2,8,128]{3,2,1,0:T(8,128)(2,1)S(1)}) custom-call(bf16[2,2,128,384]{3,2,1,0:T(8,128)(2,1)S(1)} %collective-permute-done.2.past_ref, bf16[27,384,384]{2,1,0:T(8,128)(2,1)S(1)} %get-tuple-element.19.w_ref, f32[256,2304]{1,0:T(8,128)S(1)} %get-tuple-element.21.sum_ref, ...), custom_call_target="tpu_custom_call" | custom-call | flops 679477248 | bytes 1000000 | tf_op jit(solution)/shard_map/pallas_call | solution.py:36
  39.8 0.0 collective-permute-start.4
  39.8 7.0 %collective-permute-start.5 = (bf16[4,2,8,128]{3,2,1,0:T(8,128)(2,1)S(1)}, bf16[4,2,8,128]{3,2,1,0:T(8,128)(2,1)S(1)}, u32[]{:S(2)}, u32[]{:S(2)}) collective-permute-start(bf16[4,2,8,128]{3,2,1,0:T(8,128)(2,1)S(1)} %get-tuple-element.25.own_ref), channel_id=1, source_target_pairs={{1,2},{2,1},{3,4},{4,3},{5,6},{6,5},{7,8},{8,7},{9,10},{10,9},{11,... | collective-permute-start | bytes 49160 | tf_op jit(solution)/shard_map/ppermute | solution.py:24
  46.8 0.0 collective-permute-done.4.a_ref
  46.8 2.0 %collective-permute-done.5.b_ref = bf16[4,2,8,128]{3,2,1,0:T(8,128)(2,1)S(1)} collective-permute-done((bf16[4,2,8,128]{3,2,1,0:T(8,128)(2,1)S(1)}, bf16[4,2,8,128]{3,2,1,0:T(8,128)(2,1)S(1)}, u32[]{:S(2)}, u32[]{:S(2)}) %collective-permute-start.5) | collective-permute-done | bytes 16416 | tf_op jit(solution)/shard_map/ppermute | solution.py:24
  48.8 0.2 collective-permute-start.6
  49.0 4.1 %collective-permute-start.7 = (bf16[2,6,8,128]{3,2,1,0:T(8,128)(2,1)S(1)}, bf16[2,6,8,128]{3,2,1,0:T(8,128)(2,1)S(1)}, u32[]{:S(2)}, u32[]{:S(2)}) collective-permute-start(bf16[2,6,8,128]{3,2,1,0:T(8,128)(2,1)S(1)} %get-tuple-element.27), channel_id=1, source_target_pairs={{32,64},{64,32},{33,65},{65,33},{34,66},{66,34},{35,67},{67,35},{3... | collective-permute-start | bytes 73736 | tf_op jit(solution)/shard_map/ppermute | solution.py:24
  53.1 0.0 copy-done.1
  53.1 0.0 copy-done.3
  53.1 0.3 shard_map.91
  53.4 0.0 collective-permute-done.6.ta_ref
  53.4 1.1 %collective-permute-done.7.tb_ref = bf16[2,6,8,128]{3,2,1,0:T(8,128)(2,1)S(1)} collective-permute-done((bf16[2,6,8,128]{3,2,1,0:T(8,128)(2,1)S(1)}, bf16[2,6,8,128]{3,2,1,0:T(8,128)(2,1)S(1)}, u32[]{:S(2)}, u32[]{:S(2)}) %collective-permute-start.7) | collective-permute-done | bytes 24608 | tf_op jit(solution)/shard_map/ppermute | solution.py:24
  54.6 2.4 %shard_map.92 = f32[4,2,128]{2,1,0:T(2,128)} custom-call(bf16[4,2,8,128]{3,2,1,0:T(8,128)(2,1)S(1)} %collective-permute-done.4.a_ref, bf16[4,2,8,128]{3,2,1,0:T(8,128)(2,1)S(1)} %get-tuple-element.25.own_ref, bf16[4,2,8,128]{3,2,1,0:T(8,128)(2,1)S(1)} %collective-permute-done.5.b_ref, bf16[2,6,8,128]{3,2,1,0:T(8,128)(2,1)S(1)} %collective-permute-done.6.ta_ref, ...), custom_call_target="tpu_custom_call" | custom-call | bytes 1000000 | tf_op jit(solution)/shard_map/pallas_call | solution.py:36
  (4 shorter events, 0.1 us)
Async XLA Ops:
  2.3 16.4 %collective-permute-start.1 = (bf16[4,128,384]{2,1,0:T(8,128)(2,1)S(1)}, bf16[4,128,384]{2,1,0:T(8,128)(2,1)S(1)}, u32[]{:S(2)}, u32[]{:S(2)}) collective-permute-start(bf16[4,128,384]{2,1,0:T(8,128)(2,1)S(1)} %get-tuple-element.17.b_ref), channel_id=1, source_target_pairs={{1,2},{2,1},{3,4},{4,3},{5,6},{6,5},{7,8},{8,7},{9,10},{10,9},{11,... | collective-permute-start | bytes 1179656 | tf_op jit(solution)/shard_map/ppermute | solution.py:24
  9.9 9.8 %collective-permute-start = (bf16[4,128,384]{2,1,0:T(8,128)(2,1)S(1)}, bf16[4,128,384]{2,1,0:T(8,128)(2,1)S(1)}, u32[]{:S(2)}, u32[]{:S(2)}) collective-permute-start(bf16[4,128,384]{2,1,0:T(8,128)(2,1)S(1)} %get-tuple-element.16.a_ref), channel_id=1, source_target_pairs={{0,1},{1,0},{2,3},{3,2},{4,5},{5,4},{6,7},{7,6},{8,9},{9,8},{10,11... | collective-permute-start | bytes 1179656 | tf_op jit(solution)/shard_map/ppermute | solution.py:24
  10.0 14.3 %collective-permute-start.3 = (bf16[2,2,128,384]{3,2,1,0:T(8,128)(2,1)S(1)}, bf16[2,2,128,384]{3,2,1,0:T(8,128)(2,1)S(1)}, u32[]{:S(2)}, u32[]{:S(2)}) collective-permute-start(bf16[2,2,128,384]{3,2,1,0:T(8,128)(2,1)S(1)} %get-tuple-element.18), channel_id=1, source_target_pairs={{0,32},{32,64},{64,96},{1,33},{33,65},{65,97},{2,34},{34,66},{66,9... | collective-permute-start | bytes 1179656 | tf_op jit(solution)/shard_map/ppermute | solution.py:28
  19.8 13.1 %copy-start = (bf16[4,2,128,384]{3,2,1,0:T(8,128)(2,1)S(1)}, bf16[4,2,128,384]{3,2,1,0:T(8,128)(2,1)}, u32[]{:S(2)}) copy-start(bf16[4,2,128,384]{3,2,1,0:T(8,128)(2,1)} %feat_ref.5) | copy-start | bytes 2359300
  19.8 13.1 %copy-start.2 = (bf16[3,4,2,128]{3,2,1,0:T(2,128)(2,1)S(1)}, bf16[3,4,2,128]{3,2,1,0:T(2,128)(2,1)}, u32[]{:S(2)}) copy-start(bf16[3,4,2,128]{3,2,1,0:T(2,128)(2,1)} %real_ref.3) | copy-start | bytes 18436
  19.8 13.1 %copy-start.4 = (bf16[384,3]{0,1:T(4,128)(2,1)S(1)}, bf16[384,3]{0,1:T(4,128)(2,1)}, u32[]{:S(2)}) copy-start(bf16[384,3]{0,1:T(4,128)(2,1)} %param.10) | copy-start | bytes 6916
  19.8 17.5 %collective-permute-start.2 = (bf16[2,2,128,384]{3,2,1,0:T(8,128)(2,1)S(1)}, bf16[2,2,128,384]{3,2,1,0:T(8,128)(2,1)S(1)}, u32[]{:S(2)}, u32[]{:S(2)}) collective-permute-start(bf16[2,2,128,384]{3,2,1,0:T(8,128)(2,1)S(1)} %pad_maximum_fusion), channel_id=1, source_target_pairs={{0,32},{32,64},{64,96},{1,33},{33,65},{65,97},{2,34},{34,66},{66,9... | collective-permute-start | bytes 1179656 | tf_op jit(solution)/shard_map/ppermute | solution.py:28
  37.3 15.7 %copy-start.1 = (bf16[27,128,64]{1,2,0:T(8,128)(2,1)S(1)}, bf16[27,128,64]{1,2,0:T(8,128)(2,1)}, u32[]{:S(2)}) copy-start(bf16[27,128,64]{1,2,0:T(8,128)(2,1)} %param.13) | copy-start | bytes 1327108
  37.3 15.7 %copy-start.3 = (bf16[27,64,3]{1,0,2:T(8,128)(2,1)S(1)}, bf16[27,64,3]{1,0,2:T(8,128)(2,1)}, u32[]{:S(2)}) copy-start(bf16[27,64,3]{1,0,2:T(8,128)(2,1)} %param.12) | copy-start | bytes 31108
  39.8 7.0 %collective-permute-start.4 = (bf16[4,2,8,128]{3,2,1,0:T(8,128)(2,1)S(1)}, bf16[4,2,8,128]{3,2,1,0:T(8,128)(2,1)S(1)}, u32[]{:S(2)}, u32[]{:S(2)}) collective-permute-start(bf16[4,2,8,128]{3,2,1,0:T(8,128)(2,1)S(1)} %get-tuple-element.25.own_ref), channel_id=1, source_target_pairs={{0,1},{1,0},{2,3},{3,2},{4,5},{5,4},{6,7},{7,6},{8,9},{9,8},{10,11... | collective-permute-start | bytes 49160 | tf_op jit(solution)/shard_map/ppermute | solution.py:24
  39.8 9.0 %collective-permute-start.5 = (bf16[4,2,8,128]{3,2,1,0:T(8,128)(2,1)S(1)}, bf16[4,2,8,128]{3,2,1,0:T(8,128)(2,1)S(1)}, u32[]{:S(2)}, u32[]{:S(2)}) collective-permute-start(bf16[4,2,8,128]{3,2,1,0:T(8,128)(2,1)S(1)} %get-tuple-element.25.own_ref), channel_id=1, source_target_pairs={{1,2},{2,1},{3,4},{4,3},{5,6},{6,5},{7,8},{8,7},{9,10},{10,9},{11,... | collective-permute-start | bytes 49160 | tf_op jit(solution)/shard_map/ppermute | solution.py:24
  48.8 4.6 %collective-permute-start.6 = (bf16[2,6,8,128]{3,2,1,0:T(8,128)(2,1)S(1)}, bf16[2,6,8,128]{3,2,1,0:T(8,128)(2,1)S(1)}, u32[]{:S(2)}, u32[]{:S(2)}) collective-permute-start(bf16[2,6,8,128]{3,2,1,0:T(8,128)(2,1)S(1)} %get-tuple-element.26), channel_id=1, source_target_pairs={{0,32},{32,0},{64,96},{96,64},{1,33},{33,1},{65,97},{97,65},{2,34}... | collective-permute-start | bytes 73736 | tf_op jit(solution)/shard_map/ppermute | solution.py:24
  49.0 5.6 %collective-permute-start.7 = (bf16[2,6,8,128]{3,2,1,0:T(8,128)(2,1)S(1)}, bf16[2,6,8,128]{3,2,1,0:T(8,128)(2,1)S(1)}, u32[]{:S(2)}, u32[]{:S(2)}) collective-permute-start(bf16[2,6,8,128]{3,2,1,0:T(8,128)(2,1)S(1)} %get-tuple-element.27), channel_id=1, source_target_pairs={{32,64},{64,32},{33,65},{65,33},{34,66},{66,34},{35,67},{67,35},{3... | collective-permute-start | bytes 73736 | tf_op jit(solution)/shard_map/ppermute | solution.py:24

commit v4 on v3

--- a/solution.py
+++ b/solution.py
@@ -106,18 +106,23 @@
     for k, (row, line_ref) in enumerate(((1 - odd, a_ref), (odd, b_ref))):
         lines_ref[row, pl.ds(0, 2)] = past_ref[k]
         lines_ref[row, pl.ds(2, frames)] = line_ref[...]
-    for dt in (2, 1, 0):
-        for tap in range(9 * dt, 9 * dt + 9):
-            loads[tap].wait()
+    for dts in ((2,), (1, 0)):
+        for dt in dts:
+            for tap in range(9 * dt, 9 * dt + 9):
+                loads[tap].wait()
         lhs = jnp.concatenate(
-            [lines_ref[i, dt : dt + frames].reshape(frames * width, chans) for i in range(2)], axis=1
+            [
+                lines_ref[i, dt : dt + frames].reshape(frames * width, chans)
+                for dt in dts
+                for i in range(2)
+            ],
+            axis=1,
         )
+        inputs = [(dt, i) for dt in dts for i in range(2)]
         for j, some in tiles(column_blocks((0, 1), chans)):
             cols = slice(j * 128, (j + len(some)) * 128)
-            got = jnp.dot(
-                lhs, rhs_tile(w_ref, some, [(dt, 0), (dt, 1)]), preferred_element_type=F32
-            )
-            if dt == 2:
+            got = jnp.dot(lhs, rhs_tile(w_ref, some, inputs), preferred_element_type=F32)
+            if 2 in dts:
                 y_ref[:, cols] = got
             else:
                 y_ref[:, cols] += got
@@ -201,7 +206,7 @@
                 late_ref[t * width : (t + 1) * width, base + dw * chans : base + (dw + 1) * chans]
                 for dw in range(3)
             ]
-            decoded_ref[t, o], colour_ref[t, o] = finish(
+            decoded_ref[t + 2, o], colour_ref[t + 2, o] = finish(
                 ys,
                 feat_ref[t + 2, o],
                 rgb_ref[...],
@@ -215,8 +220,6 @@
 ):
     odd = lax.rem(lax.axis_index("rows"), 2)
     width, chans = past_ref.shape[2:]
-    decoded_ref[2:] = done_ref[...]
-    colour_ref[2:] = shown_ref[...]
     lines_ref[1 - odd] = past_ref[0]
     lines_ref[odd] = past_ref[1]
     zeros = jnp.zeros((width, chans), BF16)
@@ -383,8 +386,8 @@
         rows_kernel,
         (
             kept(2 * width, 6 * chans, dtype=F32),
-            kept(frames - 2, height, width, chans),
-            kept(frames - 2, height, 8, width),
+            kept(frames, height, width, chans),
+            kept(frames, height, 8, width),
         ),
         (from_a, from_b, weight, y, latent_feat, rgb, real_frames),
         scratch=[
@@ -395,12 +398,13 @@
     )
     decoded, colour = local(
         corner_kernel,
-        (jax.ShapeDtypeStruct((frames, height, width, chans), BF16), kept(frames, height, 8, width)),
+        (kept(frames, height, width, chans), kept(frames, height, 8, width)),
         (corner, weight, y, latent_feat, rgb, real_frames, done, shown),
         scratch=[
             pltpu.VMEM((2 * width, 6 * chans), F32),
             pltpu.VMEM((2, 2, width, chans), BF16),
         ],
+        aliases={6: 0, 7: 1},
         flops=6 * 3 * line,
     )
     w2, w1 = local(

time: 57.3 us -> 56.4 us (0.984)
  local copies, waits for them, and re-layouts: 0.07 us -> 0.95 us
  waiting for transfers between devices: 9.33 us -> 8.47 us
  Pallas kernels: 19.8 us -> 19 us
    unnamed x10 -> x11, local copies, waits for them, and re-layouts: 0.03 us -> 0.91 us
    pallas_call x7, Pallas kernels: 19.8 us -> 19 us  [local(): pl.pallas_call(kernel, out_shape=outs, in_specs=[HBM if i in hbm else VME...]
    ppermute x6, waiting for transfers between devices: 9.32 us -> 8.47 us  [swap(): return lax.ppermute(block, axis, pairs(lax.axis_size(axis), first))]
  transfers between devices with their start and end apart: 8 -> 8, of which waited for: 4 -> 4; matrix products, arithmetic and copies ran while one was open for 0% -> 2% of each run, Pallas kernels for 23% -> 23%
where the time goes in v4:
time: 56.4 us; the launch traced here: 56.2 us
  starting transfers between devices  26.9 us (48%)
  Pallas kernels  19 us (34%)
  waiting for transfers between devices  8.47 us (15%)
  local copies, waits for them, and re-layouts  0.95 us (2%)
  between operations  0.83 us (1%)
    ppermute x6, starting transfers between devices, swap(): return lax.ppermute(block, axis, pairs(lax.axis_size(axis), first))  19 us
    pallas_call x7, Pallas kernels, local(): pl.pallas_call(kernel, out_shape=outs, in_specs=[HBM if i in hbm else VME...  19 us
    ppermute x6, waiting for transfers between devices, swap(): return lax.ppermute(block, axis, pairs(lax.axis_size(axis), first))  8.47 us
    ppermute x2, starting transfers between devices, onward(): lax.ppermute(block, axis, [(i, i + 1) for i in range(lax.axis_size(axis)...  7.96 us
  transfers between devices with their start and end apart: 8, of which 4 were waited for; matrix products, arithmetic and copies ran while one was open for 2% of the time, Pallas kernels for 23%

profile of v4, /device:TPU:17, one launch (start us, length us, event | category | flops | bytes accessed | tf_op | source)
XLA Modules:
  0.0 56.2 jit_solution(9241828286306445049)
XLA Ops:
  0.6 1.7 %shard_map.86 = (bf16[4,128,384]{2,1,0:T(8,128)(2,1)S(1)}, bf16[4,128,384]{2,1,0:T(8,128)(2,1)S(1)}, bf16[2,2,128,384]{3,2,1,0:T(8,128)(2,1)S(1)}) custom-call(bf16[4,2,128,384]{3,2,1,0:T(8,128)(2,1)} %feat_ref.5, f32[384]{0:T(512)} %gain_ref.1), custom_call_target="tpu_custom_call" | custom-call | bytes 1000000 | tf_op jit(solution)/shard_map/pallas_call | solution.py:36
  2.3 7.6 %collective-permute-start.1 = (bf16[4,128,384]{2,1,0:T(8,128)(2,1)S(1)}, bf16[4,128,384]{2,1,0:T(8,128)(2,1)S(1)}, u32[]{:S(2)}, u32[]{:S(2)}) collective-permute-start(bf16[4,128,384]{2,1,0:T(8,128)(2,1)S(1)} %get-tuple-element.17.b_ref), channel_id=1, source_target_pairs={{1,2},{2,1},{3,4},{4,3},{5,6},{6,5},{7,8},{8,7},{9,10},{10,9},{11,... | collective-permute-start | bytes 1179656 | tf_op jit(solution)/shard_map/ppermute | solution.py:24
  9.9 0.1 collective-permute-start
  10.0 3.5 %collective-permute-start.3 = (bf16[2,2,128,384]{3,2,1,0:T(8,128)(2,1)S(1)}, bf16[2,2,128,384]{3,2,1,0:T(8,128)(2,1)S(1)}, u32[]{:S(2)}, u32[]{:S(2)}) collective-permute-start(bf16[2,2,128,384]{3,2,1,0:T(8,128)(2,1)S(1)} %get-tuple-element.18), channel_id=1, source_target_pairs={{0,32},{32,64},{64,96},{1,33},{33,65},{65,97},{2,34},{34,66},{66,9... | collective-permute-start | bytes 1179656 | tf_op jit(solution)/shard_map/ppermute | solution.py:28
  13.5 5.2 %collective-permute-done.1.b_ref = bf16[4,128,384]{2,1,0:T(8,128)(2,1)S(1)} collective-permute-done((bf16[4,128,384]{2,1,0:T(8,128)(2,1)S(1)}, bf16[4,128,384]{2,1,0:T(8,128)(2,1)S(1)}, u32[]{:S(2)}, u32[]{:S(2)}) %collective-permute-start.1) | collective-permute-done | bytes 393248 | tf_op jit(solution)/shard_map/ppermute | solution.py:24
  18.8 1.0 %collective-permute-done.a_ref = bf16[4,128,384]{2,1,0:T(8,128)(2,1)S(1)} collective-permute-done((bf16[4,128,384]{2,1,0:T(8,128)(2,1)S(1)}, bf16[4,128,384]{2,1,0:T(8,128)(2,1)S(1)}, u32[]{:S(2)}, u32[]{:S(2)}) %collective-permute-start) | collective-permute-done | bytes 393248 | tf_op jit(solution)/shard_map/ppermute | solution.py:24
  19.8 0.0 copy-start
  19.8 0.0 copy-start.2
  19.8 0.0 copy-start.4
  19.8 4.5 %collective-permute-start.2 = (bf16[2,2,128,384]{3,2,1,0:T(8,128)(2,1)S(1)}, bf16[2,2,128,384]{3,2,1,0:T(8,128)(2,1)S(1)}, u32[]{:S(2)}, u32[]{:S(2)}) collective-permute-start(bf16[2,2,128,384]{3,2,1,0:T(8,128)(2,1)S(1)} %pad_maximum_fusion), channel_id=1, source_target_pairs={{0,32},{32,64},{64,96},{1,33},{33,65},{65,97},{2,34},{34,66},{66,9... | collective-permute-start | bytes 1179656 | tf_op jit(solution)/shard_map/ppermute | solution.py:28
  24.3 0.0 collective-permute-done.3.past_ref
  24.3 8.5 %shard_map.87 = (f32[512,2304]{1,0:T(8,128)S(1)}, bf16[27,384,384]{2,1,0:T(8,128)(2,1)S(1)}) custom-call(bf16[4,128,384]{2,1,0:T(8,128)(2,1)S(1)} %get-tuple-element.16.a_ref, bf16[4,128,384]{2,1,0:T(8,128)(2,1)S(1)} %get-tuple-element.17.b_ref, bf16[2,2,128,384]{3,2,1,0:T(8,128)(2,1)S(1)} %collective-permute-done.3.past_ref, bf16[27,384,384]{2,1,0:T(8,128)(2,1)} %weight_ref.1), custom_call_target="tpu_custom_call" | custom-call | flops 5435817984 | bytes 1000000 | tf_op jit(solution)/shard_map/pallas_call | solution.py:36
  32.9 0.0 copy-done
  32.9 0.0 copy-done.2
  32.9 0.0 copy-done.4
  32.9 4.4 %shard_map.88 = (f32[256,2304]{1,0:T(8,128)S(1)}, bf16[4,2,128,384]{3,2,1,0:T(8,128)(2,1)S(1)}, bf16[4,2,8,128]{3,2,1,0:T(8,128)(2,1)S(1)}) custom-call(bf16[4,128,384]{2,1,0:T(8,128)(2,1)S(1)} %collective-permute-done.a_ref, bf16[4,128,384]{2,1,0:T(8,128)(2,1)S(1)} %collective-permute-done.1.b_ref, bf16[27,384,384]{2,1,0:T(8,128)(2,1)S(1)} %get-tuple-element.19.w_ref, ...), custom_call_target="tpu_custom_call" | custom-call | flops 2038431744 | bytes 1000000 | tf_op jit(solution)/shard_map/pallas_call | solution.py:36
  37.3 0.0 copy-start.1
  37.3 0.0 collective-permute-done.2.past_ref
  37.3 1.6 %shard_map.89 = (bf16[4,2,128,384]{3,2,1,0:T(8,128)(2,1)S(1)}, bf16[4,2,8,128]{3,2,1,0:T(8,128)(2,1)S(1)}) custom-call(bf16[2,2,128,384]{3,2,1,0:T(8,128)(2,1)S(1)} %collective-permute-done.2.past_ref, bf16[27,384,384]{2,1,0:T(8,128)(2,1)S(1)} %get-tuple-element.19.w_ref, ...), custom_call_target="tpu_custom_call", output_to_operand_aliasing={{0}: (6, {}), {1}: (7, {})} | custom-call | flops 679477248 | bytes 1000000 | tf_op jit(solution)/shard_map/pallas_call | solution.py:36
  38.9 0.1 collective-permute-start.4
  39.0 7.0 %collective-permute-start.5 = (bf16[4,2,8,128]{3,2,1,0:T(8,128)(2,1)S(1)}, bf16[4,2,8,128]{3,2,1,0:T(8,128)(2,1)S(1)}, u32[]{:S(2)}, u32[]{:S(2)}) collective-permute-start(bf16[4,2,8,128]{3,2,1,0:T(8,128)(2,1)S(1)} %get-tuple-element.25.own_ref), channel_id=1, source_target_pairs={{1,2},{2,1},{3,4},{4,3},{5,6},{6,5},{7,8},{8,7},{9,10},{10,9},{11,... | collective-permute-start | bytes 49160 | tf_op jit(solution)/shard_map/ppermute | solution.py:24
  45.9 0.0 collective-permute-done.4.a_ref
  46.0 2.0 %collective-permute-done.5.b_ref = bf16[4,2,8,128]{3,2,1,0:T(8,128)(2,1)S(1)} collective-permute-done((bf16[4,2,8,128]{3,2,1,0:T(8,128)(2,1)S(1)}, bf16[4,2,8,128]{3,2,1,0:T(8,128)(2,1)S(1)}, u32[]{:S(2)}, u32[]{:S(2)}) %collective-permute-start.5) | collective-permute-done | bytes 16416 | tf_op jit(solution)/shard_map/ppermute | solution.py:24
  48.0 0.2 collective-permute-start.6
  48.2 4.1 %collective-permute-start.7 = (bf16[2,6,8,128]{3,2,1,0:T(8,128)(2,1)S(1)}, bf16[2,6,8,128]{3,2,1,0:T(8,128)(2,1)S(1)}, u32[]{:S(2)}, u32[]{:S(2)}) collective-permute-start(bf16[2,6,8,128]{3,2,1,0:T(8,128)(2,1)S(1)} %get-tuple-element.27), channel_id=1, source_target_pairs={{32,64},{64,32},{33,65},{65,33},{34,66},{66,34},{35,67},{67,35},{3... | collective-permute-start | bytes 73736 | tf_op jit(solution)/shard_map/ppermute | solution.py:24
  52.3 0.0 copy-done.1
  52.3 0.0 copy-done.3
  52.3 0.3 shard_map.91
  52.6 0.9 %copy.13 = bf16[4,2,128,384]{3,2,1,0:T(8,128)(2,1)} copy(bf16[4,2,128,384]{3,2,1,0:T(8,128)(2,1)S(1)} %get-tuple-element.30) | data formatting | bytes 1572864
  53.5 0.0 collective-permute-done.6.ta_ref
  53.5 0.3 collective-permute-done.7.tb_ref
  53.8 2.4 %shard_map.92 = f32[4,2,128]{2,1,0:T(2,128)} custom-call(bf16[4,2,8,128]{3,2,1,0:T(8,128)(2,1)S(1)} %collective-permute-done.4.a_ref, bf16[4,2,8,128]{3,2,1,0:T(8,128)(2,1)S(1)} %get-tuple-element.25.own_ref, bf16[4,2,8,128]{3,2,1,0:T(8,128)(2,1)S(1)} %collective-permute-done.5.b_ref, bf16[2,6,8,128]{3,2,1,0:T(8,128)(2,1)S(1)} %collective-permute-done.6.ta_ref, ...), custom_call_target="tpu_custom_call" | custom-call | bytes 1000000 | tf_op jit(solution)/shard_map/pallas_call | solution.py:36
  (5 shorter events, 0.1 us)
Async XLA Ops:
  2.3 16.4 %collective-permute-start.1 = (bf16[4,128,384]{2,1,0:T(8,128)(2,1)S(1)}, bf16[4,128,384]{2,1,0:T(8,128)(2,1)S(1)}, u32[]{:S(2)}, u32[]{:S(2)}) collective-permute-start(bf16[4,128,384]{2,1,0:T(8,128)(2,1)S(1)} %get-tuple-element.17.b_ref), channel_id=1, source_target_pairs={{1,2},{2,1},{3,4},{4,3},{5,6},{6,5},{7,8},{8,7},{9,10},{10,9},{11,... | collective-permute-start | bytes 1179656 | tf_op jit(solution)/shard_map/ppermute | solution.py:24
  9.9 9.8 %collective-permute-start = (bf16[4,128,384]{2,1,0:T(8,128)(2,1)S(1)}, bf16[4,128,384]{2,1,0:T(8,128)(2,1)S(1)}, u32[]{:S(2)}, u32[]{:S(2)}) collective-permute-start(bf16[4,128,384]{2,1,0:T(8,128)(2,1)S(1)} %get-tuple-element.16.a_ref), channel_id=1, source_target_pairs={{0,1},{1,0},{2,3},{3,2},{4,5},{5,4},{6,7},{7,6},{8,9},{9,8},{10,11... | collective-permute-start | bytes 1179656 | tf_op jit(solution)/shard_map/ppermute | solution.py:24
  10.0 14.3 %collective-permute-start.3 = (bf16[2,2,128,384]{3,2,1,0:T(8,128)(2,1)S(1)}, bf16[2,2,128,384]{3,2,1,0:T(8,128)(2,1)S(1)}, u32[]{:S(2)}, u32[]{:S(2)}) collective-permute-start(bf16[2,2,128,384]{3,2,1,0:T(8,128)(2,1)S(1)} %get-tuple-element.18), channel_id=1, source_target_pairs={{0,32},{32,64},{64,96},{1,33},{33,65},{65,97},{2,34},{34,66},{66,9... | collective-permute-start | bytes 1179656 | tf_op jit(solution)/shard_map/ppermute | solution.py:28
  19.8 13.1 %copy-start = (bf16[4,2,128,384]{3,2,1,0:T(8,128)(2,1)S(1)}, bf16[4,2,128,384]{3,2,1,0:T(8,128)(2,1)}, u32[]{:S(2)}) copy-start(bf16[4,2,128,384]{3,2,1,0:T(8,128)(2,1)} %feat_ref.5) | copy-start | bytes 2359300
  19.8 13.0 %copy-start.2 = (bf16[3,4,2,128]{3,2,1,0:T(2,128)(2,1)S(1)}, bf16[3,4,2,128]{3,2,1,0:T(2,128)(2,1)}, u32[]{:S(2)}) copy-start(bf16[3,4,2,128]{3,2,1,0:T(2,128)(2,1)} %real_ref.3) | copy-start | bytes 18436
  19.8 13.0 %copy-start.4 = (bf16[384,3]{0,1:T(4,128)(2,1)S(1)}, bf16[384,3]{0,1:T(4,128)(2,1)}, u32[]{:S(2)}) copy-start(bf16[384,3]{0,1:T(4,128)(2,1)} %param.10) | copy-start | bytes 6916
  19.8 17.4 %collective-permute-start.2 = (bf16[2,2,128,384]{3,2,1,0:T(8,128)(2,1)S(1)}, bf16[2,2,128,384]{3,2,1,0:T(8,128)(2,1)S(1)}, u32[]{:S(2)}, u32[]{:S(2)}) collective-permute-start(bf16[2,2,128,384]{3,2,1,0:T(8,128)(2,1)S(1)} %pad_maximum_fusion), channel_id=1, source_target_pairs={{0,32},{32,64},{64,96},{1,33},{33,65},{65,97},{2,34},{34,66},{66,9... | collective-permute-start | bytes 1179656 | tf_op jit(solution)/shard_map/ppermute | solution.py:28
  37.3 15.0 %copy-start.1 = (bf16[27,128,64]{1,2,0:T(8,128)(2,1)S(1)}, bf16[27,128,64]{1,2,0:T(8,128)(2,1)}, u32[]{:S(2)}) copy-start(bf16[27,128,64]{1,2,0:T(8,128)(2,1)} %param.13) | copy-start | bytes 1327108
  37.3 15.0 %copy-start.3 = (bf16[27,64,3]{1,0,2:T(8,128)(2,1)S(1)}, bf16[27,64,3]{1,0,2:T(8,128)(2,1)}, u32[]{:S(2)}) copy-start(bf16[27,64,3]{1,0,2:T(8,128)(2,1)} %param.12) | copy-start | bytes 31108
  38.9 7.0 %collective-permute-start.4 = (bf16[4,2,8,128]{3,2,1,0:T(8,128)(2,1)S(1)}, bf16[4,2,8,128]{3,2,1,0:T(8,128)(2,1)S(1)}, u32[]{:S(2)}, u32[]{:S(2)}) collective-permute-start(bf16[4,2,8,128]{3,2,1,0:T(8,128)(2,1)S(1)} %get-tuple-element.25.own_ref), channel_id=1, source_target_pairs={{0,1},{1,0},{2,3},{3,2},{4,5},{5,4},{6,7},{7,6},{8,9},{9,8},{10,11... | collective-permute-start | bytes 49160 | tf_op jit(solution)/shard_map/ppermute | solution.py:24
  39.0 9.0 %collective-permute-start.5 = (bf16[4,2,8,128]{3,2,1,0:T(8,128)(2,1)S(1)}, bf16[4,2,8,128]{3,2,1,0:T(8,128)(2,1)S(1)}, u32[]{:S(2)}, u32[]{:S(2)}) collective-permute-start(bf16[4,2,8,128]{3,2,1,0:T(8,128)(2,1)S(1)} %get-tuple-element.25.own_ref), channel_id=1, source_target_pairs={{1,2},{2,1},{3,4},{4,3},{5,6},{6,5},{7,8},{8,7},{9,10},{10,9},{11,... | collective-permute-start | bytes 49160 | tf_op jit(solution)/shard_map/ppermute | solution.py:24
  48.0 5.5 %collective-permute-start.6 = (bf16[2,6,8,128]{3,2,1,0:T(8,128)(2,1)S(1)}, bf16[2,6,8,128]{3,2,1,0:T(8,128)(2,1)S(1)}, u32[]{:S(2)}, u32[]{:S(2)}) collective-permute-start(bf16[2,6,8,128]{3,2,1,0:T(8,128)(2,1)S(1)} %get-tuple-element.26), channel_id=1, source_target_pairs={{0,32},{32,0},{64,96},{96,64},{1,33},{33,1},{65,97},{97,65},{2,34}... | collective-permute-start | bytes 73736 | tf_op jit(solution)/shard_map/ppermute | solution.py:24
  48.2 5.6 %collective-permute-start.7 = (bf16[2,6,8,128]{3,2,1,0:T(8,128)(2,1)S(1)}, bf16[2,6,8,128]{3,2,1,0:T(8,128)(2,1)S(1)}, u32[]{:S(2)}, u32[]{:S(2)}) collective-permute-start(bf16[2,6,8,128]{3,2,1,0:T(8,128)(2,1)S(1)} %get-tuple-element.27), channel_id=1, source_target_pairs={{32,64},{64,32},{33,65},{65,33},{34,66},{66,34},{35,67},{67,35},{3... | collective-permute-start | bytes 73736 | tf_op jit(solution)/shard_map/ppermute | solution.py:24

commit v5 on v4

--- a/solution.py
+++ b/solution.py
@@ -94,38 +94,30 @@
     return [(j, blocks[j : j + 2]) for j in range(0, len(blocks), 2)]
 
 
-def own_kernel(a_ref, b_ref, past_ref, weight_ref, y_ref, w_ref, lines_ref, sems):
+def fetch_kernel(weight_ref, w_ref, sems):
+    loads = [
+        pltpu.make_async_copy(weight_ref.at[tap], w_ref.at[tap], sems.at[tap]) for tap in range(27)
+    ]
+    for load in loads:
+        load.start()
+    for load in loads:
+        load.wait()
+
+
+def own_kernel(a_ref, b_ref, past_ref, w_ref, y_ref, lines_ref):
     odd = lax.rem(lax.axis_index("rows"), 2)
     frames, width, chans = a_ref.shape
-    order = [9 * dt + k for dt in (2, 1, 0) for k in range(9)]
-    loads = {
-        tap: pltpu.make_async_copy(weight_ref.at[tap], w_ref.at[tap], sems.at[tap]) for tap in order
-    }
-    for tap in order:
-        loads[tap].start()
     for k, (row, line_ref) in enumerate(((1 - odd, a_ref), (odd, b_ref))):
         lines_ref[row, pl.ds(0, 2)] = past_ref[k]
         lines_ref[row, pl.ds(2, frames)] = line_ref[...]
-    for dts in ((2,), (1, 0)):
-        for dt in dts:
-            for tap in range(9 * dt, 9 * dt + 9):
-                loads[tap].wait()
-        lhs = jnp.concatenate(
-            [
-                lines_ref[i, dt : dt + frames].reshape(frames * width, chans)
-                for dt in dts
-                for i in range(2)
-            ],
-            axis=1,
+    inputs = [(dt, i) for dt in range(3) for i in range(2)]
+    lhs = jnp.concatenate(
+        [lines_ref[i, dt : dt + frames].reshape(frames * width, chans) for dt, i in inputs], axis=1
+    )
+    for j, some in tiles(column_blocks((0, 1), chans)):
+        y_ref[:, j * 128 : (j + len(some)) * 128] = jnp.dot(
+            lhs, rhs_tile(w_ref, some, inputs), preferred_element_type=F32
         )
-        inputs = [(dt, i) for dt in dts for i in range(2)]
-        for j, some in tiles(column_blocks((0, 1), chans)):
-            cols = slice(j * 128, (j + len(some)) * 128)
-            got = jnp.dot(lhs, rhs_tile(w_ref, some, inputs), preferred_element_type=F32)
-            if 2 in dts:
-                y_ref[:, cols] = got
-            else:
-                y_ref[:, cols] += got
 
 
 def prep_kernel(d2_ref, d1_ref, w2_ref, w1_ref):
@@ -369,15 +361,18 @@
     from_a = swap(to_a, "rows", 0)
 
     line = 2 * width * chans * chans
-    y, weight = local(
+    weight = local(
+        fetch_kernel,
+        kept(*conv_weight.shape),
+        (conv_weight,),
+        hbm=(0,),
+        scratch=[pltpu.SemaphoreType.DMA((27,))],
+    )
+    y = local(
         own_kernel,
-        (kept(cells, 6 * chans, dtype=F32), kept(*conv_weight.shape)),
-        (to_a, to_b, past, conv_weight),
-        hbm=(3,),
-        scratch=[
-            pltpu.VMEM((2, frames + 2, width, chans), BF16),
-            pltpu.SemaphoreType.DMA((27,)),
-        ],
+        kept(cells, 6 * chans, dtype=F32),
+        (to_a, to_b, past, weight),
+        scratch=[pltpu.VMEM((2, frames + 2, width, chans), BF16)],
         flops=48 * 3 * line,
     )
     corner = onward(jnp.stack([from_a[frames - 2 :], from_b[frames - 2 :]]), "tm")

time: 56.4 us -> 53.7 us (0.952)
  waiting for transfers between devices: 8.47 us -> 4.99 us
  Pallas kernels: 19 us -> 19.7 us
    ppermute x6, waiting for transfers between devices: 8.47 us -> 4.98 us  [swap(): return lax.ppermute(block, axis, pairs(lax.axis_size(axis), first))]
    pallas_call x7 -> x8, Pallas kernels: 19 us -> 19.7 us  [local(): pl.pallas_call(kernel, out_shape=outs, in_specs=[HBM if i in hbm else VME...]
  transfers between devices with their start and end apart: 8 -> 8, of which waited for: 4 -> 4; matrix products, arithmetic and copies ran while one was open for 2% -> 2% of each run, Pallas kernels for 23% -> 26%
where the time goes in v5:
time: 53.7 us; the launch traced here: 53.5 us
  starting transfers between devices  26.9 us (50%)
  Pallas kernels  19.7 us (37%)
  waiting for transfers between devices  4.99 us (9%)
  local copies, waits for them, and re-layouts  0.95 us (2%)
  between operations  0.84 us (2%)
    pallas_call x8, Pallas kernels, local(): pl.pallas_call(kernel, out_shape=outs, in_specs=[HBM if i in hbm else VME...  19.7 us
    ppermute x6, starting transfers between devices, swap(): return lax.ppermute(block, axis, pairs(lax.axis_size(axis), first))  19 us
    ppermute x2, starting transfers between devices, onward(): lax.ppermute(block, axis, [(i, i + 1) for i in range(lax.axis_size(axis)...  7.96 us
    ppermute x6, waiting for transfers between devices, swap(): return lax.ppermute(block, axis, pairs(lax.axis_size(axis), first))  4.98 us
  transfers between devices with their start and end apart: 8, of which 4 were waited for; matrix products, arithmetic and copies ran while one was open for 2% of the time, Pallas kernels for 26%

profile of v5, /device:TPU:17, one launch (start us, length us, event | category | flops | bytes accessed | tf_op | source)
XLA Modules:
  0.0 53.5 jit_solution(11840803727597148448)
XLA Ops:
  0.6 1.7 %shard_map.86 = (bf16[4,128,384]{2,1,0:T(8,128)(2,1)S(1)}, bf16[4,128,384]{2,1,0:T(8,128)(2,1)S(1)}, bf16[2,2,128,384]{3,2,1,0:T(8,128)(2,1)S(1)}) custom-call(bf16[4,2,128,384]{3,2,1,0:T(8,128)(2,1)} %feat_ref.5, f32[384]{0:T(512)} %gain_ref.1), custom_call_target="tpu_custom_call" | custom-call | bytes 1000000 | tf_op jit(solution)/shard_map/pallas_call | solution.py:36
  2.3 7.6 %collective-permute-start.1 = (bf16[4,128,384]{2,1,0:T(8,128)(2,1)S(1)}, bf16[4,128,384]{2,1,0:T(8,128)(2,1)S(1)}, u32[]{:S(2)}, u32[]{:S(2)}) collective-permute-start(bf16[4,128,384]{2,1,0:T(8,128)(2,1)S(1)} %get-tuple-element.15.b_ref), channel_id=1, source_target_pairs={{1,2},{2,1},{3,4},{4,3},{5,6},{6,5},{7,8},{8,7},{9,10},{10,9},{11,... | collective-permute-start | bytes 1179656 | tf_op jit(solution)/shard_map/ppermute | solution.py:24
  9.9 0.1 collective-permute-start
  10.0 3.5 %collective-permute-start.3 = (bf16[2,2,128,384]{3,2,1,0:T(8,128)(2,1)S(1)}, bf16[2,2,128,384]{3,2,1,0:T(8,128)(2,1)S(1)}, u32[]{:S(2)}, u32[]{:S(2)}) collective-permute-start(bf16[2,2,128,384]{3,2,1,0:T(8,128)(2,1)S(1)} %get-tuple-element.16), channel_id=1, source_target_pairs={{0,32},{32,64},{64,96},{1,33},{33,65},{65,97},{2,34},{34,66},{66,9... | collective-permute-start | bytes 1179656 | tf_op jit(solution)/shard_map/ppermute | solution.py:28
  13.5 3.5 %shard_map.87.w_ref = bf16[27,384,384]{2,1,0:T(8,128)(2,1)S(1)} custom-call(bf16[27,384,384]{2,1,0:T(8,128)(2,1)} %weight_ref.1), custom_call_target="tpu_custom_call" | custom-call | bytes 1000000 | tf_op jit(solution)/shard_map/pallas_call | solution.py:36
  17.0 1.7 %collective-permute-done.1.b_ref = bf16[4,128,384]{2,1,0:T(8,128)(2,1)S(1)} collective-permute-done((bf16[4,128,384]{2,1,0:T(8,128)(2,1)S(1)}, bf16[4,128,384]{2,1,0:T(8,128)(2,1)S(1)}, u32[]{:S(2)}, u32[]{:S(2)}) %collective-permute-start.1) | collective-permute-done | bytes 393248 | tf_op jit(solution)/shard_map/ppermute | solution.py:24
  18.8 1.0 %collective-permute-done.a_ref = bf16[4,128,384]{2,1,0:T(8,128)(2,1)S(1)} collective-permute-done((bf16[4,128,384]{2,1,0:T(8,128)(2,1)S(1)}, bf16[4,128,384]{2,1,0:T(8,128)(2,1)S(1)}, u32[]{:S(2)}, u32[]{:S(2)}) %collective-permute-start) | collective-permute-done | bytes 393248 | tf_op jit(solution)/shard_map/ppermute | solution.py:24
  19.8 0.0 copy-start
  19.8 0.0 copy-start.2
  19.8 0.0 copy-start.4
  19.8 4.5 %collective-permute-start.2 = (bf16[2,2,128,384]{3,2,1,0:T(8,128)(2,1)S(1)}, bf16[2,2,128,384]{3,2,1,0:T(8,128)(2,1)S(1)}, u32[]{:S(2)}, u32[]{:S(2)}) collective-permute-start(bf16[2,2,128,384]{3,2,1,0:T(8,128)(2,1)S(1)} %pad_maximum_fusion), channel_id=1, source_target_pairs={{0,32},{32,64},{64,96},{1,33},{33,65},{65,97},{2,34},{34,66},{66,9... | collective-permute-start | bytes 1179656 | tf_op jit(solution)/shard_map/ppermute | solution.py:28
  24.3 0.0 collective-permute-done.3.past_ref
  24.3 5.8 %shard_map.88.sum_ref = f32[512,2304]{1,0:T(8,128)S(1)} custom-call(bf16[4,128,384]{2,1,0:T(8,128)(2,1)S(1)} %get-tuple-element.14.a_ref, bf16[4,128,384]{2,1,0:T(8,128)(2,1)S(1)} %get-tuple-element.15.b_ref, bf16[2,2,128,384]{3,2,1,0:T(8,128)(2,1)S(1)} %collective-permute-done.3.past_ref, bf16[27,384,384]{2,1,0:T(8,128)(2,1)S(1)} %shard_map.87.w_ref), custom_call_target="tpu_custom_call" | custom-call | flops 5435817984 | bytes 1000000 | tf_op jit(solution)/shard_map/pallas_call | solution.py:36
  30.1 0.0 copy-done
  30.1 0.0 copy-done.2
  30.1 0.0 copy-done.4
  30.1 4.3 %shard_map.89 = (f32[256,2304]{1,0:T(8,128)S(1)}, bf16[4,2,128,384]{3,2,1,0:T(8,128)(2,1)S(1)}, bf16[4,2,8,128]{3,2,1,0:T(8,128)(2,1)S(1)}) custom-call(bf16[4,128,384]{2,1,0:T(8,128)(2,1)S(1)} %collective-permute-done.a_ref, bf16[4,128,384]{2,1,0:T(8,128)(2,1)S(1)} %collective-permute-done.1.b_ref, bf16[27,384,384]{2,1,0:T(8,128)(2,1)S(1)} %shard_map.87.w_ref, ...), custom_call_target="tpu_custom_call" | custom-call | flops 2038431744 | bytes 1000000 | tf_op jit(solution)/shard_map/pallas_call | solution.py:36
  34.5 0.0 collective-permute-done.2.past_ref
  34.5 1.6 %shard_map.90 = (bf16[4,2,128,384]{3,2,1,0:T(8,128)(2,1)S(1)}, bf16[4,2,8,128]{3,2,1,0:T(8,128)(2,1)S(1)}) custom-call(bf16[2,2,128,384]{3,2,1,0:T(8,128)(2,1)S(1)} %collective-permute-done.2.past_ref, bf16[27,384,384]{2,1,0:T(8,128)(2,1)S(1)} %shard_map.87.w_ref, ...), custom_call_target="tpu_custom_call", output_to_operand_aliasing={{0}: (6, {}), {1}: (7, {})} | custom-call | flops 679477248 | bytes 1000000 | tf_op jit(solution)/shard_map/pallas_call | solution.py:36
  36.2 0.1 collective-permute-start.4
  36.2 7.0 %collective-permute-start.5 = (bf16[4,2,8,128]{3,2,1,0:T(8,128)(2,1)S(1)}, bf16[4,2,8,128]{3,2,1,0:T(8,128)(2,1)S(1)}, u32[]{:S(2)}, u32[]{:S(2)}) collective-permute-start(bf16[4,2,8,128]{3,2,1,0:T(8,128)(2,1)S(1)} %get-tuple-element.21.own_ref), channel_id=1, source_target_pairs={{1,2},{2,1},{3,4},{4,3},{5,6},{6,5},{7,8},{8,7},{9,10},{10,9},{11,... | collective-permute-start | bytes 49160 | tf_op jit(solution)/shard_map/ppermute | solution.py:24
  43.2 0.0 collective-permute-done.4.a_ref
  43.2 2.0 %collective-permute-done.5.b_ref = bf16[4,2,8,128]{3,2,1,0:T(8,128)(2,1)S(1)} collective-permute-done((bf16[4,2,8,128]{3,2,1,0:T(8,128)(2,1)S(1)}, bf16[4,2,8,128]{3,2,1,0:T(8,128)(2,1)S(1)}, u32[]{:S(2)}, u32[]{:S(2)}) %collective-permute-start.5) | collective-permute-done | bytes 16416 | tf_op jit(solution)/shard_map/ppermute | solution.py:24
  45.2 0.2 collective-permute-start.6
  45.4 4.1 %collective-permute-start.7 = (bf16[2,6,8,128]{3,2,1,0:T(8,128)(2,1)S(1)}, bf16[2,6,8,128]{3,2,1,0:T(8,128)(2,1)S(1)}, u32[]{:S(2)}, u32[]{:S(2)}) collective-permute-start(bf16[2,6,8,128]{3,2,1,0:T(8,128)(2,1)S(1)} %get-tuple-element.23), channel_id=1, source_target_pairs={{32,64},{64,32},{33,65},{65,33},{34,66},{66,34},{35,67},{67,35},{3... | collective-permute-start | bytes 73736 | tf_op jit(solution)/shard_map/ppermute | solution.py:24
  49.5 0.0 copy-done.1
  49.5 0.0 copy-done.3
  49.5 0.3 shard_map.92
  49.9 0.9 %copy.13 = bf16[4,2,128,384]{3,2,1,0:T(8,128)(2,1)} copy(bf16[4,2,128,384]{3,2,1,0:T(8,128)(2,1)S(1)} %get-tuple-element.26) | data formatting | bytes 1572864
  50.8 0.0 collective-permute-done.6.ta_ref
  50.8 0.3 collective-permute-done.7.tb_ref
  51.0 2.4 %shard_map.93 = f32[4,2,128]{2,1,0:T(2,128)} custom-call(bf16[4,2,8,128]{3,2,1,0:T(8,128)(2,1)S(1)} %collective-permute-done.4.a_ref, bf16[4,2,8,128]{3,2,1,0:T(8,128)(2,1)S(1)} %get-tuple-element.21.own_ref, bf16[4,2,8,128]{3,2,1,0:T(8,128)(2,1)S(1)} %collective-permute-done.5.b_ref, bf16[2,6,8,128]{3,2,1,0:T(8,128)(2,1)S(1)} %collective-permute-done.6.ta_ref, ...), custom_call_target="tpu_custom_call" | custom-call | bytes 1000000 | tf_op jit(solution)/shard_map/pallas_call | solution.py:36
  (6 shorter events, 0.1 us)
Async XLA Ops:
  2.3 16.4 %collective-permute-start.1 = (bf16[4,128,384]{2,1,0:T(8,128)(2,1)S(1)}, bf16[4,128,384]{2,1,0:T(8,128)(2,1)S(1)}, u32[]{:S(2)}, u32[]{:S(2)}) collective-permute-start(bf16[4,128,384]{2,1,0:T(8,128)(2,1)S(1)} %get-tuple-element.15.b_ref), channel_id=1, source_target_pairs={{1,2},{2,1},{3,4},{4,3},{5,6},{6,5},{7,8},{8,7},{9,10},{10,9},{11,... | collective-permute-start | bytes 1179656 | tf_op jit(solution)/shard_map/ppermute | solution.py:24
  9.9 9.8 %collective-permute-start = (bf16[4,128,384]{2,1,0:T(8,128)(2,1)S(1)}, bf16[4,128,384]{2,1,0:T(8,128)(2,1)S(1)}, u32[]{:S(2)}, u32[]{:S(2)}) collective-permute-start(bf16[4,128,384]{2,1,0:T(8,128)(2,1)S(1)} %get-tuple-element.14.a_ref), channel_id=1, source_target_pairs={{0,1},{1,0},{2,3},{3,2},{4,5},{5,4},{6,7},{7,6},{8,9},{9,8},{10,11... | collective-permute-start | bytes 1179656 | tf_op jit(solution)/shard_map/ppermute | solution.py:24
  10.0 14.3 %collective-permute-start.3 = (bf16[2,2,128,384]{3,2,1,0:T(8,128)(2,1)S(1)}, bf16[2,2,128,384]{3,2,1,0:T(8,128)(2,1)S(1)}, u32[]{:S(2)}, u32[]{:S(2)}) collective-permute-start(bf16[2,2,128,384]{3,2,1,0:T(8,128)(2,1)S(1)} %get-tuple-element.16), channel_id=1, source_target_pairs={{0,32},{32,64},{64,96},{1,33},{33,65},{65,97},{2,34},{34,66},{66,9... | collective-permute-start | bytes 1179656 | tf_op jit(solution)/shard_map/ppermute | solution.py:28
  19.8 10.3 %copy-start = (bf16[4,2,128,384]{3,2,1,0:T(8,128)(2,1)S(1)}, bf16[4,2,128,384]{3,2,1,0:T(8,128)(2,1)}, u32[]{:S(2)}) copy-start(bf16[4,2,128,384]{3,2,1,0:T(8,128)(2,1)} %feat_ref.5) | copy-start | bytes 2359300
  19.8 10.3 %copy-start.2 = (bf16[3,4,2,128]{3,2,1,0:T(2,128)(2,1)S(1)}, bf16[3,4,2,128]{3,2,1,0:T(2,128)(2,1)}, u32[]{:S(2)}) copy-start(bf16[3,4,2,128]{3,2,1,0:T(2,128)(2,1)} %real_ref.3) | copy-start | bytes 18436
  19.8 10.3 %copy-start.4 = (bf16[384,3]{0,1:T(4,128)(2,1)S(1)}, bf16[384,3]{0,1:T(4,128)(2,1)}, u32[]{:S(2)}) copy-start(bf16[384,3]{0,1:T(4,128)(2,1)} %param.10) | copy-start | bytes 6916
  19.8 14.7 %collective-permute-start.2 = (bf16[2,2,128,384]{3,2,1,0:T(8,128)(2,1)S(1)}, bf16[2,2,128,384]{3,2,1,0:T(8,128)(2,1)S(1)}, u32[]{:S(2)}, u32[]{:S(2)}) collective-permute-start(bf16[2,2,128,384]{3,2,1,0:T(8,128)(2,1)S(1)} %pad_maximum_fusion), channel_id=1, source_target_pairs={{0,32},{32,64},{64,96},{1,33},{33,65},{65,97},{2,34},{34,66},{66,9... | collective-permute-start | bytes 1179656 | tf_op jit(solution)/shard_map/ppermute | solution.py:28
  34.5 15.0 %copy-start.1 = (bf16[27,128,64]{1,2,0:T(8,128)(2,1)S(1)}, bf16[27,128,64]{1,2,0:T(8,128)(2,1)}, u32[]{:S(2)}) copy-start(bf16[27,128,64]{1,2,0:T(8,128)(2,1)} %param.13) | copy-start | bytes 1327108
  34.5 15.0 %copy-start.3 = (bf16[27,64,3]{1,0,2:T(8,128)(2,1)S(1)}, bf16[27,64,3]{1,0,2:T(8,128)(2,1)}, u32[]{:S(2)}) copy-start(bf16[27,64,3]{1,0,2:T(8,128)(2,1)} %param.12) | copy-start | bytes 31108
  36.2 7.0 %collective-permute-start.4 = (bf16[4,2,8,128]{3,2,1,0:T(8,128)(2,1)S(1)}, bf16[4,2,8,128]{3,2,1,0:T(8,128)(2,1)S(1)}, u32[]{:S(2)}, u32[]{:S(2)}) collective-permute-start(bf16[4,2,8,128]{3,2,1,0:T(8,128)(2,1)S(1)} %get-tuple-element.21.own_ref), channel_id=1, source_target_pairs={{0,1},{1,0},{2,3},{3,2},{4,5},{5,4},{6,7},{7,6},{8,9},{9,8},{10,11... | collective-permute-start | bytes 49160 | tf_op jit(solution)/shard_map/ppermute | solution.py:24
  36.2 9.0 %collective-permute-start.5 = (bf16[4,2,8,128]{3,2,1,0:T(8,128)(2,1)S(1)}, bf16[4,2,8,128]{3,2,1,0:T(8,128)(2,1)S(1)}, u32[]{:S(2)}, u32[]{:S(2)}) collective-permute-start(bf16[4,2,8,128]{3,2,1,0:T(8,128)(2,1)S(1)} %get-tuple-element.21.own_ref), channel_id=1, source_target_pairs={{1,2},{2,1},{3,4},{4,3},{5,6},{6,5},{7,8},{8,7},{9,10},{10,9},{11,... | collective-permute-start | bytes 49160 | tf_op jit(solution)/shard_map/ppermute | solution.py:24
  45.2 5.5 %collective-permute-start.6 = (bf16[2,6,8,128]{3,2,1,0:T(8,128)(2,1)S(1)}, bf16[2,6,8,128]{3,2,1,0:T(8,128)(2,1)S(1)}, u32[]{:S(2)}, u32[]{:S(2)}) collective-permute-start(bf16[2,6,8,128]{3,2,1,0:T(8,128)(2,1)S(1)} %get-tuple-element.22), channel_id=1, source_target_pairs={{0,32},{32,0},{64,96},{96,64},{1,33},{33,1},{65,97},{97,65},{2,34}... | collective-permute-start | bytes 73736 | tf_op jit(solution)/shard_map/ppermute | solution.py:24
  45.4 5.6 %collective-permute-start.7 = (bf16[2,6,8,128]{3,2,1,0:T(8,128)(2,1)S(1)}, bf16[2,6,8,128]{3,2,1,0:T(8,128)(2,1)S(1)}, u32[]{:S(2)}, u32[]{:S(2)}) collective-permute-start(bf16[2,6,8,128]{3,2,1,0:T(8,128)(2,1)S(1)} %get-tuple-element.23), channel_id=1, source_target_pairs={{32,64},{64,32},{33,65},{65,33},{34,66},{66,34},{35,67},{67,35},{3... | collective-permute-start | bytes 73736 | tf_op jit(solution)/shard_map/ppermute | solution.py:24

commit v6 on v5

--- a/solution.py
+++ b/solution.py
@@ -1,3 +1,5 @@
+import functools
+
 import jax
 import jax.numpy as jnp
 from jax import lax
@@ -76,37 +78,37 @@
                 tail_ref[k, t - frames + 2] = act
 
 
-def column_blocks(rows, chans):
-    return [(o, dw, off) for o in rows for dw in range(3) for off in range(0, chans, 128)]
-
-
-def rhs_tile(w_ref, blocks, inputs):
-    halves = [
-        jnp.concatenate(
-            [w_ref[9 * dt + 3 * (i - o + 1) + dw, :, off : off + 128] for dt, i in inputs], axis=0
-        )
-        for o, dw, off in blocks
-    ]
-    return halves[0] if len(halves) == 1 else jnp.concatenate(halves, axis=1)
-
-
-def tiles(blocks):
-    return [(j, blocks[j : j + 2]) for j in range(0, len(blocks), 2)]
+def column_blocks(chans):
+    return [(dw, off) for dw in range(3) for off in range(0, chans, 128)]
+
+
+def rhs_block(w_ref, dw, off, taps):
+    return jnp.concatenate([w_ref[9 * dt + 3 * dh + dw, :, off : off + 128] for dt, dh in taps], axis=0)
+
+
+def load_taps(weight_ref, w_ref, sems, dws):
+    loads = {
+        dw: [
+            pltpu.make_async_copy(weight_ref.at[tap], w_ref.at[tap], sems.at[tap])
+            for tap in range(dw, 27, 3)
+        ]
+        for dw in dws
+    }
+    for dw in dws:
+        for load in loads[dw]:
+            load.start()
+    return loads
 
 
 def fetch_kernel(weight_ref, w_ref, sems):
-    loads = [
-        pltpu.make_async_copy(weight_ref.at[tap], w_ref.at[tap], sems.at[tap]) for tap in range(27)
-    ]
-    for load in loads:
-        load.start()
-    for load in loads:
+    for load in load_taps(weight_ref, w_ref, sems, (0,))[0]:
         load.wait()
 
 
-def own_kernel(a_ref, b_ref, past_ref, w_ref, y_ref, lines_ref):
+def own_kernel(a_ref, b_ref, past_ref, weight_ref, some_ref, y_ref, w_ref, lines_ref, sems):
     odd = lax.rem(lax.axis_index("rows"), 2)
     frames, width, chans = a_ref.shape
+    loads = load_taps(weight_ref, w_ref, sems, (1, 2))
     for k, (row, line_ref) in enumerate(((1 - odd, a_ref), (odd, b_ref))):
         lines_ref[row, pl.ds(0, 2)] = past_ref[k]
         lines_ref[row, pl.ds(2, frames)] = line_ref[...]
@@ -114,10 +116,17 @@
     lhs = jnp.concatenate(
         [lines_ref[i, dt : dt + frames].reshape(frames * width, chans) for dt, i in inputs], axis=1
     )
-    for j, some in tiles(column_blocks((0, 1), chans)):
-        y_ref[:, j * 128 : (j + len(some)) * 128] = jnp.dot(
-            lhs, rhs_tile(w_ref, some, inputs), preferred_element_type=F32
-        )
+    for dw in range(3):
+        for load in loads.get(dw, ()):
+            load.wait()
+        blocks = [(o, off) for o in range(2) for off in range(0, chans, 128)]
+        for j in range(0, len(blocks), 2):
+            pair = blocks[j : j + 2]
+            rhs = [rhs_block(w_ref, dw, off, [(dt, i - o + 1) for dt, i in inputs]) for o, off in pair]
+            got = jnp.dot(lhs, jnp.concatenate(rhs, axis=1), preferred_element_type=F32)
+            for k, (o, off) in enumerate(pair):
+                at = dw * chans + off
+                y_ref[o, :, at : at + 128] = got[:, k * 128 : (k + 1) * 128]
 
 
 def prep_kernel(d2_ref, d1_ref, w2_ref, w1_ref):
@@ -144,14 +153,6 @@
         w1_ref[side * depth1 : (side + 1) * depth1] = total.astype(BF16)
 
 
-def past_lhs(lines, zeros):
-    first = [line[0] for line in lines] + [line[1] for line in lines]
-    second = [line[1] for line in lines] + [zeros for _ in lines]
-    return jnp.concatenate(
-        [jnp.concatenate(first, axis=1), jnp.concatenate(second, axis=1)], axis=0
-    )
-
-
 def finish(ys, feats, rgb, reals):
     width, chans = ys[1].shape
     col = lax.broadcasted_iota(jnp.int32, (width, chans), 0)
@@ -171,70 +172,64 @@
     return decoded, both.astype(BF16)
 
 
-def rows_kernel(
-    a_ref, b_ref, w_ref, sum_ref, feat_ref, rgb_ref, real_ref, y_ref, decoded_ref, colour_ref,
-    lines_ref, late_ref,
-):
+def add_row(lhs, dts, row, w_ref, sums_ref, out_ref):
+    chans = w_ref.shape[1]
+    blocks = column_blocks(chans)
+    for j in range(0, len(blocks), 2):
+        some = blocks[j : j + 2]
+        rhs = [rhs_block(w_ref, dw, off, [(dt, 2 * row) for dt in dts]) for dw, off in some]
+        cols = slice(j * 128, (j + len(some)) * 128)
+        out_ref[:, cols] = sums_ref[:, cols] + jnp.dot(
+            lhs, rhs[0] if len(rhs) == 1 else jnp.concatenate(rhs, axis=1), preferred_element_type=F32
+        )
+
+
+def finish_row(ts, row, sums, feat_ref, rgb_ref, real_ref, decoded_ref, colour_ref):
+    width, chans = feat_ref.shape[2:]
+    for k, t in enumerate(ts):
+        ys = [sums[k * width : (k + 1) * width, dw * chans : (dw + 1) * chans] for dw in range(3)]
+        reals = []
+        for c in range(3):
+            both = real_ref[c, t].astype(F32)
+            reals.append(jnp.where(row == 0, both[0:1], both[1:2]))
+        decoded_ref[t, row], colour_ref[t, row] = finish(ys, feat_ref[t, row], rgb_ref[...], reals)
+
+
+def side_row(side):
     odd = lax.rem(lax.axis_index("rows"), 2)
-    frames, width, chans = a_ref.shape
-    lines_ref[1 - odd] = a_ref[...]
-    lines_ref[odd] = b_ref[...]
+    return 1 - odd if side == 0 else odd
+
+
+def near_kernel(side, line_ref, w_ref, sums_ref, feat_ref, rgb_ref, real_ref, *refs):
+    y_ref, decoded_ref, colour_ref, all_ref = refs[-4:]
+    row = side_row(side)
+    frames, width, chans = line_ref.shape
     zeros = jnp.zeros((width, chans), BF16)
-    for o in range(2):
-        line = [zeros, zeros] + [lines_ref[o, t] for t in range(frames)]
-        lhs = jnp.concatenate(
-            [jnp.concatenate(line[dt : dt + frames], axis=0) for dt in range(3)], axis=1
-        )
-        inputs = [(dt, 3 * o - 1) for dt in range(3)]
-        base = o * 3 * chans
-        for j, some in tiles(column_blocks((o,), chans)):
-            cols = slice(base + j * 128, base + (j + len(some)) * 128)
-            got = jnp.dot(lhs, rhs_tile(w_ref, some, inputs), preferred_element_type=F32)
-            got = got + sum_ref[:, cols]
-            y_ref[:, cols] = got[: 2 * width]
-            late_ref[:, cols] = got[2 * width :]
-        for t in range(frames - 2):
-            ys = [
-                late_ref[t * width : (t + 1) * width, base + dw * chans : base + (dw + 1) * chans]
-                for dw in range(3)
-            ]
-            decoded_ref[t + 2, o], colour_ref[t + 2, o] = finish(
-                ys,
-                feat_ref[t + 2, o],
-                rgb_ref[...],
-                [real_ref[c, t + 2, o : o + 1] for c in range(3)],
-            )
-
-
-def corner_kernel(
-    past_ref, w_ref, sum_ref, feat_ref, rgb_ref, real_ref, done_ref, shown_ref,
-    decoded_ref, colour_ref, y_ref, lines_ref,
-):
-    odd = lax.rem(lax.axis_index("rows"), 2)
-    width, chans = past_ref.shape[2:]
-    lines_ref[1 - odd] = past_ref[0]
-    lines_ref[odd] = past_ref[1]
-    zeros = jnp.zeros((width, chans), BF16)
-    for o in range(2):
-        lhs = past_lhs([lines_ref[o]], zeros)
-        inputs = [(dt, 3 * o - 1) for dt in range(2)]
-        base = o * 3 * chans
-        for j, some in tiles(column_blocks((o,), chans)):
-            cols = slice(base + j * 128, base + (j + len(some)) * 128)
-            y_ref[:, cols] = sum_ref[:, cols] + jnp.dot(
-                lhs, rhs_tile(w_ref, some, inputs), preferred_element_type=F32
-            )
-        for t in range(2):
-            ys = [
-                y_ref[t * width : (t + 1) * width, base + dw * chans : base + (dw + 1) * chans]
-                for dw in range(3)
-            ]
-            decoded_ref[t, o], colour_ref[t, o] = finish(
-                ys,
-                feat_ref[t, o],
-                rgb_ref[...],
-                [real_ref[c, t, o : o + 1] for c in range(3)],
-            )
+    line = [zeros, zeros] + [line_ref[t] for t in range(frames)]
+    lhs = jnp.concatenate(
+        [jnp.concatenate(line[dt : dt + frames], axis=0) for dt in range(3)], axis=1
+    )
+    add_row(lhs, range(3), row, w_ref, sums_ref.at[row], all_ref)
+    y_ref[...] = all_ref[: 2 * width]
+    late = range(2, frames)
+    finish_row(
+        late, row, all_ref.at[2 * width :], feat_ref, rgb_ref, real_ref, decoded_ref, colour_ref
+    )
+
+
+def corner_kernel(side, past_ref, w_ref, sums_ref, feat_ref, rgb_ref, real_ref, *refs):
+    decoded_ref, colour_ref, all_ref = refs[-3:]
+    row = side_row(side)
+    width, chans = past_ref.shape[1:]
+    lhs = jnp.concatenate(
+        [
+            jnp.concatenate([past_ref[0], past_ref[1]], axis=0),
+            jnp.concatenate([past_ref[1], jnp.zeros((width, chans), BF16)], axis=0),
+        ],
+        axis=1,
+    )
+    add_row(lhs, range(2), row, w_ref, sums_ref, all_ref)
+    finish_row(range(2), row, all_ref, feat_ref, rgb_ref, real_ref, decoded_ref, colour_ref)
 
 
 def pack_kernel(a_ref, own_ref, b_ref, for_a_ref, for_b_ref):
@@ -361,47 +356,52 @@
     from_a = swap(to_a, "rows", 0)
 
     line = 2 * width * chans * chans
-    weight = local(
+    first_taps = local(
         fetch_kernel,
         kept(*conv_weight.shape),
         (conv_weight,),
         hbm=(0,),
         scratch=[pltpu.SemaphoreType.DMA((27,))],
     )
-    y = local(
+    sums, weight = local(
         own_kernel,
-        kept(cells, 6 * chans, dtype=F32),
-        (to_a, to_b, past, weight),
-        scratch=[pltpu.VMEM((2, frames + 2, width, chans), BF16)],
+        (kept(height, cells, 3 * chans, dtype=F32), kept(*conv_weight.shape)),
+        (to_a, to_b, past, conv_weight, first_taps),
+        hbm=(3,),
+        scratch=[
+            pltpu.VMEM((2, frames + 2, width, chans), BF16),
+            pltpu.SemaphoreType.DMA((27,)),
+        ],
+        aliases={4: 1},
         flops=48 * 3 * line,
     )
-    corner = onward(jnp.stack([from_a[frames - 2 :], from_b[frames - 2 :]]), "tm")
-    rgb = rgb_weight.T
-    y, done, shown = local(
-        rows_kernel,
-        (
-            kept(2 * width, 6 * chans, dtype=F32),
-            kept(frames, height, width, chans),
-            kept(frames, height, 8, width),
-        ),
-        (from_a, from_b, weight, y, latent_feat, rgb, real_frames),
-        scratch=[
-            pltpu.VMEM((2, frames, width, chans), BF16),
-            pltpu.VMEM((cells - 2 * width, 6 * chans), F32),
-        ],
-        flops=18 * 3 * line,
-    )
-    decoded, colour = local(
-        corner_kernel,
-        (kept(frames, height, width, chans), kept(frames, height, 8, width)),
-        (corner, weight, y, latent_feat, rgb, real_frames, done, shown),
-        scratch=[
-            pltpu.VMEM((2 * width, 6 * chans), F32),
-            pltpu.VMEM((2, 2, width, chans), BF16),
-        ],
-        aliases={6: 0, 7: 1},
-        flops=6 * 3 * line,
-    )
+    corner_a = onward(from_a[frames - 2 :], "tm")
+    corner_b = onward(from_b[frames - 2 :], "tm")
+    rest = (latent_feat, rgb_weight.T, real_frames)
+    early = kept(2 * width, 3 * chans, dtype=F32)
+    shown = (kept(frames, height, width, chans), kept(frames, height, 8, width))
+    ends = []
+    outs = ()
+    for side, row in enumerate((from_a, from_b)):
+        y, *outs = local(
+            functools.partial(near_kernel, side),
+            (early,) + shown,
+            (row, weight, sums) + rest + tuple(outs),
+            scratch=[pltpu.VMEM((cells, 3 * chans), F32)],
+            aliases={6: 1, 7: 2} if side else {},
+            flops=12 * 3 * line,
+        )
+        ends.append(y)
+    for side, row in enumerate((corner_a, corner_b)):
+        outs = local(
+            functools.partial(corner_kernel, side),
+            shown,
+            (row, weight, ends[side]) + rest + tuple(outs),
+            scratch=[pltpu.VMEM((2 * width, 3 * chans), F32)],
+            aliases={6: 0, 7: 1},
+            flops=4 * 3 * line,
+        )
+    decoded, colour = outs
     w2, w1 = local(
         prep_kernel,
         (kept(3 * depth2, 9 * depth1), kept(2 * depth1, 27 * 8)),

time: 53.7 us -> 56.7 us (1.056)
  starting transfers between devices: 26.9 us -> 30.6 us
  waiting for transfers between devices: 4.99 us -> 4.15 us
    ppermute x2 -> x3, starting transfers between devices: 7.96 us -> 11.1 us  [onward(): lax.ppermute(block, axis, [(i, i + 1) for i in range(lax.axis_size(axis)...]
    ppermute x6, waiting for transfers between devices: 4.98 us -> 4.14 us  [swap(): return lax.ppermute(block, axis, pairs(lax.axis_size(axis), first))]
    ppermute x6, starting transfers between devices: 19 us -> 19.6 us  [swap(): return lax.ppermute(block, axis, pairs(lax.axis_size(axis), first))]
    pallas_call x8 -> x10, Pallas kernels: 19.7 us -> 19.8 us  [local(): pl.pallas_call(kernel, out_shape=outs, in_specs=[HBM if i in hbm else VME...]
  transfers between devices with their start and end apart: 8 -> 9, of which waited for: 4 -> 3; matrix products, arithmetic and copies ran while one was open for 2% -> 2% of each run, Pallas kernels for 26% -> 26%
where the time goes in v6:
time: 56.7 us; the launch traced here: 56.4 us
  starting transfers between devices  30.6 us (54%)
  Pallas kernels  19.8 us (35%)
  waiting for transfers between devices  4.15 us (7%)
  local copies, waits for them, and re-layouts  0.95 us (2%)
  between operations  0.83 us (1%)
    pallas_call x10, Pallas kernels, local(): pl.pallas_call(kernel, out_shape=outs, in_specs=[HBM if i in hbm else VME...  19.8 us
    ppermute x6, starting transfers between devices, swap(): return lax.ppermute(block, axis, pairs(lax.axis_size(axis), first))  19.6 us
    ppermute x3, starting transfers between devices, onward(): lax.ppermute(block, axis, [(i, i + 1) for i in range(lax.axis_size(axis)...  11.1 us
    ppermute x6, waiting for transfers between devices, swap(): return lax.ppermute(block, axis, pairs(lax.axis_size(axis), first))  4.14 us
  transfers between devices with their start and end apart: 9, of which 3 were waited for; matrix products, arithmetic and copies ran while one was open for 2% of the time, Pallas kernels for 26%

profile of v6, /device:TPU:17, one launch (start us, length us, event | category | flops | bytes accessed | tf_op | source)
XLA Modules:
  0.0 56.4 jit_solution(17783595662943308991)
XLA Ops:
  0.6 1.7 %shard_map.86 = (bf16[4,128,384]{2,1,0:T(8,128)(2,1)S(1)}, bf16[4,128,384]{2,1,0:T(8,128)(2,1)S(1)}, bf16[2,2,128,384]{3,2,1,0:T(8,128)(2,1)S(1)}) custom-call(bf16[4,2,128,384]{3,2,1,0:T(8,128)(2,1)} %feat_ref.9, f32[384]{0:T(512)} %gain_ref.1), custom_call_target="tpu_custom_call" | custom-call | bytes 1000000 | tf_op jit(solution)/shard_map/pallas_call | solution.py:38
  2.3 1.3 %collective-permute-start.3 = (bf16[4,128,384]{2,1,0:T(8,128)(2,1)S(1)}, bf16[4,128,384]{2,1,0:T(8,128)(2,1)S(1)}, u32[]{:S(2)}, u32[]{:S(2)}) collective-permute-start(bf16[4,128,384]{2,1,0:T(8,128)(2,1)S(1)} %get-tuple-element.22.a_ref), channel_id=1, source_target_pairs={{0,1},{1,0},{2,3},{3,2},{4,5},{5,4},{6,7},{7,6},{8,9},{9,8},{10,11... | collective-permute-start | bytes 1179656 | tf_op jit(solution)/shard_map/ppermute | solution.py:26
  3.6 6.9 %collective-permute-start = (bf16[4,128,384]{2,1,0:T(8,128)(2,1)S(1)}, bf16[4,128,384]{2,1,0:T(8,128)(2,1)S(1)}, u32[]{:S(2)}, u32[]{:S(2)}) collective-permute-start(bf16[4,128,384]{2,1,0:T(8,128)(2,1)S(1)} %get-tuple-element.21.b_ref), channel_id=1, source_target_pairs={{1,2},{2,1},{3,4},{4,3},{5,6},{6,5},{7,8},{8,7},{9,10},{10,9},{11,... | collective-permute-start | bytes 1179656 | tf_op jit(solution)/shard_map/ppermute | solution.py:26
  10.6 3.8 %collective-permute-start.2 = (bf16[2,2,128,384]{3,2,1,0:T(8,128)(2,1)S(1)}, bf16[2,2,128,384]{3,2,1,0:T(8,128)(2,1)S(1)}, u32[]{:S(2)}, u32[]{:S(2)}) collective-permute-start(bf16[2,2,128,384]{3,2,1,0:T(8,128)(2,1)S(1)} %get-tuple-element.23), channel_id=1, source_target_pairs={{0,32},{32,64},{64,96},{1,33},{33,65},{65,97},{2,34},{34,66},{66,9... | collective-permute-start | bytes 1179656 | tf_op jit(solution)/shard_map/ppermute | solution.py:30
  14.3 1.9 %shard_map.87.some_ref = bf16[27,384,384]{2,1,0:T(8,128)(2,1)S(1)} custom-call(bf16[27,384,384]{2,1,0:T(8,128)(2,1)} %weight_ref.3), custom_call_target="tpu_custom_call" | custom-call | bytes 1000000 | tf_op jit(solution)/shard_map/pallas_call | solution.py:38
  16.2 0.0 collective-permute-done.3.line_ref
  16.3 1.9 %collective-permute-start.4 = (bf16[2,128,384]{2,1,0:T(8,128)(2,1)S(1)}, bf16[2,128,384]{2,1,0:T(8,128)(2,1)S(1)}, u32[]{:S(2)}, u32[]{:S(2)}) collective-permute-start(bf16[2,128,384]{2,1,0:T(8,128)(2,1)S(1)} %slice.9), channel_id=1, source_target_pairs={{0,32},{32,64},{64,96},{1,33},{33,65},{65,97},{2,34},{34,66},{66,9... | collective-permute-start | bytes 589832 | tf_op jit(solution)/shard_map/ppermute | solution.py:30
  18.2 1.5 %collective-permute-done.line_ref = bf16[4,128,384]{2,1,0:T(8,128)(2,1)S(1)} collective-permute-done((bf16[4,128,384]{2,1,0:T(8,128)(2,1)S(1)}, bf16[4,128,384]{2,1,0:T(8,128)(2,1)S(1)}, u32[]{:S(2)}, u32[]{:S(2)}) %collective-permute-start) | collective-permute-done | bytes 393248 | tf_op jit(solution)/shard_map/ppermute | solution.py:26
  19.8 0.0 copy-start
  19.8 0.0 copy-start.2
  19.8 0.0 copy-start.3
  19.8 5.4 %collective-permute-start.1 = (bf16[2,128,384]{2,1,0:T(8,128)(2,1)S(1)}, bf16[2,128,384]{2,1,0:T(8,128)(2,1)S(1)}, u32[]{:S(2)}, u32[]{:S(2)}) collective-permute-start(bf16[2,128,384]{2,1,0:T(8,128)(2,1)S(1)} %slice.8), channel_id=1, source_target_pairs={{0,32},{32,64},{64,96},{1,33},{33,65},{65,97},{2,34},{34,66},{66,9... | collective-permute-start | bytes 589832 | tf_op jit(solution)/shard_map/ppermute | solution.py:30
  25.2 0.0 collective-permute-done.2.past_ref
  25.2 7.6 %shard_map.88 = (f32[2,512,1152]{2,1,0:T(8,128)S(1)}, bf16[27,384,384]{2,1,0:T(8,128)(2,1)S(1)}) custom-call(bf16[4,128,384]{2,1,0:T(8,128)(2,1)S(1)} %get-tuple-element.22.a_ref, bf16[4,128,384]{2,1,0:T(8,128)(2,1)S(1)} %get-tuple-element.21.b_ref, bf16[2,2,128,384]{3,2,1,0:T(8,128)(2,1)S(1)} %collective-permute-done.2.past_ref, ...), custom_call_target="tpu_custom_call", output_to_operand_aliasing={{1}: (4, {})} | custom-call | flops 5435817984 | bytes 1000000 | tf_op jit(solution)/shard_map/pallas_call | solution.py:38
  32.8 2.1 %shard_map.89 = (f32[256,1152]{1,0:T(8,128)S(1)}, bf16[4,2,128,384]{3,2,1,0:T(8,128)(2,1)S(1)}, bf16[4,2,8,128]{3,2,1,0:T(8,128)(2,1)S(1)}) custom-call(bf16[4,128,384]{2,1,0:T(8,128)(2,1)S(1)} %collective-permute-done.3.line_ref, bf16[27,384,384]{2,1,0:T(8,128)(2,1)S(1)} %get-tuple-element.24.w_ref, f32[2,512,1152]{2,1,0:T(8,128)S(1)} %get-tuple-element.25.sums_ref, ...), custom_call_target="tpu_custom_call" | custom-call | flops 1358954496 | bytes 1000000 | tf_op jit(solution)/shard_map/pallas_call | solution.py:38
  34.9 2.1 %shard_map.90 = (f32[256,1152]{1,0:T(8,128)S(1)}, bf16[4,2,128,384]{3,2,1,0:T(8,128)(2,1)S(1)}, bf16[4,2,8,128]{3,2,1,0:T(8,128)(2,1)S(1)}) custom-call(bf16[4,128,384]{2,1,0:T(8,128)(2,1)S(1)} %collective-permute-done.line_ref, bf16[27,384,384]{2,1,0:T(8,128)(2,1)S(1)} %get-tuple-element.24.w_ref, ...), custom_call_target="tpu_custom_call", output_to_operand_aliasing={{1}: (6, {}), {2}: (7, {})} | custom-call | flops 1358954496 | bytes 1000000 | tf_op jit(solution)/shard_map/pallas_call | solution.py:38
  37.0 0.0 collective-permute-done.4.past_ref
  37.0 0.9 %shard_map.91 = (bf16[4,2,128,384]{3,2,1,0:T(8,128)(2,1)S(1)}, bf16[4,2,8,128]{3,2,1,0:T(8,128)(2,1)S(1)}) custom-call(bf16[2,128,384]{2,1,0:T(8,128)(2,1)S(1)} %collective-permute-done.4.past_ref, bf16[27,384,384]{2,1,0:T(8,128)(2,1)S(1)} %get-tuple-element.24.w_ref, ...), custom_call_target="tpu_custom_call", output_to_operand_aliasing={{0}: (6, {}), {1}: (7, {})} | custom-call | flops 452984832 | bytes 1000000 | tf_op jit(solution)/shard_map/pallas_call | solution.py:38
  37.8 0.0 collective-permute-done.1.past_ref
  37.8 0.8 %shard_map.92 = (bf16[4,2,128,384]{3,2,1,0:T(8,128)(2,1)S(1)}, bf16[4,2,8,128]{3,2,1,0:T(8,128)(2,1)S(1)}) custom-call(bf16[2,128,384]{2,1,0:T(8,128)(2,1)S(1)} %collective-permute-done.1.past_ref, bf16[27,384,384]{2,1,0:T(8,128)(2,1)S(1)} %get-tuple-element.24.w_ref, ...), custom_call_target="tpu_custom_call", output_to_operand_aliasing={{0}: (6, {}), {1}: (7, {})} | custom-call | flops 452984832 | bytes 1000000 | tf_op jit(solution)/shard_map/pallas_call | solution.py:38
  38.7 0.1 collective-permute-start.5
  38.8 6.6 %collective-permute-start.6 = (bf16[4,2,8,128]{3,2,1,0:T(8,128)(2,1)S(1)}, bf16[4,2,8,128]{3,2,1,0:T(8,128)(2,1)S(1)}, u32[]{:S(2)}, u32[]{:S(2)}) collective-permute-start(bf16[4,2,8,128]{3,2,1,0:T(8,128)(2,1)S(1)} %get-tuple-element.35.own_ref), channel_id=1, source_target_pairs={{1,2},{2,1},{3,4},{4,3},{5,6},{6,5},{7,8},{8,7},{9,10},{10,9},{11,... | collective-permute-start | bytes 49160 | tf_op jit(solution)/shard_map/ppermute | solution.py:26
  45.4 0.0 collective-permute-done.5.a_ref
  45.4 2.3 %collective-permute-done.6.b_ref = bf16[4,2,8,128]{3,2,1,0:T(8,128)(2,1)S(1)} collective-permute-done((bf16[4,2,8,128]{3,2,1,0:T(8,128)(2,1)S(1)}, bf16[4,2,8,128]{3,2,1,0:T(8,128)(2,1)S(1)}, u32[]{:S(2)}, u32[]{:S(2)}) %collective-permute-start.6) | collective-permute-done | bytes 16416 | tf_op jit(solution)/shard_map/ppermute | solution.py:26
  47.8 0.0 collective-permute-start.7
  47.8 4.7 %collective-permute-start.8 = (bf16[2,6,8,128]{3,2,1,0:T(8,128)(2,1)S(1)}, bf16[2,6,8,128]{3,2,1,0:T(8,128)(2,1)S(1)}, u32[]{:S(2)}, u32[]{:S(2)}) collective-permute-start(bf16[2,6,8,128]{3,2,1,0:T(8,128)(2,1)S(1)} %get-tuple-element.37), channel_id=1, source_target_pairs={{32,64},{64,32},{33,65},{65,33},{34,66},{66,34},{35,67},{67,35},{3... | collective-permute-start | bytes 73736 | tf_op jit(solution)/shard_map/ppermute | solution.py:26
  52.5 0.0 copy-done.1
  52.5 0.3 shard_map.94
  52.8 0.9 %copy.23 = bf16[4,2,128,384]{3,2,1,0:T(8,128)(2,1)} copy(bf16[4,2,128,384]{3,2,1,0:T(8,128)(2,1)S(1)} %get-tuple-element.40) | data formatting | bytes 1572864
  53.7 0.0 collective-permute-done.7.ta_ref
  53.7 0.3 collective-permute-done.8.tb_ref
  54.0 2.4 %shard_map.95 = f32[4,2,128]{2,1,0:T(2,128)} custom-call(bf16[4,2,8,128]{3,2,1,0:T(8,128)(2,1)S(1)} %collective-permute-done.5.a_ref, bf16[4,2,8,128]{3,2,1,0:T(8,128)(2,1)S(1)} %get-tuple-element.35.own_ref, bf16[4,2,8,128]{3,2,1,0:T(8,128)(2,1)S(1)} %collective-permute-done.6.b_ref, bf16[2,6,8,128]{3,2,1,0:T(8,128)(2,1)S(1)} %collective-permute-done.7.ta_ref, ...), custom_call_target="tpu_custom_call" | custom-call | bytes 1000000 | tf_op jit(solution)/shard_map/pallas_call | solution.py:38
  (9 shorter events, 0.1 us)
Async XLA Ops:
  2.3 13.9 %collective-permute-start.3 = (bf16[4,128,384]{2,1,0:T(8,128)(2,1)S(1)}, bf16[4,128,384]{2,1,0:T(8,128)(2,1)S(1)}, u32[]{:S(2)}, u32[]{:S(2)}) collective-permute-start(bf16[4,128,384]{2,1,0:T(8,128)(2,1)S(1)} %get-tuple-element.22.a_ref), channel_id=1, source_target_pairs={{0,1},{1,0},{2,3},{3,2},{4,5},{5,4},{6,7},{7,6},{8,9},{9,8},{10,11... | collective-permute-start | bytes 1179656 | tf_op jit(solution)/shard_map/ppermute | solution.py:26
  3.6 16.1 %collective-permute-start = (bf16[4,128,384]{2,1,0:T(8,128)(2,1)S(1)}, bf16[4,128,384]{2,1,0:T(8,128)(2,1)S(1)}, u32[]{:S(2)}, u32[]{:S(2)}) collective-permute-start(bf16[4,128,384]{2,1,0:T(8,128)(2,1)S(1)} %get-tuple-element.21.b_ref), channel_id=1, source_target_pairs={{1,2},{2,1},{3,4},{4,3},{5,6},{6,5},{7,8},{8,7},{9,10},{10,9},{11,... | collective-permute-start | bytes 1179656 | tf_op jit(solution)/shard_map/ppermute | solution.py:26
  10.6 14.6 %collective-permute-start.2 = (bf16[2,2,128,384]{3,2,1,0:T(8,128)(2,1)S(1)}, bf16[2,2,128,384]{3,2,1,0:T(8,128)(2,1)S(1)}, u32[]{:S(2)}, u32[]{:S(2)}) collective-permute-start(bf16[2,2,128,384]{3,2,1,0:T(8,128)(2,1)S(1)} %get-tuple-element.23), channel_id=1, source_target_pairs={{0,32},{32,64},{64,96},{1,33},{33,65},{65,97},{2,34},{34,66},{66,9... | collective-permute-start | bytes 1179656 | tf_op jit(solution)/shard_map/ppermute | solution.py:30
  16.3 20.7 %collective-permute-start.4 = (bf16[2,128,384]{2,1,0:T(8,128)(2,1)S(1)}, bf16[2,128,384]{2,1,0:T(8,128)(2,1)S(1)}, u32[]{:S(2)}, u32[]{:S(2)}) collective-permute-start(bf16[2,128,384]{2,1,0:T(8,128)(2,1)S(1)} %slice.9), channel_id=1, source_target_pairs={{0,32},{32,64},{64,96},{1,33},{33,65},{65,97},{2,34},{34,66},{66,9... | collective-permute-start | bytes 589832 | tf_op jit(solution)/shard_map/ppermute | solution.py:30
  19.8 13.0 %copy-start = (bf16[4,2,128,384]{3,2,1,0:T(8,128)(2,1)S(1)}, bf16[4,2,128,384]{3,2,1,0:T(8,128)(2,1)}, u32[]{:S(2)}) copy-start(bf16[4,2,128,384]{3,2,1,0:T(8,128)(2,1)} %feat_ref.9) | copy-start | bytes 2359300
  19.8 13.0 %copy-start.2 = (bf16[3,4,2,128]{3,2,1,0:T(2,128)(2,1)S(1)}, bf16[3,4,2,128]{3,2,1,0:T(2,128)(2,1)}, u32[]{:S(2)}) copy-start(bf16[3,4,2,128]{3,2,1,0:T(2,128)(2,1)} %real_ref.7) | copy-start | bytes 18436
  19.8 13.0 %copy-start.3 = (bf16[384,3]{0,1:T(4,128)(2,1)S(1)}, bf16[384,3]{0,1:T(4,128)(2,1)}, u32[]{:S(2)}) copy-start(bf16[384,3]{0,1:T(4,128)(2,1)} %param.10) | copy-start | bytes 6916
  19.8 18.0 %collective-permute-start.1 = (bf16[2,128,384]{2,1,0:T(8,128)(2,1)S(1)}, bf16[2,128,384]{2,1,0:T(8,128)(2,1)S(1)}, u32[]{:S(2)}, u32[]{:S(2)}) collective-permute-start(bf16[2,128,384]{2,1,0:T(8,128)(2,1)S(1)} %slice.8), channel_id=1, source_target_pairs={{0,32},{32,64},{64,96},{1,33},{33,65},{65,97},{2,34},{34,66},{66,9... | collective-permute-start | bytes 589832 | tf_op jit(solution)/shard_map/ppermute | solution.py:30
  37.8 14.6 %copy-start.1 = (bf16[27,128,64]{1,2,0:T(8,128)(2,1)S(1)}, bf16[27,128,64]{1,2,0:T(8,128)(2,1)}, u32[]{:S(2)}) copy-start(bf16[27,128,64]{1,2,0:T(8,128)(2,1)} %param.13) | copy-start | bytes 1327108
  37.8 14.6 %copy-start.4 = (bf16[27,64,3]{1,0,2:T(8,128)(2,1)S(1)}, bf16[27,64,3]{1,0,2:T(8,128)(2,1)}, u32[]{:S(2)}) copy-start(bf16[27,64,3]{1,0,2:T(8,128)(2,1)} %param.12) | copy-start | bytes 31108
  38.7 6.7 %collective-permute-start.5 = (bf16[4,2,8,128]{3,2,1,0:T(8,128)(2,1)S(1)}, bf16[4,2,8,128]{3,2,1,0:T(8,128)(2,1)S(1)}, u32[]{:S(2)}, u32[]{:S(2)}) collective-permute-start(bf16[4,2,8,128]{3,2,1,0:T(8,128)(2,1)S(1)} %get-tuple-element.35.own_ref), channel_id=1, source_target_pairs={{0,1},{1,0},{2,3},{3,2},{4,5},{5,4},{6,7},{7,6},{8,9},{9,8},{10,11... | collective-permute-start | bytes 49160 | tf_op jit(solution)/shard_map/ppermute | solution.py:26
  38.8 9.0 %collective-permute-start.6 = (bf16[4,2,8,128]{3,2,1,0:T(8,128)(2,1)S(1)}, bf16[4,2,8,128]{3,2,1,0:T(8,128)(2,1)S(1)}, u32[]{:S(2)}, u32[]{:S(2)}) collective-permute-start(bf16[4,2,8,128]{3,2,1,0:T(8,128)(2,1)S(1)} %get-tuple-element.35.own_ref), channel_id=1, source_target_pairs={{1,2},{2,1},{3,4},{4,3},{5,6},{6,5},{7,8},{8,7},{9,10},{10,9},{11,... | collective-permute-start | bytes 49160 | tf_op jit(solution)/shard_map/ppermute | solution.py:26
  47.8 5.9 %collective-permute-start.7 = (bf16[2,6,8,128]{3,2,1,0:T(8,128)(2,1)S(1)}, bf16[2,6,8,128]{3,2,1,0:T(8,128)(2,1)S(1)}, u32[]{:S(2)}, u32[]{:S(2)}) collective-permute-start(bf16[2,6,8,128]{3,2,1,0:T(8,128)(2,1)S(1)} %get-tuple-element.36), channel_id=1, source_target_pairs={{0,32},{32,0},{64,96},{96,64},{1,33},{33,1},{65,97},{97,65},{2,34}... | collective-permute-start | bytes 73736 | tf_op jit(solution)/shard_map/ppermute | solution.py:26
  47.8 6.2 %collective-permute-start.8 = (bf16[2,6,8,128]{3,2,1,0:T(8,128)(2,1)S(1)}, bf16[2,6,8,128]{3,2,1,0:T(8,128)(2,1)S(1)}, u32[]{:S(2)}, u32[]{:S(2)}) collective-permute-start(bf16[2,6,8,128]{3,2,1,0:T(8,128)(2,1)S(1)} %get-tuple-element.37), channel_id=1, source_target_pairs={{32,64},{64,32},{33,65},{65,33},{34,66},{66,34},{35,67},{67,35},{3... | collective-permute-start | bytes 73736 | tf_op jit(solution)/shard_map/ppermute | solution.py:26

commit v7 on v6

--- a/solution.py
+++ b/solution.py
@@ -86,47 +86,65 @@
     return jnp.concatenate([w_ref[9 * dt + 3 * dh + dw, :, off : off + 128] for dt, dh in taps], axis=0)
 
 
-def load_taps(weight_ref, w_ref, sems, dws):
-    loads = {
-        dw: [
-            pltpu.make_async_copy(weight_ref.at[tap], w_ref.at[tap], sems.at[tap])
-            for tap in range(dw, 27, 3)
-        ]
-        for dw in dws
-    }
-    for dw in dws:
-        for load in loads[dw]:
-            load.start()
-    return loads
-
-
-def fetch_kernel(weight_ref, w_ref, sems):
-    for load in load_taps(weight_ref, w_ref, sems, (0,))[0]:
-        load.wait()
-
-
-def own_kernel(a_ref, b_ref, past_ref, weight_ref, some_ref, y_ref, w_ref, lines_ref, sems):
+def start_taps(weight_ref, w_ref, sems, taps):
+    for tap in taps:
+        pltpu.make_async_copy(weight_ref.at[tap], w_ref.at[tap], sems.at[tap]).start()
+
+
+def wait_taps(weight_ref, w_ref, sems, taps):
+    for tap in taps:
+        pltpu.make_async_copy(weight_ref.at[tap], w_ref.at[tap], sems.at[tap]).wait()
+
+
+def taps_of(dts, dws):
+    return [9 * dt + 3 * dh + dw for dw in dws for dt in dts for dh in range(3)]
+
+
+def own_products(lhs, w_ref, inputs, dw):
+    chans = w_ref.shape[1]
+    blocks = [(o, off) for o in range(2) for off in range(0, chans, 128)]
+    for j in range(0, len(blocks), 2):
+        pair = blocks[j : j + 2]
+        rhs = [rhs_block(w_ref, dw, off, [(dt, i - o + 1) for dt, i in inputs]) for o, off in pair]
+        got = jnp.dot(lhs, jnp.concatenate(rhs, axis=1), preferred_element_type=F32)
+        for k, (o, off) in enumerate(pair):
+            at = dw * chans + off
+            yield o, slice(at, at + 128), got[:, k * 128 : (k + 1) * 128]
+
+
+def ahead_kernel(a_ref, b_ref, weight_ref, y_ref, w_ref, lines_ref, sems):
     odd = lax.rem(lax.axis_index("rows"), 2)
     frames, width, chans = a_ref.shape
-    loads = load_taps(weight_ref, w_ref, sems, (1, 2))
+    more = taps_of((0, 1), (0,))
+    start_taps(weight_ref, w_ref, sems, taps_of((2,), range(3)) + more)
+    lines_ref[1 - odd] = a_ref[...]
+    lines_ref[odd] = b_ref[...]
+    lhs = jnp.concatenate([lines_ref[i].reshape(frames * width, chans) for i in range(2)], axis=1)
+    for dw in range(3):
+        wait_taps(weight_ref, w_ref, sems, taps_of((2,), (dw,)))
+        for o, cols, got in own_products(lhs, w_ref, [(2, 0), (2, 1)], dw):
+            y_ref[o, :, cols] = got
+    wait_taps(weight_ref, w_ref, sems, more)
+
+
+def own_kernel(
+    a_ref, b_ref, past_ref, weight_ref, some_ref, sums_ref, y_ref, w_ref, lines_ref, sems
+):
+    odd = lax.rem(lax.axis_index("rows"), 2)
+    frames, width, chans = a_ref.shape
+    start_taps(weight_ref, w_ref, sems, taps_of((0, 1), (1, 2)))
     for k, (row, line_ref) in enumerate(((1 - odd, a_ref), (odd, b_ref))):
         lines_ref[row, pl.ds(0, 2)] = past_ref[k]
-        lines_ref[row, pl.ds(2, frames)] = line_ref[...]
-    inputs = [(dt, i) for dt in range(3) for i in range(2)]
+        lines_ref[row, pl.ds(2, frames - 1)] = line_ref[: frames - 1]
+    inputs = [(dt, i) for dt in range(2) for i in range(2)]
     lhs = jnp.concatenate(
         [lines_ref[i, dt : dt + frames].reshape(frames * width, chans) for dt, i in inputs], axis=1
     )
     for dw in range(3):
-        for load in loads.get(dw, ()):
-            load.wait()
-        blocks = [(o, off) for o in range(2) for off in range(0, chans, 128)]
-        for j in range(0, len(blocks), 2):
-            pair = blocks[j : j + 2]
-            rhs = [rhs_block(w_ref, dw, off, [(dt, i - o + 1) for dt, i in inputs]) for o, off in pair]
-            got = jnp.dot(lhs, jnp.concatenate(rhs, axis=1), preferred_element_type=F32)
-            for k, (o, off) in enumerate(pair):
-                at = dw * chans + off
-                y_ref[o, :, at : at + 128] = got[:, k * 128 : (k + 1) * 128]
+        if dw:
+            wait_taps(weight_ref, w_ref, sems, taps_of((0, 1), (dw,)))
+        for o, cols, got in own_products(lhs, w_ref, inputs, dw):
+            y_ref[o, :, cols] = sums_ref[o, :, cols] + got
 
 
 def prep_kernel(d2_ref, d1_ref, w2_ref, w1_ref):
@@ -356,24 +374,27 @@
     from_a = swap(to_a, "rows", 0)
 
     line = 2 * width * chans * chans
-    first_taps = local(
-        fetch_kernel,
-        kept(*conv_weight.shape),
-        (conv_weight,),
-        hbm=(0,),
-        scratch=[pltpu.SemaphoreType.DMA((27,))],
+    partial = kept(height, cells, 3 * chans, dtype=F32)
+    held = kept(*conv_weight.shape)
+    sums, some_taps = local(
+        ahead_kernel,
+        (partial, held),
+        (to_a, to_b, conv_weight),
+        hbm=(2,),
+        scratch=[pltpu.VMEM((2, frames, width, chans), BF16), pltpu.SemaphoreType.DMA((27,))],
+        flops=16 * 3 * line,
     )
     sums, weight = local(
         own_kernel,
-        (kept(height, cells, 3 * chans, dtype=F32), kept(*conv_weight.shape)),
-        (to_a, to_b, past, conv_weight, first_taps),
+        (partial, held),
+        (to_a, to_b, past, conv_weight, some_taps, sums),
         hbm=(3,),
         scratch=[
-            pltpu.VMEM((2, frames + 2, width, chans), BF16),
+            pltpu.VMEM((2, frames + 1, width, chans), BF16),
             pltpu.SemaphoreType.DMA((27,)),
         ],
-        aliases={4: 1},
-        flops=48 * 3 * line,
+        aliases={4: 1, 5: 0},
+        flops=32 * 3 * line,
     )
     corner_a = onward(from_a[frames - 2 :], "tm")
     corner_b = onward(from_b[frames - 2 :], "tm")

time: 56.7 us -> 54.5 us (0.961)
  waiting for transfers between devices: 4.15 us -> 2.62 us
  starting transfers between devices: 30.6 us -> 30 us
    ppermute x6, waiting for transfers between devices: 4.14 us -> 2.62 us  [swap(): return lax.ppermute(block, axis, pairs(lax.axis_size(axis), first))]
    ppermute x3, starting transfers between devices: 11.1 us -> 10.2 us  [onward(): lax.ppermute(block, axis, [(i, i + 1) for i in range(lax.axis_size(axis)...]
  transfers between devices with their start and end apart: 9 -> 9, of which waited for: 3 -> 2; matrix products, arithmetic and copies ran while one was open for 2% -> 2% of each run, Pallas kernels for 26% -> 27%
where the time goes in v7:
time: 54.5 us; the launch traced here: 54.3 us
  starting transfers between devices  30 us (55%)
  Pallas kernels  19.9 us (37%)
  waiting for transfers between devices  2.62 us (5%)
  local copies, waits for them, and re-layouts  0.96 us (2%)
  between operations  0.85 us (2%)
    pallas_call x10, Pallas kernels, local(): pl.pallas_call(kernel, out_shape=outs, in_specs=[HBM if i in hbm else VME...  19.9 us
    ppermute x6, starting transfers between devices, swap(): return lax.ppermute(block, axis, pairs(lax.axis_size(axis), first))  19.7 us
    ppermute x3, starting transfers between devices, onward(): lax.ppermute(block, axis, [(i, i + 1) for i in range(lax.axis_size(axis)...  10.2 us
    ppermute x6, waiting for transfers between devices, swap(): return lax.ppermute(block, axis, pairs(lax.axis_size(axis), first))  2.62 us
  transfers between devices with their start and end apart: 9, of which 2 were waited for; matrix products, arithmetic and copies ran while one was open for 2% of the time, Pallas kernels for 27%

profile of v7, /device:TPU:17, one launch (start us, length us, event | category | flops | bytes accessed | tf_op | source)
XLA Modules:
  0.0 54.3 jit_solution(16770559160465275792)
XLA Ops:
  0.6 1.7 %shard_map.86 = (bf16[4,128,384]{2,1,0:T(8,128)(2,1)S(1)}, bf16[4,128,384]{2,1,0:T(8,128)(2,1)S(1)}, bf16[2,2,128,384]{3,2,1,0:T(8,128)(2,1)S(1)}) custom-call(bf16[4,2,128,384]{3,2,1,0:T(8,128)(2,1)} %feat_ref.9, f32[384]{0:T(512)} %gain_ref.1), custom_call_target="tpu_custom_call" | custom-call | bytes 1000000 | tf_op jit(solution)/shard_map/pallas_call | solution.py:38
  2.3 1.3 %collective-permute-start.3 = (bf16[4,128,384]{2,1,0:T(8,128)(2,1)S(1)}, bf16[4,128,384]{2,1,0:T(8,128)(2,1)S(1)}, u32[]{:S(2)}, u32[]{:S(2)}) collective-permute-start(bf16[4,128,384]{2,1,0:T(8,128)(2,1)S(1)} %get-tuple-element.24.a_ref), channel_id=1, source_target_pairs={{0,1},{1,0},{2,3},{3,2},{4,5},{5,4},{6,7},{7,6},{8,9},{9,8},{10,11... | collective-permute-start | bytes 1179656 | tf_op jit(solution)/shard_map/ppermute | solution.py:26
  3.6 6.9 %collective-permute-start = (bf16[4,128,384]{2,1,0:T(8,128)(2,1)S(1)}, bf16[4,128,384]{2,1,0:T(8,128)(2,1)S(1)}, u32[]{:S(2)}, u32[]{:S(2)}) collective-permute-start(bf16[4,128,384]{2,1,0:T(8,128)(2,1)S(1)} %get-tuple-element.23.b_ref), channel_id=1, source_target_pairs={{1,2},{2,1},{3,4},{4,3},{5,6},{6,5},{7,8},{8,7},{9,10},{10,9},{11,... | collective-permute-start | bytes 1179656 | tf_op jit(solution)/shard_map/ppermute | solution.py:26
  10.6 3.8 %collective-permute-start.2 = (bf16[2,2,128,384]{3,2,1,0:T(8,128)(2,1)S(1)}, bf16[2,2,128,384]{3,2,1,0:T(8,128)(2,1)S(1)}, u32[]{:S(2)}, u32[]{:S(2)}) collective-permute-start(bf16[2,2,128,384]{3,2,1,0:T(8,128)(2,1)S(1)} %get-tuple-element.25), channel_id=1, source_target_pairs={{0,32},{32,64},{64,96},{1,33},{33,65},{65,97},{2,34},{34,66},{66,9... | collective-permute-start | bytes 1179656 | tf_op jit(solution)/shard_map/ppermute | solution.py:30
  14.3 4.1 %shard_map.87 = (f32[2,512,1152]{2,1,0:T(8,128)S(1)}, bf16[27,384,384]{2,1,0:T(8,128)(2,1)S(1)}) custom-call(bf16[4,128,384]{2,1,0:T(8,128)(2,1)S(1)} %get-tuple-element.24.a_ref, bf16[4,128,384]{2,1,0:T(8,128)(2,1)S(1)} %get-tuple-element.23.b_ref, bf16[27,384,384]{2,1,0:T(8,128)(2,1)} %weight_ref.3), custom_call_target="tpu_custom_call" | custom-call | flops 1811939328 | bytes 1000000 | tf_op jit(solution)/shard_map/pallas_call | solution.py:38
  18.5 0.0 collective-permute-done.3.line_ref
  18.5 1.9 %collective-permute-start.4 = (bf16[2,128,384]{2,1,0:T(8,128)(2,1)S(1)}, bf16[2,128,384]{2,1,0:T(8,128)(2,1)S(1)}, u32[]{:S(2)}, u32[]{:S(2)}) collective-permute-start(bf16[2,128,384]{2,1,0:T(8,128)(2,1)S(1)} %slice.9), channel_id=1, source_target_pairs={{0,32},{32,64},{64,96},{1,33},{33,65},{65,97},{2,34},{34,66},{66,9... | collective-permute-start | bytes 589832 | tf_op jit(solution)/shard_map/ppermute | solution.py:30
  20.4 0.0 collective-permute-done.line_ref
  20.5 4.5 %collective-permute-start.1 = (bf16[2,128,384]{2,1,0:T(8,128)(2,1)S(1)}, bf16[2,128,384]{2,1,0:T(8,128)(2,1)S(1)}, u32[]{:S(2)}, u32[]{:S(2)}) collective-permute-start(bf16[2,128,384]{2,1,0:T(8,128)(2,1)S(1)} %slice.8), channel_id=1, source_target_pairs={{0,32},{32,64},{64,96},{1,33},{33,65},{65,97},{2,34},{34,66},{66,9... | collective-permute-start | bytes 589832 | tf_op jit(solution)/shard_map/ppermute | solution.py:30
  25.0 0.0 collective-permute-done.2.past_ref
  25.0 0.0 copy-start
  25.0 0.0 copy-start.2
  25.1 0.0 copy-start.3
  25.1 5.5 %shard_map.88 = (f32[2,512,1152]{2,1,0:T(8,128)S(1)}, bf16[27,384,384]{2,1,0:T(8,128)(2,1)S(1)}) custom-call(bf16[4,128,384]{2,1,0:T(8,128)(2,1)S(1)} %get-tuple-element.24.a_ref, bf16[4,128,384]{2,1,0:T(8,128)(2,1)S(1)} %get-tuple-element.23.b_ref, ...), custom_call_target="tpu_custom_call", output_to_operand_aliasing={{1}: (4, {}), {0}: (5, {})} | custom-call | flops 3623878656 | bytes 1000000 | tf_op jit(solution)/shard_map/pallas_call | solution.py:38
  30.6 2.1 %shard_map.89 = (f32[256,1152]{1,0:T(8,128)S(1)}, bf16[4,2,128,384]{3,2,1,0:T(8,128)(2,1)S(1)}, bf16[4,2,8,128]{3,2,1,0:T(8,128)(2,1)S(1)}) custom-call(bf16[4,128,384]{2,1,0:T(8,128)(2,1)S(1)} %collective-permute-done.3.line_ref, bf16[27,384,384]{2,1,0:T(8,128)(2,1)S(1)} %get-tuple-element.28.w_ref, f32[2,512,1152]{2,1,0:T(8,128)S(1)} %get-tuple-element.29.sums_ref, ...), custom_call_target="tpu_custom_call" | custom-call | flops 1358954496 | bytes 1000000 | tf_op jit(solution)/shard_map/pallas_call | solution.py:38
  32.6 2.1 %shard_map.90 = (f32[256,1152]{1,0:T(8,128)S(1)}, bf16[4,2,128,384]{3,2,1,0:T(8,128)(2,1)S(1)}, bf16[4,2,8,128]{3,2,1,0:T(8,128)(2,1)S(1)}) custom-call(bf16[4,128,384]{2,1,0:T(8,128)(2,1)S(1)} %collective-permute-done.line_ref, bf16[27,384,384]{2,1,0:T(8,128)(2,1)S(1)} %get-tuple-element.28.w_ref, ...), custom_call_target="tpu_custom_call", output_to_operand_aliasing={{1}: (6, {}), {2}: (7, {})} | custom-call | flops 1358954496 | bytes 1000000 | tf_op jit(solution)/shard_map/pallas_call | solution.py:38
  34.7 0.0 collective-permute-done.4.past_ref
  34.7 0.9 %shard_map.91 = (bf16[4,2,128,384]{3,2,1,0:T(8,128)(2,1)S(1)}, bf16[4,2,8,128]{3,2,1,0:T(8,128)(2,1)S(1)}) custom-call(bf16[2,128,384]{2,1,0:T(8,128)(2,1)S(1)} %collective-permute-done.4.past_ref, bf16[27,384,384]{2,1,0:T(8,128)(2,1)S(1)} %get-tuple-element.28.w_ref, ...), custom_call_target="tpu_custom_call", output_to_operand_aliasing={{0}: (6, {}), {1}: (7, {})} | custom-call | flops 452984832 | bytes 1000000 | tf_op jit(solution)/shard_map/pallas_call | solution.py:38
  35.5 0.0 collective-permute-done.1.past_ref
  35.5 0.0 copy-start.1
  35.6 0.0 copy-start.4
  35.6 0.8 %shard_map.92 = (bf16[4,2,128,384]{3,2,1,0:T(8,128)(2,1)S(1)}, bf16[4,2,8,128]{3,2,1,0:T(8,128)(2,1)S(1)}) custom-call(bf16[2,128,384]{2,1,0:T(8,128)(2,1)S(1)} %collective-permute-done.1.past_ref, bf16[27,384,384]{2,1,0:T(8,128)(2,1)S(1)} %get-tuple-element.28.w_ref, ...), custom_call_target="tpu_custom_call", output_to_operand_aliasing={{0}: (6, {}), {1}: (7, {})} | custom-call | flops 452984832 | bytes 1000000 | tf_op jit(solution)/shard_map/pallas_call | solution.py:38
  36.4 0.1 collective-permute-start.5
  36.5 6.6 %collective-permute-start.6 = (bf16[4,2,8,128]{3,2,1,0:T(8,128)(2,1)S(1)}, bf16[4,2,8,128]{3,2,1,0:T(8,128)(2,1)S(1)}, u32[]{:S(2)}, u32[]{:S(2)}) collective-permute-start(bf16[4,2,8,128]{3,2,1,0:T(8,128)(2,1)S(1)} %get-tuple-element.39.own_ref), channel_id=1, source_target_pairs={{1,2},{2,1},{3,4},{4,3},{5,6},{6,5},{7,8},{8,7},{9,10},{10,9},{11,... | collective-permute-start | bytes 49160 | tf_op jit(solution)/shard_map/ppermute | solution.py:26
  43.1 0.0 collective-permute-done.5.a_ref
  43.1 2.3 %collective-permute-done.6.b_ref = bf16[4,2,8,128]{3,2,1,0:T(8,128)(2,1)S(1)} collective-permute-done((bf16[4,2,8,128]{3,2,1,0:T(8,128)(2,1)S(1)}, bf16[4,2,8,128]{3,2,1,0:T(8,128)(2,1)S(1)}, u32[]{:S(2)}, u32[]{:S(2)}) %collective-permute-start.6) | collective-permute-done | bytes 16416 | tf_op jit(solution)/shard_map/ppermute | solution.py:26
  45.5 4.8 %collective-permute-start.8 = (bf16[2,6,8,128]{3,2,1,0:T(8,128)(2,1)S(1)}, bf16[2,6,8,128]{3,2,1,0:T(8,128)(2,1)S(1)}, u32[]{:S(2)}, u32[]{:S(2)}) collective-permute-start(bf16[2,6,8,128]{3,2,1,0:T(8,128)(2,1)S(1)} %get-tuple-element.41), channel_id=1, source_target_pairs={{32,64},{64,32},{33,65},{65,33},{34,66},{66,34},{35,67},{67,35},{3... | collective-permute-start | bytes 73736 | tf_op jit(solution)/shard_map/ppermute | solution.py:26
  50.4 0.3 shard_map.94
  50.7 0.9 %copy.25 = bf16[4,2,128,384]{3,2,1,0:T(8,128)(2,1)} copy(bf16[4,2,128,384]{3,2,1,0:T(8,128)(2,1)S(1)} %get-tuple-element.44) | data formatting | bytes 1572864
  51.6 0.0 collective-permute-done.7.ta_ref
  51.6 0.3 collective-permute-done.8.tb_ref
  51.8 2.4 %shard_map.95 = f32[4,2,128]{2,1,0:T(2,128)} custom-call(bf16[4,2,8,128]{3,2,1,0:T(8,128)(2,1)S(1)} %collective-permute-done.5.a_ref, bf16[4,2,8,128]{3,2,1,0:T(8,128)(2,1)S(1)} %get-tuple-element.39.own_ref, bf16[4,2,8,128]{3,2,1,0:T(8,128)(2,1)S(1)} %collective-permute-done.6.b_ref, bf16[2,6,8,128]{3,2,1,0:T(8,128)(2,1)S(1)} %collective-permute-done.7.ta_ref, ...), custom_call_target="tpu_custom_call" | custom-call | bytes 1000000 | tf_op jit(solution)/shard_map/pallas_call | solution.py:38
  (9 shorter events, 0.1 us)
Async XLA Ops:
  2.3 16.1 %collective-permute-start.3 = (bf16[4,128,384]{2,1,0:T(8,128)(2,1)S(1)}, bf16[4,128,384]{2,1,0:T(8,128)(2,1)S(1)}, u32[]{:S(2)}, u32[]{:S(2)}) collective-permute-start(bf16[4,128,384]{2,1,0:T(8,128)(2,1)S(1)} %get-tuple-element.24.a_ref), channel_id=1, source_target_pairs={{0,1},{1,0},{2,3},{3,2},{4,5},{5,4},{6,7},{7,6},{8,9},{9,8},{10,11... | collective-permute-start | bytes 1179656 | tf_op jit(solution)/shard_map/ppermute | solution.py:26
  3.6 16.8 %collective-permute-start = (bf16[4,128,384]{2,1,0:T(8,128)(2,1)S(1)}, bf16[4,128,384]{2,1,0:T(8,128)(2,1)S(1)}, u32[]{:S(2)}, u32[]{:S(2)}) collective-permute-start(bf16[4,128,384]{2,1,0:T(8,128)(2,1)S(1)} %get-tuple-element.23.b_ref), channel_id=1, source_target_pairs={{1,2},{2,1},{3,4},{4,3},{5,6},{6,5},{7,8},{8,7},{9,10},{10,9},{11,... | collective-permute-start | bytes 1179656 | tf_op jit(solution)/shard_map/ppermute | solution.py:26
  10.6 14.5 %collective-permute-start.2 = (bf16[2,2,128,384]{3,2,1,0:T(8,128)(2,1)S(1)}, bf16[2,2,128,384]{3,2,1,0:T(8,128)(2,1)S(1)}, u32[]{:S(2)}, u32[]{:S(2)}) collective-permute-start(bf16[2,2,128,384]{3,2,1,0:T(8,128)(2,1)S(1)} %get-tuple-element.25), channel_id=1, source_target_pairs={{0,32},{32,64},{64,96},{1,33},{33,65},{65,97},{2,34},{34,66},{66,9... | collective-permute-start | bytes 1179656 | tf_op jit(solution)/shard_map/ppermute | solution.py:30
  18.5 16.2 %collective-permute-start.4 = (bf16[2,128,384]{2,1,0:T(8,128)(2,1)S(1)}, bf16[2,128,384]{2,1,0:T(8,128)(2,1)S(1)}, u32[]{:S(2)}, u32[]{:S(2)}) collective-permute-start(bf16[2,128,384]{2,1,0:T(8,128)(2,1)S(1)} %slice.9), channel_id=1, source_target_pairs={{0,32},{32,64},{64,96},{1,33},{33,65},{65,97},{2,34},{34,66},{66,9... | collective-permute-start | bytes 589832 | tf_op jit(solution)/shard_map/ppermute | solution.py:30
  20.5 15.1 %collective-permute-start.1 = (bf16[2,128,384]{2,1,0:T(8,128)(2,1)S(1)}, bf16[2,128,384]{2,1,0:T(8,128)(2,1)S(1)}, u32[]{:S(2)}, u32[]{:S(2)}) collective-permute-start(bf16[2,128,384]{2,1,0:T(8,128)(2,1)S(1)} %slice.8), channel_id=1, source_target_pairs={{0,32},{32,64},{64,96},{1,33},{33,65},{65,97},{2,34},{34,66},{66,9... | collective-permute-start | bytes 589832 | tf_op jit(solution)/shard_map/ppermute | solution.py:30
  25.0 5.5 %copy-start = (bf16[4,2,128,384]{3,2,1,0:T(8,128)(2,1)S(1)}, bf16[4,2,128,384]{3,2,1,0:T(8,128)(2,1)}, u32[]{:S(2)}) copy-start(bf16[4,2,128,384]{3,2,1,0:T(8,128)(2,1)} %feat_ref.9) | copy-start | bytes 2359300
  25.0 5.5 %copy-start.2 = (bf16[3,4,2,128]{3,2,1,0:T(2,128)(2,1)S(1)}, bf16[3,4,2,128]{3,2,1,0:T(2,128)(2,1)}, u32[]{:S(2)}) copy-start(bf16[3,4,2,128]{3,2,1,0:T(2,128)(2,1)} %real_ref.7) | copy-start | bytes 18436
  25.1 5.5 %copy-start.3 = (bf16[384,3]{0,1:T(4,128)(2,1)S(1)}, bf16[384,3]{0,1:T(4,128)(2,1)}, u32[]{:S(2)}) copy-start(bf16[384,3]{0,1:T(4,128)(2,1)} %param.10) | copy-start | bytes 6916
  35.5 14.8 %copy-start.1 = (bf16[27,128,64]{1,2,0:T(8,128)(2,1)S(1)}, bf16[27,128,64]{1,2,0:T(8,128)(2,1)}, u32[]{:S(2)}) copy-start(bf16[27,128,64]{1,2,0:T(8,128)(2,1)} %param.13) | copy-start | bytes 1327108
  35.6 14.8 %copy-start.4 = (bf16[27,64,3]{1,0,2:T(8,128)(2,1)S(1)}, bf16[27,64,3]{1,0,2:T(8,128)(2,1)}, u32[]{:S(2)}) copy-start(bf16[27,64,3]{1,0,2:T(8,128)(2,1)} %param.12) | copy-start | bytes 31108
  36.4 6.7 %collective-permute-start.5 = (bf16[4,2,8,128]{3,2,1,0:T(8,128)(2,1)S(1)}, bf16[4,2,8,128]{3,2,1,0:T(8,128)(2,1)S(1)}, u32[]{:S(2)}, u32[]{:S(2)}) collective-permute-start(bf16[4,2,8,128]{3,2,1,0:T(8,128)(2,1)S(1)} %get-tuple-element.39.own_ref), channel_id=1, source_target_pairs={{0,1},{1,0},{2,3},{3,2},{4,5},{5,4},{6,7},{7,6},{8,9},{9,8},{10,11... | collective-permute-start | bytes 49160 | tf_op jit(solution)/shard_map/ppermute | solution.py:26
  36.5 9.0 %collective-permute-start.6 = (bf16[4,2,8,128]{3,2,1,0:T(8,128)(2,1)S(1)}, bf16[4,2,8,128]{3,2,1,0:T(8,128)(2,1)S(1)}, u32[]{:S(2)}, u32[]{:S(2)}) collective-permute-start(bf16[4,2,8,128]{3,2,1,0:T(8,128)(2,1)S(1)} %get-tuple-element.39.own_ref), channel_id=1, source_target_pairs={{1,2},{2,1},{3,4},{4,3},{5,6},{6,5},{7,8},{8,7},{9,10},{10,9},{11,... | collective-permute-start | bytes 49160 | tf_op jit(solution)/shard_map/ppermute | solution.py:26
  45.5 6.1 %collective-permute-start.7 = (bf16[2,6,8,128]{3,2,1,0:T(8,128)(2,1)S(1)}, bf16[2,6,8,128]{3,2,1,0:T(8,128)(2,1)S(1)}, u32[]{:S(2)}, u32[]{:S(2)}) collective-permute-start(bf16[2,6,8,128]{3,2,1,0:T(8,128)(2,1)S(1)} %get-tuple-element.40), channel_id=1, source_target_pairs={{0,32},{32,0},{64,96},{96,64},{1,33},{33,1},{65,97},{97,65},{2,34}... | collective-permute-start | bytes 73736 | tf_op jit(solution)/shard_map/ppermute | solution.py:26
  45.5 6.3 %collective-permute-start.8 = (bf16[2,6,8,128]{3,2,1,0:T(8,128)(2,1)S(1)}, bf16[2,6,8,128]{3,2,1,0:T(8,128)(2,1)S(1)}, u32[]{:S(2)}, u32[]{:S(2)}) collective-permute-start(bf16[2,6,8,128]{3,2,1,0:T(8,128)(2,1)S(1)} %get-tuple-element.41), channel_id=1, source_target_pairs={{32,64},{64,32},{33,65},{65,33},{34,66},{66,34},{35,67},{67,35},{3... | collective-permute-start | bytes 73736 | tf_op jit(solution)/shard_map/ppermute | solution.py:26

commit v8 on v6

--- a/solution.py
+++ b/solution.py
@@ -30,7 +30,7 @@
     return lax.ppermute(block, axis, [(i, i + 1) for i in range(lax.axis_size(axis) - 1)])
 
 
-def local(kernel, outs, args, scratch=(), aliases=None, flops=0, hbm=(), limit=24):
+def local(kernel, outs, args, scratch=(), aliases=None, flops=0, hbm=(), stored=(), limit=24):
     args = [
         pltpu.with_memory_space_constraint(a, pltpu.HBM if i in hbm else pltpu.VMEM)
         for i, a in enumerate(args)
@@ -39,7 +39,9 @@
         kernel,
         out_shape=outs,
         in_specs=[HBM if i in hbm else VMEM for i in range(len(args))],
-        out_specs=jax.tree.map(lambda _: VMEM, outs),
+        out_specs=tuple(HBM if i in stored else VMEM for i in range(len(outs)))
+        if isinstance(outs, tuple)
+        else VMEM,
         scratch_shapes=scratch,
         input_output_aliases=aliases or {},
         compiler_params=pltpu.CompilerParams(vmem_limit_bytes=limit << 20),
@@ -86,29 +88,25 @@
     return jnp.concatenate([w_ref[9 * dt + 3 * dh + dw, :, off : off + 128] for dt, dh in taps], axis=0)
 
 
-def load_taps(weight_ref, w_ref, sems, dws):
-    loads = {
-        dw: [
-            pltpu.make_async_copy(weight_ref.at[tap], w_ref.at[tap], sems.at[tap])
-            for tap in range(dw, 27, 3)
-        ]
-        for dw in dws
-    }
-    for dw in dws:
-        for load in loads[dw]:
-            load.start()
-    return loads
+def start_taps(weight_ref, w_ref, sems, dw):
+    for tap in range(dw, 27, 3):
+        pltpu.make_async_copy(weight_ref.at[tap], w_ref.at[tap], sems.at[tap]).start()
+
+
+def wait_taps(weight_ref, w_ref, sems, dw):
+    for tap in range(dw, 27, 3):
+        pltpu.make_async_copy(weight_ref.at[tap], w_ref.at[tap], sems.at[tap]).wait()
 
 
 def fetch_kernel(weight_ref, w_ref, sems):
-    for load in load_taps(weight_ref, w_ref, sems, (0,))[0]:
-        load.wait()
+    start_taps(weight_ref, w_ref, sems, 0)
+    wait_taps(weight_ref, w_ref, sems, 0)
 
 
 def own_kernel(a_ref, b_ref, past_ref, weight_ref, some_ref, y_ref, w_ref, lines_ref, sems):
     odd = lax.rem(lax.axis_index("rows"), 2)
     frames, width, chans = a_ref.shape
-    loads = load_taps(weight_ref, w_ref, sems, (1, 2))
+    start_taps(weight_ref, w_ref, sems, 1)
     for k, (row, line_ref) in enumerate(((1 - odd, a_ref), (odd, b_ref))):
         lines_ref[row, pl.ds(0, 2)] = past_ref[k]
         lines_ref[row, pl.ds(2, frames)] = line_ref[...]
@@ -117,8 +115,10 @@
         [lines_ref[i, dt : dt + frames].reshape(frames * width, chans) for dt, i in inputs], axis=1
     )
     for dw in range(3):
-        for load in loads.get(dw, ()):
-            load.wait()
+        if dw:
+            wait_taps(weight_ref, w_ref, sems, dw)
+        if dw == 1:
+            start_taps(weight_ref, w_ref, sems, 2)
         blocks = [(o, off) for o in range(2) for off in range(0, chans, 128)]
         for j in range(0, len(blocks), 2):
             pair = blocks[j : j + 2]
@@ -129,18 +129,18 @@
                 y_ref[o, :, at : at + 128] = got[:, k * 128 : (k + 1) * 128]
 
 
-def prep_kernel(d2_ref, d1_ref, w2_ref, w1_ref):
+def prep_kernel(d2_ref, d1_ref, decoded_ref, w2_ref, w1_ref, out_ref, sem):
+    store = pltpu.make_async_copy(decoded_ref, out_ref, sem)
+    store.start()
     depth1, depth2 = d2_ref.shape[1:]
-    for tap in range(27):
-        dw, rest = tap % 3, tap // 3
-        if rest % 2 == 0:
-            parts = [d2_ref[tap].astype(F32)]
-            if rest < 8:
-                parts.append(d2_ref[tap + 3].astype(F32))
-            wide = jnp.concatenate(parts, axis=0)
-            w2_ref[dw * depth2 : (dw + 1) * depth2, rest * depth1 : rest * depth1 + wide.shape[0]] = (
-                wide.T.astype(BF16)
-            )
+    for dt in range(3):
+        for dw in range(3):
+            parts = [d2_ref[9 * dt + 3 * dh + dw].astype(F32) for dh in range(3)]
+            parts.append(jnp.zeros((depth1, depth2), F32))
+            for k in range(2):
+                wide = jnp.concatenate(parts[2 * k : 2 * k + 2], axis=0)
+                at = 4 * dt * depth1 + 2 * k * depth1
+                w2_ref[dw * depth2 : (dw + 1) * depth2, at : at + 2 * depth1] = wide.T.astype(BF16)
     tap = lax.broadcasted_iota(jnp.int32, (27, 27 * 8), 0)
     place = lax.broadcasted_iota(jnp.int32, (27, 27 * 8), 1)
     for side in range(2):
@@ -151,6 +151,7 @@
                 d1_ref[c], pick, (((0,), (0,)), ((), ())), preferred_element_type=F32
             )
         w1_ref[side * depth1 : (side + 1) * depth1] = total.astype(BF16)
+    store.wait()
 
 
 def finish(ys, feats, rgb, reals):
@@ -240,84 +241,110 @@
             out_ref[:, 2 * k : 2 * k + 2] = ref[pl.ds(start, 2)]
 
 
-def disc_kernel(a_ref, own_ref, b_ref, ta_ref, tb_ref, w1_ref, w2_ref, out_ref, x_ref, f_ref):
+def put_line(x_ref, t, h, line):
+    x = line.astype(F32)
+    width = x.shape[1]
+    col = lax.broadcasted_iota(jnp.int32, x.shape, 1)
+    x_ref[t, h, 0:8] = jnp.where(col == 0, 0.0, pltpu.roll(x, 1, 1))
+    x_ref[t, h, 8:16] = x
+    x_ref[t, h, 16:24] = jnp.where(col == width - 1, 0.0, pltpu.roll(x, width - 1, 1))
+
+
+def band_rows():
+    odd = lax.rem(lax.axis_index("rows"), 2)
+    return [4 * (1 - odd), 4 * (1 - odd) + 1, 2, 3, 4 * odd, 4 * odd + 1]
+
+
+def first_layer(t, frames, x_ref, w1_ref, f_ref, near_ref):
     tm, band = lax.axis_index("tm"), lax.axis_index("rows")
-    tm_count, row_count = lax.axis_size("tm"), lax.axis_size("rows")
-    odd_t, odd_r = lax.rem(tm, 2), lax.rem(band, 2)
-    width = out_ref.shape[-1]
-    frames = out_ref.shape[0]
-    col = lax.broadcasted_iota(jnp.int32, (8, width), 1)
-
-    def put(t, h, line):
-        x = line.astype(F32)
-        x_ref[t, h, 0:8] = jnp.where(col == 0, 0.0, pltpu.roll(x, 1, 1))
-        x_ref[t, h, 8:16] = x
-        x_ref[t, h, 16:24] = jnp.where(col == width - 1, 0.0, pltpu.roll(x, width - 1, 1))
-
-    row_at = [4 * (1 - odd_r), 4 * (1 - odd_r) + 1, 2, 3, 4 * odd_r, 4 * odd_r + 1]
-    a_at = (frames + 2) * (1 - odd_t)
-    b_at = (frames + 2) * odd_t
-    for k in range(6):
-        for t in range(frames):
-            put(t + 2, row_at[k], (a_ref, own_ref, b_ref)[k // 2][t, k % 2])
-        for t in range(2):
-            put(a_at + t, row_at[k], ta_ref[t, k])
-            put(b_at + t, row_at[k], tb_ref[t, k])
-
-    w1 = w1_ref[...]
-    near = {}
-    for t in range(frames + 2):
-        for h in range(0, 4, 2):
-            cols = []
-            for hh in (h, h + 1):
-                cols.append(
-                    jnp.concatenate(
-                        [x_ref[t + dt, hh + dh] for dt in range(3) for dh in range(3)], axis=0
-                    ).astype(BF16)
+    width = x_ref.shape[3]
+    for h in range(0, 4, 2):
+        cols = []
+        for hh in (h, h + 1):
+            cols.append(
+                jnp.concatenate(
+                    [x_ref[t + dt, hh + dh] for dt in range(3) for dh in range(3)], axis=0
+                ).astype(BF16)
+            )
+        first = leaky(
+            jnp.dot(w1_ref[...], jnp.concatenate(cols, axis=1), preferred_element_type=F32)
+        )
+        for i, hh in enumerate((h, h + 1)):
+            part = first[:, i * width : (i + 1) * width]
+            inside = []
+            if t == 0:
+                inside.append(tm > 0)
+            if t == frames + 1:
+                inside.append(tm < lax.axis_size("tm") - 1)
+            if hh == 0:
+                inside.append(band > 0)
+            if hh == 3:
+                inside.append(band < lax.axis_size("rows") - 1)
+            if inside:
+                keep = inside[0] if len(inside) == 1 else jnp.logical_and(*inside)
+                part = jnp.where(keep, part, 0.0)
+            part = part.astype(BF16)
+            f_ref[t, hh] = part
+            if 1 <= t <= frames and 1 <= hh <= 2:
+                wide = part.astype(F32)
+                half = wide.shape[0] // 2
+                at = 2 * (t - 1) + hh - 1
+                near_ref[at : at + 1] = jnp.mean(
+                    jnp.abs(wide[:half] - wide[half:]), axis=0, keepdims=True
                 )
-            first = leaky(jnp.dot(w1, jnp.concatenate(cols, axis=1), preferred_element_type=F32))
-            for i, hh in enumerate((h, h + 1)):
-                part = first[:, i * width : (i + 1) * width]
-                inside = []
-                if t == 0:
-                    inside.append(tm > 0)
-                if t == frames + 1:
-                    inside.append(tm < tm_count - 1)
-                if hh == 0:
-                    inside.append(band > 0)
-                if hh == 3:
-                    inside.append(band < row_count - 1)
-                if inside:
-                    keep = inside[0] if len(inside) == 1 else jnp.logical_and(*inside)
-                    part = jnp.where(keep, part, 0.0)
-                part = part.astype(BF16)
-                f_ref[t, hh] = part
-                if 1 <= t <= frames and 1 <= hh <= 2:
-                    wide = part.astype(F32)
-                    half = wide.shape[0] // 2
-                    near[t - 1, hh - 1] = jnp.mean(
-                        jnp.abs(wide[:half] - wide[half:]), axis=0, keepdims=True
-                    )
-
-    w2 = w2_ref[...]
-    depth2 = w2.shape[0] // 3
-    half = f_ref.shape[2] // 2
-    colw = lax.broadcasted_iota(jnp.int32, (depth2, width), 1)
+
+
+def second_sums(t, h, dts, w2_ref, f_ref):
+    half, width = f_ref.shape[2] // 2, f_ref.shape[3]
+    zeros = jnp.zeros((half, width), BF16)
+    sides = []
+    for s in range(2):
+        rows = []
+        for dt in dts:
+            rows += [f_ref[t + dt, h + dh, s * half : (s + 1) * half] for dh in range(3)] + [zeros]
+        sides.append(jnp.concatenate(rows, axis=0))
+    return jnp.dot(
+        w2_ref[:, 4 * half * dts[0] : 4 * half * (dts[-1] + 1)],
+        jnp.concatenate(sides, axis=1),
+        preferred_element_type=F32,
+    )
+
+
+def inner_dts(t, frames):
+    return [dt for dt in range(3) if 2 <= t + dt <= frames - 1]
+
+
+def inner_kernel(a_ref, own_ref, b_ref, w1_ref, w2_ref, x_ref, f_ref, near_ref, part_ref):
+    frames = own_ref.shape[0]
+    rows = band_rows()
+    for t in range(frames):
+        for k in range(6):
+            put_line(x_ref, t + 2, rows[k], (a_ref, own_ref, b_ref)[k // 2][t, k % 2])
+    for t in range(2, frames):
+        first_layer(t, frames, x_ref, w1_ref, f_ref, near_ref)
     for t in range(frames):
         for h in range(2):
-            sides = []
-            for s in range(2):
-                sides.append(
-                    jnp.concatenate(
-                        [
-                            f_ref[t + dt, h + dh, s * half : (s + 1) * half]
-                            for dt in range(3)
-                            for dh in range(3)
-                        ],
-                        axis=0,
-                    )
-                )
-            y = jnp.dot(w2, jnp.concatenate(sides, axis=1), preferred_element_type=F32)
+            part_ref[2 * t + h] = second_sums(t, h, inner_dts(t, frames), w2_ref, f_ref)
+
+
+def disc_kernel(
+    ta_ref, tb_ref, w1_ref, w2_ref, part_ref, x_in, f_in, near_in, out_ref, x_ref, f_ref, near_ref
+):
+    odd = lax.rem(lax.axis_index("tm"), 2)
+    frames, height, width = out_ref.shape
+    rows = band_rows()
+    for k in range(6):
+        for t in range(2):
+            put_line(x_ref, (frames + 2) * (1 - odd) + t, rows[k], ta_ref[t, k])
+            put_line(x_ref, (frames + 2) * odd + t, rows[k], tb_ref[t, k])
+    for t in (0, 1, frames, frames + 1):
+        first_layer(t, frames, x_ref, w1_ref, f_ref, near_ref)
+    depth2 = w2_ref.shape[0] // 3
+    col = lax.broadcasted_iota(jnp.int32, (depth2, width), 1)
+    for t in range(frames):
+        dts = [dt for dt in range(3) if dt not in inner_dts(t, frames)]
+        for h in range(height):
+            y = part_ref[2 * t + h] + second_sums(t, h, dts, w2_ref, f_ref)
             outs = []
             for s in range(2):
                 y0, y1, y2 = (
@@ -325,12 +352,13 @@
                 )
                 total = (
                     y1
-                    + jnp.where(colw == 0, 0.0, pltpu.roll(y0, 1, 1))
-                    + jnp.where(colw == width - 1, 0.0, pltpu.roll(y2, width - 1, 1))
+                    + jnp.where(col == 0, 0.0, pltpu.roll(y0, 1, 1))
+                    + jnp.where(col == width - 1, 0.0, pltpu.roll(y2, width - 1, 1))
                 )
                 outs.append(leaky(total).astype(BF16).astype(F32))
             far = jnp.mean(jnp.abs(outs[0] - outs[1]), axis=0, keepdims=True)
-            out_ref[t, h : h + 1] = near[t, h] + far
+            at = 2 * t + h
+            out_ref[t, h : h + 1] = near_ref[at : at + 1] + far
 
 
 def per_device(
@@ -402,10 +430,16 @@
             flops=4 * 3 * line,
         )
     decoded, colour = outs
-    w2, w1 = local(
+    w2, w1, stored = local(
         prep_kernel,
-        (kept(3 * depth2, 9 * depth1), kept(2 * depth1, 27 * 8)),
-        (jnp.transpose(disc_second, (0, 2, 1)), jnp.transpose(disc_first, (2, 0, 1))),
+        (
+            kept(3 * depth2, 12 * depth1),
+            kept(2 * depth1, 27 * 8),
+            jax.ShapeDtypeStruct(decoded.shape, BF16),
+        ),
+        (jnp.transpose(disc_second, (0, 2, 1)), jnp.transpose(disc_first, (2, 0, 1)), decoded),
+        stored=(2,),
+        scratch=[pltpu.SemaphoreType.DMA],
     )
 
     side_b = swap(colour, "rows", 1)
@@ -415,16 +449,24 @@
     time_b = swap(for_b, "tm", 1)
     time_a = swap(for_a, "tm", 0)
 
-    match_map = local(
+    inner = local(
+        inner_kernel,
+        (
+            kept(frames + 4, height + 4, 24, width, dtype=F32),
+            kept(frames + 2, height + 2, 2 * depth1, width),
+            kept(frames * height, width, dtype=F32),
+            kept(frames * height, 3 * depth2, 2 * width, dtype=F32),
+        ),
+        (side_a, colour, side_b, w1, w2),
+    )
+    match_map, *_ = local(
         disc_kernel,
-        jax.ShapeDtypeStruct((frames, height, width), F32),
-        (side_a, colour, side_b, time_a, time_b, w1, w2),
-        scratch=[
-            pltpu.VMEM((frames + 4, height + 4, 24, width), F32),
-            pltpu.VMEM((frames + 2, height + 2, 2 * depth1, width), BF16),
-        ],
-    )
-    return (decoded, match_map)
+        (jax.ShapeDtypeStruct((frames, height, width), F32),)
+        + tuple(kept(*x.shape, dtype=x.dtype) for x in inner[:3]),
+        (time_a, time_b, w1, w2, inner[3]) + tuple(inner[:3]),
+        aliases={5: 1, 6: 2, 7: 3},
+    )
+    return (stored, match_map)
 
 
 def solution(mesh):

time: 56.7 us -> 56.7 us (level)
  Pallas kernels: 19.8 us -> 21 us
  local copies, waits for them, and re-layouts: 0.95 us -> 0.07 us
    pallas_call x10 -> x11, Pallas kernels: 19.8 us -> 21 us  [local(): pl.pallas_call(kernel, out_shape=outs, in_specs=[HBM if i in hbm else VME...]
    unnamed x11 -> x10, local copies, waits for them, and re-layouts: 0.91 us -> 0.03 us
  transfers between devices with their start and end apart: 9 -> 9, of which waited for: 3 -> 2; matrix products, arithmetic and copies ran while one was open for 2% -> 0% of each run, Pallas kernels for 26% -> 29%
where the time goes in v8:
time: 56.7 us; the launch traced here: 56.4 us
  starting transfers between devices  30.7 us (54%)
  Pallas kernels  21 us (37%)
  waiting for transfers between devices  3.89 us (7%)
  between operations  0.86 us (2%)
    pallas_call x11, Pallas kernels, local(): pl.pallas_call(kernel, out_shape=outs, in_specs=[HBM if i in hbm else VME...  21 us
    ppermute x6, starting transfers between devices, swap(): return lax.ppermute(block, axis, pairs(lax.axis_size(axis), first))  19.6 us
    ppermute x3, starting transfers between devices, onward(): lax.ppermute(block, axis, [(i, i + 1) for i in range(lax.axis_size(axis)...  11.1 us
    ppermute x6, waiting for transfers between devices, swap(): return lax.ppermute(block, axis, pairs(lax.axis_size(axis), first))  3.89 us
  transfers between devices with their start and end apart: 9, of which 2 were waited for; matrix products, arithmetic and copies ran while one was open for 0% of the time, Pallas kernels for 29%

profile of v8, /device:TPU:17, one launch (start us, length us, event | category | flops | bytes accessed | tf_op | source)
XLA Modules:
  0.0 56.4 jit_solution(11159426041488743716)
XLA Ops:
  0.6 1.7 %shard_map.86 = (bf16[4,128,384]{2,1,0:T(8,128)(2,1)S(1)}, bf16[4,128,384]{2,1,0:T(8,128)(2,1)S(1)}, bf16[2,2,128,384]{3,2,1,0:T(8,128)(2,1)S(1)}) custom-call(bf16[4,2,128,384]{3,2,1,0:T(8,128)(2,1)} %feat_ref.9, f32[384]{0:T(512)} %gain_ref.1), custom_call_target="tpu_custom_call" | custom-call | bytes 1000000 | tf_op jit(solution)/shard_map/pallas_call | solution.py:38
  2.3 1.3 %collective-permute-start.3 = (bf16[4,128,384]{2,1,0:T(8,128)(2,1)S(1)}, bf16[4,128,384]{2,1,0:T(8,128)(2,1)S(1)}, u32[]{:S(2)}, u32[]{:S(2)}) collective-permute-start(bf16[4,128,384]{2,1,0:T(8,128)(2,1)S(1)} %get-tuple-element.28.a_ref), channel_id=1, source_target_pairs={{0,1},{1,0},{2,3},{3,2},{4,5},{5,4},{6,7},{7,6},{8,9},{9,8},{10,11... | collective-permute-start | bytes 1179656 | tf_op jit(solution)/shard_map/ppermute | solution.py:26
  3.6 6.9 %collective-permute-start = (bf16[4,128,384]{2,1,0:T(8,128)(2,1)S(1)}, bf16[4,128,384]{2,1,0:T(8,128)(2,1)S(1)}, u32[]{:S(2)}, u32[]{:S(2)}) collective-permute-start(bf16[4,128,384]{2,1,0:T(8,128)(2,1)S(1)} %get-tuple-element.27.b_ref), channel_id=1, source_target_pairs={{1,2},{2,1},{3,4},{4,3},{5,6},{6,5},{7,8},{8,7},{9,10},{10,9},{11,... | collective-permute-start | bytes 1179656 | tf_op jit(solution)/shard_map/ppermute | solution.py:26
  10.6 3.8 %collective-permute-start.2 = (bf16[2,2,128,384]{3,2,1,0:T(8,128)(2,1)S(1)}, bf16[2,2,128,384]{3,2,1,0:T(8,128)(2,1)S(1)}, u32[]{:S(2)}, u32[]{:S(2)}) collective-permute-start(bf16[2,2,128,384]{3,2,1,0:T(8,128)(2,1)S(1)} %get-tuple-element.29), channel_id=1, source_target_pairs={{0,32},{32,64},{64,96},{1,33},{33,65},{65,97},{2,34},{34,66},{66,9... | collective-permute-start | bytes 1179656 | tf_op jit(solution)/shard_map/ppermute | solution.py:30
  14.3 1.9 %shard_map.87.some_ref = bf16[27,384,384]{2,1,0:T(8,128)(2,1)S(1)} custom-call(bf16[27,384,384]{2,1,0:T(8,128)(2,1)} %weight_ref.3), custom_call_target="tpu_custom_call" | custom-call | bytes 1000000 | tf_op jit(solution)/shard_map/pallas_call | solution.py:38
  16.2 0.0 collective-permute-done.3.line_ref
  16.3 1.9 %collective-permute-start.4 = (bf16[2,128,384]{2,1,0:T(8,128)(2,1)S(1)}, bf16[2,128,384]{2,1,0:T(8,128)(2,1)S(1)}, u32[]{:S(2)}, u32[]{:S(2)}) collective-permute-start(bf16[2,128,384]{2,1,0:T(8,128)(2,1)S(1)} %slice.9), channel_id=1, source_target_pairs={{0,32},{32,64},{64,96},{1,33},{33,65},{65,97},{2,34},{34,66},{66,9... | collective-permute-start | bytes 589832 | tf_op jit(solution)/shard_map/ppermute | solution.py:30
  18.2 1.5 %collective-permute-done.line_ref = bf16[4,128,384]{2,1,0:T(8,128)(2,1)S(1)} collective-permute-done((bf16[4,128,384]{2,1,0:T(8,128)(2,1)S(1)}, bf16[4,128,384]{2,1,0:T(8,128)(2,1)S(1)}, u32[]{:S(2)}, u32[]{:S(2)}) %collective-permute-start) | collective-permute-done | bytes 393248 | tf_op jit(solution)/shard_map/ppermute | solution.py:26
  19.8 0.0 copy-start
  19.8 0.0 copy-start.2
  19.8 0.0 copy-start.3
  19.8 5.4 %collective-permute-start.1 = (bf16[2,128,384]{2,1,0:T(8,128)(2,1)S(1)}, bf16[2,128,384]{2,1,0:T(8,128)(2,1)S(1)}, u32[]{:S(2)}, u32[]{:S(2)}) collective-permute-start(bf16[2,128,384]{2,1,0:T(8,128)(2,1)S(1)} %slice.8), channel_id=1, source_target_pairs={{0,32},{32,64},{64,96},{1,33},{33,65},{65,97},{2,34},{34,66},{66,9... | collective-permute-start | bytes 589832 | tf_op jit(solution)/shard_map/ppermute | solution.py:30
  25.2 0.0 collective-permute-done.2.past_ref
  25.2 7.6 %shard_map.88 = (f32[2,512,1152]{2,1,0:T(8,128)S(1)}, bf16[27,384,384]{2,1,0:T(8,128)(2,1)S(1)}) custom-call(bf16[4,128,384]{2,1,0:T(8,128)(2,1)S(1)} %get-tuple-element.28.a_ref, bf16[4,128,384]{2,1,0:T(8,128)(2,1)S(1)} %get-tuple-element.27.b_ref, bf16[2,2,128,384]{3,2,1,0:T(8,128)(2,1)S(1)} %collective-permute-done.2.past_ref, ...), custom_call_target="tpu_custom_call", output_to_operand_aliasing={{1}: (4, {})} | custom-call | flops 5435817984 | bytes 1000000 | tf_op jit(solution)/shard_map/pallas_call | solution.py:38
  32.8 2.1 %shard_map.89 = (f32[256,1152]{1,0:T(8,128)S(1)}, bf16[4,2,128,384]{3,2,1,0:T(8,128)(2,1)S(1)}, bf16[4,2,8,128]{3,2,1,0:T(8,128)(2,1)S(1)}) custom-call(bf16[4,128,384]{2,1,0:T(8,128)(2,1)S(1)} %collective-permute-done.3.line_ref, bf16[27,384,384]{2,1,0:T(8,128)(2,1)S(1)} %get-tuple-element.30.w_ref, f32[2,512,1152]{2,1,0:T(8,128)S(1)} %get-tuple-element.31.sums_ref, ...), custom_call_target="tpu_custom_call" | custom-call | flops 1358954496 | bytes 1000000 | tf_op jit(solution)/shard_map/pallas_call | solution.py:38
  34.9 2.1 %shard_map.90 = (f32[256,1152]{1,0:T(8,128)S(1)}, bf16[4,2,128,384]{3,2,1,0:T(8,128)(2,1)S(1)}, bf16[4,2,8,128]{3,2,1,0:T(8,128)(2,1)S(1)}) custom-call(bf16[4,128,384]{2,1,0:T(8,128)(2,1)S(1)} %collective-permute-done.line_ref, bf16[27,384,384]{2,1,0:T(8,128)(2,1)S(1)} %get-tuple-element.30.w_ref, ...), custom_call_target="tpu_custom_call", output_to_operand_aliasing={{1}: (6, {}), {2}: (7, {})} | custom-call | flops 1358954496 | bytes 1000000 | tf_op jit(solution)/shard_map/pallas_call | solution.py:38
  37.0 0.0 collective-permute-done.4.past_ref
  37.0 0.9 %shard_map.91 = (bf16[4,2,128,384]{3,2,1,0:T(8,128)(2,1)S(1)}, bf16[4,2,8,128]{3,2,1,0:T(8,128)(2,1)S(1)}) custom-call(bf16[2,128,384]{2,1,0:T(8,128)(2,1)S(1)} %collective-permute-done.4.past_ref, bf16[27,384,384]{2,1,0:T(8,128)(2,1)S(1)} %get-tuple-element.30.w_ref, ...), custom_call_target="tpu_custom_call", output_to_operand_aliasing={{0}: (6, {}), {1}: (7, {})} | custom-call | flops 452984832 | bytes 1000000 | tf_op jit(solution)/shard_map/pallas_call | solution.py:38
  37.8 0.0 collective-permute-done.1.past_ref
  37.8 0.0 copy-start.1
  37.8 0.0 copy-start.4
  37.8 0.8 %shard_map.92 = (bf16[4,2,128,384]{3,2,1,0:T(8,128)(2,1)S(1)}, bf16[4,2,8,128]{3,2,1,0:T(8,128)(2,1)S(1)}) custom-call(bf16[2,128,384]{2,1,0:T(8,128)(2,1)S(1)} %collective-permute-done.1.past_ref, bf16[27,384,384]{2,1,0:T(8,128)(2,1)S(1)} %get-tuple-element.30.w_ref, ...), custom_call_target="tpu_custom_call", output_to_operand_aliasing={{0}: (6, {}), {1}: (7, {})} | custom-call | flops 452984832 | bytes 1000000 | tf_op jit(solution)/shard_map/pallas_call | solution.py:38
  38.7 0.1 collective-permute-start.5
  38.7 6.6 %collective-permute-start.6 = (bf16[4,2,8,128]{3,2,1,0:T(8,128)(2,1)S(1)}, bf16[4,2,8,128]{3,2,1,0:T(8,128)(2,1)S(1)}, u32[]{:S(2)}, u32[]{:S(2)}) collective-permute-start(bf16[4,2,8,128]{3,2,1,0:T(8,128)(2,1)S(1)} %get-tuple-element.42.own_ref), channel_id=1, source_target_pairs={{1,2},{2,1},{3,4},{4,3},{5,6},{6,5},{7,8},{8,7},{9,10},{10,9},{11,... | collective-permute-start | bytes 49160 | tf_op jit(solution)/shard_map/ppermute | solution.py:26
  45.4 0.0 collective-permute-done.5.a_ref
  45.4 2.3 %collective-permute-done.6.b_ref = bf16[4,2,8,128]{3,2,1,0:T(8,128)(2,1)S(1)} collective-permute-done((bf16[4,2,8,128]{3,2,1,0:T(8,128)(2,1)S(1)}, bf16[4,2,8,128]{3,2,1,0:T(8,128)(2,1)S(1)}, u32[]{:S(2)}, u32[]{:S(2)}) %collective-permute-start.6) | collective-permute-done | bytes 16416 | tf_op jit(solution)/shard_map/ppermute | solution.py:26
  47.8 0.0 collective-permute-start.7
  47.8 4.7 %collective-permute-start.8 = (bf16[2,6,8,128]{3,2,1,0:T(8,128)(2,1)S(1)}, bf16[2,6,8,128]{3,2,1,0:T(8,128)(2,1)S(1)}, u32[]{:S(2)}, u32[]{:S(2)}) collective-permute-start(bf16[2,6,8,128]{3,2,1,0:T(8,128)(2,1)S(1)} %get-tuple-element.44), channel_id=1, source_target_pairs={{32,64},{64,32},{33,65},{65,33},{34,66},{66,34},{35,67},{67,35},{3... | collective-permute-start | bytes 73736 | tf_op jit(solution)/shard_map/ppermute | solution.py:26
  52.5 0.9 %shard_map.93 = (bf16[384,768]{1,0:T(8,128)(2,1)S(1)}, bf16[128,216]{1,0:T(8,128)(2,1)S(1)}, bf16[4,2,128,384]{3,2,1,0:T(8,128)(2,1)}) custom-call(bf16[27,64,128]{2,1,0:T(8,128)(2,1)S(1)} %bitcast.3, bf16[3,27,64]{2,1,0:T(8,128)(2,1)S(1)} %bitcast.8, bf16[4,2,128,384]{3,2,1,0:T(8,128)(2,1)S(1)} %get-tuple-element.40.decoded_ref), custom_call_target="tpu_custom_call" | custom-call | bytes 1000000 | tf_op jit(solution)/shard_map/pallas_call | solution.py:38
  53.4 1.1 %shard_map.95 = (f32[8,6,24,128]{3,2,1,0:T(8,128)S(1)}, bf16[6,4,128,128]{3,2,1,0:T(8,128)(2,1)S(1)}, f32[8,128]{1,0:T(8,128)S(1)}, f32[8,384,256]{2,1,0:T(8,128)S(1)}) custom-call(bf16[4,2,8,128]{3,2,1,0:T(8,128)(2,1)S(1)} %collective-permute-done.5.a_ref, bf16[4,2,8,128]{3,2,1,0:T(8,128)(2,1)S(1)} %get-tuple-element.42.own_ref, ...), custom_call_target="tpu_custom_call" | custom-call | bytes 1000000 | tf_op jit(solution)/shard_map/pallas_call | solution.py:38
  54.4 0.0 collective-permute-done.7.ta_ref
  54.5 2.0 %shard_map.96 = (f32[4,2,128]{2,1,0:T(2,128)}, f32[8,6,24,128]{3,2,1,0:T(8,128)S(1)}, bf16[6,4,128,128]{3,2,1,0:T(8,128)(2,1)S(1)}, f32[8,128]{1,0:T(8,128)S(1)}) custom-call(bf16[2,6,8,128]{3,2,1,0:T(8,128)(2,1)S(1)} %collective-permute-done.7.ta_ref, ...), custom_call_target="tpu_custom_call", output_to_operand_aliasing={{1}: (5, {}), {2}: (6, {}), {3}: (7, {})} | custom-call | bytes 1000000 | tf_op jit(solution)/shard_map/pallas_call | solution.py:38
  (9 shorter events, 0.1 us)
Async XLA Ops:
  2.3 13.9 %collective-permute-start.3 = (bf16[4,128,384]{2,1,0:T(8,128)(2,1)S(1)}, bf16[4,128,384]{2,1,0:T(8,128)(2,1)S(1)}, u32[]{:S(2)}, u32[]{:S(2)}) collective-permute-start(bf16[4,128,384]{2,1,0:T(8,128)(2,1)S(1)} %get-tuple-element.28.a_ref), channel_id=1, source_target_pairs={{0,1},{1,0},{2,3},{3,2},{4,5},{5,4},{6,7},{7,6},{8,9},{9,8},{10,11... | collective-permute-start | bytes 1179656 | tf_op jit(solution)/shard_map/ppermute | solution.py:26
  3.6 16.1 %collective-permute-start = (bf16[4,128,384]{2,1,0:T(8,128)(2,1)S(1)}, bf16[4,128,384]{2,1,0:T(8,128)(2,1)S(1)}, u32[]{:S(2)}, u32[]{:S(2)}) collective-permute-start(bf16[4,128,384]{2,1,0:T(8,128)(2,1)S(1)} %get-tuple-element.27.b_ref), channel_id=1, source_target_pairs={{1,2},{2,1},{3,4},{4,3},{5,6},{6,5},{7,8},{8,7},{9,10},{10,9},{11,... | collective-permute-start | bytes 1179656 | tf_op jit(solution)/shard_map/ppermute | solution.py:26
  10.6 14.6 %collective-permute-start.2 = (bf16[2,2,128,384]{3,2,1,0:T(8,128)(2,1)S(1)}, bf16[2,2,128,384]{3,2,1,0:T(8,128)(2,1)S(1)}, u32[]{:S(2)}, u32[]{:S(2)}) collective-permute-start(bf16[2,2,128,384]{3,2,1,0:T(8,128)(2,1)S(1)} %get-tuple-element.29), channel_id=1, source_target_pairs={{0,32},{32,64},{64,96},{1,33},{33,65},{65,97},{2,34},{34,66},{66,9... | collective-permute-start | bytes 1179656 | tf_op jit(solution)/shard_map/ppermute | solution.py:30
  16.3 20.7 %collective-permute-start.4 = (bf16[2,128,384]{2,1,0:T(8,128)(2,1)S(1)}, bf16[2,128,384]{2,1,0:T(8,128)(2,1)S(1)}, u32[]{:S(2)}, u32[]{:S(2)}) collective-permute-start(bf16[2,128,384]{2,1,0:T(8,128)(2,1)S(1)} %slice.9), channel_id=1, source_target_pairs={{0,32},{32,64},{64,96},{1,33},{33,65},{65,97},{2,34},{34,66},{66,9... | collective-permute-start | bytes 589832 | tf_op jit(solution)/shard_map/ppermute | solution.py:30
  19.8 13.0 %copy-start = (bf16[4,2,128,384]{3,2,1,0:T(8,128)(2,1)S(1)}, bf16[4,2,128,384]{3,2,1,0:T(8,128)(2,1)}, u32[]{:S(2)}) copy-start(bf16[4,2,128,384]{3,2,1,0:T(8,128)(2,1)} %feat_ref.9) | copy-start | bytes 2359300
  19.8 13.0 %copy-start.2 = (bf16[3,4,2,128]{3,2,1,0:T(2,128)(2,1)S(1)}, bf16[3,4,2,128]{3,2,1,0:T(2,128)(2,1)}, u32[]{:S(2)}) copy-start(bf16[3,4,2,128]{3,2,1,0:T(2,128)(2,1)} %real_ref.7) | copy-start | bytes 18436
  19.8 13.0 %copy-start.3 = (bf16[384,3]{0,1:T(4,128)(2,1)S(1)}, bf16[384,3]{0,1:T(4,128)(2,1)}, u32[]{:S(2)}) copy-start(bf16[384,3]{0,1:T(4,128)(2,1)} %param.10) | copy-start | bytes 6916
  19.8 18.0 %collective-permute-start.1 = (bf16[2,128,384]{2,1,0:T(8,128)(2,1)S(1)}, bf16[2,128,384]{2,1,0:T(8,128)(2,1)S(1)}, u32[]{:S(2)}, u32[]{:S(2)}) collective-permute-start(bf16[2,128,384]{2,1,0:T(8,128)(2,1)S(1)} %slice.8), channel_id=1, source_target_pairs={{0,32},{32,64},{64,96},{1,33},{33,65},{65,97},{2,34},{34,66},{66,9... | collective-permute-start | bytes 589832 | tf_op jit(solution)/shard_map/ppermute | solution.py:30
  37.8 14.6 %copy-start.1 = (bf16[27,128,64]{1,2,0:T(8,128)(2,1)S(1)}, bf16[27,128,64]{1,2,0:T(8,128)(2,1)}, u32[]{:S(2)}) copy-start(bf16[27,128,64]{1,2,0:T(8,128)(2,1)} %param.13) | copy-start | bytes 1327108
  37.8 14.6 %copy-start.4 = (bf16[27,64,3]{1,0,2:T(8,128)(2,1)S(1)}, bf16[27,64,3]{1,0,2:T(8,128)(2,1)}, u32[]{:S(2)}) copy-start(bf16[27,64,3]{1,0,2:T(8,128)(2,1)} %param.12) | copy-start | bytes 31108
  38.7 6.7 %collective-permute-start.5 = (bf16[4,2,8,128]{3,2,1,0:T(8,128)(2,1)S(1)}, bf16[4,2,8,128]{3,2,1,0:T(8,128)(2,1)S(1)}, u32[]{:S(2)}, u32[]{:S(2)}) collective-permute-start(bf16[4,2,8,128]{3,2,1,0:T(8,128)(2,1)S(1)} %get-tuple-element.42.own_ref), channel_id=1, source_target_pairs={{0,1},{1,0},{2,3},{3,2},{4,5},{5,4},{6,7},{7,6},{8,9},{9,8},{10,11... | collective-permute-start | bytes 49160 | tf_op jit(solution)/shard_map/ppermute | solution.py:26
  38.7 9.0 %collective-permute-start.6 = (bf16[4,2,8,128]{3,2,1,0:T(8,128)(2,1)S(1)}, bf16[4,2,8,128]{3,2,1,0:T(8,128)(2,1)S(1)}, u32[]{:S(2)}, u32[]{:S(2)}) collective-permute-start(bf16[4,2,8,128]{3,2,1,0:T(8,128)(2,1)S(1)} %get-tuple-element.42.own_ref), channel_id=1, source_target_pairs={{1,2},{2,1},{3,4},{4,3},{5,6},{6,5},{7,8},{8,7},{9,10},{10,9},{11,... | collective-permute-start | bytes 49160 | tf_op jit(solution)/shard_map/ppermute | solution.py:26
  47.8 6.7 %collective-permute-start.7 = (bf16[2,6,8,128]{3,2,1,0:T(8,128)(2,1)S(1)}, bf16[2,6,8,128]{3,2,1,0:T(8,128)(2,1)S(1)}, u32[]{:S(2)}, u32[]{:S(2)}) collective-permute-start(bf16[2,6,8,128]{3,2,1,0:T(8,128)(2,1)S(1)} %get-tuple-element.43), channel_id=1, source_target_pairs={{0,32},{32,0},{64,96},{96,64},{1,33},{33,1},{65,97},{97,65},{2,34}... | collective-permute-start | bytes 73736 | tf_op jit(solution)/shard_map/ppermute | solution.py:26
  47.8 6.7 %collective-permute-start.8 = (bf16[2,6,8,128]{3,2,1,0:T(8,128)(2,1)S(1)}, bf16[2,6,8,128]{3,2,1,0:T(8,128)(2,1)S(1)}, u32[]{:S(2)}, u32[]{:S(2)}) collective-permute-start(bf16[2,6,8,128]{3,2,1,0:T(8,128)(2,1)S(1)} %get-tuple-element.44), channel_id=1, source_target_pairs={{32,64},{64,32},{33,65},{65,33},{34,66},{66,34},{35,67},{67,35},{3... | collective-permute-start | bytes 73736 | tf_op jit(solution)/shard_map/ppermute | solution.py:26

commit v9 on v8

--- a/solution.py
+++ b/solution.py
@@ -88,38 +88,19 @@
     return jnp.concatenate([w_ref[9 * dt + 3 * dh + dw, :, off : off + 128] for dt, dh in taps], axis=0)
 
 
-def start_taps(weight_ref, w_ref, sems, dw):
-    for tap in range(dw, 27, 3):
-        pltpu.make_async_copy(weight_ref.at[tap], w_ref.at[tap], sems.at[tap]).start()
-
-
-def wait_taps(weight_ref, w_ref, sems, dw):
-    for tap in range(dw, 27, 3):
-        pltpu.make_async_copy(weight_ref.at[tap], w_ref.at[tap], sems.at[tap]).wait()
-
-
-def fetch_kernel(weight_ref, w_ref, sems):
-    start_taps(weight_ref, w_ref, sems, 0)
-    wait_taps(weight_ref, w_ref, sems, 0)
-
-
-def own_kernel(a_ref, b_ref, past_ref, weight_ref, some_ref, y_ref, w_ref, lines_ref, sems):
+def own_kernel(lines_ref, past_ref, w_ref, y_ref):
     odd = lax.rem(lax.axis_index("rows"), 2)
-    frames, width, chans = a_ref.shape
-    start_taps(weight_ref, w_ref, sems, 1)
-    for k, (row, line_ref) in enumerate(((1 - odd, a_ref), (odd, b_ref))):
-        lines_ref[row, pl.ds(0, 2)] = past_ref[k]
-        lines_ref[row, pl.ds(2, frames)] = line_ref[...]
+    frames, _, chans = lines_ref.shape[1:]
+    past = [past_ref[lax.rem(1 + i + odd, 2)] for i in range(2)]
     inputs = [(dt, i) for dt in range(3) for i in range(2)]
-    lhs = jnp.concatenate(
-        [lines_ref[i, dt : dt + frames].reshape(frames * width, chans) for dt, i in inputs], axis=1
-    )
+    parts = []
+    for dt, i in inputs:
+        part = [past[i][dt:].reshape(-1, chans)] if dt < 2 else []
+        part.append(lines_ref[i, : frames - 2 + dt].reshape(-1, chans))
+        parts.append(jnp.concatenate(part, axis=0))
+    lhs = jnp.concatenate(parts, axis=1)
+    blocks = [(o, off) for o in range(2) for off in range(0, chans, 128)]
     for dw in range(3):
-        if dw:
-            wait_taps(weight_ref, w_ref, sems, dw)
-        if dw == 1:
-            start_taps(weight_ref, w_ref, sems, 2)
-        blocks = [(o, off) for o in range(2) for off in range(0, chans, 128)]
         for j in range(0, len(blocks), 2):
             pair = blocks[j : j + 2]
             rhs = [rhs_block(w_ref, dw, off, [(dt, i - o + 1) for dt, i in inputs]) for o, off in pair]
@@ -129,9 +110,16 @@
                 y_ref[o, :, at : at + 128] = got[:, k * 128 : (k + 1) * 128]
 
 
-def prep_kernel(d2_ref, d1_ref, decoded_ref, w2_ref, w1_ref, out_ref, sem):
+def store_kernel(decoded_ref, out_ref, sem):
     store = pltpu.make_async_copy(decoded_ref, out_ref, sem)
     store.start()
+    store.wait()
+
+
+def prep_kernel(a_ref, b_ref, d2_ref, d1_ref, lines_ref, w2_ref, w1_ref):
+    odd = lax.rem(lax.axis_index("rows"), 2)
+    lines_ref[1 - odd] = a_ref[...]
+    lines_ref[odd] = b_ref[...]
     depth1, depth2 = d2_ref.shape[1:]
     for dt in range(3):
         for dw in range(3):
@@ -151,7 +139,6 @@
                 d1_ref[c], pick, (((0,), (0,)), ((), ())), preferred_element_type=F32
             )
         w1_ref[side * depth1 : (side + 1) * depth1] = total.astype(BF16)
-    store.wait()
 
 
 def finish(ys, feats, rgb, reals):
@@ -384,23 +371,20 @@
     from_a = swap(to_a, "rows", 0)
 
     line = 2 * width * chans * chans
-    first_taps = local(
-        fetch_kernel,
-        kept(*conv_weight.shape),
-        (conv_weight,),
-        hbm=(0,),
-        scratch=[pltpu.SemaphoreType.DMA((27,))],
-    )
-    sums, weight = local(
+    lines, w2, w1 = local(
+        prep_kernel,
+        (
+            kept(height, frames, width, chans),
+            kept(3 * depth2, 12 * depth1),
+            kept(2 * depth1, 27 * 8),
+        ),
+        (to_a, to_b, jnp.transpose(disc_second, (0, 2, 1)), jnp.transpose(disc_first, (2, 0, 1))),
+        flops=40 * 3 * line,
+    )
+    sums = local(
         own_kernel,
-        (kept(height, cells, 3 * chans, dtype=F32), kept(*conv_weight.shape)),
-        (to_a, to_b, past, conv_weight, first_taps),
-        hbm=(3,),
-        scratch=[
-            pltpu.VMEM((2, frames + 2, width, chans), BF16),
-            pltpu.SemaphoreType.DMA((27,)),
-        ],
-        aliases={4: 1},
+        kept(height, cells, 3 * chans, dtype=F32),
+        (lines, past, conv_weight),
         flops=48 * 3 * line,
     )
     corner_a = onward(from_a[frames - 2 :], "tm")
@@ -414,7 +398,7 @@
         y, *outs = local(
             functools.partial(near_kernel, side),
             (early,) + shown,
-            (row, weight, sums) + rest + tuple(outs),
+            (row, conv_weight, sums) + rest + tuple(outs),
             scratch=[pltpu.VMEM((cells, 3 * chans), F32)],
             aliases={6: 1, 7: 2} if side else {},
             flops=12 * 3 * line,
@@ -424,21 +408,17 @@
         outs = local(
             functools.partial(corner_kernel, side),
             shown,
-            (row, weight, ends[side]) + rest + tuple(outs),
+            (row, conv_weight, ends[side]) + rest + tuple(outs),
             scratch=[pltpu.VMEM((2 * width, 3 * chans), F32)],
             aliases={6: 0, 7: 1},
             flops=4 * 3 * line,
         )
     decoded, colour = outs
-    w2, w1, stored = local(
-        prep_kernel,
-        (
-            kept(3 * depth2, 12 * depth1),
-            kept(2 * depth1, 27 * 8),
-            jax.ShapeDtypeStruct(decoded.shape, BF16),
-        ),
-        (jnp.transpose(disc_second, (0, 2, 1)), jnp.transpose(disc_first, (2, 0, 1)), decoded),
-        stored=(2,),
+    stored, = local(
+        store_kernel,
+        (jax.ShapeDtypeStruct(decoded.shape, BF16),),
+        (decoded,),
+        stored=(0,),
         scratch=[pltpu.SemaphoreType.DMA],
     )
 

time: 56.7 us -> 58.5 us (1.032)
  waiting for transfers between devices: 3.89 us -> 10.7 us
  starting transfers between devices: 30.7 us -> 26.8 us
  Pallas kernels: 21 us -> 17.7 us
  local copies, waits for them, and re-layouts: 0.07 us -> 1.82 us
    ppermute x6, waiting for transfers between devices: 3.89 us -> 10.7 us  [swap(): return lax.ppermute(block, axis, pairs(lax.axis_size(axis), first))]
    pallas_call x11, Pallas kernels: 21 us -> 17.7 us  [local(): pl.pallas_call(kernel, out_shape=outs, in_specs=[HBM if i in hbm else VME...]
    ppermute x3, starting transfers between devices: 11.1 us -> 8.44 us  [onward(): lax.ppermute(block, axis, [(i, i + 1) for i in range(lax.axis_size(axis)...]
    unnamed x10 -> x14, local copies, waits for them, and re-layouts: 0.03 us -> 1.78 us
    ppermute x6, starting transfers between devices: 19.6 us -> 18.3 us  [swap(): return lax.ppermute(block, axis, pairs(lax.axis_size(axis), first))]
  transfers between devices with their start and end apart: 9 -> 9, of which waited for: 2 -> 4; matrix products, arithmetic and copies ran while one was open for 0% -> 0% of each run, Pallas kernels for 29% -> 23%
where the time goes in v9:
time: 58.5 us; the launch traced here: 57.8 us
  starting transfers between devices  26.8 us (46%)
  Pallas kernels  17.7 us (30%)
  waiting for transfers between devices  10.7 us (18%)
  local copies, waits for them, and re-layouts  1.82 us (3%)
  between operations  0.85 us (1%)
    ppermute x6, starting transfers between devices, swap(): return lax.ppermute(block, axis, pairs(lax.axis_size(axis), first))  18.3 us
    pallas_call x11, Pallas kernels, local(): pl.pallas_call(kernel, out_shape=outs, in_specs=[HBM if i in hbm else VME...  17.7 us
    ppermute x6, waiting for transfers between devices, swap(): return lax.ppermute(block, axis, pairs(lax.axis_size(axis), first))  10.7 us
    ppermute x3, starting transfers between devices, onward(): lax.ppermute(block, axis, [(i, i + 1) for i in range(lax.axis_size(axis)...  8.44 us
    unnamed x14, local copies, waits for them, and re-layouts  1.78 us
  transfers between devices with their start and end apart: 9, of which 4 were waited for; matrix products, arithmetic and copies ran while one was open for 0% of the time, Pallas kernels for 23%

profile of v9, /device:TPU:17, one launch (start us, length us, event | category | flops | bytes accessed | tf_op | source)
XLA Modules:
  0.0 57.8 jit_solution(8822272369025084639)
XLA Ops:
  0.6 0.0 slice-start
  0.6 1.9 %shard_map.86 = (bf16[4,128,384]{2,1,0:T(8,128)(2,1)S(1)}, bf16[4,128,384]{2,1,0:T(8,128)(2,1)S(1)}, bf16[2,2,128,384]{3,2,1,0:T(8,128)(2,1)S(1)}) custom-call(bf16[4,2,128,384]{3,2,1,0:T(8,128)(2,1)} %feat_ref.9, f32[384]{0:T(512)} %gain_ref.1), custom_call_target="tpu_custom_call" | custom-call | bytes 1000000 | tf_op jit(solution)/shard_map/pallas_call | solution.py:38
  2.5 4.1 %collective-permute-start.2 = (bf16[2,2,128,384]{3,2,1,0:T(8,128)(2,1)S(1)}, bf16[2,2,128,384]{3,2,1,0:T(8,128)(2,1)S(1)}, u32[]{:S(2)}, u32[]{:S(2)}) collective-permute-start(bf16[2,2,128,384]{3,2,1,0:T(8,128)(2,1)S(1)} %get-tuple-element.28), channel_id=1, source_target_pairs={{0,32},{32,64},{64,96},{1,33},{33,65},{65,97},{2,34},{34,66},{66,9... | collective-permute-start | bytes 1179656 | tf_op jit(solution)/shard_map/ppermute | solution.py:30
  6.6 7.3 %collective-permute-start = (bf16[4,128,384]{2,1,0:T(8,128)(2,1)S(1)}, bf16[4,128,384]{2,1,0:T(8,128)(2,1)S(1)}, u32[]{:S(2)}, u32[]{:S(2)}) collective-permute-start(bf16[4,128,384]{2,1,0:T(8,128)(2,1)S(1)} %get-tuple-element.25.b_ref), channel_id=1, source_target_pairs={{1,2},{2,1},{3,4},{4,3},{5,6},{6,5},{7,8},{8,7},{9,10},{10,9},{11,... | collective-permute-start | bytes 1179656 | tf_op jit(solution)/shard_map/ppermute | solution.py:26
  13.9 0.1 collective-permute-start.3
  14.0 0.0 copy-start.3
  14.0 1.0 %copy-done.3 = bf16[27,128,64]{1,2,0:T(8,128)(2,1)S(1)} copy-done((bf16[27,128,64]{1,2,0:T(8,128)(2,1)S(1)}, bf16[27,128,64]{1,2,0:T(8,128)(2,1)}, u32[]{:S(2)}) %copy-start.3) | copy-done | bytes 442392
  15.0 0.7 %copy-done.4 = bf16[27,64,3]{1,0,2:T(8,128)(2,1)S(1)} copy-done((bf16[27,64,3]{1,0,2:T(8,128)(2,1)S(1)}, bf16[27,64,3]{1,0,2:T(8,128)(2,1)}, u32[]{:S(2)}) %copy-start.4) | copy-done | bytes 10392
  15.8 0.4 shard_map.87
  16.2 6.6 %collective-permute-done.line_ref = bf16[4,128,384]{2,1,0:T(8,128)(2,1)S(1)} collective-permute-done((bf16[4,128,384]{2,1,0:T(8,128)(2,1)S(1)}, bf16[4,128,384]{2,1,0:T(8,128)(2,1)S(1)}, u32[]{:S(2)}, u32[]{:S(2)}) %collective-permute-start) | collective-permute-done | bytes 393248 | tf_op jit(solution)/shard_map/ppermute | solution.py:26
  22.8 2.4 %collective-permute-start.1 = (bf16[2,128,384]{2,1,0:T(8,128)(2,1)S(1)}, bf16[2,128,384]{2,1,0:T(8,128)(2,1)S(1)}, u32[]{:S(2)}, u32[]{:S(2)}) collective-permute-start(bf16[2,128,384]{2,1,0:T(8,128)(2,1)S(1)} %slice.8), channel_id=1, source_target_pairs={{0,32},{32,64},{64,96},{1,33},{33,65},{65,97},{2,34},{34,66},{66,9... | collective-permute-start | bytes 589832 | tf_op jit(solution)/shard_map/ppermute | solution.py:30
  25.2 0.0 collective-permute-done.3.line_ref
  25.2 1.9 %collective-permute-start.4 = (bf16[2,128,384]{2,1,0:T(8,128)(2,1)S(1)}, bf16[2,128,384]{2,1,0:T(8,128)(2,1)S(1)}, u32[]{:S(2)}, u32[]{:S(2)}) collective-permute-start(bf16[2,128,384]{2,1,0:T(8,128)(2,1)S(1)} %slice.9), channel_id=1, source_target_pairs={{0,32},{32,64},{64,96},{1,33},{33,65},{65,97},{2,34},{34,66},{66,9... | collective-permute-start | bytes 589832 | tf_op jit(solution)/shard_map/ppermute | solution.py:30
  27.2 0.0 collective-permute-done.2.past_ref
  27.2 0.0 copy-start
  27.2 0.0 copy-start.1
  27.2 0.0 copy-start.2
  27.2 5.6 %shard_map.88.sums_ref = f32[2,512,1152]{2,1,0:T(8,128)S(1)} custom-call(bf16[2,4,128,384]{3,2,1,0:T(8,128)(2,1)S(1)} %get-tuple-element.27.lines_ref, bf16[2,2,128,384]{3,2,1,0:T(8,128)(2,1)S(1)} %collective-permute-done.2.past_ref, bf16[27,384,384]{2,1,0:T(8,128)(2,1)S(1)} %bitcast.4), custom_call_target="tpu_custom_call" | custom-call | flops 5435817984 | bytes 1000000 | tf_op jit(solution)/shard_map/pallas_call | solution.py:38
  32.9 2.1 %shard_map.89 = (f32[256,1152]{1,0:T(8,128)S(1)}, bf16[4,2,128,384]{3,2,1,0:T(8,128)(2,1)S(1)}, bf16[4,2,8,128]{3,2,1,0:T(8,128)(2,1)S(1)}) custom-call(bf16[4,128,384]{2,1,0:T(8,128)(2,1)S(1)} %collective-permute-done.3.line_ref, bf16[27,384,384]{2,1,0:T(8,128)(2,1)S(1)} %bitcast.4, f32[2,512,1152]{2,1,0:T(8,128)S(1)} %shard_map.88.sums_ref, ...), custom_call_target="tpu_custom_call" | custom-call | flops 1358954496 | bytes 1000000 | tf_op jit(solution)/shard_map/pallas_call | solution.py:38
  35.0 2.1 %shard_map.90 = (f32[256,1152]{1,0:T(8,128)S(1)}, bf16[4,2,128,384]{3,2,1,0:T(8,128)(2,1)S(1)}, bf16[4,2,8,128]{3,2,1,0:T(8,128)(2,1)S(1)}) custom-call(bf16[4,128,384]{2,1,0:T(8,128)(2,1)S(1)} %collective-permute-done.line_ref, bf16[27,384,384]{2,1,0:T(8,128)(2,1)S(1)} %bitcast.4, ...), custom_call_target="tpu_custom_call", output_to_operand_aliasing={{1}: (6, {}), {2}: (7, {})} | custom-call | flops 1358954496 | bytes 1000000 | tf_op jit(solution)/shard_map/pallas_call | solution.py:38
  37.1 0.9 %shard_map.91 = (bf16[4,2,128,384]{3,2,1,0:T(8,128)(2,1)S(1)}, bf16[4,2,8,128]{3,2,1,0:T(8,128)(2,1)S(1)}) custom-call(bf16[2,128,384]{2,1,0:T(8,128)(2,1)S(1)} %collective-permute-done.4.past_ref, bf16[27,384,384]{2,1,0:T(8,128)(2,1)S(1)} %bitcast.4, f32[256,1152]{1,0:T(8,128)S(1)} %get-tuple-element.32.sums_ref, ...), custom_call_target="tpu_custom_call", output_to_operand_aliasing={{0}: (6, {}), {1}: (7, {})} | custom-call | flops 452984832 | bytes 1000000 | tf_op jit(solution)/shard_map/pallas_call | solution.py:38
  38.0 0.8 %shard_map.92 = (bf16[4,2,128,384]{3,2,1,0:T(8,128)(2,1)S(1)}, bf16[4,2,8,128]{3,2,1,0:T(8,128)(2,1)S(1)}) custom-call(bf16[2,128,384]{2,1,0:T(8,128)(2,1)S(1)} %collective-permute-done.1.past_ref, bf16[27,384,384]{2,1,0:T(8,128)(2,1)S(1)} %bitcast.4, f32[256,1152]{1,0:T(8,128)S(1)} %get-tuple-element.31.sums_ref, ...), custom_call_target="tpu_custom_call", output_to_operand_aliasing={{0}: (6, {}), {1}: (7, {})} | custom-call | flops 452984832 | bytes 1000000 | tf_op jit(solution)/shard_map/pallas_call | solution.py:38
  38.8 7.3 %collective-permute-start.6 = (bf16[4,2,8,128]{3,2,1,0:T(8,128)(2,1)S(1)}, bf16[4,2,8,128]{3,2,1,0:T(8,128)(2,1)S(1)}, u32[]{:S(2)}, u32[]{:S(2)}) collective-permute-start(bf16[4,2,8,128]{3,2,1,0:T(8,128)(2,1)S(1)} %get-tuple-element.38.own_ref), channel_id=1, source_target_pairs={{1,2},{2,1},{3,4},{4,3},{5,6},{6,5},{7,8},{8,7},{9,10},{10,9},{11,... | collective-permute-start | bytes 49160 | tf_op jit(solution)/shard_map/ppermute | solution.py:26
  46.1 0.1 collective-permute-start.5
  46.2 1.6 %collective-permute-done.6.b_ref = bf16[4,2,8,128]{3,2,1,0:T(8,128)(2,1)S(1)} collective-permute-done((bf16[4,2,8,128]{3,2,1,0:T(8,128)(2,1)S(1)}, bf16[4,2,8,128]{3,2,1,0:T(8,128)(2,1)S(1)}, u32[]{:S(2)}, u32[]{:S(2)}) %collective-permute-start.6) | collective-permute-done | bytes 16416 | tf_op jit(solution)/shard_map/ppermute | solution.py:26
  47.8 1.3 %collective-permute-done.5.a_ref = bf16[4,2,8,128]{3,2,1,0:T(8,128)(2,1)S(1)} collective-permute-done((bf16[4,2,8,128]{3,2,1,0:T(8,128)(2,1)S(1)}, bf16[4,2,8,128]{3,2,1,0:T(8,128)(2,1)S(1)}, u32[]{:S(2)}, u32[]{:S(2)}) %collective-permute-start.5) | collective-permute-done | bytes 16416 | tf_op jit(solution)/shard_map/ppermute | solution.py:26
  49.1 1.6 %collective-permute-start.7 = (bf16[2,6,8,128]{3,2,1,0:T(8,128)(2,1)S(1)}, bf16[2,6,8,128]{3,2,1,0:T(8,128)(2,1)S(1)}, u32[]{:S(2)}, u32[]{:S(2)}) collective-permute-start(bf16[2,6,8,128]{3,2,1,0:T(8,128)(2,1)S(1)} %get-tuple-element.39), channel_id=1, source_target_pairs={{0,32},{32,0},{64,96},{96,64},{1,33},{33,1},{65,97},{97,65},{2,34}... | collective-permute-start | bytes 73736 | tf_op jit(solution)/shard_map/ppermute | solution.py:26
  50.7 1.9 %collective-permute-start.8 = (bf16[2,6,8,128]{3,2,1,0:T(8,128)(2,1)S(1)}, bf16[2,6,8,128]{3,2,1,0:T(8,128)(2,1)S(1)}, u32[]{:S(2)}, u32[]{:S(2)}) collective-permute-start(bf16[2,6,8,128]{3,2,1,0:T(8,128)(2,1)S(1)} %get-tuple-element.40), channel_id=1, source_target_pairs={{32,64},{64,32},{33,65},{65,33},{34,66},{66,34},{35,67},{67,35},{3... | collective-permute-start | bytes 73736 | tf_op jit(solution)/shard_map/ppermute | solution.py:26
  52.6 0.9 %shard_map.93 = bf16[4,2,128,384]{3,2,1,0:T(8,128)(2,1)} custom-call(bf16[4,2,128,384]{3,2,1,0:T(8,128)(2,1)S(1)} %get-tuple-element.37.decoded_ref), custom_call_target="tpu_custom_call" | custom-call | bytes 1000000 | tf_op jit(solution)/shard_map/pallas_call | solution.py:38
  53.5 1.1 %shard_map.95 = (f32[8,6,24,128]{3,2,1,0:T(8,128)S(1)}, bf16[6,4,128,128]{3,2,1,0:T(8,128)(2,1)S(1)}, f32[8,128]{1,0:T(8,128)S(1)}, f32[8,384,256]{2,1,0:T(8,128)S(1)}) custom-call(bf16[4,2,8,128]{3,2,1,0:T(8,128)(2,1)S(1)} %collective-permute-done.5.a_ref, bf16[4,2,8,128]{3,2,1,0:T(8,128)(2,1)S(1)} %get-tuple-element.38.own_ref, ...), custom_call_target="tpu_custom_call" | custom-call | bytes 1000000 | tf_op jit(solution)/shard_map/pallas_call | solution.py:38
  54.6 1.2 %collective-permute-done.8.tb_ref = bf16[2,6,8,128]{3,2,1,0:T(8,128)(2,1)S(1)} collective-permute-done((bf16[2,6,8,128]{3,2,1,0:T(8,128)(2,1)S(1)}, bf16[2,6,8,128]{3,2,1,0:T(8,128)(2,1)S(1)}, u32[]{:S(2)}, u32[]{:S(2)}) %collective-permute-start.8) | collective-permute-done | bytes 24608 | tf_op jit(solution)/shard_map/ppermute | solution.py:26
  55.8 2.0 %shard_map.96 = (f32[4,2,128]{2,1,0:T(2,128)}, f32[8,6,24,128]{3,2,1,0:T(8,128)S(1)}, bf16[6,4,128,128]{3,2,1,0:T(8,128)(2,1)S(1)}, f32[8,128]{1,0:T(8,128)S(1)}) custom-call(bf16[2,6,8,128]{3,2,1,0:T(8,128)(2,1)S(1)} %collective-permute-done.7.ta_ref, ...), custom_call_target="tpu_custom_call", output_to_operand_aliasing={{1}: (5, {}), {2}: (6, {}), {3}: (7, {})} | custom-call | bytes 1000000 | tf_op jit(solution)/shard_map/pallas_call | solution.py:38
  (14 shorter events, 0.1 us)
Async XLA Ops:
  0.6 26.6 %slice-start = ((s8[7962624]{0:T(1024)(128)(4,1)}), s8[4194304]{0:T(1024)(128)(4,1)S(1)}, s32[]{:S(2)}) async-start(s8[7962624]{0:T(1024)(128)(4,1)} %bitcast.3), calls=%async_computation | async-start | bytes 8388608
  2.5 24.7 %collective-permute-start.2 = (bf16[2,2,128,384]{3,2,1,0:T(8,128)(2,1)S(1)}, bf16[2,2,128,384]{3,2,1,0:T(8,128)(2,1)S(1)}, u32[]{:S(2)}, u32[]{:S(2)}) collective-permute-start(bf16[2,2,128,384]{3,2,1,0:T(8,128)(2,1)S(1)} %get-tuple-element.28), channel_id=1, source_target_pairs={{0,32},{32,64},{64,96},{1,33},{33,65},{65,97},{2,34},{34,66},{66,9... | collective-permute-start | bytes 1179656 | tf_op jit(solution)/shard_map/ppermute | solution.py:30
  6.6 16.1 %collective-permute-start = (bf16[4,128,384]{2,1,0:T(8,128)(2,1)S(1)}, bf16[4,128,384]{2,1,0:T(8,128)(2,1)S(1)}, u32[]{:S(2)}, u32[]{:S(2)}) collective-permute-start(bf16[4,128,384]{2,1,0:T(8,128)(2,1)S(1)} %get-tuple-element.25.b_ref), channel_id=1, source_target_pairs={{1,2},{2,1},{3,4},{4,3},{5,6},{6,5},{7,8},{8,7},{9,10},{10,9},{11,... | collective-permute-start | bytes 1179656 | tf_op jit(solution)/shard_map/ppermute | solution.py:26
  13.9 11.3 %collective-permute-start.3 = (bf16[4,128,384]{2,1,0:T(8,128)(2,1)S(1)}, bf16[4,128,384]{2,1,0:T(8,128)(2,1)S(1)}, u32[]{:S(2)}, u32[]{:S(2)}) collective-permute-start(bf16[4,128,384]{2,1,0:T(8,128)(2,1)S(1)} %get-tuple-element.26.a_ref), channel_id=1, source_target_pairs={{0,1},{1,0},{2,3},{3,2},{4,5},{5,4},{6,7},{7,6},{8,9},{9,8},{10,11... | collective-permute-start | bytes 1179656 | tf_op jit(solution)/shard_map/ppermute | solution.py:26
  14.0 1.0 %copy-start.3 = (bf16[27,128,64]{1,2,0:T(8,128)(2,1)S(1)}, bf16[27,128,64]{1,2,0:T(8,128)(2,1)}, u32[]{:S(2)}) copy-start(bf16[27,128,64]{1,2,0:T(8,128)(2,1)} %param.13) | copy-start | bytes 1327108
  15.0 0.7 %copy-start.4 = (bf16[27,64,3]{1,0,2:T(8,128)(2,1)S(1)}, bf16[27,64,3]{1,0,2:T(8,128)(2,1)}, u32[]{:S(2)}) copy-start(bf16[27,64,3]{1,0,2:T(8,128)(2,1)} %param.12) | copy-start | bytes 31108
  15.8 11.4 %slice-start.1 = ((s8[7962624]{0:T(1024)(128)(4,1)}), s8[3768320]{0:T(1024)(128)(4,1)S(1)}, s32[]{:S(2)}) async-start(s8[7962624]{0:T(1024)(128)(4,1)} %bitcast.3), calls=%async_computation.1 | async-start | bytes 7536640
  22.8 15.2 %collective-permute-start.1 = (bf16[2,128,384]{2,1,0:T(8,128)(2,1)S(1)}, bf16[2,128,384]{2,1,0:T(8,128)(2,1)S(1)}, u32[]{:S(2)}, u32[]{:S(2)}) collective-permute-start(bf16[2,128,384]{2,1,0:T(8,128)(2,1)S(1)} %slice.8), channel_id=1, source_target_pairs={{0,32},{32,64},{64,96},{1,33},{33,65},{65,97},{2,34},{34,66},{66,9... | collective-permute-start | bytes 589832 | tf_op jit(solution)/shard_map/ppermute | solution.py:30
  25.2 11.9 %collective-permute-start.4 = (bf16[2,128,384]{2,1,0:T(8,128)(2,1)S(1)}, bf16[2,128,384]{2,1,0:T(8,128)(2,1)S(1)}, u32[]{:S(2)}, u32[]{:S(2)}) collective-permute-start(bf16[2,128,384]{2,1,0:T(8,128)(2,1)S(1)} %slice.9), channel_id=1, source_target_pairs={{0,32},{32,64},{64,96},{1,33},{33,65},{65,97},{2,34},{34,66},{66,9... | collective-permute-start | bytes 589832 | tf_op jit(solution)/shard_map/ppermute | solution.py:30
  27.2 5.7 %copy-start = (bf16[4,2,128,384]{3,2,1,0:T(8,128)(2,1)S(1)}, bf16[4,2,128,384]{3,2,1,0:T(8,128)(2,1)}, u32[]{:S(2)}) copy-start(bf16[4,2,128,384]{3,2,1,0:T(8,128)(2,1)} %feat_ref.9) | copy-start | bytes 2359300
  27.2 5.7 %copy-start.1 = (bf16[3,4,2,128]{3,2,1,0:T(2,128)(2,1)S(1)}, bf16[3,4,2,128]{3,2,1,0:T(2,128)(2,1)}, u32[]{:S(2)}) copy-start(bf16[3,4,2,128]{3,2,1,0:T(2,128)(2,1)} %real_ref.7) | copy-start | bytes 18436
  27.2 5.7 %copy-start.2 = (bf16[384,3]{0,1:T(4,128)(2,1)S(1)}, bf16[384,3]{0,1:T(4,128)(2,1)}, u32[]{:S(2)}) copy-start(bf16[384,3]{0,1:T(4,128)(2,1)} %param.10) | copy-start | bytes 6916
  38.8 9.0 %collective-permute-start.6 = (bf16[4,2,8,128]{3,2,1,0:T(8,128)(2,1)S(1)}, bf16[4,2,8,128]{3,2,1,0:T(8,128)(2,1)S(1)}, u32[]{:S(2)}, u32[]{:S(2)}) collective-permute-start(bf16[4,2,8,128]{3,2,1,0:T(8,128)(2,1)S(1)} %get-tuple-element.38.own_ref), channel_id=1, source_target_pairs={{1,2},{2,1},{3,4},{4,3},{5,6},{6,5},{7,8},{8,7},{9,10},{10,9},{11,... | collective-permute-start | bytes 49160 | tf_op jit(solution)/shard_map/ppermute | solution.py:26
  46.1 3.0 %collective-permute-start.5 = (bf16[4,2,8,128]{3,2,1,0:T(8,128)(2,1)S(1)}, bf16[4,2,8,128]{3,2,1,0:T(8,128)(2,1)S(1)}, u32[]{:S(2)}, u32[]{:S(2)}) collective-permute-start(bf16[4,2,8,128]{3,2,1,0:T(8,128)(2,1)S(1)} %get-tuple-element.38.own_ref), channel_id=1, source_target_pairs={{0,1},{1,0},{2,3},{3,2},{4,5},{5,4},{6,7},{7,6},{8,9},{9,8},{10,11... | collective-permute-start | bytes 49160 | tf_op jit(solution)/shard_map/ppermute | solution.py:26
  49.1 5.5 %collective-permute-start.7 = (bf16[2,6,8,128]{3,2,1,0:T(8,128)(2,1)S(1)}, bf16[2,6,8,128]{3,2,1,0:T(8,128)(2,1)S(1)}, u32[]{:S(2)}, u32[]{:S(2)}) collective-permute-start(bf16[2,6,8,128]{3,2,1,0:T(8,128)(2,1)S(1)} %get-tuple-element.39), channel_id=1, source_target_pairs={{0,32},{32,0},{64,96},{96,64},{1,33},{33,1},{65,97},{97,65},{2,34}... | collective-permute-start | bytes 73736 | tf_op jit(solution)/shard_map/ppermute | solution.py:26
  50.7 5.1 %collective-permute-start.8 = (bf16[2,6,8,128]{3,2,1,0:T(8,128)(2,1)S(1)}, bf16[2,6,8,128]{3,2,1,0:T(8,128)(2,1)S(1)}, u32[]{:S(2)}, u32[]{:S(2)}) collective-permute-start(bf16[2,6,8,128]{3,2,1,0:T(8,128)(2,1)S(1)} %get-tuple-element.40), channel_id=1, source_target_pairs={{32,64},{64,32},{33,65},{65,33},{34,66},{66,34},{35,67},{67,35},{3... | collective-permute-start | bytes 73736 | tf_op jit(solution)/shard_map/ppermute | solution.py:26

commit v10 on v9

--- a/solution.py
+++ b/solution.py
@@ -116,10 +116,20 @@
     store.wait()
 
 
-def prep_kernel(a_ref, b_ref, d2_ref, d1_ref, lines_ref, w2_ref, w1_ref):
+def prep_kernel(
+    a_ref, b_ref, second_ref, first_ref, lines_ref, w2_ref, w1_ref, d2_ref, d1_ref, sems
+):
+    loads = [
+        pltpu.make_async_copy(second_ref, d2_ref, sems.at[0]),
+        pltpu.make_async_copy(first_ref, d1_ref, sems.at[1]),
+    ]
+    for load in loads:
+        load.start()
     odd = lax.rem(lax.axis_index("rows"), 2)
     lines_ref[1 - odd] = a_ref[...]
     lines_ref[odd] = b_ref[...]
+    for load in loads:
+        load.wait()
     depth1, depth2 = d2_ref.shape[1:]
     for dt in range(3):
         for dw in range(3):
@@ -160,18 +170,6 @@
     return decoded, both.astype(BF16)
 
 
-def add_row(lhs, dts, row, w_ref, sums_ref, out_ref):
-    chans = w_ref.shape[1]
-    blocks = column_blocks(chans)
-    for j in range(0, len(blocks), 2):
-        some = blocks[j : j + 2]
-        rhs = [rhs_block(w_ref, dw, off, [(dt, 2 * row) for dt in dts]) for dw, off in some]
-        cols = slice(j * 128, (j + len(some)) * 128)
-        out_ref[:, cols] = sums_ref[:, cols] + jnp.dot(
-            lhs, rhs[0] if len(rhs) == 1 else jnp.concatenate(rhs, axis=1), preferred_element_type=F32
-        )
-
-
 def finish_row(ts, row, sums, feat_ref, rgb_ref, real_ref, decoded_ref, colour_ref):
     width, chans = feat_ref.shape[2:]
     for k, t in enumerate(ts):
@@ -183,41 +181,26 @@
         decoded_ref[t, row], colour_ref[t, row] = finish(ys, feat_ref[t, row], rgb_ref[...], reals)
 
 
-def side_row(side):
+def near_kernel(side, line_ref, past_ref, w_ref, sums_ref, feat_ref, rgb_ref, real_ref, *refs):
+    decoded_ref, colour_ref, all_ref = refs[-3:]
     odd = lax.rem(lax.axis_index("rows"), 2)
-    return 1 - odd if side == 0 else odd
-
-
-def near_kernel(side, line_ref, w_ref, sums_ref, feat_ref, rgb_ref, real_ref, *refs):
-    y_ref, decoded_ref, colour_ref, all_ref = refs[-4:]
-    row = side_row(side)
-    frames, width, chans = line_ref.shape
-    zeros = jnp.zeros((width, chans), BF16)
-    line = [zeros, zeros] + [line_ref[t] for t in range(frames)]
+    row = 1 - odd if side == 0 else odd
+    frames, _, chans = line_ref.shape
+    line = [past_ref[0], past_ref[1]] + [line_ref[t] for t in range(frames)]
     lhs = jnp.concatenate(
         [jnp.concatenate(line[dt : dt + frames], axis=0) for dt in range(3)], axis=1
     )
-    add_row(lhs, range(3), row, w_ref, sums_ref.at[row], all_ref)
-    y_ref[...] = all_ref[: 2 * width]
-    late = range(2, frames)
+    blocks = column_blocks(chans)
+    for j in range(0, len(blocks), 2):
+        some = blocks[j : j + 2]
+        rhs = [rhs_block(w_ref, dw, off, [(dt, 2 * row) for dt in range(3)]) for dw, off in some]
+        cols = slice(j * 128, (j + len(some)) * 128)
+        all_ref[:, cols] = sums_ref[row, :, cols] + jnp.dot(
+            lhs, rhs[0] if len(rhs) == 1 else jnp.concatenate(rhs, axis=1), preferred_element_type=F32
+        )
     finish_row(
-        late, row, all_ref.at[2 * width :], feat_ref, rgb_ref, real_ref, decoded_ref, colour_ref
-    )
-
-
-def corner_kernel(side, past_ref, w_ref, sums_ref, feat_ref, rgb_ref, real_ref, *refs):
-    decoded_ref, colour_ref, all_ref = refs[-3:]
-    row = side_row(side)
-    width, chans = past_ref.shape[1:]
-    lhs = jnp.concatenate(
-        [
-            jnp.concatenate([past_ref[0], past_ref[1]], axis=0),
-            jnp.concatenate([past_ref[1], jnp.zeros((width, chans), BF16)], axis=0),
-        ],
-        axis=1,
-    )
-    add_row(lhs, range(2), row, w_ref, sums_ref, all_ref)
-    finish_row(range(2), row, all_ref, feat_ref, rgb_ref, real_ref, decoded_ref, colour_ref)
+        range(frames), row, all_ref, feat_ref, rgb_ref, real_ref, decoded_ref, colour_ref
+    )
 
 
 def pack_kernel(a_ref, own_ref, b_ref, for_a_ref, for_b_ref):
@@ -369,6 +352,8 @@
     past = onward(tail, "tm")
     from_b = swap(to_b, "rows", 1)
     from_a = swap(to_a, "rows", 0)
+    past_b = swap(past[1], "rows", 1)
+    past_a = swap(past[0], "rows", 0)
 
     line = 2 * width * chans * chans
     lines, w2, w1 = local(
@@ -379,6 +364,12 @@
             kept(2 * depth1, 27 * 8),
         ),
         (to_a, to_b, jnp.transpose(disc_second, (0, 2, 1)), jnp.transpose(disc_first, (2, 0, 1))),
+        hbm=(2, 3),
+        scratch=[
+            pltpu.VMEM((27, depth1, depth2), BF16),
+            pltpu.VMEM((3, 27, depth1), BF16),
+            pltpu.SemaphoreType.DMA((2,)),
+        ],
         flops=40 * 3 * line,
     )
     sums = local(
@@ -387,31 +378,15 @@
         (lines, past, conv_weight),
         flops=48 * 3 * line,
     )
-    corner_a = onward(from_a[frames - 2 :], "tm")
-    corner_b = onward(from_b[frames - 2 :], "tm")
-    rest = (latent_feat, rgb_weight.T, real_frames)
-    early = kept(2 * width, 3 * chans, dtype=F32)
-    shown = (kept(frames, height, width, chans), kept(frames, height, 8, width))
-    ends = []
     outs = ()
-    for side, row in enumerate((from_a, from_b)):
-        y, *outs = local(
+    for side, halo in enumerate(((from_a, past_a), (from_b, past_b))):
+        outs = local(
             functools.partial(near_kernel, side),
-            (early,) + shown,
-            (row, conv_weight, sums) + rest + tuple(outs),
+            (kept(frames, height, width, chans), kept(frames, height, 8, width)),
+            halo + (conv_weight, sums, latent_feat, rgb_weight.T, real_frames) + tuple(outs),
             scratch=[pltpu.VMEM((cells, 3 * chans), F32)],
-            aliases={6: 1, 7: 2} if side else {},
+            aliases={7: 0, 8: 1} if side else {},
             flops=12 * 3 * line,
-        )
-        ends.append(y)
-    for side, row in enumerate((corner_a, corner_b)):
-        outs = local(
-            functools.partial(corner_kernel, side),
-            shown,
-            (row, conv_weight, ends[side]) + rest + tuple(outs),
-            scratch=[pltpu.VMEM((2 * width, 3 * chans), F32)],
-            aliases={6: 0, 7: 1},
-            flops=4 * 3 * line,
         )
     decoded, colour = outs
     stored, = local(

time: 58.5 us -> 60.4 us (1.032)
  starting transfers between devices: 26.8 us -> 35.8 us
  waiting for transfers between devices: 10.7 us -> 5.68 us
  local copies, waits for them, and re-layouts: 1.82 us -> 0.08 us
    ppermute x6 -> x8, starting transfers between devices: 18.3 us -> 31.7 us  [swap(): return lax.ppermute(block, axis, pairs(lax.axis_size(axis), first))]
    ppermute x6 -> x8, waiting for transfers between devices: 10.7 us -> 5.68 us  [swap(): return lax.ppermute(block, axis, pairs(lax.axis_size(axis), first))]
    ppermute x3 -> x1, starting transfers between devices: 8.44 us -> 4.11 us  [onward(): lax.ppermute(block, axis, [(i, i + 1) for i in range(lax.axis_size(axis)...]
    unnamed x14 -> x10, local copies, waits for them, and re-layouts: 1.78 us -> 0.03 us
    pallas_call x11 -> x9, Pallas kernels: 17.7 us -> 17.5 us  [local(): pl.pallas_call(kernel, out_shape=outs, in_specs=[HBM if i in hbm else VME...]
  transfers between devices with their start and end apart: 9 -> 9, of which waited for: 4 -> 1; matrix products, arithmetic and copies ran while one was open for 0% -> 0% of each run, Pallas kernels for 23% -> 19%
where the time goes in v10:
time: 60.4 us; the launch traced here: 59.9 us
  starting transfers between devices  35.8 us (59%)
  Pallas kernels  17.5 us (29%)
  waiting for transfers between devices  5.68 us (9%)
  between operations  0.87 us (1%)
    ppermute x8, starting transfers between devices, swap(): return lax.ppermute(block, axis, pairs(lax.axis_size(axis), first))  31.7 us
    pallas_call x9, Pallas kernels, local(): pl.pallas_call(kernel, out_shape=outs, in_specs=[HBM if i in hbm else VME...  17.5 us
    ppermute x8, waiting for transfers between devices, swap(): return lax.ppermute(block, axis, pairs(lax.axis_size(axis), first))  5.68 us
    ppermute x1, starting transfers between devices, onward(): lax.ppermute(block, axis, [(i, i + 1) for i in range(lax.axis_size(axis)...  4.11 us
  transfers between devices with their start and end apart: 9, of which 1 were waited for; matrix products, arithmetic and copies ran while one was open for 0% of the time, Pallas kernels for 19%

profile of v10, /device:TPU:17, one launch (start us, length us, event | category | flops | bytes accessed | tf_op | source)
XLA Modules:
  0.0 59.9 jit_solution(917278188910473039)
XLA Ops:
  0.6 0.0 slice-start
  0.6 1.9 %shard_map.86 = (bf16[4,128,384]{2,1,0:T(8,128)(2,1)S(1)}, bf16[4,128,384]{2,1,0:T(8,128)(2,1)S(1)}, bf16[2,2,128,384]{3,2,1,0:T(8,128)(2,1)S(1)}) custom-call(bf16[4,2,128,384]{3,2,1,0:T(8,128)(2,1)} %feat_ref.5, f32[384]{0:T(512)} %gain_ref.1), custom_call_target="tpu_custom_call" | custom-call | bytes 1000000 | tf_op jit(solution)/shard_map/pallas_call | solution.py:38
  2.5 4.1 %collective-permute-start.1 = (bf16[2,2,128,384]{3,2,1,0:T(8,128)(2,1)S(1)}, bf16[2,2,128,384]{3,2,1,0:T(8,128)(2,1)S(1)}, u32[]{:S(2)}, u32[]{:S(2)}) collective-permute-start(bf16[2,2,128,384]{3,2,1,0:T(8,128)(2,1)S(1)} %get-tuple-element.20), channel_id=1, source_target_pairs={{0,32},{32,64},{64,96},{1,33},{33,65},{65,97},{2,34},{34,66},{66,9... | collective-permute-start | bytes 1179656 | tf_op jit(solution)/shard_map/ppermute | solution.py:30
  6.6 1.3 %collective-permute-start.3 = (bf16[4,128,384]{2,1,0:T(8,128)(2,1)S(1)}, bf16[4,128,384]{2,1,0:T(8,128)(2,1)S(1)}, u32[]{:S(2)}, u32[]{:S(2)}) collective-permute-start(bf16[4,128,384]{2,1,0:T(8,128)(2,1)S(1)} %get-tuple-element.21.a_ref), channel_id=1, source_target_pairs={{0,1},{1,0},{2,3},{3,2},{4,5},{5,4},{6,7},{7,6},{8,9},{9,8},{10,11... | collective-permute-start | bytes 1179656 | tf_op jit(solution)/shard_map/ppermute | solution.py:26
  7.9 6.6 %collective-permute-start = (bf16[4,128,384]{2,1,0:T(8,128)(2,1)S(1)}, bf16[4,128,384]{2,1,0:T(8,128)(2,1)S(1)}, u32[]{:S(2)}, u32[]{:S(2)}) collective-permute-start(bf16[4,128,384]{2,1,0:T(8,128)(2,1)S(1)} %get-tuple-element.19.b_ref), channel_id=1, source_target_pairs={{1,2},{2,1},{3,4},{4,3},{5,6},{6,5},{7,8},{8,7},{9,10},{10,9},{11,... | collective-permute-start | bytes 1179656 | tf_op jit(solution)/shard_map/ppermute | solution.py:26
  14.5 0.0 slice-start.1
  14.5 1.6 %shard_map.87 = (bf16[2,4,128,384]{3,2,1,0:T(8,128)(2,1)S(1)}, bf16[384,768]{1,0:T(8,128)(2,1)S(1)}, bf16[128,216]{1,0:T(8,128)(2,1)S(1)}) custom-call(bf16[4,128,384]{2,1,0:T(8,128)(2,1)S(1)} %get-tuple-element.21.a_ref, bf16[4,128,384]{2,1,0:T(8,128)(2,1)S(1)} %get-tuple-element.19.b_ref, bf16[27,64,128]{2,1,0:T(8,128)(2,1)} %bitcast.11, ...), custom_call_target="tpu_custom_call" | custom-call | flops 4529848320 | bytes 1000000 | tf_op jit(solution)/shard_map/pallas_call | solution.py:38
  16.1 0.0 collective-permute-done.1.past_ref
  16.2 0.1 collective-permute-start.4
  16.3 15.1 %collective-permute-start.2 = (bf16[2,128,384]{2,1,0:T(8,128)(2,1)S(1)}, bf16[2,128,384]{2,1,0:T(8,128)(2,1)S(1)}, u32[]{:S(2)}, u32[]{:S(2)}) collective-permute-start(bf16[2,128,384]{2,1,0:T(8,128)(2,1)S(1)} %get-tuple-element.37), channel_id=1, source_target_pairs={{1,2},{2,1},{3,4},{4,3},{5,6},{6,5},{7,8},{8,7},{9,10},{10,9},{11,... | collective-permute-start | bytes 589832 | tf_op jit(solution)/shard_map/ppermute | solution.py:26
  31.4 0.0 slice-done
  31.4 0.0 copy-start
  31.4 0.0 copy-start.1
  31.4 0.0 copy-start.2
  31.5 5.7 %shard_map.88.sums_ref = f32[2,512,1152]{2,1,0:T(8,128)S(1)} custom-call(bf16[2,4,128,384]{3,2,1,0:T(8,128)(2,1)S(1)} %get-tuple-element.22.lines_ref, bf16[2,2,128,384]{3,2,1,0:T(8,128)(2,1)S(1)} %collective-permute-done.1.past_ref, bf16[27,384,384]{2,1,0:T(8,128)(2,1)S(1)} %bitcast.8), custom_call_target="tpu_custom_call" | custom-call | flops 5435817984 | bytes 1000000 | tf_op jit(solution)/shard_map/pallas_call | solution.py:38
  37.1 0.0 collective-permute-done.3.line_ref
  37.1 0.0 collective-permute-done.4.past_ref
  37.2 2.3 %shard_map.89 = (bf16[4,2,128,384]{3,2,1,0:T(8,128)(2,1)S(1)}, bf16[4,2,8,128]{3,2,1,0:T(8,128)(2,1)S(1)}) custom-call(bf16[4,128,384]{2,1,0:T(8,128)(2,1)S(1)} %collective-permute-done.3.line_ref, bf16[2,128,384]{2,1,0:T(8,128)(2,1)S(1)} %collective-permute-done.4.past_ref, bf16[27,384,384]{2,1,0:T(8,128)(2,1)S(1)} %bitcast.8, ...), custom_call_target="tpu_custom_call" | custom-call | flops 1358954496 | bytes 1000000 | tf_op jit(solution)/shard_map/pallas_call | solution.py:38
  39.4 0.0 collective-permute-done.line_ref
  39.4 0.0 collective-permute-done.2.past_ref
  39.5 2.2 %shard_map.90 = (bf16[4,2,128,384]{3,2,1,0:T(8,128)(2,1)S(1)}, bf16[4,2,8,128]{3,2,1,0:T(8,128)(2,1)S(1)}) custom-call(bf16[4,128,384]{2,1,0:T(8,128)(2,1)S(1)} %collective-permute-done.line_ref, bf16[2,128,384]{2,1,0:T(8,128)(2,1)S(1)} %collective-permute-done.2.past_ref, ...), custom_call_target="tpu_custom_call", output_to_operand_aliasing={{0}: (7, {}), {1}: (8, {})} | custom-call | flops 1358954496 | bytes 1000000 | tf_op jit(solution)/shard_map/pallas_call | solution.py:38
  41.7 0.0 collective-permute-start.5
  41.8 3.3 %collective-permute-start.6 = (bf16[4,2,8,128]{3,2,1,0:T(8,128)(2,1)S(1)}, bf16[4,2,8,128]{3,2,1,0:T(8,128)(2,1)S(1)}, u32[]{:S(2)}, u32[]{:S(2)}) collective-permute-start(bf16[4,2,8,128]{3,2,1,0:T(8,128)(2,1)S(1)} %get-tuple-element.26.own_ref), channel_id=1, source_target_pairs={{1,2},{2,1},{3,4},{4,3},{5,6},{6,5},{7,8},{8,7},{9,10},{10,9},{11,... | collective-permute-start | bytes 49160 | tf_op jit(solution)/shard_map/ppermute | solution.py:26
  45.1 0.0 collective-permute-done.5.a_ref
  45.1 5.6 %collective-permute-done.6.b_ref = bf16[4,2,8,128]{3,2,1,0:T(8,128)(2,1)S(1)} collective-permute-done((bf16[4,2,8,128]{3,2,1,0:T(8,128)(2,1)S(1)}, bf16[4,2,8,128]{3,2,1,0:T(8,128)(2,1)S(1)}, u32[]{:S(2)}, u32[]{:S(2)}) %collective-permute-start.6) | collective-permute-done | bytes 16416 | tf_op jit(solution)/shard_map/ppermute | solution.py:26
  50.8 0.0 collective-permute-start.7
  50.8 5.2 %collective-permute-start.8 = (bf16[2,6,8,128]{3,2,1,0:T(8,128)(2,1)S(1)}, bf16[2,6,8,128]{3,2,1,0:T(8,128)(2,1)S(1)}, u32[]{:S(2)}, u32[]{:S(2)}) collective-permute-start(bf16[2,6,8,128]{3,2,1,0:T(8,128)(2,1)S(1)} %get-tuple-element.28), channel_id=1, source_target_pairs={{32,64},{64,32},{33,65},{65,33},{34,66},{66,34},{35,67},{67,35},{3... | collective-permute-start | bytes 73736 | tf_op jit(solution)/shard_map/ppermute | solution.py:26
  56.0 0.9 %shard_map.91 = bf16[4,2,128,384]{3,2,1,0:T(8,128)(2,1)} custom-call(bf16[4,2,128,384]{3,2,1,0:T(8,128)(2,1)S(1)} %get-tuple-element.25.decoded_ref), custom_call_target="tpu_custom_call" | custom-call | bytes 1000000 | tf_op jit(solution)/shard_map/pallas_call | solution.py:38
  56.9 1.1 %shard_map.93 = (f32[8,6,24,128]{3,2,1,0:T(8,128)S(1)}, bf16[6,4,128,128]{3,2,1,0:T(8,128)(2,1)S(1)}, f32[8,128]{1,0:T(8,128)S(1)}, f32[8,384,256]{2,1,0:T(8,128)S(1)}) custom-call(bf16[4,2,8,128]{3,2,1,0:T(8,128)(2,1)S(1)} %collective-permute-done.5.a_ref, bf16[4,2,8,128]{3,2,1,0:T(8,128)(2,1)S(1)} %get-tuple-element.26.own_ref, ...), custom_call_target="tpu_custom_call" | custom-call | bytes 1000000 | tf_op jit(solution)/shard_map/pallas_call | solution.py:38
  57.9 0.0 collective-permute-done.7.ta_ref
  58.0 0.0 collective-permute-done.8.tb_ref
  58.0 2.0 %shard_map.94 = (f32[4,2,128]{2,1,0:T(2,128)}, f32[8,6,24,128]{3,2,1,0:T(8,128)S(1)}, bf16[6,4,128,128]{3,2,1,0:T(8,128)(2,1)S(1)}, f32[8,128]{1,0:T(8,128)S(1)}) custom-call(bf16[2,6,8,128]{3,2,1,0:T(8,128)(2,1)S(1)} %collective-permute-done.7.ta_ref, ...), custom_call_target="tpu_custom_call", output_to_operand_aliasing={{1}: (5, {}), {2}: (6, {}), {3}: (7, {})} | custom-call | bytes 1000000 | tf_op jit(solution)/shard_map/pallas_call | solution.py:38
  (7 shorter events, 0.1 us)
Async XLA Ops:
  0.6 30.8 %slice-start = ((s8[7962624]{0:T(1024)(128)(4,1)}), s8[4194304]{0:T(1024)(128)(4,1)S(1)}, s32[]{:S(2)}) async-start(s8[7962624]{0:T(1024)(128)(4,1)} %bitcast.7), calls=%async_computation | async-start | bytes 8388608
  2.5 13.6 %collective-permute-start.1 = (bf16[2,2,128,384]{3,2,1,0:T(8,128)(2,1)S(1)}, bf16[2,2,128,384]{3,2,1,0:T(8,128)(2,1)S(1)}, u32[]{:S(2)}, u32[]{:S(2)}) collective-permute-start(bf16[2,2,128,384]{3,2,1,0:T(8,128)(2,1)S(1)} %get-tuple-element.20), channel_id=1, source_target_pairs={{0,32},{32,64},{64,96},{1,33},{33,65},{65,97},{2,34},{34,66},{66,9... | collective-permute-start | bytes 1179656 | tf_op jit(solution)/shard_map/ppermute | solution.py:30
  6.6 30.5 %collective-permute-start.3 = (bf16[4,128,384]{2,1,0:T(8,128)(2,1)S(1)}, bf16[4,128,384]{2,1,0:T(8,128)(2,1)S(1)}, u32[]{:S(2)}, u32[]{:S(2)}) collective-permute-start(bf16[4,128,384]{2,1,0:T(8,128)(2,1)S(1)} %get-tuple-element.21.a_ref), channel_id=1, source_target_pairs={{0,1},{1,0},{2,3},{3,2},{4,5},{5,4},{6,7},{7,6},{8,9},{9,8},{10,11... | collective-permute-start | bytes 1179656 | tf_op jit(solution)/shard_map/ppermute | solution.py:26
  7.9 31.5 %collective-permute-start = (bf16[4,128,384]{2,1,0:T(8,128)(2,1)S(1)}, bf16[4,128,384]{2,1,0:T(8,128)(2,1)S(1)}, u32[]{:S(2)}, u32[]{:S(2)}) collective-permute-start(bf16[4,128,384]{2,1,0:T(8,128)(2,1)S(1)} %get-tuple-element.19.b_ref), channel_id=1, source_target_pairs={{1,2},{2,1},{3,4},{4,3},{5,6},{6,5},{7,8},{8,7},{9,10},{10,9},{11,... | collective-permute-start | bytes 1179656 | tf_op jit(solution)/shard_map/ppermute | solution.py:26
  14.5 16.9 %slice-start.1 = ((s8[7962624]{0:T(1024)(128)(4,1)}), s8[3768320]{0:T(1024)(128)(4,1)S(1)}, s32[]{:S(2)}) async-start(s8[7962624]{0:T(1024)(128)(4,1)} %bitcast.7), calls=%async_computation.1 | async-start | bytes 7536640
  16.2 21.0 %collective-permute-start.4 = (bf16[2,128,384]{2,1,0:T(8,128)(2,1)S(1)}, bf16[2,128,384]{2,1,0:T(8,128)(2,1)S(1)}, u32[]{:S(2)}, u32[]{:S(2)}) collective-permute-start(bf16[2,128,384]{2,1,0:T(8,128)(2,1)S(1)} %get-tuple-element.36), channel_id=1, source_target_pairs={{0,1},{1,0},{2,3},{3,2},{4,5},{5,4},{6,7},{7,6},{8,9},{9,8},{10,11... | collective-permute-start | bytes 589832 | tf_op jit(solution)/shard_map/ppermute | solution.py:26
  16.3 23.2 %collective-permute-start.2 = (bf16[2,128,384]{2,1,0:T(8,128)(2,1)S(1)}, bf16[2,128,384]{2,1,0:T(8,128)(2,1)S(1)}, u32[]{:S(2)}, u32[]{:S(2)}) collective-permute-start(bf16[2,128,384]{2,1,0:T(8,128)(2,1)S(1)} %get-tuple-element.37), channel_id=1, source_target_pairs={{1,2},{2,1},{3,4},{4,3},{5,6},{6,5},{7,8},{8,7},{9,10},{10,9},{11,... | collective-permute-start | bytes 589832 | tf_op jit(solution)/shard_map/ppermute | solution.py:26
  31.4 5.7 %copy-start = (bf16[4,2,128,384]{3,2,1,0:T(8,128)(2,1)S(1)}, bf16[4,2,128,384]{3,2,1,0:T(8,128)(2,1)}, u32[]{:S(2)}) copy-start(bf16[4,2,128,384]{3,2,1,0:T(8,128)(2,1)} %feat_ref.5) | copy-start | bytes 2359300
  31.4 5.7 %copy-start.1 = (bf16[3,4,2,128]{3,2,1,0:T(2,128)(2,1)S(1)}, bf16[3,4,2,128]{3,2,1,0:T(2,128)(2,1)}, u32[]{:S(2)}) copy-start(bf16[3,4,2,128]{3,2,1,0:T(2,128)(2,1)} %real_ref.3) | copy-start | bytes 18436
  31.4 5.7 %copy-start.2 = (bf16[384,3]{0,1:T(4,128)(2,1)S(1)}, bf16[384,3]{0,1:T(4,128)(2,1)}, u32[]{:S(2)}) copy-start(bf16[384,3]{0,1:T(4,128)(2,1)} %param.10) | copy-start | bytes 6916
  41.7 3.4 %collective-permute-start.5 = (bf16[4,2,8,128]{3,2,1,0:T(8,128)(2,1)S(1)}, bf16[4,2,8,128]{3,2,1,0:T(8,128)(2,1)S(1)}, u32[]{:S(2)}, u32[]{:S(2)}) collective-permute-start(bf16[4,2,8,128]{3,2,1,0:T(8,128)(2,1)S(1)} %get-tuple-element.26.own_ref), channel_id=1, source_target_pairs={{0,1},{1,0},{2,3},{3,2},{4,5},{5,4},{6,7},{7,6},{8,9},{9,8},{10,11... | collective-permute-start | bytes 49160 | tf_op jit(solution)/shard_map/ppermute | solution.py:26
  41.8 9.0 %collective-permute-start.6 = (bf16[4,2,8,128]{3,2,1,0:T(8,128)(2,1)S(1)}, bf16[4,2,8,128]{3,2,1,0:T(8,128)(2,1)S(1)}, u32[]{:S(2)}, u32[]{:S(2)}) collective-permute-start(bf16[4,2,8,128]{3,2,1,0:T(8,128)(2,1)S(1)} %get-tuple-element.26.own_ref), channel_id=1, source_target_pairs={{1,2},{2,1},{3,4},{4,3},{5,6},{6,5},{7,8},{8,7},{9,10},{10,9},{11,... | collective-permute-start | bytes 49160 | tf_op jit(solution)/shard_map/ppermute | solution.py:26
  50.8 7.2 %collective-permute-start.7 = (bf16[2,6,8,128]{3,2,1,0:T(8,128)(2,1)S(1)}, bf16[2,6,8,128]{3,2,1,0:T(8,128)(2,1)S(1)}, u32[]{:S(2)}, u32[]{:S(2)}) collective-permute-start(bf16[2,6,8,128]{3,2,1,0:T(8,128)(2,1)S(1)} %get-tuple-element.27), channel_id=1, source_target_pairs={{0,32},{32,0},{64,96},{96,64},{1,33},{33,1},{65,97},{97,65},{2,34}... | collective-permute-start | bytes 73736 | tf_op jit(solution)/shard_map/ppermute | solution.py:26
  50.8 7.2 %collective-permute-start.8 = (bf16[2,6,8,128]{3,2,1,0:T(8,128)(2,1)S(1)}, bf16[2,6,8,128]{3,2,1,0:T(8,128)(2,1)S(1)}, u32[]{:S(2)}, u32[]{:S(2)}) collective-permute-start(bf16[2,6,8,128]{3,2,1,0:T(8,128)(2,1)S(1)} %get-tuple-element.28), channel_id=1, source_target_pairs={{32,64},{64,32},{33,65},{65,33},{34,66},{66,34},{35,67},{67,35},{3... | collective-permute-start | bytes 73736 | tf_op jit(solution)/shard_map/ppermute | solution.py:26

commit v11 on v9

--- a/solution.py
+++ b/solution.py
@@ -116,10 +116,20 @@
     store.wait()
 
 
-def prep_kernel(a_ref, b_ref, d2_ref, d1_ref, lines_ref, w2_ref, w1_ref):
+def prep_kernel(
+    a_ref, b_ref, second_ref, first_ref, lines_ref, w2_ref, w1_ref, d2_ref, d1_ref, sems
+):
+    loads = [
+        pltpu.make_async_copy(second_ref, d2_ref, sems.at[0]),
+        pltpu.make_async_copy(first_ref, d1_ref, sems.at[1]),
+    ]
+    for load in loads:
+        load.start()
     odd = lax.rem(lax.axis_index("rows"), 2)
     lines_ref[1 - odd] = a_ref[...]
     lines_ref[odd] = b_ref[...]
+    for load in loads:
+        load.wait()
     depth1, depth2 = d2_ref.shape[1:]
     for dt in range(3):
         for dw in range(3):
@@ -160,18 +170,6 @@
     return decoded, both.astype(BF16)
 
 
-def add_row(lhs, dts, row, w_ref, sums_ref, out_ref):
-    chans = w_ref.shape[1]
-    blocks = column_blocks(chans)
-    for j in range(0, len(blocks), 2):
-        some = blocks[j : j + 2]
-        rhs = [rhs_block(w_ref, dw, off, [(dt, 2 * row) for dt in dts]) for dw, off in some]
-        cols = slice(j * 128, (j + len(some)) * 128)
-        out_ref[:, cols] = sums_ref[:, cols] + jnp.dot(
-            lhs, rhs[0] if len(rhs) == 1 else jnp.concatenate(rhs, axis=1), preferred_element_type=F32
-        )
-
-
 def finish_row(ts, row, sums, feat_ref, rgb_ref, real_ref, decoded_ref, colour_ref):
     width, chans = feat_ref.shape[2:]
     for k, t in enumerate(ts):
@@ -183,6 +181,17 @@
         decoded_ref[t, row], colour_ref[t, row] = finish(ys, feat_ref[t, row], rgb_ref[...], reals)
 
 
+def add_row(lhs, dts, row, w_ref, sums_ref, out_ref):
+    blocks = column_blocks(w_ref.shape[1])
+    for j in range(0, len(blocks), 2):
+        some = blocks[j : j + 2]
+        rhs = [rhs_block(w_ref, dw, off, [(dt, 2 * row) for dt in dts]) for dw, off in some]
+        cols = slice(j * 128, (j + len(some)) * 128)
+        out_ref[:, cols] = sums_ref[:, cols] + jnp.dot(
+            lhs, rhs[0] if len(rhs) == 1 else jnp.concatenate(rhs, axis=1), preferred_element_type=F32
+        )
+
+
 def side_row(side):
     odd = lax.rem(lax.axis_index("rows"), 2)
     return 1 - odd if side == 0 else odd
@@ -205,7 +214,7 @@
     )
 
 
-def corner_kernel(side, past_ref, w_ref, sums_ref, feat_ref, rgb_ref, real_ref, *refs):
+def late_kernel(side, past_ref, w_ref, sums_ref, feat_ref, rgb_ref, real_ref, *refs):
     decoded_ref, colour_ref, all_ref = refs[-3:]
     row = side_row(side)
     width, chans = past_ref.shape[1:]
@@ -245,54 +254,52 @@
 def first_layer(t, frames, x_ref, w1_ref, f_ref, near_ref):
     tm, band = lax.axis_index("tm"), lax.axis_index("rows")
     width = x_ref.shape[3]
-    for h in range(0, 4, 2):
-        cols = []
-        for hh in (h, h + 1):
-            cols.append(
-                jnp.concatenate(
-                    [x_ref[t + dt, hh + dh] for dt in range(3) for dh in range(3)], axis=0
-                ).astype(BF16)
+    cols = []
+    for hh in range(4):
+        cols.append(
+            jnp.concatenate(
+                [x_ref[t + dt, hh + dh] for dt in range(3) for dh in range(3)], axis=0
+            ).astype(BF16)
+        )
+    first = leaky(jnp.dot(w1_ref[...], jnp.concatenate(cols, axis=1), preferred_element_type=F32))
+    for hh in range(4):
+        part = first[:, hh * width : (hh + 1) * width]
+        inside = []
+        if t == 0:
+            inside.append(tm > 0)
+        if t == frames + 1:
+            inside.append(tm < lax.axis_size("tm") - 1)
+        if hh == 0:
+            inside.append(band > 0)
+        if hh == 3:
+            inside.append(band < lax.axis_size("rows") - 1)
+        if inside:
+            keep = inside[0] if len(inside) == 1 else jnp.logical_and(*inside)
+            part = jnp.where(keep, part, 0.0)
+        part = part.astype(BF16)
+        f_ref[t, hh] = part
+        if 1 <= t <= frames and 1 <= hh <= 2:
+            wide = part.astype(F32)
+            half = wide.shape[0] // 2
+            at = 2 * (t - 1) + hh - 1
+            near_ref[at : at + 1] = jnp.mean(
+                jnp.abs(wide[:half] - wide[half:]), axis=0, keepdims=True
             )
-        first = leaky(
-            jnp.dot(w1_ref[...], jnp.concatenate(cols, axis=1), preferred_element_type=F32)
-        )
-        for i, hh in enumerate((h, h + 1)):
-            part = first[:, i * width : (i + 1) * width]
-            inside = []
-            if t == 0:
-                inside.append(tm > 0)
-            if t == frames + 1:
-                inside.append(tm < lax.axis_size("tm") - 1)
-            if hh == 0:
-                inside.append(band > 0)
-            if hh == 3:
-                inside.append(band < lax.axis_size("rows") - 1)
-            if inside:
-                keep = inside[0] if len(inside) == 1 else jnp.logical_and(*inside)
-                part = jnp.where(keep, part, 0.0)
-            part = part.astype(BF16)
-            f_ref[t, hh] = part
-            if 1 <= t <= frames and 1 <= hh <= 2:
-                wide = part.astype(F32)
-                half = wide.shape[0] // 2
-                at = 2 * (t - 1) + hh - 1
-                near_ref[at : at + 1] = jnp.mean(
-                    jnp.abs(wide[:half] - wide[half:]), axis=0, keepdims=True
-                )
-
-
-def second_sums(t, h, dts, w2_ref, f_ref):
+
+
+def second_sums(t, dts, w2_ref, f_ref):
     half, width = f_ref.shape[2] // 2, f_ref.shape[3]
     zeros = jnp.zeros((half, width), BF16)
-    sides = []
-    for s in range(2):
-        rows = []
-        for dt in dts:
-            rows += [f_ref[t + dt, h + dh, s * half : (s + 1) * half] for dh in range(3)] + [zeros]
-        sides.append(jnp.concatenate(rows, axis=0))
+    cols = []
+    for h in range(2):
+        for s in range(2):
+            rows = []
+            for dt in dts:
+                rows += [f_ref[t + dt, h + dh, s * half : (s + 1) * half] for dh in range(3)] + [zeros]
+            cols.append(jnp.concatenate(rows, axis=0))
     return jnp.dot(
         w2_ref[:, 4 * half * dts[0] : 4 * half * (dts[-1] + 1)],
-        jnp.concatenate(sides, axis=1),
+        jnp.concatenate(cols, axis=1),
         preferred_element_type=F32,
     )
 
@@ -310,8 +317,7 @@
     for t in range(2, frames):
         first_layer(t, frames, x_ref, w1_ref, f_ref, near_ref)
     for t in range(frames):
-        for h in range(2):
-            part_ref[2 * t + h] = second_sums(t, h, inner_dts(t, frames), w2_ref, f_ref)
+        part_ref[t] = second_sums(t, inner_dts(t, frames), w2_ref, f_ref)
 
 
 def disc_kernel(
@@ -330,12 +336,13 @@
     col = lax.broadcasted_iota(jnp.int32, (depth2, width), 1)
     for t in range(frames):
         dts = [dt for dt in range(3) if dt not in inner_dts(t, frames)]
+        y = part_ref[t] + second_sums(t, dts, w2_ref, f_ref)
         for h in range(height):
-            y = part_ref[2 * t + h] + second_sums(t, h, dts, w2_ref, f_ref)
             outs = []
             for s in range(2):
+                k = 2 * h + s
                 y0, y1, y2 = (
-                    y[d * depth2 : (d + 1) * depth2, s * width : (s + 1) * width] for d in range(3)
+                    y[d * depth2 : (d + 1) * depth2, k * width : (k + 1) * width] for d in range(3)
                 )
                 total = (
                     y1
@@ -369,6 +376,8 @@
     past = onward(tail, "tm")
     from_b = swap(to_b, "rows", 1)
     from_a = swap(to_a, "rows", 0)
+    past_b = swap(past[1], "rows", 1)
+    past_a = swap(past[0], "rows", 0)
 
     line = 2 * width * chans * chans
     lines, w2, w1 = local(
@@ -379,6 +388,12 @@
             kept(2 * depth1, 27 * 8),
         ),
         (to_a, to_b, jnp.transpose(disc_second, (0, 2, 1)), jnp.transpose(disc_first, (2, 0, 1))),
+        hbm=(2, 3),
+        scratch=[
+            pltpu.VMEM((27, depth1, depth2), BF16),
+            pltpu.VMEM((3, 27, depth1), BF16),
+            pltpu.SemaphoreType.DMA((2,)),
+        ],
         flops=40 * 3 * line,
     )
     sums = local(
@@ -387,8 +402,6 @@
         (lines, past, conv_weight),
         flops=48 * 3 * line,
     )
-    corner_a = onward(from_a[frames - 2 :], "tm")
-    corner_b = onward(from_b[frames - 2 :], "tm")
     rest = (latent_feat, rgb_weight.T, real_frames)
     early = kept(2 * width, 3 * chans, dtype=F32)
     shown = (kept(frames, height, width, chans), kept(frames, height, 8, width))
@@ -404,9 +417,9 @@
             flops=12 * 3 * line,
         )
         ends.append(y)
-    for side, row in enumerate((corner_a, corner_b)):
+    for side, row in enumerate((past_a, past_b)):
         outs = local(
-            functools.partial(corner_kernel, side),
+            functools.partial(late_kernel, side),
             shown,
             (row, conv_weight, ends[side]) + rest + tuple(outs),
             scratch=[pltpu.VMEM((2 * width, 3 * chans), F32)],
@@ -435,7 +448,7 @@
             kept(frames + 4, height + 4, 24, width, dtype=F32),
             kept(frames + 2, height + 2, 2 * depth1, width),
             kept(frames * height, width, dtype=F32),
-            kept(frames * height, 3 * depth2, 2 * width, dtype=F32),
+            kept(frames, 3 * depth2, 2 * height * width, dtype=F32),
         ),
         (side_a, colour, side_b, w1, w2),
     )

time: 58.5 us -> 61.6 us (1.053)
  the two profiles are of different devices: /device:TPU:17 before, /device:TPU:9 now
where the time goes in v11:
time: 61.6 us; the launch traced here: 61.4 us
  starting transfers between devices  34.5 us (56%)
  Pallas kernels  18.9 us (31%)
  waiting for transfers between devices  7 us (11%)
  between operations  0.86 us (1%)
    ppermute x8, starting transfers between devices, swap(): return lax.ppermute(block, axis, pairs(lax.axis_size(axis), first))  30.4 us
    pallas_call x11, Pallas kernels, local(): pl.pallas_call(kernel, out_shape=outs, in_specs=[HBM if i in hbm else VME...  18.9 us
    ppermute x8, waiting for transfers between devices, swap(): return lax.ppermute(block, axis, pairs(lax.axis_size(axis), first))  6.99 us
    ppermute x1, starting transfers between devices, onward(): lax.ppermute(block, axis, [(i, i + 1) for i in range(lax.axis_size(axis)...  4.11 us
  transfers between devices with their start and end apart: 9, of which 1 were waited for; matrix products, arithmetic and copies ran while one was open for 0% of the time, Pallas kernels for 23%

profile of v11, /device:TPU:9, one launch (start us, length us, event | category | flops | bytes accessed | tf_op | source)
XLA Modules:
  0.0 61.4 jit_solution(12291220722487767146)
XLA Ops:
  0.6 0.0 slice-start
  0.6 1.9 %shard_map.86 = (bf16[4,128,384]{2,1,0:T(8,128)(2,1)S(1)}, bf16[4,128,384]{2,1,0:T(8,128)(2,1)S(1)}, bf16[2,2,128,384]{3,2,1,0:T(8,128)(2,1)S(1)}) custom-call(bf16[4,2,128,384]{3,2,1,0:T(8,128)(2,1)} %feat_ref.9, f32[384]{0:T(512)} %gain_ref.1), custom_call_target="tpu_custom_call" | custom-call | bytes 1000000 | tf_op jit(solution)/shard_map/pallas_call | solution.py:38
  2.5 4.1 %collective-permute-start = (bf16[2,2,128,384]{3,2,1,0:T(8,128)(2,1)S(1)}, bf16[2,2,128,384]{3,2,1,0:T(8,128)(2,1)S(1)}, u32[]{:S(2)}, u32[]{:S(2)}) collective-permute-start(bf16[2,2,128,384]{3,2,1,0:T(8,128)(2,1)S(1)} %get-tuple-element.25), channel_id=1, source_target_pairs={{0,32},{32,64},{64,96},{1,33},{33,65},{65,97},{2,34},{34,66},{66,9... | collective-permute-start | bytes 1179656 | tf_op jit(solution)/shard_map/ppermute | solution.py:30
  6.6 7.3 %collective-permute-start.2 = (bf16[4,128,384]{2,1,0:T(8,128)(2,1)S(1)}, bf16[4,128,384]{2,1,0:T(8,128)(2,1)S(1)}, u32[]{:S(2)}, u32[]{:S(2)}) collective-permute-start(bf16[4,128,384]{2,1,0:T(8,128)(2,1)S(1)} %get-tuple-element.26.b_ref), channel_id=1, source_target_pairs={{1,2},{2,1},{3,4},{4,3},{5,6},{6,5},{7,8},{8,7},{9,10},{10,9},{11,... | collective-permute-start | bytes 1179656 | tf_op jit(solution)/shard_map/ppermute | solution.py:26
  13.9 0.1 collective-permute-start.3
  14.0 0.0 slice-start.1
  14.0 1.6 %shard_map.87 = (bf16[2,4,128,384]{3,2,1,0:T(8,128)(2,1)S(1)}, bf16[384,768]{1,0:T(8,128)(2,1)S(1)}, bf16[128,216]{1,0:T(8,128)(2,1)S(1)}) custom-call(bf16[4,128,384]{2,1,0:T(8,128)(2,1)S(1)} %get-tuple-element.27.a_ref, bf16[4,128,384]{2,1,0:T(8,128)(2,1)S(1)} %get-tuple-element.26.b_ref, bf16[27,64,128]{2,1,0:T(8,128)(2,1)} %bitcast.13, ...), custom_call_target="tpu_custom_call" | custom-call | flops 4529848320 | bytes 1000000 | tf_op jit(solution)/shard_map/pallas_call | solution.py:38
  15.6 0.0 collective-permute-done.past_ref
  15.6 1.5 %collective-permute-start.4 = (bf16[2,128,384]{2,1,0:T(8,128)(2,1)S(1)}, bf16[2,128,384]{2,1,0:T(8,128)(2,1)S(1)}, u32[]{:S(2)}, u32[]{:S(2)}) collective-permute-start(bf16[2,128,384]{2,1,0:T(8,128)(2,1)S(1)} %get-tuple-element.48), channel_id=1, source_target_pairs={{0,1},{1,0},{2,3},{3,2},{4,5},{5,4},{6,7},{7,6},{8,9},{9,8},{10,11... | collective-permute-start | bytes 589832 | tf_op jit(solution)/shard_map/ppermute | solution.py:26
  17.2 14.2 %collective-permute-start.1 = (bf16[2,128,384]{2,1,0:T(8,128)(2,1)S(1)}, bf16[2,128,384]{2,1,0:T(8,128)(2,1)S(1)}, u32[]{:S(2)}, u32[]{:S(2)}) collective-permute-start(bf16[2,128,384]{2,1,0:T(8,128)(2,1)S(1)} %get-tuple-element.49), channel_id=1, source_target_pairs={{1,2},{2,1},{3,4},{4,3},{5,6},{6,5},{7,8},{8,7},{9,10},{10,9},{11,... | collective-permute-start | bytes 589832 | tf_op jit(solution)/shard_map/ppermute | solution.py:26
  31.4 0.0 copy-start
  31.4 0.0 copy-start.1
  31.4 0.0 copy-start.2
  31.5 5.7 %shard_map.88.sums_ref = f32[2,512,1152]{2,1,0:T(8,128)S(1)} custom-call(bf16[2,4,128,384]{3,2,1,0:T(8,128)(2,1)S(1)} %get-tuple-element.28.lines_ref, bf16[2,2,128,384]{3,2,1,0:T(8,128)(2,1)S(1)} %collective-permute-done.past_ref, bf16[27,384,384]{2,1,0:T(8,128)(2,1)S(1)} %bitcast.8), custom_call_target="tpu_custom_call" | custom-call | flops 5435817984 | bytes 1000000 | tf_op jit(solution)/shard_map/pallas_call | solution.py:38
  37.1 0.0 collective-permute-done.3.line_ref
  37.2 2.1 %shard_map.89 = (f32[256,1152]{1,0:T(8,128)S(1)}, bf16[4,2,128,384]{3,2,1,0:T(8,128)(2,1)S(1)}, bf16[4,2,8,128]{3,2,1,0:T(8,128)(2,1)S(1)}) custom-call(bf16[4,128,384]{2,1,0:T(8,128)(2,1)S(1)} %collective-permute-done.3.line_ref, bf16[27,384,384]{2,1,0:T(8,128)(2,1)S(1)} %bitcast.8, f32[2,512,1152]{2,1,0:T(8,128)S(1)} %shard_map.88.sums_ref, ...), custom_call_target="tpu_custom_call" | custom-call | flops 1358954496 | bytes 1000000 | tf_op jit(solution)/shard_map/pallas_call | solution.py:38
  39.2 0.0 collective-permute-done.2.line_ref
  39.3 2.1 %shard_map.90 = (f32[256,1152]{1,0:T(8,128)S(1)}, bf16[4,2,128,384]{3,2,1,0:T(8,128)(2,1)S(1)}, bf16[4,2,8,128]{3,2,1,0:T(8,128)(2,1)S(1)}) custom-call(bf16[4,128,384]{2,1,0:T(8,128)(2,1)S(1)} %collective-permute-done.2.line_ref, bf16[27,384,384]{2,1,0:T(8,128)(2,1)S(1)} %bitcast.8, ...), custom_call_target="tpu_custom_call", output_to_operand_aliasing={{1}: (6, {}), {2}: (7, {})} | custom-call | flops 1358954496 | bytes 1000000 | tf_op jit(solution)/shard_map/pallas_call | solution.py:38
  41.4 0.0 collective-permute-done.4.past_ref
  41.4 0.9 %shard_map.91 = (bf16[4,2,128,384]{3,2,1,0:T(8,128)(2,1)S(1)}, bf16[4,2,8,128]{3,2,1,0:T(8,128)(2,1)S(1)}) custom-call(bf16[2,128,384]{2,1,0:T(8,128)(2,1)S(1)} %collective-permute-done.4.past_ref, bf16[27,384,384]{2,1,0:T(8,128)(2,1)S(1)} %bitcast.8, f32[256,1152]{1,0:T(8,128)S(1)} %get-tuple-element.32.sums_ref, ...), custom_call_target="tpu_custom_call", output_to_operand_aliasing={{0}: (6, {}), {1}: (7, {})} | custom-call | flops 452984832 | bytes 1000000 | tf_op jit(solution)/shard_map/pallas_call | solution.py:38
  42.2 0.8 %shard_map.92 = (bf16[4,2,128,384]{3,2,1,0:T(8,128)(2,1)S(1)}, bf16[4,2,8,128]{3,2,1,0:T(8,128)(2,1)S(1)}) custom-call(bf16[2,128,384]{2,1,0:T(8,128)(2,1)S(1)} %collective-permute-done.1.past_ref, bf16[27,384,384]{2,1,0:T(8,128)(2,1)S(1)} %bitcast.8, f32[256,1152]{1,0:T(8,128)S(1)} %get-tuple-element.31.sums_ref, ...), custom_call_target="tpu_custom_call", output_to_operand_aliasing={{0}: (6, {}), {1}: (7, {})} | custom-call | flops 452984832 | bytes 1000000 | tf_op jit(solution)/shard_map/pallas_call | solution.py:38
  43.0 1.9 %collective-permute-start.6 = (bf16[4,2,8,128]{3,2,1,0:T(8,128)(2,1)S(1)}, bf16[4,2,8,128]{3,2,1,0:T(8,128)(2,1)S(1)}, u32[]{:S(2)}, u32[]{:S(2)}) collective-permute-start(bf16[4,2,8,128]{3,2,1,0:T(8,128)(2,1)S(1)} %get-tuple-element.38.own_ref), channel_id=1, source_target_pairs={{1,2},{2,1},{3,4},{4,3},{5,6},{6,5},{7,8},{8,7},{9,10},{10,9},{11,... | collective-permute-start | bytes 49160 | tf_op jit(solution)/shard_map/ppermute | solution.py:26
  45.0 0.1 collective-permute-start.5
  45.1 7.0 %collective-permute-done.6.b_ref = bf16[4,2,8,128]{3,2,1,0:T(8,128)(2,1)S(1)} collective-permute-done((bf16[4,2,8,128]{3,2,1,0:T(8,128)(2,1)S(1)}, bf16[4,2,8,128]{3,2,1,0:T(8,128)(2,1)S(1)}, u32[]{:S(2)}, u32[]{:S(2)}) %collective-permute-start.6) | collective-permute-done | bytes 16416 | tf_op jit(solution)/shard_map/ppermute | solution.py:26
  52.0 0.0 collective-permute-done.5.a_ref
  52.1 0.1 collective-permute-start.7
  52.1 5.2 %collective-permute-start.8 = (bf16[2,6,8,128]{3,2,1,0:T(8,128)(2,1)S(1)}, bf16[2,6,8,128]{3,2,1,0:T(8,128)(2,1)S(1)}, u32[]{:S(2)}, u32[]{:S(2)}) collective-permute-start(bf16[2,6,8,128]{3,2,1,0:T(8,128)(2,1)S(1)} %get-tuple-element.40), channel_id=1, source_target_pairs={{32,64},{64,32},{33,65},{65,33},{34,66},{66,34},{35,67},{67,35},{3... | collective-permute-start | bytes 73736 | tf_op jit(solution)/shard_map/ppermute | solution.py:26
  57.4 0.9 %shard_map.93 = bf16[4,2,128,384]{3,2,1,0:T(8,128)(2,1)} custom-call(bf16[4,2,128,384]{3,2,1,0:T(8,128)(2,1)S(1)} %get-tuple-element.37.decoded_ref), custom_call_target="tpu_custom_call" | custom-call | bytes 1000000 | tf_op jit(solution)/shard_map/pallas_call | solution.py:38
  58.3 1.1 %shard_map.95 = (f32[8,6,24,128]{3,2,1,0:T(8,128)S(1)}, bf16[6,4,128,128]{3,2,1,0:T(8,128)(2,1)S(1)}, f32[8,128]{1,0:T(8,128)S(1)}, f32[4,384,512]{2,1,0:T(8,128)S(1)}) custom-call(bf16[4,2,8,128]{3,2,1,0:T(8,128)(2,1)S(1)} %collective-permute-done.5.a_ref, bf16[4,2,8,128]{3,2,1,0:T(8,128)(2,1)S(1)} %get-tuple-element.38.own_ref, ...), custom_call_target="tpu_custom_call" | custom-call | bytes 1000000 | tf_op jit(solution)/shard_map/pallas_call | solution.py:38
  59.3 0.0 collective-permute-done.7.ta_ref
  59.4 0.0 collective-permute-done.8.tb_ref
  59.4 2.0 %shard_map.96 = (f32[4,2,128]{2,1,0:T(2,128)}, f32[8,6,24,128]{3,2,1,0:T(8,128)S(1)}, bf16[6,4,128,128]{3,2,1,0:T(8,128)(2,1)S(1)}, f32[8,128]{1,0:T(8,128)S(1)}) custom-call(bf16[2,6,8,128]{3,2,1,0:T(8,128)(2,1)S(1)} %collective-permute-done.7.ta_ref, ...), custom_call_target="tpu_custom_call", output_to_operand_aliasing={{1}: (5, {}), {2}: (6, {}), {3}: (7, {})} | custom-call | bytes 1000000 | tf_op jit(solution)/shard_map/pallas_call | solution.py:38
  (9 shorter events, 0.1 us)
Async XLA Ops:
  0.6 30.8 %slice-start = ((s8[7962624]{0:T(1024)(128)(4,1)}), s8[4194304]{0:T(1024)(128)(4,1)S(1)}, s32[]{:S(2)}) async-start(s8[7962624]{0:T(1024)(128)(4,1)} %bitcast.7), calls=%async_computation | async-start | bytes 8388608
  2.5 13.1 %collective-permute-start = (bf16[2,2,128,384]{3,2,1,0:T(8,128)(2,1)S(1)}, bf16[2,2,128,384]{3,2,1,0:T(8,128)(2,1)S(1)}, u32[]{:S(2)}, u32[]{:S(2)}) collective-permute-start(bf16[2,2,128,384]{3,2,1,0:T(8,128)(2,1)S(1)} %get-tuple-element.25), channel_id=1, source_target_pairs={{0,32},{32,64},{64,96},{1,33},{33,65},{65,97},{2,34},{34,66},{66,9... | collective-permute-start | bytes 1179656 | tf_op jit(solution)/shard_map/ppermute | solution.py:30
  6.6 32.6 %collective-permute-start.2 = (bf16[4,128,384]{2,1,0:T(8,128)(2,1)S(1)}, bf16[4,128,384]{2,1,0:T(8,128)(2,1)S(1)}, u32[]{:S(2)}, u32[]{:S(2)}) collective-permute-start(bf16[4,128,384]{2,1,0:T(8,128)(2,1)S(1)} %get-tuple-element.26.b_ref), channel_id=1, source_target_pairs={{1,2},{2,1},{3,4},{4,3},{5,6},{6,5},{7,8},{8,7},{9,10},{10,9},{11,... | collective-permute-start | bytes 1179656 | tf_op jit(solution)/shard_map/ppermute | solution.py:26
  13.9 23.2 %collective-permute-start.3 = (bf16[4,128,384]{2,1,0:T(8,128)(2,1)S(1)}, bf16[4,128,384]{2,1,0:T(8,128)(2,1)S(1)}, u32[]{:S(2)}, u32[]{:S(2)}) collective-permute-start(bf16[4,128,384]{2,1,0:T(8,128)(2,1)S(1)} %get-tuple-element.27.a_ref), channel_id=1, source_target_pairs={{0,1},{1,0},{2,3},{3,2},{4,5},{5,4},{6,7},{7,6},{8,9},{9,8},{10,11... | collective-permute-start | bytes 1179656 | tf_op jit(solution)/shard_map/ppermute | solution.py:26
  14.0 17.4 %slice-start.1 = ((s8[7962624]{0:T(1024)(128)(4,1)}), s8[3768320]{0:T(1024)(128)(4,1)S(1)}, s32[]{:S(2)}) async-start(s8[7962624]{0:T(1024)(128)(4,1)} %bitcast.7), calls=%async_computation.1 | async-start | bytes 7536640
  15.6 25.7 %collective-permute-start.4 = (bf16[2,128,384]{2,1,0:T(8,128)(2,1)S(1)}, bf16[2,128,384]{2,1,0:T(8,128)(2,1)S(1)}, u32[]{:S(2)}, u32[]{:S(2)}) collective-permute-start(bf16[2,128,384]{2,1,0:T(8,128)(2,1)S(1)} %get-tuple-element.48), channel_id=1, source_target_pairs={{0,1},{1,0},{2,3},{3,2},{4,5},{5,4},{6,7},{7,6},{8,9},{9,8},{10,11... | collective-permute-start | bytes 589832 | tf_op jit(solution)/shard_map/ppermute | solution.py:26
  17.2 25.0 %collective-permute-start.1 = (bf16[2,128,384]{2,1,0:T(8,128)(2,1)S(1)}, bf16[2,128,384]{2,1,0:T(8,128)(2,1)S(1)}, u32[]{:S(2)}, u32[]{:S(2)}) collective-permute-start(bf16[2,128,384]{2,1,0:T(8,128)(2,1)S(1)} %get-tuple-element.49), channel_id=1, source_target_pairs={{1,2},{2,1},{3,4},{4,3},{5,6},{6,5},{7,8},{8,7},{9,10},{10,9},{11,... | collective-permute-start | bytes 589832 | tf_op jit(solution)/shard_map/ppermute | solution.py:26
  31.4 5.7 %copy-start = (bf16[4,2,128,384]{3,2,1,0:T(8,128)(2,1)S(1)}, bf16[4,2,128,384]{3,2,1,0:T(8,128)(2,1)}, u32[]{:S(2)}) copy-start(bf16[4,2,128,384]{3,2,1,0:T(8,128)(2,1)} %feat_ref.9) | copy-start | bytes 2359300
  31.4 5.7 %copy-start.1 = (bf16[3,4,2,128]{3,2,1,0:T(2,128)(2,1)S(1)}, bf16[3,4,2,128]{3,2,1,0:T(2,128)(2,1)}, u32[]{:S(2)}) copy-start(bf16[3,4,2,128]{3,2,1,0:T(2,128)(2,1)} %real_ref.7) | copy-start | bytes 18436
  31.4 5.7 %copy-start.2 = (bf16[384,3]{0,1:T(4,128)(2,1)S(1)}, bf16[384,3]{0,1:T(4,128)(2,1)}, u32[]{:S(2)}) copy-start(bf16[384,3]{0,1:T(4,128)(2,1)} %param.10) | copy-start | bytes 6916
  43.0 9.0 %collective-permute-start.6 = (bf16[4,2,8,128]{3,2,1,0:T(8,128)(2,1)S(1)}, bf16[4,2,8,128]{3,2,1,0:T(8,128)(2,1)S(1)}, u32[]{:S(2)}, u32[]{:S(2)}) collective-permute-start(bf16[4,2,8,128]{3,2,1,0:T(8,128)(2,1)S(1)} %get-tuple-element.38.own_ref), channel_id=1, source_target_pairs={{1,2},{2,1},{3,4},{4,3},{5,6},{6,5},{7,8},{8,7},{9,10},{10,9},{11,... | collective-permute-start | bytes 49160 | tf_op jit(solution)/shard_map/ppermute | solution.py:26
  45.0 7.1 %collective-permute-start.5 = (bf16[4,2,8,128]{3,2,1,0:T(8,128)(2,1)S(1)}, bf16[4,2,8,128]{3,2,1,0:T(8,128)(2,1)S(1)}, u32[]{:S(2)}, u32[]{:S(2)}) collective-permute-start(bf16[4,2,8,128]{3,2,1,0:T(8,128)(2,1)S(1)} %get-tuple-element.38.own_ref), channel_id=1, source_target_pairs={{0,1},{1,0},{2,3},{3,2},{4,5},{5,4},{6,7},{7,6},{8,9},{9,8},{10,11... | collective-permute-start | bytes 49160 | tf_op jit(solution)/shard_map/ppermute | solution.py:26
  52.1 7.3 %collective-permute-start.7 = (bf16[2,6,8,128]{3,2,1,0:T(8,128)(2,1)S(1)}, bf16[2,6,8,128]{3,2,1,0:T(8,128)(2,1)S(1)}, u32[]{:S(2)}, u32[]{:S(2)}) collective-permute-start(bf16[2,6,8,128]{3,2,1,0:T(8,128)(2,1)S(1)} %get-tuple-element.39), channel_id=1, source_target_pairs={{0,32},{32,0},{64,96},{96,64},{1,33},{33,1},{65,97},{97,65},{2,34}... | collective-permute-start | bytes 73736 | tf_op jit(solution)/shard_map/ppermute | solution.py:26
  52.1 7.2 %collective-permute-start.8 = (bf16[2,6,8,128]{3,2,1,0:T(8,128)(2,1)S(1)}, bf16[2,6,8,128]{3,2,1,0:T(8,128)(2,1)S(1)}, u32[]{:S(2)}, u32[]{:S(2)}) collective-permute-start(bf16[2,6,8,128]{3,2,1,0:T(8,128)(2,1)S(1)} %get-tuple-element.40), channel_id=1, source_target_pairs={{32,64},{64,32},{33,65},{65,33},{34,66},{66,34},{35,67},{67,35},{3... | collective-permute-start | bytes 73736 | tf_op jit(solution)/shard_map/ppermute | solution.py:26

commit v12 on v11

--- a/solution.py
+++ b/solution.py
@@ -57,27 +57,61 @@
     return jnp.maximum(value, 0.2 * value)
 
 
-def act_kernel(feat_ref, gain_ref, to_a_ref, to_b_ref, tail_ref, feats_ref, scale_ref, sems):
+def activation(feats, gain):
+    feats = feats.astype(F32)
+    mean = jnp.mean(feats * feats, axis=-1, keepdims=True)
+    normed = feats * lax.rsqrt(mean + 1e-06) * gain
+    return (normed * jax.nn.sigmoid(normed)).astype(BF16)
+
+
+def tail_kernel(feat_ref, gain_ref, tail_ref, feats_ref, scale_ref, sems):
     odd = lax.rem(lax.axis_index("rows"), 2)
     frames = feat_ref.shape[0]
-    order = [frames - 2, frames - 1] + list(range(frames - 2))
-    fetch_gain = pltpu.make_async_copy(gain_ref, scale_ref, sems.at[frames])
-    fetch = [pltpu.make_async_copy(feat_ref.at[t], feats_ref.at[t], sems.at[t]) for t in range(frames)]
-    fetch_gain.start()
-    for t in order:
-        fetch[t].start()
-    fetch_gain.wait()
-    gain = scale_ref[...]
-    for t in order:
-        fetch[t].wait()
-        for k, (row, out_ref) in enumerate(((1 - odd, to_a_ref), (odd, to_b_ref))):
-            feats = feats_ref[t, row].astype(F32)
-            mean = jnp.mean(feats * feats, axis=-1, keepdims=True)
-            normed = feats * lax.rsqrt(mean + 1e-06) * gain
-            act = (normed * jax.nn.sigmoid(normed)).astype(BF16)
+    loads = [
+        pltpu.make_async_copy(feat_ref.at[frames - 2 + t], feats_ref.at[t], sems.at[t])
+        for t in range(2)
+    ]
+    loads.append(pltpu.make_async_copy(gain_ref, scale_ref, sems.at[2]))
+    for load in reversed(loads):
+        load.start()
+    loads[2].wait()
+    for t in reversed(range(2)):
+        loads[t].wait()
+        for k, row in enumerate((1 - odd, odd)):
+            tail_ref[k, t] = activation(feats_ref[t, row], scale_ref[...])
+
+
+def act_kernel(
+    feat_ref, gain_ref, tail_ref, second_ref, first_ref,
+    to_a_ref, to_b_ref, lines_ref, w2_ref, w1_ref, feats_ref, scale_ref, d2_ref, d1_ref, sems,
+):
+    odd = lax.rem(lax.axis_index("rows"), 2)
+    frames = feat_ref.shape[0]
+    loads = [pltpu.make_async_copy(gain_ref, scale_ref, sems.at[0])]
+    loads += [
+        pltpu.make_async_copy(feat_ref.at[t], feats_ref.at[t], sems.at[t + 1])
+        for t in range(frames - 2)
+    ]
+    more = [
+        pltpu.make_async_copy(second_ref, d2_ref, sems.at[frames]),
+        pltpu.make_async_copy(first_ref, d1_ref, sems.at[frames + 1]),
+    ]
+    for load in loads + more:
+        load.start()
+    for k, (row, out_ref) in enumerate(((1 - odd, to_a_ref), (odd, to_b_ref))):
+        for t in range(2):
+            out_ref[frames - 2 + t] = tail_ref[k, t]
+            lines_ref[row, frames - 2 + t] = tail_ref[k, t]
+    loads[0].wait()
+    for t in range(frames - 2):
+        loads[t + 1].wait()
+        for row, out_ref in ((1 - odd, to_a_ref), (odd, to_b_ref)):
+            act = activation(feats_ref[t, row], scale_ref[...])
             out_ref[t] = act
-            if t >= frames - 2:
-                tail_ref[k, t - frames + 2] = act
+            lines_ref[row, t] = act
+    for load in more:
+        load.wait()
+    prepare(d2_ref, d1_ref, w2_ref, w1_ref)
 
 
 def column_blocks(chans):
@@ -116,20 +150,7 @@
     store.wait()
 
 
-def prep_kernel(
-    a_ref, b_ref, second_ref, first_ref, lines_ref, w2_ref, w1_ref, d2_ref, d1_ref, sems
-):
-    loads = [
-        pltpu.make_async_copy(second_ref, d2_ref, sems.at[0]),
-        pltpu.make_async_copy(first_ref, d1_ref, sems.at[1]),
-    ]
-    for load in loads:
-        load.start()
-    odd = lax.rem(lax.axis_index("rows"), 2)
-    lines_ref[1 - odd] = a_ref[...]
-    lines_ref[odd] = b_ref[...]
-    for load in loads:
-        load.wait()
+def prepare(d2_ref, d1_ref, w2_ref, w1_ref):
     depth1, depth2 = d2_ref.shape[1:]
     for dt in range(3):
         for dw in range(3):
@@ -181,15 +202,21 @@
         decoded_ref[t, row], colour_ref[t, row] = finish(ys, feat_ref[t, row], rgb_ref[...], reals)
 
 
-def add_row(lhs, dts, row, w_ref, sums_ref, out_ref):
+def row_products(pieces, row, w_ref):
     blocks = column_blocks(w_ref.shape[1])
     for j in range(0, len(blocks), 2):
         some = blocks[j : j + 2]
-        rhs = [rhs_block(w_ref, dw, off, [(dt, 2 * row) for dt in dts]) for dw, off in some]
-        cols = slice(j * 128, (j + len(some)) * 128)
-        out_ref[:, cols] = sums_ref[:, cols] + jnp.dot(
-            lhs, rhs[0] if len(rhs) == 1 else jnp.concatenate(rhs, axis=1), preferred_element_type=F32
-        )
+        got = []
+        for lhs, dts in pieces:
+            rhs = [rhs_block(w_ref, dw, off, [(dt, 2 * row) for dt in dts]) for dw, off in some]
+            got.append(
+                jnp.dot(
+                    lhs,
+                    rhs[0] if len(rhs) == 1 else jnp.concatenate(rhs, axis=1),
+                    preferred_element_type=F32,
+                )
+            )
+        yield slice(j * 128, (j + len(some)) * 128), got
 
 
 def side_row(side):
@@ -201,16 +228,19 @@
     y_ref, decoded_ref, colour_ref, all_ref = refs[-4:]
     row = side_row(side)
     frames, width, chans = line_ref.shape
+    head = 2 * width
     zeros = jnp.zeros((width, chans), BF16)
-    line = [zeros, zeros] + [line_ref[t] for t in range(frames)]
-    lhs = jnp.concatenate(
-        [jnp.concatenate(line[dt : dt + frames], axis=0) for dt in range(3)], axis=1
-    )
-    add_row(lhs, range(3), row, w_ref, sums_ref.at[row], all_ref)
-    y_ref[...] = all_ref[: 2 * width]
+    line = [zeros] + [line_ref[t] for t in range(frames)]
+    most = jnp.concatenate(
+        [jnp.concatenate(line[dt : dt + frames], axis=0) for dt in range(2)], axis=1
+    )
+    last = jnp.concatenate([line_ref[t] for t in range(frames - 2)], axis=0)
+    for cols, (got, more) in row_products(((most, (1, 2)), (last, (0,))), row, w_ref):
+        y_ref[:, cols] = sums_ref[row, :head, cols] + got[:head]
+        all_ref[:, cols] = sums_ref[row, head:, cols] + got[head:] + more
     late = range(2, frames)
     finish_row(
-        late, row, all_ref.at[2 * width :], feat_ref, rgb_ref, real_ref, decoded_ref, colour_ref
+        late, row, all_ref, feat_ref, rgb_ref, real_ref, decoded_ref, colour_ref
     )
 
 
@@ -225,7 +255,8 @@
         ],
         axis=1,
     )
-    add_row(lhs, range(2), row, w_ref, sums_ref, all_ref)
+    for cols, (got,) in row_products(((lhs, (0, 1)),), row, w_ref):
+        all_ref[:, cols] = sums_ref[:, cols] + got
     finish_row(range(2), row, all_ref, feat_ref, rgb_ref, real_ref, decoded_ref, colour_ref)
 
 
@@ -362,40 +393,50 @@
     depth1, depth2 = disc_first.shape[1], disc_second.shape[1]
     cells = frames * width
 
-    to_a, to_b, tail = local(
-        act_kernel,
-        (kept(frames, width, chans), kept(frames, width, chans), kept(2, 2, width, chans)),
+    tail = local(
+        tail_kernel,
+        kept(2, 2, width, chans),
         (latent_feat, norm_gain),
         hbm=(0, 1),
         scratch=[
-            pltpu.VMEM(latent_feat.shape, BF16),
+            pltpu.VMEM((2, height, width, chans), BF16),
             pltpu.VMEM(norm_gain.shape, F32),
-            pltpu.SemaphoreType.DMA((frames + 1,)),
+            pltpu.SemaphoreType.DMA((3,)),
         ],
     )
     past = onward(tail, "tm")
+    line = 2 * width * chans * chans
+    to_a, to_b, lines, w2, w1 = local(
+        act_kernel,
+        (
+            kept(frames, width, chans),
+            kept(frames, width, chans),
+            kept(height, frames, width, chans),
+            kept(3 * depth2, 12 * depth1),
+            kept(2 * depth1, 27 * 8),
+        ),
+        (
+            latent_feat,
+            norm_gain,
+            tail,
+            jnp.transpose(disc_second, (0, 2, 1)),
+            jnp.transpose(disc_first, (2, 0, 1)),
+        ),
+        hbm=(0, 1, 3, 4),
+        scratch=[
+            pltpu.VMEM((frames - 2, height, width, chans), BF16),
+            pltpu.VMEM(norm_gain.shape, F32),
+            pltpu.VMEM((27, depth1, depth2), BF16),
+            pltpu.VMEM((3, 27, depth1), BF16),
+            pltpu.SemaphoreType.DMA((frames + 2,)),
+        ],
+        flops=40 * 3 * line,
+    )
     from_b = swap(to_b, "rows", 1)
     from_a = swap(to_a, "rows", 0)
     past_b = swap(past[1], "rows", 1)
     past_a = swap(past[0], "rows", 0)
 
-    line = 2 * width * chans * chans
-    lines, w2, w1 = local(
-        prep_kernel,
-        (
-            kept(height, frames, width, chans),
-            kept(3 * depth2, 12 * depth1),
-            kept(2 * depth1, 27 * 8),
-        ),
-        (to_a, to_b, jnp.transpose(disc_second, (0, 2, 1)), jnp.transpose(disc_first, (2, 0, 1))),
-        hbm=(2, 3),
-        scratch=[
-            pltpu.VMEM((27, depth1, depth2), BF16),
-            pltpu.VMEM((3, 27, depth1), BF16),
-            pltpu.SemaphoreType.DMA((2,)),
-        ],
-        flops=40 * 3 * line,
-    )
     sums = local(
         own_kernel,
         kept(height, cells, 3 * chans, dtype=F32),
@@ -412,7 +453,7 @@
             functools.partial(near_kernel, side),
             (early,) + shown,
             (row, conv_weight, sums) + rest + tuple(outs),
-            scratch=[pltpu.VMEM((cells, 3 * chans), F32)],
+            scratch=[pltpu.VMEM((cells - 2 * width, 3 * chans), F32)],
             aliases={6: 1, 7: 2} if side else {},
             flops=12 * 3 * line,
         )

time: 61.6 us -> 49.5 us (0.80)
  the two profiles are of different devices: /device:TPU:9 before, /device:TPU:17 now
where the time goes in v12:
time: 49.5 us; the launch traced here: 49 us
  starting transfers between devices  25 us (51%)
  Pallas kernels  18 us (36%)
  waiting for transfers between devices  5.09 us (10%)
  between operations  0.83 us (2%)
    ppermute x8, starting transfers between devices, swap(): return lax.ppermute(block, axis, pairs(lax.axis_size(axis), first))  20.9 us
    pallas_call x11, Pallas kernels, local(): pl.pallas_call(kernel, out_shape=outs, in_specs=[HBM if i in hbm else VME...  18 us
    ppermute x8, waiting for transfers between devices, swap(): return lax.ppermute(block, axis, pairs(lax.axis_size(axis), first))  5.08 us
    ppermute x1, starting transfers between devices, onward(): lax.ppermute(block, axis, [(i, i + 1) for i in range(lax.axis_size(axis)...  4.11 us
  transfers between devices with their start and end apart: 9, of which 4 were waited for; matrix products, arithmetic and copies ran while one was open for 0% of the time, Pallas kernels for 28%

profile of v12, /device:TPU:17, one launch (start us, length us, event | category | flops | bytes accessed | tf_op | source)
XLA Modules:
  0.0 49.0 jit_solution(2750245391465016966)
XLA Ops:
  0.6 0.0 slice-start
  0.6 1.5 %shard_map.86.tail_ref = bf16[2,2,128,384]{3,2,1,0:T(8,128)(2,1)S(1)} custom-call(bf16[4,2,128,384]{3,2,1,0:T(8,128)(2,1)} %feat_ref.11, f32[384]{0:T(512)} %gain_ref.3), custom_call_target="tpu_custom_call" | custom-call | bytes 1000000 | tf_op jit(solution)/shard_map/pallas_call | solution.py:38
  2.1 4.1 %collective-permute-start = (bf16[2,2,128,384]{3,2,1,0:T(8,128)(2,1)S(1)}, bf16[2,2,128,384]{3,2,1,0:T(8,128)(2,1)S(1)}, u32[]{:S(2)}, u32[]{:S(2)}) collective-permute-start(bf16[2,2,128,384]{3,2,1,0:T(8,128)(2,1)S(1)} %shard_map.86.tail_ref), channel_id=1, source_target_pairs={{0,32},{32,64},{64,96},{1,33},{33,65},{65,97},{2,34},{34,66},{66,9... | collective-permute-start | bytes 1179656 | tf_op jit(solution)/shard_map/ppermute | solution.py:30
  6.2 0.0 slice-start.1
  6.3 1.9 %shard_map.87 = (bf16[4,128,384]{2,1,0:T(8,128)(2,1)S(1)}, bf16[4,128,384]{2,1,0:T(8,128)(2,1)S(1)}, bf16[2,4,128,384]{3,2,1,0:T(8,128)(2,1)S(1)}, bf16[384,768]{1,0:T(8,128)(2,1)S(1)}, bf16[128,216]{1,0:T(8,128)(2,1)S(1)}) custom-call(bf16[4,2,128,384]{3,2,1,0:T(8,128)(2,1)} %feat_ref.11, f32[384]{0:T(512)} %gain_ref.3, ...), custom_call_target="tpu_custom_call" | custom-call | flops 4529848320 | bytes 1000000 | tf_op jit(solution)/shard_map/pallas_call | solution.py:38
  8.1 7.3 %collective-permute-start.2 = (bf16[4,128,384]{2,1,0:T(8,128)(2,1)S(1)}, bf16[4,128,384]{2,1,0:T(8,128)(2,1)S(1)}, u32[]{:S(2)}, u32[]{:S(2)}) collective-permute-start(bf16[4,128,384]{2,1,0:T(8,128)(2,1)S(1)} %get-tuple-element.24), channel_id=1, source_target_pairs={{1,2},{2,1},{3,4},{4,3},{5,6},{6,5},{7,8},{8,7},{9,10},{10,9},{11,... | collective-permute-start | bytes 1179656 | tf_op jit(solution)/shard_map/ppermute | solution.py:26
  15.4 0.1 collective-permute-start.3
  15.5 0.0 collective-permute-done.past_ref
  15.6 1.5 %collective-permute-start.4 = (bf16[2,128,384]{2,1,0:T(8,128)(2,1)S(1)}, bf16[2,128,384]{2,1,0:T(8,128)(2,1)S(1)}, u32[]{:S(2)}, u32[]{:S(2)}) collective-permute-start(bf16[2,128,384]{2,1,0:T(8,128)(2,1)S(1)} %get-tuple-element.46), channel_id=1, source_target_pairs={{0,1},{1,0},{2,3},{3,2},{4,5},{5,4},{6,7},{7,6},{8,9},{9,8},{10,11... | collective-permute-start | bytes 589832 | tf_op jit(solution)/shard_map/ppermute | solution.py:26
  17.1 2.5 %collective-permute-start.1 = (bf16[2,128,384]{2,1,0:T(8,128)(2,1)S(1)}, bf16[2,128,384]{2,1,0:T(8,128)(2,1)S(1)}, u32[]{:S(2)}, u32[]{:S(2)}) collective-permute-start(bf16[2,128,384]{2,1,0:T(8,128)(2,1)S(1)} %get-tuple-element.47), channel_id=1, source_target_pairs={{1,2},{2,1},{3,4},{4,3},{5,6},{6,5},{7,8},{8,7},{9,10},{10,9},{11,... | collective-permute-start | bytes 589832 | tf_op jit(solution)/shard_map/ppermute | solution.py:26
  19.6 0.0 copy-start
  19.7 0.0 copy-start.1
  19.7 0.0 copy-start.2
  19.7 5.7 %shard_map.88.sums_ref = f32[2,512,1152]{2,1,0:T(8,128)S(1)} custom-call(bf16[2,4,128,384]{3,2,1,0:T(8,128)(2,1)S(1)} %get-tuple-element.25.lines_ref, bf16[2,2,128,384]{3,2,1,0:T(8,128)(2,1)S(1)} %collective-permute-done.past_ref, bf16[27,384,384]{2,1,0:T(8,128)(2,1)S(1)} %bitcast.8), custom_call_target="tpu_custom_call" | custom-call | flops 5435817984 | bytes 1000000 | tf_op jit(solution)/shard_map/pallas_call | solution.py:38
  25.4 1.3 %collective-permute-done.3.line_ref = bf16[4,128,384]{2,1,0:T(8,128)(2,1)S(1)} collective-permute-done((bf16[4,128,384]{2,1,0:T(8,128)(2,1)S(1)}, bf16[4,128,384]{2,1,0:T(8,128)(2,1)S(1)}, u32[]{:S(2)}, u32[]{:S(2)}) %collective-permute-start.3) | collective-permute-done | bytes 393248 | tf_op jit(solution)/shard_map/ppermute | solution.py:26
  26.7 1.7 %shard_map.89 = (f32[256,1152]{1,0:T(8,128)S(1)}, bf16[4,2,128,384]{3,2,1,0:T(8,128)(2,1)S(1)}, bf16[4,2,8,128]{3,2,1,0:T(8,128)(2,1)S(1)}) custom-call(bf16[4,128,384]{2,1,0:T(8,128)(2,1)S(1)} %collective-permute-done.3.line_ref, bf16[27,384,384]{2,1,0:T(8,128)(2,1)S(1)} %bitcast.8, f32[2,512,1152]{2,1,0:T(8,128)S(1)} %shard_map.88.sums_ref, ...), custom_call_target="tpu_custom_call" | custom-call | flops 1358954496 | bytes 1000000 | tf_op jit(solution)/shard_map/pallas_call | solution.py:38
  28.3 0.0 collective-permute-done.2.line_ref
  28.4 1.7 %shard_map.90 = (f32[256,1152]{1,0:T(8,128)S(1)}, bf16[4,2,128,384]{3,2,1,0:T(8,128)(2,1)S(1)}, bf16[4,2,8,128]{3,2,1,0:T(8,128)(2,1)S(1)}) custom-call(bf16[4,128,384]{2,1,0:T(8,128)(2,1)S(1)} %collective-permute-done.2.line_ref, bf16[27,384,384]{2,1,0:T(8,128)(2,1)S(1)} %bitcast.8, ...), custom_call_target="tpu_custom_call", output_to_operand_aliasing={{1}: (6, {}), {2}: (7, {})} | custom-call | flops 1358954496 | bytes 1000000 | tf_op jit(solution)/shard_map/pallas_call | solution.py:38
  30.1 0.2 collective-permute-done.4.past_ref
  30.2 0.8 %shard_map.91 = (bf16[4,2,128,384]{3,2,1,0:T(8,128)(2,1)S(1)}, bf16[4,2,8,128]{3,2,1,0:T(8,128)(2,1)S(1)}) custom-call(bf16[2,128,384]{2,1,0:T(8,128)(2,1)S(1)} %collective-permute-done.4.past_ref, bf16[27,384,384]{2,1,0:T(8,128)(2,1)S(1)} %bitcast.8, f32[256,1152]{1,0:T(8,128)S(1)} %get-tuple-element.30.sums_ref, ...), custom_call_target="tpu_custom_call", output_to_operand_aliasing={{0}: (6, {}), {1}: (7, {})} | custom-call | flops 452984832 | bytes 1000000 | tf_op jit(solution)/shard_map/pallas_call | solution.py:38
  31.1 0.8 %shard_map.92 = (bf16[4,2,128,384]{3,2,1,0:T(8,128)(2,1)S(1)}, bf16[4,2,8,128]{3,2,1,0:T(8,128)(2,1)S(1)}) custom-call(bf16[2,128,384]{2,1,0:T(8,128)(2,1)S(1)} %collective-permute-done.1.past_ref, bf16[27,384,384]{2,1,0:T(8,128)(2,1)S(1)} %bitcast.8, f32[256,1152]{1,0:T(8,128)S(1)} %get-tuple-element.29.sums_ref, ...), custom_call_target="tpu_custom_call", output_to_operand_aliasing={{0}: (6, {}), {1}: (7, {})} | custom-call | flops 452984832 | bytes 1000000 | tf_op jit(solution)/shard_map/pallas_call | solution.py:38
  31.9 5.9 %collective-permute-start.6 = (bf16[4,2,8,128]{3,2,1,0:T(8,128)(2,1)S(1)}, bf16[4,2,8,128]{3,2,1,0:T(8,128)(2,1)S(1)}, u32[]{:S(2)}, u32[]{:S(2)}) collective-permute-start(bf16[4,2,8,128]{3,2,1,0:T(8,128)(2,1)S(1)} %get-tuple-element.36.own_ref), channel_id=1, source_target_pairs={{1,2},{2,1},{3,4},{4,3},{5,6},{6,5},{7,8},{8,7},{9,10},{10,9},{11,... | collective-permute-start | bytes 49160 | tf_op jit(solution)/shard_map/ppermute | solution.py:26
  37.8 0.1 collective-permute-start.5
  37.9 3.0 %collective-permute-done.6.b_ref = bf16[4,2,8,128]{3,2,1,0:T(8,128)(2,1)S(1)} collective-permute-done((bf16[4,2,8,128]{3,2,1,0:T(8,128)(2,1)S(1)}, bf16[4,2,8,128]{3,2,1,0:T(8,128)(2,1)S(1)}, u32[]{:S(2)}, u32[]{:S(2)}) %collective-permute-start.6) | collective-permute-done | bytes 16416 | tf_op jit(solution)/shard_map/ppermute | solution.py:26
  40.9 0.0 collective-permute-done.5.a_ref
  40.9 1.0 %collective-permute-start.7 = (bf16[2,6,8,128]{3,2,1,0:T(8,128)(2,1)S(1)}, bf16[2,6,8,128]{3,2,1,0:T(8,128)(2,1)S(1)}, u32[]{:S(2)}, u32[]{:S(2)}) collective-permute-start(bf16[2,6,8,128]{3,2,1,0:T(8,128)(2,1)S(1)} %get-tuple-element.37), channel_id=1, source_target_pairs={{0,32},{32,0},{64,96},{96,64},{1,33},{33,1},{65,97},{97,65},{2,34}... | collective-permute-start | bytes 73736 | tf_op jit(solution)/shard_map/ppermute | solution.py:26
  41.9 2.5 %collective-permute-start.8 = (bf16[2,6,8,128]{3,2,1,0:T(8,128)(2,1)S(1)}, bf16[2,6,8,128]{3,2,1,0:T(8,128)(2,1)S(1)}, u32[]{:S(2)}, u32[]{:S(2)}) collective-permute-start(bf16[2,6,8,128]{3,2,1,0:T(8,128)(2,1)S(1)} %get-tuple-element.38), channel_id=1, source_target_pairs={{32,64},{64,32},{33,65},{65,33},{34,66},{66,34},{35,67},{67,35},{3... | collective-permute-start | bytes 73736 | tf_op jit(solution)/shard_map/ppermute | solution.py:26
  44.4 0.9 %shard_map.93 = bf16[4,2,128,384]{3,2,1,0:T(8,128)(2,1)} custom-call(bf16[4,2,128,384]{3,2,1,0:T(8,128)(2,1)S(1)} %get-tuple-element.35.decoded_ref), custom_call_target="tpu_custom_call" | custom-call | bytes 1000000 | tf_op jit(solution)/shard_map/pallas_call | solution.py:38
  45.3 1.1 %shard_map.95 = (f32[8,6,24,128]{3,2,1,0:T(8,128)S(1)}, bf16[6,4,128,128]{3,2,1,0:T(8,128)(2,1)S(1)}, f32[8,128]{1,0:T(8,128)S(1)}, f32[4,384,512]{2,1,0:T(8,128)S(1)}) custom-call(bf16[4,2,8,128]{3,2,1,0:T(8,128)(2,1)S(1)} %collective-permute-done.5.a_ref, bf16[4,2,8,128]{3,2,1,0:T(8,128)(2,1)S(1)} %get-tuple-element.36.own_ref, ...), custom_call_target="tpu_custom_call" | custom-call | bytes 1000000 | tf_op jit(solution)/shard_map/pallas_call | solution.py:38
  46.4 0.0 collective-permute-done.7.ta_ref
  46.4 0.6 %collective-permute-done.8.tb_ref = bf16[2,6,8,128]{3,2,1,0:T(8,128)(2,1)S(1)} collective-permute-done((bf16[2,6,8,128]{3,2,1,0:T(8,128)(2,1)S(1)}, bf16[2,6,8,128]{3,2,1,0:T(8,128)(2,1)S(1)}, u32[]{:S(2)}, u32[]{:S(2)}) %collective-permute-start.8) | collective-permute-done | bytes 24608 | tf_op jit(solution)/shard_map/ppermute | solution.py:26
  47.0 2.0 %shard_map.96 = (f32[4,2,128]{2,1,0:T(2,128)}, f32[8,6,24,128]{3,2,1,0:T(8,128)S(1)}, bf16[6,4,128,128]{3,2,1,0:T(8,128)(2,1)S(1)}, f32[8,128]{1,0:T(8,128)S(1)}) custom-call(bf16[2,6,8,128]{3,2,1,0:T(8,128)(2,1)S(1)} %collective-permute-done.7.ta_ref, ...), custom_call_target="tpu_custom_call", output_to_operand_aliasing={{1}: (5, {}), {2}: (6, {}), {3}: (7, {})} | custom-call | bytes 1000000 | tf_op jit(solution)/shard_map/pallas_call | solution.py:38
  (9 shorter events, 0.1 us)
Async XLA Ops:
  0.6 19.0 %slice-start = ((s8[7962624]{0:T(1024)(128)(4,1)}), s8[4194304]{0:T(1024)(128)(4,1)S(1)}, s32[]{:S(2)}) async-start(s8[7962624]{0:T(1024)(128)(4,1)} %bitcast.7), calls=%async_computation | async-start | bytes 8388608
  2.1 13.4 %collective-permute-start = (bf16[2,2,128,384]{3,2,1,0:T(8,128)(2,1)S(1)}, bf16[2,2,128,384]{3,2,1,0:T(8,128)(2,1)S(1)}, u32[]{:S(2)}, u32[]{:S(2)}) collective-permute-start(bf16[2,2,128,384]{3,2,1,0:T(8,128)(2,1)S(1)} %shard_map.86.tail_ref), channel_id=1, source_target_pairs={{0,32},{32,64},{64,96},{1,33},{33,65},{65,97},{2,34},{34,66},{66,9... | collective-permute-start | bytes 1179656 | tf_op jit(solution)/shard_map/ppermute | solution.py:30
  6.2 13.4 %slice-start.1 = ((s8[7962624]{0:T(1024)(128)(4,1)}), s8[3768320]{0:T(1024)(128)(4,1)S(1)}, s32[]{:S(2)}) async-start(s8[7962624]{0:T(1024)(128)(4,1)} %bitcast.7), calls=%async_computation.1 | async-start | bytes 7536640
  8.1 20.2 %collective-permute-start.2 = (bf16[4,128,384]{2,1,0:T(8,128)(2,1)S(1)}, bf16[4,128,384]{2,1,0:T(8,128)(2,1)S(1)}, u32[]{:S(2)}, u32[]{:S(2)}) collective-permute-start(bf16[4,128,384]{2,1,0:T(8,128)(2,1)S(1)} %get-tuple-element.24), channel_id=1, source_target_pairs={{1,2},{2,1},{3,4},{4,3},{5,6},{6,5},{7,8},{8,7},{9,10},{10,9},{11,... | collective-permute-start | bytes 1179656 | tf_op jit(solution)/shard_map/ppermute | solution.py:26
  15.4 11.2 %collective-permute-start.3 = (bf16[4,128,384]{2,1,0:T(8,128)(2,1)S(1)}, bf16[4,128,384]{2,1,0:T(8,128)(2,1)S(1)}, u32[]{:S(2)}, u32[]{:S(2)}) collective-permute-start(bf16[4,128,384]{2,1,0:T(8,128)(2,1)S(1)} %get-tuple-element.26), channel_id=1, source_target_pairs={{0,1},{1,0},{2,3},{3,2},{4,5},{5,4},{6,7},{7,6},{8,9},{9,8},{10,11... | collective-permute-start | bytes 1179656 | tf_op jit(solution)/shard_map/ppermute | solution.py:26
  15.6 14.6 %collective-permute-start.4 = (bf16[2,128,384]{2,1,0:T(8,128)(2,1)S(1)}, bf16[2,128,384]{2,1,0:T(8,128)(2,1)S(1)}, u32[]{:S(2)}, u32[]{:S(2)}) collective-permute-start(bf16[2,128,384]{2,1,0:T(8,128)(2,1)S(1)} %get-tuple-element.46), channel_id=1, source_target_pairs={{0,1},{1,0},{2,3},{3,2},{4,5},{5,4},{6,7},{7,6},{8,9},{9,8},{10,11... | collective-permute-start | bytes 589832 | tf_op jit(solution)/shard_map/ppermute | solution.py:26
  17.1 13.9 %collective-permute-start.1 = (bf16[2,128,384]{2,1,0:T(8,128)(2,1)S(1)}, bf16[2,128,384]{2,1,0:T(8,128)(2,1)S(1)}, u32[]{:S(2)}, u32[]{:S(2)}) collective-permute-start(bf16[2,128,384]{2,1,0:T(8,128)(2,1)S(1)} %get-tuple-element.47), channel_id=1, source_target_pairs={{1,2},{2,1},{3,4},{4,3},{5,6},{6,5},{7,8},{8,7},{9,10},{10,9},{11,... | collective-permute-start | bytes 589832 | tf_op jit(solution)/shard_map/ppermute | solution.py:26
  19.6 7.0 %copy-start = (bf16[4,2,128,384]{3,2,1,0:T(8,128)(2,1)S(1)}, bf16[4,2,128,384]{3,2,1,0:T(8,128)(2,1)}, u32[]{:S(2)}) copy-start(bf16[4,2,128,384]{3,2,1,0:T(8,128)(2,1)} %feat_ref.11) | copy-start | bytes 2359300
  19.7 7.0 %copy-start.1 = (bf16[3,4,2,128]{3,2,1,0:T(2,128)(2,1)S(1)}, bf16[3,4,2,128]{3,2,1,0:T(2,128)(2,1)}, u32[]{:S(2)}) copy-start(bf16[3,4,2,128]{3,2,1,0:T(2,128)(2,1)} %real_ref.7) | copy-start | bytes 18436
  19.7 7.0 %copy-start.2 = (bf16[384,3]{0,1:T(4,128)(2,1)S(1)}, bf16[384,3]{0,1:T(4,128)(2,1)}, u32[]{:S(2)}) copy-start(bf16[384,3]{0,1:T(4,128)(2,1)} %param.10) | copy-start | bytes 6916
  31.9 9.0 %collective-permute-start.6 = (bf16[4,2,8,128]{3,2,1,0:T(8,128)(2,1)S(1)}, bf16[4,2,8,128]{3,2,1,0:T(8,128)(2,1)S(1)}, u32[]{:S(2)}, u32[]{:S(2)}) collective-permute-start(bf16[4,2,8,128]{3,2,1,0:T(8,128)(2,1)S(1)} %get-tuple-element.36.own_ref), channel_id=1, source_target_pairs={{1,2},{2,1},{3,4},{4,3},{5,6},{6,5},{7,8},{8,7},{9,10},{10,9},{11,... | collective-permute-start | bytes 49160 | tf_op jit(solution)/shard_map/ppermute | solution.py:26
  37.8 3.1 %collective-permute-start.5 = (bf16[4,2,8,128]{3,2,1,0:T(8,128)(2,1)S(1)}, bf16[4,2,8,128]{3,2,1,0:T(8,128)(2,1)S(1)}, u32[]{:S(2)}, u32[]{:S(2)}) collective-permute-start(bf16[4,2,8,128]{3,2,1,0:T(8,128)(2,1)S(1)} %get-tuple-element.36.own_ref), channel_id=1, source_target_pairs={{0,1},{1,0},{2,3},{3,2},{4,5},{5,4},{6,7},{7,6},{8,9},{9,8},{10,11... | collective-permute-start | bytes 49160 | tf_op jit(solution)/shard_map/ppermute | solution.py:26
  40.9 5.5 %collective-permute-start.7 = (bf16[2,6,8,128]{3,2,1,0:T(8,128)(2,1)S(1)}, bf16[2,6,8,128]{3,2,1,0:T(8,128)(2,1)S(1)}, u32[]{:S(2)}, u32[]{:S(2)}) collective-permute-start(bf16[2,6,8,128]{3,2,1,0:T(8,128)(2,1)S(1)} %get-tuple-element.37), channel_id=1, source_target_pairs={{0,32},{32,0},{64,96},{96,64},{1,33},{33,1},{65,97},{97,65},{2,34}... | collective-permute-start | bytes 73736 | tf_op jit(solution)/shard_map/ppermute | solution.py:26
  41.9 5.1 %collective-permute-start.8 = (bf16[2,6,8,128]{3,2,1,0:T(8,128)(2,1)S(1)}, bf16[2,6,8,128]{3,2,1,0:T(8,128)(2,1)S(1)}, u32[]{:S(2)}, u32[]{:S(2)}) collective-permute-start(bf16[2,6,8,128]{3,2,1,0:T(8,128)(2,1)S(1)} %get-tuple-element.38), channel_id=1, source_target_pairs={{32,64},{64,32},{33,65},{65,33},{34,66},{66,34},{35,67},{67,35},{3... | collective-permute-start | bytes 73736 | tf_op jit(solution)/shard_map/ppermute | solution.py:26
